TPU v7x, 128 devices: a whole 4x4x4 slice. The times are simulated.
128 devices in a mesh: section: 2 (over core), seq: 16 (over z, y), head: 4 (over x).
Axes of the slice: x: 4, y: 4, z: 4, core: 2. Of those that a mesh axis runs over, the one named last changes fastest.
Arguments:
- query_vectors: bfloat16 [2, 2048, 8192], P('section', 'seq', 'head'), may hold values from -400 to 400
- key_vectors: bfloat16 [2, 2048, 8192], P('section', 'seq', 'head'), may hold values from -6 to 6
- value_vectors: bfloat16 [2, 2048, 8192], P('section', 'seq', 'head'), may hold values from -6 to 6
- prior_state: float32 [2, 64, 128, 128], P('section', 'head'), may hold values from -128 to 128
- doc_ids: int32 [2, 2048], P('section', 'seq'), may hold values from 0 to 3, never falling along the last dimension, each value on 1 to 1024 neighbouring positions
- norm_gain: float32 [2, 8192], P('section', 'head'), may hold values from 0.25 to 1.75
- residual: bfloat16 [2, 2048, 6144], P('section', 'head', 'seq'), may hold values from -6 to 6
- out_weight: bfloat16 [2, 8192, 6144], P('section', 'head', 'seq'), may hold values from -0.0625 to 0.0625
- enc_weight: bfloat16 [2, 6144, 32768], P('section', None, ('seq', 'head')), may hold values from -0.078125 to 0.078125
- enc_bias: float32 [2, 32768], P('section', ('seq', 'head')), may hold values from -5 to 5
Outputs:
- handoff: bfloat16 [2, 2048, 6144], P('section', 'head', 'seq')
- monitor: bfloat16 [2, 32, 32768], P('section', None, ('seq', 'head'))
Inputs may be any that keep to these rules, and one draw needn't show every extreme that they name: `doc_ids`: document numbers never fall along a section's tokens, are 0 at its first token and rise by at most 1 from one token to the next; a document has at most 1024 tokens, and one has exactly that many.
All inputs are finite; a program needn't handle non-finite values.
Results may differ from a plain program's by a relative error of at most 0.0039.
Values may be sent and summed in bfloat16 or wider, within the bound.
No kernel may reach another device: no remote copies, remote signals or barrier semaphores. Data moves between devices by JAX's collectives and lax.ppermute only.
A program may use at most 128 MiB of HBM per device.

v0:
```python
import jax
import jax.numpy as jnp
from jax import lax
from jax.sharding import PartitionSpec as P

HD = 128
POOL = 64
HDIM = 8192


epsilon = 1e-06


def entering(part, axis, combine, identity):
    place = lax.axis_index(axis)
    gathered = jax.tree.map(lambda a: lax.all_gather(a, axis), part)
    state = jax.tree.map(lambda a, e: jnp.zeros_like(a) + jnp.asarray(e, a.dtype), part, identity)

    def one(hop, state):
        return combine(
            state, jax.tree.map(lambda a: lax.dynamic_index_in_dim(a, hop, 0, False), gathered)
        )

    return lax.fori_loop(0, place, one, state)


def passed_along(x, axis, by):
    devices = lax.axis_size(axis)
    return lax.ppermute(x, axis, [(i, (i + by) % devices) for i in range(devices)])


def merge_states(first_pair, second_pair):
    first_state, first_doc = first_pair
    second_state, second_doc = second_pair
    top_doc = jnp.maximum(first_doc, second_doc)
    merged = jnp.where(first_doc == top_doc, first_state, 0.0) + jnp.where(
        second_doc == top_doc, second_state, 0.0
    )
    return (merged, top_doc)


def local(
    query_vectors,
    key_vectors,
    value_vectors,
    prior_state,
    doc_ids,
    norm_gain,
    residual,
    out_weight,
    enc_weight,
    enc_bias,
):
    highest = lax.Precision.HIGHEST
    row_count = query_vectors.shape[1]
    local_heads = query_vectors.shape[2] // HD
    queries = query_vectors[0].reshape(row_count, local_heads, HD)
    keys_block = key_vectors[0].reshape(row_count, local_heads, HD)
    values_block = value_vectors[0].reshape(row_count, local_heads, HD)
    doc_index = doc_ids[0]
    doc_float = doc_index.astype(jnp.float32)
    last_doc = doc_float[-1]
    keys_last = jnp.where(
        (doc_index == doc_index[-1])[:, None, None], keys_block, jnp.zeros_like(keys_block)
    )
    summary = jnp.einsum(
        "thd,the->hde", keys_last, values_block, preferred_element_type=jnp.float32
    )
    identity_pair = (jnp.zeros_like(summary), jnp.full((1,), -1.0, jnp.float32))
    earlier_state, earlier_last = entering(
        (summary, last_doc[None]), "seq", merge_states, identity_pair
    )
    earlier_doc = earlier_last[0]
    incoming_state, incoming_doc = merge_states(
        (prior_state[0], jnp.zeros((), jnp.float32)), (earlier_state, earlier_doc)
    )
    inter = jnp.einsum(
        "thd,hde->the", queries.astype(jnp.float32), incoming_state, precision=highest
    )
    inter = inter * (doc_float == incoming_doc).astype(jnp.float32)[:, None, None]
    scores = jnp.einsum("thd,uhd->htu", queries, keys_block, preferred_element_type=jnp.float32)
    positions = jnp.arange(row_count)
    same_doc = (positions[None, :] <= positions[:, None]) & (
        doc_index[:, None] == doc_index[None, :]
    )
    scores = jnp.where(same_doc[None, :, :], scores, 0.0)
    intra = jnp.einsum("htu,uhe->the", scores, values_block.astype(jnp.float32), precision=highest)
    attended = (inter + intra).reshape(row_count, local_heads * HD)
    total_square = lax.psum(jnp.sum(attended * attended, axis=1), "head")
    inverse_rms = lax.rsqrt(total_square / HDIM + epsilon)
    normed = (attended * inverse_rms[:, None] * norm_gain[0]).astype(jnp.bfloat16)
    projection = out_weight[0]
    partial_sums = jnp.dot(
        lax.all_gather(normed, "seq", axis=0, tiled=True),
        projection,
        preferred_element_type=jnp.float32,
    )
    own_rows = residual[0]
    encoder = enc_weight[0]
    latent_width = encoder.shape[1]
    reduced = lax.psum_scatter(partial_sums, "head", scatter_dimension=0, tiled=True)
    layer_out = (own_rows.astype(jnp.float32) + reduced).astype(jnp.bfloat16)
    features = lax.all_gather(layer_out, "head", axis=0, tiled=True)
    pre_scores = jnp.dot(
        lax.all_gather(features, "seq", axis=1, tiled=True),
        encoder,
        preferred_element_type=jnp.float32,
    )
    latent = jax.nn.relu(pre_scores + enc_bias[0])
    pooled = jnp.mean(latent.reshape(-1, POOL, latent_width), axis=1).astype(jnp.bfloat16)
    handoff, monitor = passed_along((layer_out[None], pooled[None]), "section", 1)
    return (handoff, monitor)


def solution(mesh):
    return jax.shard_map(
        local,
        mesh=mesh,
        in_specs=(
            P("section", "seq", "head"),
            P("section", "seq", "head"),
            P("section", "seq", "head"),
            P("section", "head", None, None),
            P("section", "seq"),
            P("section", "head"),
            P("section", "head", "seq"),
            P("section", "head", "seq"),
            P("section", None, ("seq", "head")),
            P("section", ("seq", "head")),
        ),
        out_specs=(P("section", "head", "seq"), P("section", None, ("seq", "head"))),
        check_vma=False,
    )
```

profile of v0, /device:TPU:1, one launch (start us, length us, event | category | flops | bytes accessed | tf_op | source)
XLA Modules:
  0.0 542.9 jit_solution(13562496052584884869)
XLA Ops:
  7.2 0.0 copy-start
  7.2 0.0 copy-start.4
  7.2 0.0 all-gather.13.cloned.1.call-start
  7.2 1.3 slice.8
  8.6 1.3 broadcast_compare_fusion
  9.9 1.3 copy.23
  11.2 1.3 copy.24
  12.5 1.5 fusion.14
  14.0 0.0 all-gather.13.cloned.1.call-update
  14.1 0.0 all-gather.7.cloned.1.call-start
  14.1 1.2 dynamic-slice
  15.4 0.7 bitcast_convert_fusion
  16.0 0.8 slice_dynamic-update-slice_fusion
  16.8 35.9 %all-reduce = f32[16]{0:T(128)S(1)} all-reduce(f32[16]{0:T(128)S(1)} %slice_dynamic-update-slice_fusion), channel_id=2, replica_groups=mesh['section'=2,'seq'=16,'head'=4] {'seq'}, use_global_device_ids=true, to_apply=%add | all-reduce | flops 16 | bytes 128
  52.8 1.1 copy.25
  53.9 0.0 copy-done.4
  53.9 0.1 fusion.23
  54.0 0.3 convolution_select_fusion
  54.3 2.2 convolution_bitcast_fusion
  56.5 72.5 %all-gather.13.cloned.1.call-done = f32[256,128,128]{2,1,0:T(8,128)} async-done(((f32[16,128,128]{2,1,0:T(8,128)}), f32[256,128,128]{2,1,0:T(8,128)}) %all-gather.13.cloned.1.call-update) | async-done | bytes 16777232 | tf_op jit(solution)/shard_map/all_gather | solution.py:16
  129.0 0.1 broadcast_in_dim.59
  129.1 0.0 copy-start.3
  129.1 3.6 multiply_reduce_fusion
  132.7 8.4 %psum.7 = f32[128]{0:T(128)S(1)} all-reduce(f32[128]{0:T(128)S(1)} %get-tuple-element.50), channel_id=1, replica_groups=mesh['section'=2,'seq'=16,'head'=4] {'head'}, use_global_device_ids=true, to_apply=%region_3.4 | all-reduce | flops 128 | bytes 1024 | tf_op jit(solution)/shard_map/psum | solution.py:89
  141.1 0.0 copy-done.3
  141.1 2.4 fusion.9
  143.5 0.0 all-gather.7.cloned.1.call-update
  143.5 0.0 copy-start.2
  143.5 0.0 reduce-scatter.2.cloned.1.call-start
  143.6 128.4 %all-gather.7.cloned.1.call-done = bf16[2048,2048]{0,1:T(8,128)(2,1)} async-done(((bf16[128,2048]{0,1:T(8,128)(2,1)}), bf16[2048,2048]{0,1:T(8,128)(2,1)}) %all-gather.7.cloned.1.call-update) | async-done | bytes 8388624 | tf_op jit(solution)/shard_map/all_gather | solution.py:94
  272.0 0.0 copy-done
  272.0 8.7 %fusion.4 = f32[2048,384]{1,0:T(8,128)} fusion(bf16[2048,2048]{0,1:T(8,128)(2,1)} %all-gather.7.cloned.1.call-done, bf16[1,2048,384]{2,1,0:T(8,128)(2,1)S(1)} %copy-done), kind=kOutput, calls=%fused_computation.6 | convolution fusion | flops 3221225472 | bytes 13107200 | tf_op jit(solution)/shard_map/dot_general | solution.py:93
  280.7 0.0 copy-start.5
  280.7 0.0 reduce-scatter.2.cloned.1.call-update
  280.7 0.0 all-gather.9.cloned.1.call-start
  280.7 38.5 %reduce-scatter.2.cloned.1.call-done = f32[512,384]{1,0:T(8,128)} async-done(((f32[2048,384]{1,0:T(8,128)}), f32[512,384]{1,0:T(8,128)}) %reduce-scatter.2.cloned.1.call-update) | async-done | bytes 786448 | tf_op jit(solution)/shard_map/reduce_scatter | solution.py:101
  319.2 0.0 copy-done.2
  319.2 1.9 fusion.12
  321.1 0.0 all-gather.9.cloned.1.call-update
  321.2 0.0 all-gather.11.cloned.1.call-start
  321.2 26.3 %all-gather.9.cloned.1.call-done = bf16[2048,384]{1,0:T(8,128)(2,1)} async-done(((bf16[512,384]{1,0:T(8,128)(2,1)}), bf16[2048,384]{1,0:T(8,128)(2,1)}) %all-gather.9.cloned.1.call-update) | async-done | bytes 1572880 | tf_op jit(solution)/shard_map/all_gather | solution.py:103
  347.5 0.0 all-gather.11.cloned.1.call-update
  347.6 0.8 collective-permute-start
  348.3 164.4 %all-gather.11.cloned.1.call-done = bf16[2048,6144]{1,0:T(8,128)(2,1)} async-done(((bf16[2048,384]{1,0:T(8,128)(2,1)}), bf16[2048,6144]{1,0:T(8,128)(2,1)}) %all-gather.11.cloned.1.call-update) | async-done | bytes 25165840 | tf_op jit(solution)/shard_map/all_gather | solution.py:105
  512.7 0.0 copy-done.5
  512.7 0.0 copy-start.1
  512.7 19.8 %bitcast_reduce_fusion = f32[32,512]{1,0:T(8,128)S(1)} fusion(bf16[2048,6144]{1,0:T(8,128)(2,1)} %all-gather.11.cloned.1.call-done, bf16[1,6144,512]{2,1,0:T(8,128)(2,1)} %param.20, f32[512]{0:T(512)S(1)} %bitcast.80), kind=kOutput, calls=%fused_computation.4 | convolution fusion | flops 12888031232 | bytes 31524864 | tf_op jit(solution)/shard_map/dot_general | solution.py:104
  532.5 1.6 collective-permute-start.1
  534.1 0.0 collective-permute-done
  534.1 0.9 collective-permute-done.1
  535.0 0.7 copy.46
  535.7 0.6 copy.47
  536.3 0.0 copy-done.1
  (5 shorter events, 0.0 us)
Async XLA Ops:
  7.2 264.8 %copy-start = (bf16[1,2048,384]{2,1,0:T(8,128)(2,1)S(1)}, bf16[1,2048,384]{2,1,0:T(8,128)(2,1)}, u32[]{:S(2)}) copy-start(bf16[1,2048,384]{2,1,0:T(8,128)(2,1)} %param.19) | copy-start | bytes 4718596
  7.2 46.7 %copy-start.4 = (s32[1,128]{1,0:T(1,128)S(1)}, s32[1,128]{1,0:T(1,128)}, u32[]{:S(2)}) copy-start(s32[1,128]{1,0:T(1,128)} %param.16) | copy-start | bytes 1540
  7.2 121.8 %all-gather.13.cloned.1.call-start = ((), (), s32[]{:S(2)}) async-start(), calls=%async_computation.5 | async-start | bytes 17825792 | tf_op jit(solution)/shard_map/all_gather | solution.py:16
  14.1 257.9 %all-gather.7.cloned.1.call-start = ((), (), s32[]{:S(2)}) async-start(), calls=%async_computation.1 | async-start | bytes 8912896 | tf_op jit(solution)/shard_map/all_gather | solution.py:94
  129.1 12.0 %copy-start.3 = (f32[1,2048]{1,0:T(1,128)S(1)}, f32[1,2048]{1,0:T(1,128)}, u32[]{:S(2)}) copy-start(f32[1,2048]{1,0:T(1,128)} %param.17) | copy-start | bytes 24580
  143.5 175.7 %copy-start.2 = (bf16[1,512,384]{2,1,0:T(8,128)(2,1)S(1)}, bf16[1,512,384]{2,1,0:T(8,128)(2,1)}, u32[]{:S(2)}) copy-start(bf16[1,512,384]{2,1,0:T(8,128)(2,1)} %param.18) | copy-start | bytes 1179652
  143.5 175.6 %reduce-scatter.2.cloned.1.call-start = ((), (), s32[]{:S(2)}) async-start(), calls=%async_computation.2 | async-start | bytes 3932160 | tf_op jit(solution)/shard_map/reduce_scatter | solution.py:101
  280.7 232.0 %copy-start.5 = (f32[1,512]{1,0:T(1,128)S(1)}, f32[1,512]{1,0:T(1,128)}, u32[]{:S(2)}) copy-start(f32[1,512]{1,0:T(1,128)} %param.21) | copy-start | bytes 6148
  280.7 66.8 %all-gather.9.cloned.1.call-start = ((), (), s32[]{:S(2)}) async-start(), calls=%async_computation.3 | async-start | bytes 1966080 | tf_op jit(solution)/shard_map/all_gather | solution.py:103
  321.2 191.5 %all-gather.11.cloned.1.call-start = ((), (), s32[]{:S(2)}) async-start(), calls=%async_computation.4 | async-start | bytes 26738688 | tf_op jit(solution)/shard_map/all_gather | solution.py:105
  347.6 186.6 %collective-permute-start = (bf16[1,512,384]{2,1,0:T(8,128)(2,1)}, bf16[1,512,384]{2,1,0:T(8,128)(2,1)S(1)}, u32[]{:S(2)}, u32[]{:S(2)}) collective-permute-start(bf16[1,512,384]{2,1,0:T(8,128)(2,1)} %bitcast.76), channel_id=1, source_target_pairs={{0,64},{64,0},{1,65},{65,1},{2,66},{66,2},{3,67},{67,3},{4,68},{68... | collective-permute-start | bytes 1179656 | tf_op jit(solution)/shard_map/ppermute | solution.py:29
  512.7 23.7 %copy-start.1 = (bf16[1,2048,384]{2,1,0:T(8,128)(2,1)S(1)}, bf16[1,2048,384]{2,1,0:T(8,128)(2,1)}, u32[]{:S(2)}) copy-start(bf16[1,2048,384]{2,1,0:T(8,128)(2,1)} %param.19) | copy-start | bytes 4718596
  532.5 2.5 collective-permute-start.1
Sparse Core Ops, SparseCore 0:
  14.2 114.7 all-gather.12
  143.7 128.2 all-gather.6
  280.8 38.3 reduce-scatter.1
  321.3 26.1 all-gather.8
  349.5 163.1 all-gather.10
where the time goes:
time: 544 us; the launch traced here: 543 us
  waiting for transfers between devices  431 us (79%)
  blocking collectives  44.3 us (8%)
  matrix products  36.1 us (7%)
  between operations  13.9 us (3%)
  local copies, waits for them, and re-layouts  8.65 us (2%)
  other arithmetic  6.43 us (1%)
    all_gather x1, waiting for transfers between devices, local(): lax.all_gather(features, 'seq', axis=1, tiled=True)  164 us
    all_gather x1, waiting for transfers between devices, local(): lax.all_gather(normed, 'seq', axis=0, tiled=True)  128 us
    all_gather x1, waiting for transfers between devices, entering(): gathered = jax.tree.map(lambda a: lax.all_gather(a, axis), part)  72.5 us
    reduce_scatter x1, waiting for transfers between devices, local(): lax.psum_scatter(partial_sums, 'head', scatter_dimension=0, tiled=True)  38.5 us
    unnamed x1, blocking collectives  35.9 us
    all_gather x1, waiting for transfers between devices, local(): features = lax.all_gather(layer_out, 'head', axis=0, tiled=True)  26.3 us
    dot_general x1, matrix products, local(): jnp.dot(lax.all_gather(features, 'seq', axis=1, tiled=True), encoder, pre...  19.8 us
  transfers between devices with their start and end apart: 7, of which 6 were waited for; matrix products, arithmetic and copies ran while one was open for 5% of the time, Pallas kernels for 0%

commit v1 on v0

v1 whole, which is shorter than its diff:
```python
import functools

import jax
import jax.numpy as jnp
from jax import lax
from jax.experimental import pallas as pl
from jax.experimental.pallas import tpu as pltpu
from jax.sharding import PartitionSpec as P

HD = 128
POOL = 64
HDIM = 8192
BLK = 128
PACK = 3 * BLK + 16

epsilon = 1e-06


def dot(a, b, dims=((1,), (0,))):
    return lax.dot_general(a, b, (dims, ((), ())), preferred_element_type=jnp.float32)


def split(x):
    high = x.astype(jnp.bfloat16)
    return high, (x - high.astype(jnp.float32)).astype(jnp.bfloat16)


def attend_kernel(packed_ref, prior_ref, out_ref):
    blocks = packed_ref.shape[0]
    row = lax.broadcasted_iota(jnp.int32, (BLK, BLK), 0)
    col = lax.broadcasted_iota(jnp.int32, (BLK, BLK), 1)
    causal = col <= row
    state = prior_ref[...]
    last = jnp.zeros((BLK, BLK), jnp.float32)
    for block in range(blocks):
        queries = packed_ref[block, 0:BLK, :]
        keys = packed_ref[block, BLK : 2 * BLK, :]
        values = packed_ref[block, 2 * BLK : 3 * BLK, :]
        along = jnp.broadcast_to(
            packed_ref[block, 3 * BLK : 3 * BLK + 16, :].astype(jnp.float32)[0:1, :], (BLK, BLK)
        )
        down = along.T
        scores = dot(queries, keys, ((1,), (1,)))
        scores = jnp.where(causal & (along == down), scores, 0.0)
        high, low = split(scores)
        intra = dot(high, values) + dot(low, values)
        high, low = split(state)
        inter = dot(queries, high) + dot(queries, low)
        attended = jnp.where(down == last, inter, 0.0) + intra
        out_ref[block * BLK : (block + 1) * BLK, :] = attended.astype(out_ref.dtype)
        newest = jnp.broadcast_to(along[:, BLK - 1 :], (BLK, BLK))
        chosen = jnp.where(down == newest, keys.astype(jnp.float32), 0.0).astype(jnp.bfloat16)
        summary = dot(chosen, values, ((0,), (0,)))
        state = jnp.where(last == newest, state, 0.0) + summary
        last = newest


def attend(packed, prior):
    blocks = packed.shape[0]
    return pl.pallas_call(
        attend_kernel,
        out_shape=jax.ShapeDtypeStruct((blocks * BLK, HD), jnp.bfloat16),
        compiler_params=pltpu.CompilerParams(vmem_limit_bytes=40 << 20),
    )(packed, prior)


def project_kernel(steps, a_ref, w0, w1, w2, w3, residual_ref, out_ref, acc, square):
    step = pl.program_id(0)

    @pl.when(step == 0)
    def _():
        acc[...] = jnp.zeros_like(acc)
        square[...] = jnp.zeros_like(square)

    for i in range(a_ref.shape[0]):
        rows = slice(i * HD, (i + 1) * HD)
        a = a_ref[i]
        w = jnp.concatenate([w[rows, :] for w in (w0, w1, w2, w3)], axis=0)
        acc[...] += dot(a, w)
        wide = a.astype(jnp.float32)
        wide = wide * wide
        total = square[...]
        for j in range(wide.shape[1] // HD):
            total = total + wide[:, j * HD : (j + 1) * HD]
        square[...] = total

    @pl.when(step == steps - 1)
    def _():
        mean = jnp.sum(square[...], axis=1, keepdims=True) / HDIM
        scaled = acc[...] * lax.rsqrt(mean + epsilon)
        out_ref[...] = (residual_ref[...].astype(jnp.float32) + scaled).astype(out_ref.dtype)


def project(gathered, weights, residual, per_step=2):
    parts, rows, depth = gathered.shape
    columns = residual.shape[1]
    steps = parts // per_step
    return pl.pallas_call(
        functools.partial(project_kernel, steps),
        grid=(steps,),
        in_specs=[pl.BlockSpec((per_step, rows, depth), lambda i: (i, 0, 0))]
        + [pl.BlockSpec((per_step * HD, columns), lambda i: (i, 0))] * 4
        + [pl.BlockSpec((rows, columns), lambda i: (0, 0))],
        out_specs=pl.BlockSpec((rows, columns), lambda i: (0, 0)),
        out_shape=jax.ShapeDtypeStruct((rows, columns), jnp.bfloat16),
        scratch_shapes=[
            pltpu.VMEM((rows, columns), jnp.float32),
            pltpu.VMEM((rows, HD), jnp.float32),
        ],
        compiler_params=pltpu.CompilerParams(vmem_limit_bytes=40 << 20),
    )(gathered, *weights, residual)


def encode_kernel(steps, a_ref, e_ref, bias_ref, out_ref, acc):
    step = pl.program_id(1)
    a = jnp.concatenate([a_ref[i, 0] for i in range(a_ref.shape[0])], axis=1)
    product = dot(a, e_ref[...])

    @pl.when(step == 0)
    def _():
        acc[...] = product

    @pl.when(step > 0)
    def _():
        acc[...] += product

    @pl.when(step == steps - 1)
    def _():
        latent = jnp.maximum(acc[...] + bias_ref[...], 0.0)
        rows, width = latent.shape
        pooled = jnp.sum(latent.reshape(rows // POOL, POOL, width), axis=1) * (1.0 / POOL)
        out_ref[...] = pooled.astype(out_ref.dtype)


def encode(features, encoder, bias, per_step=4):
    parts, groups, rows, columns = features.shape
    width = encoder.shape[1]
    steps = parts // per_step
    return pl.pallas_call(
        functools.partial(encode_kernel, steps),
        grid=(groups, steps),
        in_specs=[
            pl.BlockSpec((per_step, 1, rows, columns), lambda g, i: (i, g, 0, 0)),
            pl.BlockSpec((per_step * columns, width), lambda g, i: (i, 0)),
            pl.BlockSpec((1, width), lambda g, i: (0, 0)),
        ],
        out_specs=pl.BlockSpec((rows // POOL, width), lambda g, i: (g, 0)),
        out_shape=jax.ShapeDtypeStruct((groups * rows // POOL, width), jnp.bfloat16),
        scratch_shapes=[pltpu.VMEM((rows, width), jnp.float32)],
        compiler_params=pltpu.CompilerParams(vmem_limit_bytes=40 << 20),
    )(features, encoder, bias)


def swapped(x):
    devices = lax.axis_size("section")
    return lax.ppermute(x, "section", [(i, (i + 1) % devices) for i in range(devices)])


def local(
    query_vectors,
    key_vectors,
    value_vectors,
    prior_state,
    doc_ids,
    norm_gain,
    residual,
    out_weight,
    enc_weight,
    enc_bias,
):
    groups = lax.axis_size("head")
    group, place = lax.axis_index("head"), lax.axis_index("seq")
    local_heads = query_vectors.shape[2] // HD

    def by_head(x):
        return x[0].reshape(BLK, local_heads, HD).transpose(1, 0, 2)

    docs = jnp.broadcast_to(doc_ids.astype(jnp.bfloat16)[None], (local_heads, 16, BLK))
    packed = jnp.concatenate(
        [by_head(query_vectors), by_head(key_vectors), by_head(value_vectors), docs], axis=1
    )
    packed = lax.all_to_all(packed, "seq", 0, 0, tiled=True)
    prior = lax.dynamic_index_in_dim(prior_state[0], place, 0, False)
    attended = attend(packed, prior)

    weight = (out_weight[0].astype(jnp.float32) * norm_gain[0][:, None]).astype(jnp.bfloat16)
    weights = [weight] + [
        lax.ppermute(weight, "head", [((i + k) % groups, i) for i in range(groups)])
        for k in range(1, groups)
    ]

    rows = attended.shape[0] // groups
    own = lax.all_to_all(attended.reshape(groups, rows, HD), "head", 0, 0, tiled=True)
    own = jnp.concatenate(
        [
            lax.dynamic_index_in_dim(own, (group + k) % groups, 0, False)
            for k in range(groups)
        ],
        axis=1,
    )
    layer_out = project(lax.all_gather(own, "seq"), weights, residual[0])
    features = lax.all_gather(layer_out, ("seq", "head"))
    features = features.reshape(lax.axis_size("seq"), groups, *layer_out.shape)
    pooled = encode(features, enc_weight[0], enc_bias)
    return (swapped(layer_out[None]), swapped(pooled[None]))


def solution(mesh):
    return jax.shard_map(
        local,
        mesh=mesh,
        in_specs=(
            P("section", "seq", "head"),
            P("section", "seq", "head"),
            P("section", "seq", "head"),
            P("section", "head", None, None),
            P("section", "seq"),
            P("section", "head"),
            P("section", "head", "seq"),
            P("section", "head", "seq"),
            P("section", None, ("seq", "head")),
            P("section", ("seq", "head")),
        ),
        out_specs=(P("section", "head", "seq"), P("section", None, ("seq", "head"))),
        check_vma=False,
    )
```

time: 544 us -> 318 us (0.58)
  waiting for transfers between devices: 431 us -> 227 us
  blocking collectives: 44.3 us -> 0 us
  matrix products: 36.1 us -> 0 us
  Pallas kernels: 0 us -> 35.8 us
  starting transfers between devices: 2.58 us -> 20 us
  local copies, waits for them, and re-layouts: 8.65 us -> 15.8 us
    all_gather x4 -> x2, waiting for transfers between devices: 392 us -> 130 us  [the longest x1 130 us: local(): features = lax.all_gather(layer_out, ('seq', 'head'))]
    ppermute x2 -> x5, waiting for transfers between devices: 0.86 us -> 66.1 us  [the longest x3 65.3 us: local(): lax.ppermute(weight, 'head', [((i + k) % groups, i) for i in range(groups)])]
    reduce_scatter x1 -> x0, waiting for transfers between devices: 38.5 us -> none  [local(): lax.psum_scatter(partial_sums, 'head', scatter_dimension=0, tiled=True)]
    dot_general x6 -> x0, matrix products: 36.1 us -> none  [the longest x1 19.8 us: local(): jnp.dot(lax.all_gather(features, 'seq', axis=1, tiled=True), encoder, pre...]
    unnamed x1 -> x0, blocking collectives: 35.9 us -> none
    pallas_call x0 -> x3, Pallas kernels: none -> 35.8 us  [the longest x1 21.9 us: encode(): pl.pallas_call(functools.partial(encode_kernel, steps), grid=(groups, ste...]
    all_to_all x0 -> x2, waiting for transfers between devices: none -> 30.7 us  [the longest x1 23.8 us: local(): packed = lax.all_to_all(packed, 'seq', 0, 0, tiled=True)]
    all_to_all x0 -> x2, starting transfers between devices: none -> 12.6 us  [the longest x1 8.6 us: local(): packed = lax.all_to_all(packed, 'seq', 0, 0, tiled=True)]
  transfers between devices with their start and end apart: 7 -> 9, of which waited for: 6 -> 7; matrix products, arithmetic and copies ran while one was open for 5% -> 1% of each run, Pallas kernels for 0% -> 7%
where the time goes in v1:
time: 318 us; the launch traced here: 317 us
  waiting for transfers between devices  227 us (71%)
  Pallas kernels  35.8 us (11%)
  starting transfers between devices  20 us (6%)
  local copies, waits for them, and re-layouts  15.8 us (5%)
  between operations  14.2 us (4%)
  other arithmetic  4.75 us (1%)
    all_gather x1, waiting for transfers between devices, local(): features = lax.all_gather(layer_out, ('seq', 'head'))  130 us
    ppermute x3, waiting for transfers between devices, local(): lax.ppermute(weight, 'head', [((i + k) % groups, i) for i in range(groups)])  65.3 us
    all_to_all x1, waiting for transfers between devices, local(): packed = lax.all_to_all(packed, 'seq', 0, 0, tiled=True)  23.8 us
    pallas_call x1, Pallas kernels, encode(): pl.pallas_call(functools.partial(encode_kernel, steps), grid=(groups, ste...  21.9 us
    unnamed x29, local copies, waits for them, and re-layouts  14.9 us
    pallas_call x1, Pallas kernels, project(): pl.pallas_call(functools.partial(project_kernel, steps), grid=(steps,), i...  9.82 us
    all_to_all x1, starting transfers between devices, local(): packed = lax.all_to_all(packed, 'seq', 0, 0, tiled=True)  8.6 us
    all_to_all x1, waiting for transfers between devices, local(): lax.all_to_all(attended.reshape(groups, rows, HD), 'head', 0, 0, tiled=True)  6.93 us
  transfers between devices with their start and end apart: 9, of which 7 were waited for; matrix products, arithmetic and copies ran while one was open for 1% of the time, Pallas kernels for 7%

profile of v1, /device:TPU:1, one launch (start us, length us, event | category | flops | bytes accessed | tf_op | source)
XLA Modules:
  0.0 317.1 jit_solution(14448104488610474733)
XLA Ops:
  7.2 0.0 copy-start
  7.2 0.0 copy-start.10
  7.2 0.8 convert_bitcast_fusion
  8.0 1.3 copy.12
  9.3 0.3 copy.13
  9.6 0.0 copy-done.10
  9.6 0.3 copy.14
  9.9 0.3 copy.15
  10.1 1.3 copy.16
  11.5 0.3 copy.17
  11.8 1.3 pad_maximum_fusion
  13.1 8.6 %all-to-all-start = ((bf16[16,400,128]{2,1,0:T(8,128)(2,1)}), bf16[16,400,128]{2,1,0:T(8,128)(2,1)S(1)}, u32[]{:S(2)}, u32[]{:S(2)}) async-start(bf16[16,400,128]{2,1,0:T(8,128)(2,1)} %pad_maximum_fusion), calls=%async_computation | async-start | bytes 3276800 | tf_op jit(solution)/shard_map/all_to_all | solution.py:182
  21.7 0.0 copy-done
  21.7 23.8 %all-to-all-done.packed_ref = bf16[16,400,128]{2,1,0:T(8,128)(2,1)S(1)} async-done(((bf16[16,400,128]{2,1,0:T(8,128)(2,1)}), bf16[16,400,128]{2,1,0:T(8,128)(2,1)S(1)}, u32[]{:S(2)}, u32[]{:S(2)}) %all-to-all-start) | async-done | bytes 1638432 | tf_op jit(solution)/shard_map/all_to_all | solution.py:182
  45.5 4.1 %shard_map.113 = bf16[2048,128]{1,0:T(8,128)(2,1)} custom-call(bf16[16,400,128]{2,1,0:T(8,128)(2,1)S(1)} %all-to-all-done.packed_ref, f32[128,128]{1,0:T(8,128)S(1)} %dynamic-slice_bitcast_fusion.4.prior_ref), custom_call_target="tpu_custom_call" | custom-call | tf_op jit(solution)/shard_map/pallas_call | solution.py:60
  49.6 4.0 %all-to-all-start.1 = ((bf16[4,512,128]{2,1,0:T(8,128)(2,1)}), bf16[4,512,128]{2,1,0:T(8,128)(2,1)S(1)}, u32[]{:S(2)}, u32[]{:S(2)}) async-start(bf16[4,512,128]{2,1,0:T(8,128)(2,1)} %bitcast.8), calls=%async_computation.1 | async-start | bytes 1048576 | tf_op jit(solution)/shard_map/all_to_all | solution.py:193
  53.6 0.0 copy-start.11
  53.6 0.0 all-gather.5.cloned.1.call-start
  53.6 6.9 %all-to-all-done.1 = bf16[4,512,128]{2,1,0:T(8,128)(2,1)S(1)} async-done(((bf16[4,512,128]{2,1,0:T(8,128)(2,1)}), bf16[4,512,128]{2,1,0:T(8,128)(2,1)S(1)}, u32[]{:S(2)}, u32[]{:S(2)}) %all-to-all-start.1) | async-done | bytes 524320 | tf_op jit(solution)/shard_map/all_to_all | solution.py:193
  60.6 0.9 pad_maximum_fusion.1
  61.5 0.0 all-gather.5.cloned.1.call-update
  61.5 0.0 copy-start.8
  61.5 0.0 all-gather.7.cloned.1.call-start
  61.5 0.0 copy-done.11
  61.6 1.8 fusion.w0
  63.3 0.4 collective-permute-start.2
  63.7 1.9 collective-permute-start.1
  65.6 0.6 collective-permute-start
  66.2 30.8 %collective-permute-done.2.w3 = bf16[2048,384]{1,0:T(8,128)(2,1)S(1)} collective-permute-done((bf16[2048,384]{1,0:T(8,128)(2,1)S(1)}, bf16[2048,384]{1,0:T(8,128)(2,1)S(1)}, u32[]{:S(2)}, u32[]{:S(2)}) %collective-permute-start.2) | collective-permute-done | bytes 1572896 | tf_op jit(solution)/shard_map/ppermute | solution.py:188
  97.0 0.0 copy-start.2
  97.0 1.2 copy-done.2
  98.2 31.7 %collective-permute-done.1.w2 = bf16[2048,384]{1,0:T(8,128)(2,1)S(1)} collective-permute-done((bf16[2048,384]{1,0:T(8,128)(2,1)S(1)}, bf16[2048,384]{1,0:T(8,128)(2,1)S(1)}, u32[]{:S(2)}, u32[]{:S(2)}) %collective-permute-start.1) | collective-permute-done | bytes 1572896 | tf_op jit(solution)/shard_map/ppermute | solution.py:188
  130.0 0.0 copy-start.4
  130.0 1.1 copy-done.4
  131.1 2.7 collective-permute-done.w1
  133.9 0.0 copy-start.6
  133.9 1.2 copy-done.6
  135.0 0.0 all-gather.5.cloned.1.call-done
  135.1 0.0 copy-done.8
  135.1 0.0 copy-start.3
  135.1 1.4 copy-done.3
  136.5 0.0 copy-start.5
  136.5 1.4 copy-done.5
  137.9 0.0 copy-start.7
  137.9 1.4 copy-done.7
  139.3 0.0 copy-start.9
  139.3 9.8 %shard_map.114 = bf16[512,384]{1,0:T(8,128)(2,1)} custom-call(bf16[16,512,512]{2,1,0:T(8,128)(2,1)} %bitcast.33, bf16[2048,384]{1,0:T(8,128)(2,1)S(1)} %fusion.w0, bf16[2048,384]{1,0:T(8,128)(2,1)S(1)} %copy-done.7, bf16[2048,384]{1,0:T(8,128)(2,1)S(1)} %copy-done.5, bf16[2048,384]{1,0:T(8,128)(2,1)S(1)} %copy-done.3, bf16[512,384]{1,0:T(8,128)(2,1)S(1)} %bitcast.30), custom_call_target="tpu_custom_call" | custom-call | tf_op jit(solution)/shard_map/pallas_call | solution.py:98
  149.1 0.0 all-gather.7.cloned.1.call-update
  149.1 3.8 %collective-permute-start.3 = (bf16[1,512,384]{2,1,0:T(8,128)(2,1)}, bf16[1,512,384]{2,1,0:T(8,128)(2,1)S(1)}, u32[]{:S(2)}, u32[]{:S(2)}) collective-permute-start(bf16[1,512,384]{2,1,0:T(8,128)(2,1)} %bitcast.17), channel_id=1, source_target_pairs={{0,64},{64,0},{1,65},{65,1},{2,66},{66,2},{3,67},{67,3},{4,68},{68... | collective-permute-start | bytes 1179656 | tf_op jit(solution)/shard_map/ppermute | solution.py:156
  152.9 129.7 %all-gather.7.cloned.1.call-done = bf16[32768,384]{1,0:T(8,128)(2,1)} async-done(((bf16[512,384]{1,0:T(8,128)(2,1)}), bf16[32768,384]{1,0:T(8,128)(2,1)}) %all-gather.7.cloned.1.call-update) | async-done | bytes 25165840 | tf_op jit(solution)/shard_map/all_gather | solution.py:202
  282.6 0.0 copy-done.9
  282.6 0.0 copy-start.1
  282.6 2.8 copy-done.1
  285.4 21.9 %shard_map.115 = bf16[32,512]{1,0:T(8,128)(2,1)S(1)} custom-call(bf16[16,4,512,384]{3,2,1,0:T(8,128)(2,1)} %bitcast.32, bf16[6144,512]{1,0:T(8,128)(2,1)S(1)} %bitcast.29, f32[1,512]{1,0:T(1,128)S(1)} %copy-done.9), custom_call_target="tpu_custom_call" | custom-call | tf_op jit(solution)/shard_map/pallas_call | solution.py:139
  307.2 0.8 collective-permute-start.4
  308.0 0.0 collective-permute-done.3
  308.0 0.9 collective-permute-done.4
  308.9 0.7 copy.20
  309.6 0.6 copy.21
  (3 shorter events, 0.1 us)
Async XLA Ops:
  7.2 14.5 %copy-start = (f32[1,16,128,128]{3,2,1,0:T(8,128)S(1)}, f32[1,16,128,128]{3,2,1,0:T(8,128)}, u32[]{:S(2)}) copy-start(f32[1,16,128,128]{3,2,1,0:T(8,128)} %param.13) | copy-start | bytes 3145732
  7.2 2.4 copy-start.10
  13.1 32.4 %all-to-all-start = ((bf16[16,400,128]{2,1,0:T(8,128)(2,1)}), bf16[16,400,128]{2,1,0:T(8,128)(2,1)S(1)}, u32[]{:S(2)}, u32[]{:S(2)}) async-start(bf16[16,400,128]{2,1,0:T(8,128)(2,1)} %pad_maximum_fusion), calls=%async_computation | async-start | bytes 3276800 | tf_op jit(solution)/shard_map/all_to_all | solution.py:182
  49.6 10.9 %all-to-all-start.1 = ((bf16[4,512,128]{2,1,0:T(8,128)(2,1)}), bf16[4,512,128]{2,1,0:T(8,128)(2,1)S(1)}, u32[]{:S(2)}, u32[]{:S(2)}) async-start(bf16[4,512,128]{2,1,0:T(8,128)(2,1)} %bitcast.8), calls=%async_computation.1 | async-start | bytes 1048576 | tf_op jit(solution)/shard_map/all_to_all | solution.py:193
  53.6 7.9 %copy-start.11 = (f32[1,2048]{1,0:T(1,128)S(1)}, f32[1,2048]{1,0:T(1,128)}, u32[]{:S(2)}) copy-start(f32[1,2048]{1,0:T(1,128)} %param.15) | copy-start | bytes 24580
  53.6 81.4 %all-gather.5.cloned.1.call-start = ((), (), s32[]{:S(2)}) async-start(), calls=%async_computation.2 | async-start | bytes 8912896 | tf_op jit(solution)/shard_map/all_gather | solution.py:201
  61.5 73.6 %copy-start.8 = (bf16[1,512,384]{2,1,0:T(8,128)(2,1)S(1)}, bf16[1,512,384]{2,1,0:T(8,128)(2,1)}, u32[]{:S(2)}) copy-start(bf16[1,512,384]{2,1,0:T(8,128)(2,1)} %param.16) | copy-start | bytes 1179652
  61.5 221.1 %all-gather.7.cloned.1.call-start = ((), (), s32[]{:S(2)}) async-start(), calls=%async_computation.3 | async-start | bytes 25559040 | tf_op jit(solution)/shard_map/all_gather | solution.py:202
  63.3 33.7 %collective-permute-start.2 = (bf16[2048,384]{1,0:T(8,128)(2,1)S(1)}, bf16[2048,384]{1,0:T(8,128)(2,1)S(1)}, u32[]{:S(2)}, u32[]{:S(2)}) collective-permute-start(bf16[2048,384]{1,0:T(8,128)(2,1)S(1)} %fusion.w0), channel_id=1, source_target_pairs={{3,0},{0,1},{1,2},{2,3},{7,4},{4,5},{5,6},{6,7},{11,8},{8,9},{9,10... | collective-permute-start | bytes 4718600 | tf_op jit(solution)/shard_map/ppermute | solution.py:188
  63.7 66.3 %collective-permute-start.1 = (bf16[2048,384]{1,0:T(8,128)(2,1)S(1)}, bf16[2048,384]{1,0:T(8,128)(2,1)S(1)}, u32[]{:S(2)}, u32[]{:S(2)}) collective-permute-start(bf16[2048,384]{1,0:T(8,128)(2,1)S(1)} %fusion.w0), channel_id=1, source_target_pairs={{2,0},{3,1},{0,2},{1,3},{6,4},{7,5},{4,6},{5,7},{10,8},{11,9},{8,1... | collective-permute-start | bytes 4718600 | tf_op jit(solution)/shard_map/ppermute | solution.py:188
  65.6 68.3 %collective-permute-start = (bf16[2048,384]{1,0:T(8,128)(2,1)S(1)}, bf16[2048,384]{1,0:T(8,128)(2,1)S(1)}, u32[]{:S(2)}, u32[]{:S(2)}) collective-permute-start(bf16[2048,384]{1,0:T(8,128)(2,1)S(1)} %fusion.w0), channel_id=1, source_target_pairs={{1,0},{2,1},{3,2},{0,3},{5,4},{6,5},{7,6},{4,7},{9,8},{10,9},{11,1... | collective-permute-start | bytes 4718600 | tf_op jit(solution)/shard_map/ppermute | solution.py:188
  97.0 1.2 copy-start.2
  130.0 1.2 copy-start.4
  133.9 1.2 copy-start.6
  135.1 1.4 copy-start.3
  136.5 1.4 copy-start.5
  137.9 1.4 copy-start.7
  139.3 143.3 %copy-start.9 = (f32[1,512]{1,0:T(1,128)S(1)}, f32[1,512]{1,0:T(1,128)}, u32[]{:S(2)}) copy-start(f32[1,512]{1,0:T(1,128)} %bias_ref.1) | copy-start | bytes 6148
  149.1 158.9 %collective-permute-start.3 = (bf16[1,512,384]{2,1,0:T(8,128)(2,1)}, bf16[1,512,384]{2,1,0:T(8,128)(2,1)S(1)}, u32[]{:S(2)}, u32[]{:S(2)}) collective-permute-start(bf16[1,512,384]{2,1,0:T(8,128)(2,1)} %bitcast.17), channel_id=1, source_target_pairs={{0,64},{64,0},{1,65},{65,1},{2,66},{66,2},{3,67},{67,3},{4,68},{68... | collective-permute-start | bytes 1179656 | tf_op jit(solution)/shard_map/ppermute | solution.py:156
  282.6 2.8 copy-start.1
  307.2 1.6 collective-permute-start.4
Sparse Core Ops, SparseCore 0:
  61.6 71.0 all-gather.4
  149.2 133.2 all-gather.6

commit v2 on v1

v2 whole, which is shorter than its diff:
```python
import functools

import jax
import jax.numpy as jnp
from jax import lax
from jax.experimental import pallas as pl
from jax.experimental.pallas import tpu as pltpu
from jax.sharding import PartitionSpec as P

HD = 128
POOL = 64
HDIM = 8192
BLK = 128
PACK = 3 * BLK + 16
EXTRA = 16

epsilon = 1e-06
MIB = 1 << 20


def dot(a, b, dims=((1,), (0,))):
    return lax.dot_general(a, b, (dims, ((), ())), preferred_element_type=jnp.float32)


def split(x):
    high = x.astype(jnp.bfloat16)
    return high, (x - high.astype(jnp.float32)).astype(jnp.bfloat16)


def pack_kernel(queries_ref, keys_ref, values_ref, docs_ref, out_ref):
    docs = jnp.broadcast_to(docs_ref[...].astype(jnp.float32), (PACK - 3 * BLK, BLK))
    docs = docs.astype(out_ref.dtype)
    for head in range(out_ref.shape[0]):
        columns = slice(head * HD, (head + 1) * HD)
        out_ref[head, 0:BLK, :] = queries_ref[:, columns]
        out_ref[head, BLK : 2 * BLK, :] = keys_ref[:, columns]
        out_ref[head, 2 * BLK : 3 * BLK, :] = values_ref[:, columns]
        out_ref[head, 3 * BLK : PACK, :] = docs


def pack(queries, keys, values, docs):
    heads = queries.shape[1] // HD
    return pl.pallas_call(
        pack_kernel,
        out_shape=jax.ShapeDtypeStruct((heads, PACK, HD), jnp.bfloat16),
        compiler_params=pltpu.CompilerParams(vmem_limit_bytes=12 * MIB),
    )(queries, keys, values, docs)


def attend_kernel(packed_ref, prior_ref, gain_ref, out_ref):
    groups, per_group = out_ref.shape[0], packed_ref.shape[0] // out_ref.shape[0]
    row = lax.broadcasted_iota(jnp.int32, (BLK, BLK), 0)
    col = lax.broadcasted_iota(jnp.int32, (BLK, BLK), 1)
    causal = col <= row
    gain = gain_ref[...]
    state = prior_ref[...]
    last = jnp.zeros((BLK, BLK), jnp.float32)
    for group in range(groups):
        highs, lows = [], []
        for member in range(per_group):
            block = group * per_group + member
            queries = packed_ref[block, 0:BLK, :]
            keys = packed_ref[block, BLK : 2 * BLK, :]
            values = packed_ref[block, 2 * BLK : 3 * BLK, :]
            along = jnp.broadcast_to(
                packed_ref[block, 3 * BLK : PACK, :].astype(jnp.float32)[0:1, :], (BLK, BLK)
            )
            down = along.T
            scores = dot(queries, keys, ((1,), (1,)))
            scores = jnp.where(causal & (along == down), scores, 0.0)
            high, low = split(scores)
            intra = dot(high, values) + dot(low, values)
            high, low = split(state)
            inter = dot(queries, high) + dot(queries, low)
            attended = jnp.where(down == last, inter, 0.0) + intra
            rows = slice(member * BLK, (member + 1) * BLK)
            out_ref[group, rows, :] = (attended * gain).astype(out_ref.dtype)
            squares = jnp.sum((attended * attended).T, axis=0, keepdims=True)
            high, low = split(squares)
            highs.append(high.astype(jnp.float32))
            lows.append(low.astype(jnp.float32))
            newest = jnp.broadcast_to(along[:, BLK - 1 :], (BLK, BLK))
            chosen = jnp.where(down == newest, keys.astype(jnp.float32), 0.0)
            summary = dot(chosen.astype(jnp.bfloat16), values, ((0,), (0,)))
            state = jnp.where(last == newest, state, 0.0) + summary
            last = newest
        spare = [jnp.zeros((EXTRA - 2 * per_group, HD), jnp.float32)]
        sums = jnp.concatenate(highs + lows + spare, axis=0)
        out_ref[group, per_group * BLK :, :] = sums.astype(out_ref.dtype)


def attend(packed, prior, gain, groups):
    rows = packed.shape[0] * BLK // groups
    return pl.pallas_call(
        attend_kernel,
        out_shape=jax.ShapeDtypeStruct((groups, rows + EXTRA, HD), jnp.bfloat16),
        compiler_params=pltpu.CompilerParams(vmem_limit_bytes=12 * MIB),
    )(packed, prior, gain)


def project_kernel(steps, width, a_ref, w0, w1, w2, w3, residual_ref, out_ref, acc, square):
    step = pl.program_id(0)
    rows = residual_ref.shape[0]

    @pl.when(step == 0)
    def _():
        acc[...] = jnp.zeros_like(acc)
        square[...] = jnp.zeros_like(square)

    parts = []
    for i in range(a_ref.shape[1] // width):
        for w in (w0, w1, w2, w3):
            parts.append(w[i * HD : (i + 1) * HD, :])
    acc[...] += dot(a_ref[:rows, :], jnp.concatenate(parts, axis=0))
    sums = a_ref[rows:, :].astype(jnp.float32)
    total = square[...]
    for j in range(sums.shape[1] // HD):
        total = total + sums[:, j * HD : (j + 1) * HD]
    square[...] = total

    @pl.when(step == steps - 1)
    def _():
        blocks = rows // BLK
        for j in range(blocks):
            mean = (total[j : j + 1, :] + total[blocks + j : blocks + j + 1, :]) / HDIM
            factor = lax.rsqrt(jnp.broadcast_to(mean, (BLK, BLK)) + epsilon).T
            here = slice(j * BLK, (j + 1) * BLK)
            for c in range(acc.shape[1] // BLK):
                there = slice(c * BLK, (c + 1) * BLK)
                scaled = acc[here, there] * factor
                out_ref[here, there] = (
                    residual_ref[here, there].astype(jnp.float32) + scaled
                ).astype(out_ref.dtype)


def project(gathered, weights, residual, steps=4):
    depth = gathered.shape[1] // steps
    rows, columns = residual.shape
    return pl.pallas_call(
        functools.partial(project_kernel, steps, len(weights) * HD),
        grid=(steps,),
        in_specs=[pl.BlockSpec((rows + EXTRA, depth), lambda i: (0, i))]
        + [pl.BlockSpec((depth // len(weights), columns), lambda i: (i, 0))] * len(weights)
        + [pl.BlockSpec((rows, columns), lambda i: (0, 0))],
        out_specs=pl.BlockSpec((rows, columns), lambda i: (0, 0)),
        out_shape=jax.ShapeDtypeStruct((rows, columns), jnp.bfloat16),
        scratch_shapes=[
            pltpu.VMEM((rows, columns), jnp.float32),
            pltpu.VMEM((EXTRA, HD), jnp.float32),
        ],
        compiler_params=pltpu.CompilerParams(vmem_limit_bytes=20 * MIB),
    )(gathered, *weights, residual)


def encode_kernel(steps, a_ref, e0, e1, e2, bias_ref, out_ref, acc):
    step = pl.program_id(0)

    @pl.when(step == 0)
    def _():
        acc[...] = jnp.zeros_like(acc)

    start = 0
    for e in (e0, e1, e2):
        columns = slice(start, start + e.shape[1])
        acc[:, columns] += dot(a_ref[...], e[...])
        start += e.shape[1]

    @pl.when(step == steps - 1)
    def _():
        for i in range(out_ref.shape[0] // 8):
            pools = []
            for j in range(8 * i, 8 * i + 8):
                latent = jnp.maximum(acc[j * POOL : (j + 1) * POOL, :] + bias_ref[...], 0.0)
                pools.append(jnp.sum(latent, axis=0, keepdims=True) * (1.0 / POOL))
            out_ref[8 * i : 8 * i + 8, :] = jnp.concatenate(pools, axis=0)


def encode(features, encoders, biases, steps=8):
    rows, depth = features.shape
    width = sum(e.shape[1] for e in encoders)
    depth = depth // steps
    return pl.pallas_call(
        functools.partial(encode_kernel, steps),
        grid=(steps,),
        in_specs=[pl.BlockSpec((rows, depth), lambda i: (0, i))]
        + [pl.BlockSpec((depth, e.shape[1]), lambda i: (i, 0)) for e in encoders]
        + [pl.BlockSpec((1, width), lambda i: (0, 0))],
        out_specs=pl.BlockSpec((rows // POOL, width), lambda i: (0, 0)),
        out_shape=jax.ShapeDtypeStruct((rows // POOL, width), jnp.float32),
        scratch_shapes=[pltpu.VMEM((rows, width), jnp.float32)],
        compiler_params=pltpu.CompilerParams(vmem_limit_bytes=32 * MIB),
    )(features, *encoders, jnp.concatenate(biases, axis=1))


def local(
    query_vectors,
    key_vectors,
    value_vectors,
    prior_state,
    doc_ids,
    norm_gain,
    residual,
    out_weight,
    enc_weight,
    enc_bias,
):
    groups, sections = lax.axis_size("head"), lax.axis_size("section")
    group, place = lax.axis_index("head"), lax.axis_index("seq")

    def from_head(x, by):
        return lax.ppermute(x, "head", [((i + by) % groups, i) for i in range(groups)])

    def from_section(x, by):
        pairs = []
        for s in range(sections):
            for i in range(groups):
                target = (s + 1) % sections
                pairs.append((s * groups + (i + by) % groups, target * groups + i))
        return lax.ppermute(x, ("section", "head"), pairs)

    packed = pack(query_vectors[0], key_vectors[0], value_vectors[0], doc_ids)
    packed = lax.all_to_all(packed, "seq", 0, 0, tiled=True)
    prior = lax.dynamic_index_in_dim(prior_state[0], place, 0, False)
    gain = lax.dynamic_slice_in_dim(norm_gain, place * HD, HD, 1)
    attended = attend(packed, prior, gain, groups)

    weights = [out_weight[0]] + [from_head(out_weight[0], k) for k in range(1, groups)]
    half = enc_weight.shape[2] // 2
    encoders = [
        enc_weight[0],
        from_head(enc_weight[0][:, :half], -1),
        from_head(enc_weight[0][:, half:], 1),
    ]
    biases = [enc_bias, from_head(enc_bias[:, :half], -1), from_head(enc_bias[:, half:], 1)]

    own = lax.all_to_all(attended, "head", 0, 0, tiled=True)
    own = jnp.concatenate(
        [
            lax.dynamic_index_in_dim(own, (group + k) % groups, 0, False)
            for k in range(groups)
        ],
        axis=1,
    )
    layer_out = project(lax.all_gather(own, "seq", axis=1, tiled=True), weights, residual[0])
    both = jnp.concatenate([layer_out, from_head(layer_out, 2)], axis=0)
    features = lax.all_gather(both, "seq", axis=1, tiled=True)
    pooled = encode(features, encoders, biases).astype(jnp.bfloat16)
    pools = pooled.shape[0] // 2
    mine = from_section(pooled[:, : 2 * half], 0)
    after = from_section(pooled[:, 2 * half : 3 * half], 1)
    before = from_section(pooled[:, 3 * half :], -1)
    turned = [
        mine[:pools],
        jnp.concatenate([after[:pools], before[pools:]], axis=1),
        mine[pools:],
        jnp.concatenate([after[pools:], before[:pools]], axis=1),
    ]
    turned = jnp.stack(turned)
    monitor = jnp.concatenate(
        [
            lax.dynamic_index_in_dim(turned, (i - group) % groups, 0, False)
            for i in range(groups)
        ],
        axis=0,
    )
    return (from_section(layer_out[None], 0), monitor[None])


def solution(mesh):
    return jax.shard_map(
        local,
        mesh=mesh,
        in_specs=(
            P("section", "seq", "head"),
            P("section", "seq", "head"),
            P("section", "seq", "head"),
            P("section", "head", None, None),
            P("section", "seq"),
            P("section", "head"),
            P("section", "head", "seq"),
            P("section", "head", "seq"),
            P("section", None, ("seq", "head")),
            P("section", ("seq", "head")),
        ),
        out_specs=(P("section", "head", "seq"), P("section", None, ("seq", "head"))),
        check_vma=False,
    )
```

time: 318 us -> 308 us (0.969)
  waiting for transfers between devices: 227 us -> 201 us
  local copies, waits for them, and re-layouts: 15.8 us -> 31.9 us
  starting transfers between devices: 20 us -> 30.2 us
  Pallas kernels: 35.8 us -> 27.1 us
    all_gather x2, waiting for transfers between devices: 130 us -> 30.4 us  [the longest x1 25 us: local(): features = lax.all_gather(both, 'seq', axis=1, tiled=True)]
    ppermute x5 -> x12, waiting for transfers between devices: 66.1 us -> 140 us  [the longest x8 136 us: from_head(): lax.ppermute(x, 'head', [((i + by) % groups, i) for i in range(groups)])]
    unnamed x29 -> x43, local copies, waits for them, and re-layouts: 14.9 us -> 26.9 us
    ppermute x5 -> x12, starting transfers between devices: 7.37 us -> 17.4 us  [the longest x8 10.4 us: from_head(): lax.ppermute(x, 'head', [((i + by) % groups, i) for i in range(groups)])]
    pallas_call x3 -> x4, Pallas kernels: 35.8 us -> 27.1 us  [the longest x1 16.6 us: encode(): pl.pallas_call(functools.partial(encode_kernel, steps), grid=(steps,), in...]
    slice x0 -> x6, local copies, waits for them, and re-layouts: none -> 3.27 us  [the longest x1 3.26 us: local(): enc_weight[0][:, half:]]
  transfers between devices with their start and end apart: 9 -> 16, of which waited for: 7 -> 11; matrix products, arithmetic and copies ran while one was open for 1% -> 1% of each run, Pallas kernels for 7% -> 5%
where the time goes in v2:
time: 308 us; the launch traced here: 307 us
  waiting for transfers between devices  201 us (65%)
  local copies, waits for them, and re-layouts  31.9 us (10%)
  starting transfers between devices  30.2 us (10%)
  Pallas kernels  27.1 us (9%)
  between operations  14.3 us (5%)
    ppermute x8, waiting for transfers between devices, from_head(): lax.ppermute(x, 'head', [((i + by) % groups, i) for i in range(groups)])  136 us
    unnamed x43, local copies, waits for them, and re-layouts  26.9 us
    all_gather x1, waiting for transfers between devices, local(): features = lax.all_gather(both, 'seq', axis=1, tiled=True)  25 us
    all_to_all x1, waiting for transfers between devices, local(): packed = lax.all_to_all(packed, 'seq', 0, 0, tiled=True)  23.1 us
    pallas_call x1, Pallas kernels, encode(): pl.pallas_call(functools.partial(encode_kernel, steps), grid=(steps,), in...  16.6 us
    ppermute x8, starting transfers between devices, from_head(): lax.ppermute(x, 'head', [((i + by) % groups, i) for i in range(groups)])  10.4 us
    all_to_all x1, starting transfers between devices, local(): packed = lax.all_to_all(packed, 'seq', 0, 0, tiled=True)  8.6 us
    ppermute x4, starting transfers between devices, from_section(): return lax.ppermute(x, ('section', 'head'), pairs)  7.02 us
  transfers between devices with their start and end apart: 16, of which 11 were waited for; matrix products, arithmetic and copies ran while one was open for 1% of the time, Pallas kernels for 5%

profile of v2, /device:TPU:1, one launch (start us, length us, event | category | flops | bytes accessed | tf_op | source)
XLA Modules:
  0.0 307.0 jit_solution(9229995776806088498)
XLA Ops:
  7.2 0.0 copy-start
  7.2 1.1 copy-done.15
  8.3 1.0 copy-done.16
  9.4 1.0 copy-done.17
  10.4 0.7 copy-done.19
  11.1 0.3 shard_map.113
  11.3 1.2 copy-done.3
  12.5 8.6 %all-to-all-start = ((bf16[16,400,128]{2,1,0:T(8,128)(2,1)}), bf16[16,400,128]{2,1,0:T(8,128)(2,1)S(1)}, u32[]{:S(2)}, u32[]{:S(2)}) async-start(bf16[16,400,128]{2,1,0:T(8,128)(2,1)} %copy-done.3), calls=%async_computation | async-start | bytes 3276800 | tf_op jit(solution)/shard_map/all_to_all | solution.py:222
  21.1 0.7 constant_dynamic-slice_fusion.gain_ref
  21.8 23.1 %all-to-all-done.packed_ref = bf16[16,400,128]{2,1,0:T(8,128)(2,1)S(1)} async-done(((bf16[16,400,128]{2,1,0:T(8,128)(2,1)}), bf16[16,400,128]{2,1,0:T(8,128)(2,1)S(1)}, u32[]{:S(2)}, u32[]{:S(2)}) %all-to-all-start) | async-done | bytes 1638432 | tf_op jit(solution)/shard_map/all_to_all | solution.py:222
  44.9 4.3 %shard_map.114 = bf16[4,528,128]{2,1,0:T(8,128)(2,1)} custom-call(bf16[16,400,128]{2,1,0:T(8,128)(2,1)S(1)} %all-to-all-done.packed_ref, f32[128,128]{1,0:T(8,128)S(1)} %dynamic-slice_bitcast_fusion.4.prior_ref, f32[1,128]{1,0:T(1,128)S(1)} %constant_dynamic-slice_fusion.gain_ref), custom_call_target="tpu_custom_call" | custom-call | tf_op jit(solution)/shard_map/pallas_call | solution.py:94
  49.2 4.1 %all-to-all-start.1 = ((bf16[4,528,128]{2,1,0:T(8,128)(2,1)}), bf16[4,528,128]{2,1,0:T(8,128)(2,1)}, u32[]{:S(2)}, u32[]{:S(2)}) async-start(bf16[4,528,128]{2,1,0:T(8,128)(2,1)} %shard_map.114), calls=%async_computation.1 | async-start | bytes 1081344 | tf_op jit(solution)/shard_map/all_to_all | solution.py:236
  53.4 0.0 copy-start.8
  53.4 0.0 copy-start.18
  53.4 0.0 all-gather.3.cloned.1.call-start
  53.5 7.0 %all-to-all-done.1 = bf16[4,528,128]{2,1,0:T(8,128)(2,1)} async-done(((bf16[4,528,128]{2,1,0:T(8,128)(2,1)}), bf16[4,528,128]{2,1,0:T(8,128)(2,1)}, u32[]{:S(2)}, u32[]{:S(2)}) %all-to-all-start.1) | async-done | bytes 540704 | tf_op jit(solution)/shard_map/all_to_all | solution.py:236
  60.5 1.1 dynamic-slice_bitcast_fusion.3
  61.6 0.9 pad_maximum_fusion.1
  62.5 0.0 all-gather.3.cloned.1.call-update
  62.5 0.0 all-gather.5.cloned.1.call-start
  62.5 1.1 collective-permute-start
  63.6 1.1 collective-permute-start.1
  64.7 0.0 collective-permute-start.2
  64.7 30.0 %collective-permute-done.w1 = bf16[2048,384]{1,0:T(8,128)(2,1)S(1)} collective-permute-done((bf16[2048,384]{1,0:T(8,128)(2,1)S(1)}, bf16[2048,384]{1,0:T(8,128)(2,1)S(1)}, u32[]{:S(2)}, u32[]{:S(2)}) %collective-permute-start) | collective-permute-done | bytes 1572896 | tf_op jit(solution)/shard_map/ppermute | solution.py:211
  94.7 1.2 copy-done.9
  95.9 1.2 collective-permute-done.1.w2
  97.1 1.1 copy-done.11
  98.2 37.0 %collective-permute-done.2.w3 = bf16[2048,384]{1,0:T(8,128)(2,1)S(1)} collective-permute-done((bf16[2048,384]{1,0:T(8,128)(2,1)S(1)}, bf16[2048,384]{1,0:T(8,128)(2,1)S(1)}, u32[]{:S(2)}, u32[]{:S(2)}) %collective-permute-start.2) | collective-permute-done | bytes 1572896 | tf_op jit(solution)/shard_map/ppermute | solution.py:211
  135.2 1.2 copy-done.13
  136.4 5.4 %all-gather.3.cloned.1.call-done.a_ref = bf16[528,8192]{1,0:T(8,128)(2,1)} async-done(((bf16[528,512]{1,0:T(8,128)(2,1)}), bf16[528,8192]{1,0:T(8,128)(2,1)}) %all-gather.3.cloned.1.call-update) | async-done | bytes 8650768 | tf_op jit(solution)/shard_map/all_gather | solution.py:244
  141.9 3.5 %copy-done.2 = bf16[528,8192]{1,0:T(8,128)(2,1)S(1)} copy-done((bf16[528,8192]{1,0:T(8,128)(2,1)S(1)}, bf16[528,8192]{1,0:T(8,128)(2,1)}, u32[]{:S(2)}) %copy-start.2) | copy-done | bytes 8650776
  145.3 1.4 copy-done.10
  146.7 1.4 copy-done.12
  148.1 1.4 copy-done.14
  149.5 5.9 %shard_map.115 = bf16[512,384]{1,0:T(8,128)(2,1)S(1)} custom-call(bf16[528,8192]{1,0:T(8,128)(2,1)S(1)} %copy-done.2, bf16[2048,384]{1,0:T(8,128)(2,1)S(1)} %bitcast.41, bf16[2048,384]{1,0:T(8,128)(2,1)S(1)} %copy-done.10, bf16[2048,384]{1,0:T(8,128)(2,1)S(1)} %copy-done.12, bf16[2048,384]{1,0:T(8,128)(2,1)S(1)} %copy-done.14, bf16[512,384]{1,0:T(8,128)(2,1)S(1)} %bitcast.45), custom_call_target="tpu_custom_call" | custom-call | tf_op jit(solution)/shard_map/pallas_call | solution.py:139
  155.5 2.8 collective-permute-start.4
  158.2 7.9 %collective-permute-done.4 = bf16[512,384]{1,0:T(8,128)(2,1)S(1)} collective-permute-done((bf16[512,384]{1,0:T(8,128)(2,1)S(1)}, bf16[512,384]{1,0:T(8,128)(2,1)S(1)}, u32[]{:S(2)}, u32[]{:S(2)}) %collective-permute-start.4) | collective-permute-done | bytes 393248 | tf_op jit(solution)/shard_map/ppermute | solution.py:211
  166.1 1.0 pad_maximum_fusion
  167.1 0.0 all-gather.5.cloned.1.call-update
  167.1 0.0 copy-start.20
  167.1 3.3 %fusion = (bf16[6144,256]{1,0:T(8,128)(2,1)S(1)}, bf16[6144,256]{1,0:T(8,128)(2,1)S(1)}) fusion(bf16[6144,512]{1,0:T(8,128)(2,1)} %bitcast.35), kind=kLoop, calls=%fused_computation.19 | loop fusion | bytes 12582912 | tf_op jit(solution)/shard_map/slice | solution.py:232
  170.4 1.3 collective-permute-start.5
  171.6 1.5 collective-permute-start.6
  173.1 3.0 collective-permute-start.3
  176.1 0.0 collective-permute-start.7
  176.2 2.7 collective-permute-start.8
  178.8 60.1 %collective-permute-done.7 = f32[1,256]{1,0:T(1,128)S(1)} collective-permute-done((f32[1,256]{1,0:T(1,128)S(1)}, f32[1,256]{1,0:T(1,128)S(1)}, u32[]{:S(2)}, u32[]{:S(2)}) %collective-permute-start.7) | collective-permute-done | bytes 1056 | tf_op jit(solution)/shard_map/ppermute | solution.py:211
  238.9 0.0 collective-permute-done.8
  238.9 0.0 collective-permute-done.5.e1
  238.9 1.6 copy-done.4
  240.6 0.0 collective-permute-done.6.e2
  240.6 1.7 copy-done.6
  242.2 25.0 %all-gather.5.cloned.1.call-done.a_ref = bf16[1024,6144]{1,0:T(8,128)(2,1)} async-done(((bf16[1024,384]{1,0:T(8,128)(2,1)}), bf16[1024,6144]{1,0:T(8,128)(2,1)}) %all-gather.5.cloned.1.call-update) | async-done | bytes 12582928 | tf_op jit(solution)/shard_map/all_gather | solution.py:246
  267.2 2.8 copy-done.1
  270.0 1.9 copy-done.5
  271.9 1.9 copy-done.7
  273.8 16.6 %shard_map.116 = f32[16,1024]{1,0:T(8,128)S(1)} custom-call(bf16[1024,6144]{1,0:T(8,128)(2,1)} %all-gather.5.cloned.1.call-done.a_ref, bf16[6144,512]{1,0:T(8,128)(2,1)S(1)} %bitcast.36, bf16[6144,256]{1,0:T(8,128)(2,1)S(1)} %copy-done.5, bf16[6144,256]{1,0:T(8,128)(2,1)S(1)} %copy-done.7, f32[1,1024]{1,0:T(1,128)S(1)} %pad_maximum_fusion.3.bias_ref), custom_call_target="tpu_custom_call" | custom-call | tf_op jit(solution)/shard_map/pallas_call | solution.py:182
  290.5 3.9 %collective-permute-start.10 = (bf16[16,256]{1,0:T(8,128)(2,1)S(1)}, bf16[16,256]{1,0:T(8,128)(2,1)S(1)}, u32[]{:S(2)}, u32[]{:S(2)}) collective-permute-start(bf16[16,256]{1,0:T(8,128)(2,1)S(1)} %get-tuple-element.12), channel_id=1, source_target_pairs={{1,64},{2,65},{3,66},{0,67},{65,0},{66,1},{67,2},{64,3},{5,68},{6,... | collective-permute-start | bytes 24584 | tf_op jit(solution)/shard_map/ppermute | solution.py:219
  294.4 0.0 collective-permute-done.3
  294.4 0.1 collective-permute-start.9
  294.5 0.7 collective-permute-done.10
  295.2 3.5 %collective-permute-done.11 = bf16[16,256]{1,0:T(8,128)(2,1)S(1)} collective-permute-done((bf16[16,256]{1,0:T(8,128)(2,1)S(1)}, bf16[16,256]{1,0:T(8,128)(2,1)S(1)}, u32[]{:S(2)}, u32[]{:S(2)}) %collective-permute-start.11) | collective-permute-done | bytes 8224 | tf_op jit(solution)/shard_map/ppermute | solution.py:219
  298.8 0.6 maximum_bitcast_fusion
  299.4 0.7 copy.13
  (35 shorter events, 0.1 us)
Async XLA Ops:
  7.2 14.6 %copy-start = (f32[1,16,128,128]{3,2,1,0:T(8,128)S(1)}, f32[1,16,128,128]{3,2,1,0:T(8,128)}, u32[]{:S(2)}) copy-start(f32[1,16,128,128]{3,2,1,0:T(8,128)} %param.13) | copy-start | bytes 3145732
  7.2 1.1 copy-start.15
  8.3 1.0 copy-start.16
  9.4 1.0 copy-start.17
  10.4 0.7 copy-start.19
  11.3 1.2 copy-start.3
  12.5 32.4 %all-to-all-start = ((bf16[16,400,128]{2,1,0:T(8,128)(2,1)}), bf16[16,400,128]{2,1,0:T(8,128)(2,1)S(1)}, u32[]{:S(2)}, u32[]{:S(2)}) async-start(bf16[16,400,128]{2,1,0:T(8,128)(2,1)} %copy-done.3), calls=%async_computation | async-start | bytes 3276800 | tf_op jit(solution)/shard_map/all_to_all | solution.py:222
  49.2 11.2 %all-to-all-start.1 = ((bf16[4,528,128]{2,1,0:T(8,128)(2,1)}), bf16[4,528,128]{2,1,0:T(8,128)(2,1)}, u32[]{:S(2)}, u32[]{:S(2)}) async-start(bf16[4,528,128]{2,1,0:T(8,128)(2,1)} %shard_map.114), calls=%async_computation.1 | async-start | bytes 1081344 | tf_op jit(solution)/shard_map/all_to_all | solution.py:236
  53.4 9.2 %copy-start.8 = (bf16[1,2048,384]{2,1,0:T(8,128)(2,1)S(1)}, bf16[1,2048,384]{2,1,0:T(8,128)(2,1)}, u32[]{:S(2)}) copy-start(bf16[1,2048,384]{2,1,0:T(8,128)(2,1)} %param.17) | copy-start | bytes 4718596
  53.4 88.5 %copy-start.18 = (bf16[1,512,384]{2,1,0:T(8,128)(2,1)S(1)}, bf16[1,512,384]{2,1,0:T(8,128)(2,1)}, u32[]{:S(2)}) copy-start(bf16[1,512,384]{2,1,0:T(8,128)(2,1)} %param.16) | copy-start | bytes 1179652
  53.4 88.5 %all-gather.3.cloned.1.call-start = ((), (), s32[]{:S(2)}) async-start(), calls=%async_computation.2 | async-start | bytes 9191424 | tf_op jit(solution)/shard_map/all_gather | solution.py:244
  62.5 204.8 %all-gather.5.cloned.1.call-start = ((), (), s32[]{:S(2)}) async-start(), calls=%async_computation.3 | async-start | bytes 13369344 | tf_op jit(solution)/shard_map/all_gather | solution.py:246
  62.5 32.2 %collective-permute-start = (bf16[2048,384]{1,0:T(8,128)(2,1)S(1)}, bf16[2048,384]{1,0:T(8,128)(2,1)S(1)}, u32[]{:S(2)}, u32[]{:S(2)}) collective-permute-start(bf16[2048,384]{1,0:T(8,128)(2,1)S(1)} %bitcast.38), channel_id=1, source_target_pairs={{1,0},{2,1},{3,2},{0,3},{5,4},{6,5},{7,6},{4,7},{9,8},{10,9},{11,1... | collective-permute-start | bytes 4718600 | tf_op jit(solution)/shard_map/ppermute | solution.py:211
  63.6 33.5 %collective-permute-start.1 = (bf16[2048,384]{1,0:T(8,128)(2,1)S(1)}, bf16[2048,384]{1,0:T(8,128)(2,1)S(1)}, u32[]{:S(2)}, u32[]{:S(2)}) collective-permute-start(bf16[2048,384]{1,0:T(8,128)(2,1)S(1)} %bitcast.39), channel_id=1, source_target_pairs={{2,0},{3,1},{0,2},{1,3},{6,4},{7,5},{4,6},{5,7},{10,8},{11,9},{8,1... | collective-permute-start | bytes 4718600 | tf_op jit(solution)/shard_map/ppermute | solution.py:211
  64.7 70.5 %collective-permute-start.2 = (bf16[2048,384]{1,0:T(8,128)(2,1)S(1)}, bf16[2048,384]{1,0:T(8,128)(2,1)S(1)}, u32[]{:S(2)}, u32[]{:S(2)}) collective-permute-start(bf16[2048,384]{1,0:T(8,128)(2,1)S(1)} %bitcast.40), channel_id=1, source_target_pairs={{3,0},{0,1},{1,2},{2,3},{7,4},{4,5},{5,6},{6,7},{11,8},{8,9},{9,10... | collective-permute-start | bytes 4718600 | tf_op jit(solution)/shard_map/ppermute | solution.py:211
  94.7 1.2 copy-start.9
  97.1 1.1 copy-start.11
  135.2 1.2 copy-start.13
  141.9 3.5 %copy-start.2 = (bf16[528,8192]{1,0:T(8,128)(2,1)S(1)}, bf16[528,8192]{1,0:T(8,128)(2,1)}, u32[]{:S(2)}) copy-start(bf16[528,8192]{1,0:T(8,128)(2,1)} %all-gather.3.cloned.1.call-done.a_ref) | copy-start | bytes 25952260
  145.3 1.4 copy-start.10
  146.7 1.4 copy-start.12
  148.1 1.4 copy-start.14
  155.5 10.7 %collective-permute-start.4 = (bf16[512,384]{1,0:T(8,128)(2,1)S(1)}, bf16[512,384]{1,0:T(8,128)(2,1)S(1)}, u32[]{:S(2)}, u32[]{:S(2)}) collective-permute-start(bf16[512,384]{1,0:T(8,128)(2,1)S(1)} %shard_map.115), channel_id=1, source_target_pairs={{2,0},{3,1},{0,2},{1,3},{6,4},{7,5},{4,6},{5,7},{10,8},{11,9},{8,1... | collective-permute-start | bytes 1179656 | tf_op jit(solution)/shard_map/ppermute | solution.py:211
  167.1 9.0 %copy-start.20 = (f32[1,512]{1,0:T(1,128)S(1)}, f32[1,512]{1,0:T(1,128)}, u32[]{:S(2)}) copy-start(f32[1,512]{1,0:T(1,128)} %param.19) | copy-start | bytes 6148
  170.4 68.5 %collective-permute-start.5 = (bf16[6144,256]{1,0:T(8,128)(2,1)S(1)}, bf16[6144,256]{1,0:T(8,128)(2,1)S(1)}, u32[]{:S(2)}, u32[]{:S(2)}) collective-permute-start(bf16[6144,256]{1,0:T(8,128)(2,1)S(1)} %get-tuple-element.3), channel_id=1, source_target_pairs={{3,0},{0,1},{1,2},{2,3},{7,4},{4,5},{5,6},{6,7},{11,8},{8,9},{9,10... | collective-permute-start | bytes 9437192 | tf_op jit(solution)/shard_map/ppermute | solution.py:211
  171.6 68.9 %collective-permute-start.6 = (bf16[6144,256]{1,0:T(8,128)(2,1)S(1)}, bf16[6144,256]{1,0:T(8,128)(2,1)S(1)}, u32[]{:S(2)}, u32[]{:S(2)}) collective-permute-start(bf16[6144,256]{1,0:T(8,128)(2,1)S(1)} %get-tuple-element.2), channel_id=1, source_target_pairs={{1,0},{2,1},{3,2},{0,3},{5,4},{6,5},{7,6},{4,7},{9,8},{10,9},{11,1... | collective-permute-start | bytes 9437192 | tf_op jit(solution)/shard_map/ppermute | solution.py:211
  173.1 121.3 %collective-permute-start.3 = (bf16[1,512,384]{2,1,0:T(8,128)(2,1)S(1)}, bf16[1,512,384]{2,1,0:T(8,128)(2,1)S(1)}, u32[]{:S(2)}, u32[]{:S(2)}) collective-permute-start(bf16[1,512,384]{2,1,0:T(8,128)(2,1)S(1)} %bitcast.37), channel_id=1, source_target_pairs={{0,64},{1,65},{2,66},{3,67},{64,0},{65,1},{66,2},{67,3},{4,68},{5,... | collective-permute-start | bytes 1179656 | tf_op jit(solution)/shard_map/ppermute | solution.py:219
  176.1 62.8 %collective-permute-start.7 = (f32[1,256]{1,0:T(1,128)S(1)}, f32[1,256]{1,0:T(1,128)S(1)}, u32[]{:S(2)}, u32[]{:S(2)}) collective-permute-start(f32[1,256]{1,0:T(1,128)S(1)} %get-tuple-element.20), channel_id=1, source_target_pairs={{3,0},{0,1},{1,2},{2,3},{7,4},{4,5},{5,6},{6,7},{11,8},{8,9},{9,10... | collective-permute-start | bytes 3080 | tf_op jit(solution)/shard_map/ppermute | solution.py:211
  176.2 62.8 %collective-permute-start.8 = (f32[1,256]{1,0:T(1,128)S(1)}, f32[1,256]{1,0:T(1,128)S(1)}, u32[]{:S(2)}, u32[]{:S(2)}) collective-permute-start(f32[1,256]{1,0:T(1,128)S(1)} %get-tuple-element.21), channel_id=1, source_target_pairs={{1,0},{2,1},{3,2},{0,3},{5,4},{6,5},{7,6},{4,7},{9,8},{10,9},{11,1... | collective-permute-start | bytes 3080 | tf_op jit(solution)/shard_map/ppermute | solution.py:211
  238.9 1.6 copy-start.4
  240.6 1.7 copy-start.6
  267.2 2.8 copy-start.1
  270.0 1.9 copy-start.5
  271.9 1.9 copy-start.7
  290.5 4.7 %collective-permute-start.10 = (bf16[16,256]{1,0:T(8,128)(2,1)S(1)}, bf16[16,256]{1,0:T(8,128)(2,1)S(1)}, u32[]{:S(2)}, u32[]{:S(2)}) collective-permute-start(bf16[16,256]{1,0:T(8,128)(2,1)S(1)} %get-tuple-element.12), channel_id=1, source_target_pairs={{1,64},{2,65},{3,66},{0,67},{65,0},{66,1},{67,2},{64,3},{5,68},{6,... | collective-permute-start | bytes 24584 | tf_op jit(solution)/shard_map/ppermute | solution.py:219
  294.4 4.3 %collective-permute-start.11 = (bf16[16,256]{1,0:T(8,128)(2,1)S(1)}, bf16[16,256]{1,0:T(8,128)(2,1)S(1)}, u32[]{:S(2)}, u32[]{:S(2)}) collective-permute-start(bf16[16,256]{1,0:T(8,128)(2,1)S(1)} %get-tuple-element.13), channel_id=1, source_target_pairs={{3,64},{0,65},{1,66},{2,67},{67,0},{64,1},{65,2},{66,3},{7,68},{4,... | collective-permute-start | bytes 24584 | tf_op jit(solution)/shard_map/ppermute | solution.py:219
  294.4 4.3 %collective-permute-start.9 = (bf16[16,512]{1,0:T(8,128)(2,1)S(1)}, bf16[16,512]{1,0:T(8,128)(2,1)S(1)}, u32[]{:S(2)}, u32[]{:S(2)}) collective-permute-start(bf16[16,512]{1,0:T(8,128)(2,1)S(1)} %slice.54), channel_id=1, source_target_pairs={{0,64},{1,65},{2,66},{3,67},{64,0},{65,1},{66,2},{67,3},{4,68},{5,... | collective-permute-start | bytes 49160 | tf_op jit(solution)/shard_map/ppermute | solution.py:219
Sparse Core Ops, SparseCore 0:
  62.6 79.2 all-gather.2
  167.2 99.9 all-gather.4

commit v3 on v2

--- a/solution.py
+++ b/solution.py
@@ -25,6 +25,10 @@
 def split(x):
     high = x.astype(jnp.bfloat16)
     return high, (x - high.astype(jnp.float32)).astype(jnp.bfloat16)
+
+
+def in_hbm(x):
+    return pltpu.with_memory_space_constraint(x, pltpu.HBM)
 
 
 def pack_kernel(queries_ref, keys_ref, values_ref, docs_ref, out_ref):
@@ -44,7 +48,7 @@
         pack_kernel,
         out_shape=jax.ShapeDtypeStruct((heads, PACK, HD), jnp.bfloat16),
         compiler_params=pltpu.CompilerParams(vmem_limit_bytes=12 * MIB),
-    )(queries, keys, values, docs)
+    )(*[in_hbm(x) for x in (queries, keys, values)], docs)
 
 
 def attend_kernel(packed_ref, prior_ref, gain_ref, out_ref):
@@ -98,7 +102,7 @@
     )(packed, prior, gain)
 
 
-def project_kernel(steps, width, a_ref, w0, w1, w2, w3, residual_ref, out_ref, acc, square):
+def project_kernel(steps, a_ref, w0, w1, w2, w3, residual_ref, out_ref, acc, square):
     step = pl.program_id(0)
     rows = residual_ref.shape[0]
 
@@ -107,15 +111,13 @@
         acc[...] = jnp.zeros_like(acc)
         square[...] = jnp.zeros_like(square)
 
-    parts = []
-    for i in range(a_ref.shape[1] // width):
-        for w in (w0, w1, w2, w3):
-            parts.append(w[i * HD : (i + 1) * HD, :])
-    acc[...] += dot(a_ref[:rows, :], jnp.concatenate(parts, axis=0))
-    sums = a_ref[rows:, :].astype(jnp.float32)
     total = square[...]
-    for j in range(sums.shape[1] // HD):
-        total = total + sums[:, j * HD : (j + 1) * HD]
+    for i in range(a_ref.shape[0]):
+        parts = [w[i * HD : (i + 1) * HD, :] for w in (w0, w1, w2, w3)]
+        acc[...] += dot(a_ref[i, :rows, :], jnp.concatenate(parts, axis=0))
+        sums = a_ref[i, rows:, :].astype(jnp.float32)
+        for j in range(sums.shape[1] // HD):
+            total = total + sums[:, j * HD : (j + 1) * HD]
     square[...] = total
 
     @pl.when(step == steps - 1)
@@ -134,13 +136,14 @@
 
 
 def project(gathered, weights, residual, steps=4):
-    depth = gathered.shape[1] // steps
+    parts, _, depth = gathered.shape
+    per_step = parts // steps
     rows, columns = residual.shape
     return pl.pallas_call(
-        functools.partial(project_kernel, steps, len(weights) * HD),
+        functools.partial(project_kernel, steps),
         grid=(steps,),
-        in_specs=[pl.BlockSpec((rows + EXTRA, depth), lambda i: (0, i))]
-        + [pl.BlockSpec((depth // len(weights), columns), lambda i: (i, 0))] * len(weights)
+        in_specs=[pl.BlockSpec((per_step, rows + EXTRA, depth), lambda i: (i, 0, 0))]
+        + [pl.BlockSpec((per_step * HD, columns), lambda i: (i, 0))] * len(weights)
         + [pl.BlockSpec((rows, columns), lambda i: (0, 0))],
         out_specs=pl.BlockSpec((rows, columns), lambda i: (0, 0)),
         out_shape=jax.ShapeDtypeStruct((rows, columns), jnp.bfloat16),
@@ -149,20 +152,43 @@
             pltpu.VMEM((EXTRA, HD), jnp.float32),
         ],
         compiler_params=pltpu.CompilerParams(vmem_limit_bytes=20 * MIB),
-    )(gathered, *weights, residual)
-
-
-def encode_kernel(steps, a_ref, e0, e1, e2, bias_ref, out_ref, acc):
+    )(in_hbm(gathered), *[in_hbm(w) for w in weights], residual)
+
+
+def encode_kernel(steps, a_hbm, e0, e1, e2, bias_ref, out_ref, acc, a_buf, sems):
     step = pl.program_id(0)
+    parts, rows, width = a_hbm.shape
+    per_step = parts // steps
+
+    def copies(step, slot):
+        return [
+            pltpu.make_async_copy(
+                a_hbm.at[step * per_step + i],
+                a_buf.at[slot, :, pl.ds(i * width, width)],
+                sems.at[slot, i],
+            )
+            for i in range(per_step)
+        ]
 
     @pl.when(step == 0)
     def _():
+        for copy in copies(0, 0):
+            copy.start()
         acc[...] = jnp.zeros_like(acc)
 
+    slot = lax.rem(step, 2)
+
+    @pl.when(step + 1 < steps)
+    def _():
+        for copy in copies(step + 1, 1 - slot):
+            copy.start()
+
+    for copy in copies(step, slot):
+        copy.wait()
     start = 0
     for e in (e0, e1, e2):
         columns = slice(start, start + e.shape[1])
-        acc[:, columns] += dot(a_ref[...], e[...])
+        acc[:, columns] += dot(a_buf[slot], e[...])
         start += e.shape[1]
 
     @pl.when(step == steps - 1)
@@ -176,20 +202,25 @@
 
 
 def encode(features, encoders, biases, steps=8):
-    rows, depth = features.shape
+    parts, rows, columns = features.shape
     width = sum(e.shape[1] for e in encoders)
-    depth = depth // steps
+    per_step = parts // steps
+    depth = per_step * columns
     return pl.pallas_call(
         functools.partial(encode_kernel, steps),
         grid=(steps,),
-        in_specs=[pl.BlockSpec((rows, depth), lambda i: (0, i))]
+        in_specs=[pl.BlockSpec(memory_space=pltpu.HBM)]
         + [pl.BlockSpec((depth, e.shape[1]), lambda i: (i, 0)) for e in encoders]
         + [pl.BlockSpec((1, width), lambda i: (0, 0))],
         out_specs=pl.BlockSpec((rows // POOL, width), lambda i: (0, 0)),
         out_shape=jax.ShapeDtypeStruct((rows // POOL, width), jnp.float32),
-        scratch_shapes=[pltpu.VMEM((rows, width), jnp.float32)],
+        scratch_shapes=[
+            pltpu.VMEM((rows, width), jnp.float32),
+            pltpu.VMEM((2, rows, depth), jnp.bfloat16),
+            pltpu.SemaphoreType.DMA((2, per_step)),
+        ],
         compiler_params=pltpu.CompilerParams(vmem_limit_bytes=32 * MIB),
-    )(features, *encoders, jnp.concatenate(biases, axis=1))
+    )(in_hbm(features), *[in_hbm(e) for e in encoders], jnp.concatenate(biases, axis=1))
 
 
 def local(
@@ -241,9 +272,9 @@
         ],
         axis=1,
     )
-    layer_out = project(lax.all_gather(own, "seq", axis=1, tiled=True), weights, residual[0])
+    layer_out = project(lax.all_gather(own, "seq"), weights, residual[0])
     both = jnp.concatenate([layer_out, from_head(layer_out, 2)], axis=0)
-    features = lax.all_gather(both, "seq", axis=1, tiled=True)
+    features = lax.all_gather(both, "seq")
     pooled = encode(features, encoders, biases).astype(jnp.bfloat16)
     pools = pooled.shape[0] // 2
     mine = from_section(pooled[:, : 2 * half], 0)

time: 308 us -> 278 us (0.903)
  local copies, waits for them, and re-layouts: 31.9 us -> 8.32 us
  waiting for transfers between devices: 201 us -> 193 us
  Pallas kernels: 27.1 us -> 32.2 us
    unnamed x43 -> x15, local copies, waits for them, and re-layouts: 26.9 us -> 4.33 us
    all_gather x2, waiting for transfers between devices: 30.4 us -> 15.8 us  [the longest x1 15.8 us: local(): features = lax.all_gather(both, 'seq')]
    ppermute x8, waiting for transfers between devices: 136 us -> 143 us  [from_head(): lax.ppermute(x, 'head', [((i + by) % groups, i) for i in range(groups)])]
  transfers between devices with their start and end apart: 16 -> 16, of which waited for: 11 -> 10; matrix products, arithmetic and copies ran while one was open for 1% -> 1% of each run, Pallas kernels for 5% -> 6%
where the time goes in v3:
time: 278 us; the launch traced here: 277 us
  waiting for transfers between devices  193 us (69%)
  Pallas kernels  32.2 us (12%)
  starting transfers between devices  27.6 us (10%)
  between operations  14.2 us (5%)
  local copies, waits for them, and re-layouts  8.32 us (3%)
    ppermute x8, waiting for transfers between devices, from_head(): lax.ppermute(x, 'head', [((i + by) % groups, i) for i in range(groups)])  143 us
    all_to_all x1, waiting for transfers between devices, local(): packed = lax.all_to_all(packed, 'seq', 0, 0, tiled=True)  23.1 us
    pallas_call x1, Pallas kernels, encode(): pl.pallas_call(functools.partial(encode_kernel, steps), grid=(steps,), in...  18 us
    all_gather x1, waiting for transfers between devices, local(): features = lax.all_gather(both, 'seq')  15.8 us
    ppermute x8, starting transfers between devices, from_head(): lax.ppermute(x, 'head', [((i + by) % groups, i) for i in range(groups)])  9.93 us
    all_to_all x1, starting transfers between devices, local(): packed = lax.all_to_all(packed, 'seq', 0, 0, tiled=True)  8.6 us
    pallas_call x1, Pallas kernels, project(): pl.pallas_call(functools.partial(project_kernel, steps), grid=(steps,), i...  8.24 us
    all_to_all x1, waiting for transfers between devices, local(): own = lax.all_to_all(attended, 'head', 0, 0, tiled=True)  7.02 us
  transfers between devices with their start and end apart: 16, of which 10 were waited for; matrix products, arithmetic and copies ran while one was open for 1% of the time, Pallas kernels for 6%

profile of v3, /device:TPU:1, one launch (start us, length us, event | category | flops | bytes accessed | tf_op | source)
XLA Modules:
  0.0 277.5 jit_solution(5065615608155993257)
XLA Ops:
  7.2 0.0 copy-start
  7.2 0.0 copy-start.3
  7.2 0.7 copy-done.3
  7.9 1.6 shard_map.113
  9.6 0.0 copy-start.1
  9.6 1.2 copy-done.1
  10.8 8.6 %all-to-all-start = ((bf16[16,400,128]{2,1,0:T(8,128)(2,1)}), bf16[16,400,128]{2,1,0:T(8,128)(2,1)S(1)}, u32[]{:S(2)}, u32[]{:S(2)}) async-start(bf16[16,400,128]{2,1,0:T(8,128)(2,1)} %copy-done.1), calls=%async_computation | async-start | bytes 3276800 | tf_op jit(solution)/shard_map/all_to_all | solution.py:253
  19.4 0.7 constant_dynamic-slice_fusion.gain_ref
  20.0 0.0 copy-done
  20.1 23.1 %all-to-all-done.packed_ref = bf16[16,400,128]{2,1,0:T(8,128)(2,1)S(1)} async-done(((bf16[16,400,128]{2,1,0:T(8,128)(2,1)}), bf16[16,400,128]{2,1,0:T(8,128)(2,1)S(1)}, u32[]{:S(2)}, u32[]{:S(2)}) %all-to-all-start) | async-done | bytes 1638432 | tf_op jit(solution)/shard_map/all_to_all | solution.py:253
  43.2 4.3 %shard_map.114 = bf16[4,528,128]{2,1,0:T(8,128)(2,1)} custom-call(bf16[16,400,128]{2,1,0:T(8,128)(2,1)S(1)} %all-to-all-done.packed_ref, f32[128,128]{1,0:T(8,128)S(1)} %dynamic-slice_bitcast_fusion.4.prior_ref, f32[1,128]{1,0:T(1,128)S(1)} %constant_dynamic-slice_fusion.gain_ref), custom_call_target="tpu_custom_call" | custom-call | tf_op jit(solution)/shard_map/pallas_call | solution.py:98
  47.5 4.0 %all-to-all-start.1 = ((bf16[4,528,128]{2,1,0:T(8,128)(2,1)}), bf16[4,528,128]{2,1,0:T(8,128)(2,1)S(1)}, u32[]{:S(2)}, u32[]{:S(2)}) async-start(bf16[4,528,128]{2,1,0:T(8,128)(2,1)} %shard_map.114), calls=%async_computation.1 | async-start | bytes 1081344 | tf_op jit(solution)/shard_map/all_to_all | solution.py:267
  51.5 0.0 copy-start.2
  51.5 0.0 all-gather.5.cloned.1.call-start
  51.5 7.0 %all-to-all-done.1 = bf16[4,528,128]{2,1,0:T(8,128)(2,1)S(1)} async-done(((bf16[4,528,128]{2,1,0:T(8,128)(2,1)}), bf16[4,528,128]{2,1,0:T(8,128)(2,1)S(1)}, u32[]{:S(2)}, u32[]{:S(2)}) %all-to-all-start.1) | async-done | bytes 540704 | tf_op jit(solution)/shard_map/all_to_all | solution.py:267
  58.5 0.9 pad_maximum_fusion.1
  59.4 0.0 all-gather.5.cloned.1.call-update
  59.4 0.0 all-gather.7.cloned.1.call-start
  59.5 1.1 collective-permute-start
  60.5 1.1 collective-permute-start.1
  61.6 0.0 collective-permute-start.2
  61.6 30.2 %collective-permute-done.w1 = bf16[2048,384]{1,0:T(8,128)(2,1)S(1)} collective-permute-done((bf16[2048,384]{1,0:T(8,128)(2,1)}, bf16[2048,384]{1,0:T(8,128)(2,1)S(1)}, u32[]{:S(2)}, u32[]{:S(2)}) %collective-permute-start) | collective-permute-done | bytes 1572896 | tf_op jit(solution)/shard_map/ppermute | solution.py:242
  91.9 0.0 copy-start.5
  91.9 2.4 collective-permute-done.1.w2
  94.3 38.1 %collective-permute-done.2.w3 = bf16[2048,384]{1,0:T(8,128)(2,1)} collective-permute-done((bf16[2048,384]{1,0:T(8,128)(2,1)}, bf16[2048,384]{1,0:T(8,128)(2,1)}, u32[]{:S(2)}, u32[]{:S(2)}) %collective-permute-start.2) | collective-permute-done | bytes 1572896 | tf_op jit(solution)/shard_map/ppermute | solution.py:242
  132.4 0.0 all-gather.5.cloned.1.call-done
  132.4 0.0 copy-done.5
  132.4 0.0 copy-done.2
  132.4 8.2 %shard_map.115 = bf16[512,384]{1,0:T(8,128)(2,1)S(1)} custom-call(bf16[16,528,512]{2,1,0:T(8,128)(2,1)} %bitcast.42, bf16[2048,384]{1,0:T(8,128)(2,1)} %bitcast.46, bf16[2048,384]{1,0:T(8,128)(2,1)} %copy-done.5, bf16[2048,384]{1,0:T(8,128)(2,1)} %collective-permute-done.1.w2, bf16[2048,384]{1,0:T(8,128)(2,1)} %collective-permute-done.2.w3, ...), custom_call_target="tpu_custom_call" | custom-call | tf_op jit(solution)/shard_map/pallas_call | solution.py:142
  140.6 2.3 collective-permute-start.4
  143.0 9.4 %collective-permute-done.4 = bf16[512,384]{1,0:T(8,128)(2,1)S(1)} collective-permute-done((bf16[512,384]{1,0:T(8,128)(2,1)S(1)}, bf16[512,384]{1,0:T(8,128)(2,1)S(1)}, u32[]{:S(2)}, u32[]{:S(2)}) %collective-permute-start.4) | collective-permute-done | bytes 393248 | tf_op jit(solution)/shard_map/ppermute | solution.py:242
  152.4 1.0 pad_maximum_fusion
  153.4 0.0 all-gather.7.cloned.1.call-update
  153.4 0.0 copy-start.6
  153.4 3.3 %fusion = (bf16[6144,256]{1,0:T(8,128)(2,1)S(1)}, bf16[6144,256]{1,0:T(8,128)(2,1)S(1)}) fusion(bf16[6144,512]{1,0:T(8,128)(2,1)} %bitcast.39), kind=kLoop, calls=%fused_computation.19 | loop fusion | bytes 12582912 | tf_op jit(solution)/shard_map/slice | solution.py:263
  156.7 0.6 collective-permute-start.5
  157.3 2.1 collective-permute-start.6
  159.4 1.9 collective-permute-start.3
  161.3 0.0 copy-done.6
  161.3 0.0 collective-permute-start.7
  161.3 2.7 collective-permute-start.8
  164.0 62.3 %collective-permute-done.7 = f32[1,256]{1,0:T(1,128)S(1)} collective-permute-done((f32[1,256]{1,0:T(1,128)S(1)}, f32[1,256]{1,0:T(1,128)S(1)}, u32[]{:S(2)}, u32[]{:S(2)}) %collective-permute-start.7) | collective-permute-done | bytes 1056 | tf_op jit(solution)/shard_map/ppermute | solution.py:242
  226.3 0.0 collective-permute-done.8
  226.4 0.0 collective-permute-done.5.e1
  226.4 0.0 copy-start.4
  226.4 1.6 copy-done.4
  228.0 0.0 collective-permute-done.6.e2
  228.0 15.8 %all-gather.7.cloned.1.call-done = bf16[16384,384]{1,0:T(8,128)(2,1)} async-done(((bf16[1024,384]{1,0:T(8,128)(2,1)}), bf16[16384,384]{1,0:T(8,128)(2,1)}) %all-gather.7.cloned.1.call-update) | async-done | bytes 12582928 | tf_op jit(solution)/shard_map/all_gather | solution.py:277
  243.8 18.0 %shard_map.116 = f32[16,1024]{1,0:T(8,128)S(1)} custom-call(bf16[16,1024,384]{2,1,0:T(8,128)(2,1)} %bitcast.41, bf16[6144,512]{1,0:T(8,128)(2,1)} %bitcast.40, bf16[6144,256]{1,0:T(8,128)(2,1)} %copy-done.4, bf16[6144,256]{1,0:T(8,128)(2,1)} %collective-permute-done.6.e2, f32[1,1024]{1,0:T(1,128)S(1)} %pad_maximum_fusion.3.bias_ref), custom_call_target="tpu_custom_call" | custom-call | tf_op jit(solution)/shard_map/pallas_call | solution.py:209
  261.9 3.0 %collective-permute-start.10 = (bf16[16,256]{1,0:T(8,128)(2,1)S(1)}, bf16[16,256]{1,0:T(8,128)(2,1)S(1)}, u32[]{:S(2)}, u32[]{:S(2)}) collective-permute-start(bf16[16,256]{1,0:T(8,128)(2,1)S(1)} %get-tuple-element.12), channel_id=1, source_target_pairs={{1,64},{2,65},{3,66},{0,67},{65,0},{66,1},{67,2},{64,3},{5,68},{6,... | collective-permute-start | bytes 24584 | tf_op jit(solution)/shard_map/ppermute | solution.py:250
  264.9 0.0 collective-permute-done.3
  264.9 0.0 collective-permute-start.11
  264.9 0.1 collective-permute-start.9
  265.0 0.7 collective-permute-done.10
  265.7 3.5 %collective-permute-done.11 = bf16[16,256]{1,0:T(8,128)(2,1)S(1)} collective-permute-done((bf16[16,256]{1,0:T(8,128)(2,1)S(1)}, bf16[16,256]{1,0:T(8,128)(2,1)S(1)}, u32[]{:S(2)}, u32[]{:S(2)}) %collective-permute-start.11) | collective-permute-done | bytes 8224 | tf_op jit(solution)/shard_map/ppermute | solution.py:250
  269.2 0.0 collective-permute-done.9
  269.3 0.6 maximum_bitcast_fusion
  269.9 0.7 copy.13
  (13 shorter events, 0.1 us)
Async XLA Ops:
  7.2 12.9 %copy-start = (f32[1,16,128,128]{3,2,1,0:T(8,128)S(1)}, f32[1,16,128,128]{3,2,1,0:T(8,128)}, u32[]{:S(2)}) copy-start(f32[1,16,128,128]{3,2,1,0:T(8,128)} %param.13) | copy-start | bytes 3145732
  7.2 0.7 copy-start.3
  9.6 1.2 copy-start.1
  10.8 32.4 %all-to-all-start = ((bf16[16,400,128]{2,1,0:T(8,128)(2,1)}), bf16[16,400,128]{2,1,0:T(8,128)(2,1)S(1)}, u32[]{:S(2)}, u32[]{:S(2)}) async-start(bf16[16,400,128]{2,1,0:T(8,128)(2,1)} %copy-done.1), calls=%async_computation | async-start | bytes 3276800 | tf_op jit(solution)/shard_map/all_to_all | solution.py:253
  47.5 11.0 %all-to-all-start.1 = ((bf16[4,528,128]{2,1,0:T(8,128)(2,1)}), bf16[4,528,128]{2,1,0:T(8,128)(2,1)S(1)}, u32[]{:S(2)}, u32[]{:S(2)}) async-start(bf16[4,528,128]{2,1,0:T(8,128)(2,1)} %shard_map.114), calls=%async_computation.1 | async-start | bytes 1081344 | tf_op jit(solution)/shard_map/all_to_all | solution.py:267
  51.5 80.9 %copy-start.2 = (bf16[1,512,384]{2,1,0:T(8,128)(2,1)S(1)}, bf16[1,512,384]{2,1,0:T(8,128)(2,1)}, u32[]{:S(2)}) copy-start(bf16[1,512,384]{2,1,0:T(8,128)(2,1)} %param.16) | copy-start | bytes 1179652
  51.5 80.9 %all-gather.5.cloned.1.call-start = ((), (), s32[]{:S(2)}) async-start(), calls=%async_computation.2 | async-start | bytes 9191424 | tf_op jit(solution)/shard_map/all_gather | solution.py:275
  59.4 184.4 %all-gather.7.cloned.1.call-start = ((), (), s32[]{:S(2)}) async-start(), calls=%async_computation.3 | async-start | bytes 13369344 | tf_op jit(solution)/shard_map/all_gather | solution.py:277
  59.5 32.4 %collective-permute-start = (bf16[2048,384]{1,0:T(8,128)(2,1)}, bf16[2048,384]{1,0:T(8,128)(2,1)S(1)}, u32[]{:S(2)}, u32[]{:S(2)}) collective-permute-start(bf16[2048,384]{1,0:T(8,128)(2,1)} %bitcast.43), channel_id=1, source_target_pairs={{1,0},{2,1},{3,2},{0,3},{5,4},{6,5},{7,6},{4,7},{9,8},{10,9},{11,1... | collective-permute-start | bytes 4718600 | tf_op jit(solution)/shard_map/ppermute | solution.py:242
  60.5 33.7 %collective-permute-start.1 = (bf16[2048,384]{1,0:T(8,128)(2,1)}, bf16[2048,384]{1,0:T(8,128)(2,1)}, u32[]{:S(2)}, u32[]{:S(2)}) collective-permute-start(bf16[2048,384]{1,0:T(8,128)(2,1)} %bitcast.44), channel_id=1, source_target_pairs={{2,0},{3,1},{0,2},{1,3},{6,4},{7,5},{4,6},{5,7},{10,8},{11,9},{8,1... | collective-permute-start | bytes 4718600 | tf_op jit(solution)/shard_map/ppermute | solution.py:242
  61.6 70.7 %collective-permute-start.2 = (bf16[2048,384]{1,0:T(8,128)(2,1)}, bf16[2048,384]{1,0:T(8,128)(2,1)}, u32[]{:S(2)}, u32[]{:S(2)}) collective-permute-start(bf16[2048,384]{1,0:T(8,128)(2,1)} %bitcast.45), channel_id=1, source_target_pairs={{3,0},{0,1},{1,2},{2,3},{7,4},{4,5},{5,6},{6,7},{11,8},{8,9},{9,10... | collective-permute-start | bytes 4718600 | tf_op jit(solution)/shard_map/ppermute | solution.py:242
  91.9 40.5 %copy-start.5 = (bf16[2048,384]{1,0:T(8,128)(2,1)}, bf16[2048,384]{1,0:T(8,128)(2,1)S(1)}, u32[]{:S(2)}) copy-start(bf16[2048,384]{1,0:T(8,128)(2,1)S(1)} %collective-permute-done.w1) | copy-start | bytes 4718596
  140.6 11.8 %collective-permute-start.4 = (bf16[512,384]{1,0:T(8,128)(2,1)S(1)}, bf16[512,384]{1,0:T(8,128)(2,1)S(1)}, u32[]{:S(2)}, u32[]{:S(2)}) collective-permute-start(bf16[512,384]{1,0:T(8,128)(2,1)S(1)} %shard_map.115), channel_id=1, source_target_pairs={{2,0},{3,1},{0,2},{1,3},{6,4},{7,5},{4,6},{5,7},{10,8},{11,9},{8,1... | collective-permute-start | bytes 1179656 | tf_op jit(solution)/shard_map/ppermute | solution.py:242
  153.4 7.9 %copy-start.6 = (f32[1,512]{1,0:T(1,128)S(1)}, f32[1,512]{1,0:T(1,128)}, u32[]{:S(2)}) copy-start(f32[1,512]{1,0:T(1,128)} %param.19) | copy-start | bytes 6148
  156.7 69.7 %collective-permute-start.5 = (bf16[6144,256]{1,0:T(8,128)(2,1)S(1)}, bf16[6144,256]{1,0:T(8,128)(2,1)S(1)}, u32[]{:S(2)}, u32[]{:S(2)}) collective-permute-start(bf16[6144,256]{1,0:T(8,128)(2,1)S(1)} %get-tuple-element.3), channel_id=1, source_target_pairs={{3,0},{0,1},{1,2},{2,3},{7,4},{4,5},{5,6},{6,7},{11,8},{8,9},{9,10... | collective-permute-start | bytes 9437192 | tf_op jit(solution)/shard_map/ppermute | solution.py:242
  157.3 70.7 %collective-permute-start.6 = (bf16[6144,256]{1,0:T(8,128)(2,1)S(1)}, bf16[6144,256]{1,0:T(8,128)(2,1)}, u32[]{:S(2)}, u32[]{:S(2)}) collective-permute-start(bf16[6144,256]{1,0:T(8,128)(2,1)S(1)} %get-tuple-element.2), channel_id=1, source_target_pairs={{1,0},{2,1},{3,2},{0,3},{5,4},{6,5},{7,6},{4,7},{9,8},{10,9},{11,1... | collective-permute-start | bytes 9437192 | tf_op jit(solution)/shard_map/ppermute | solution.py:242
  159.4 105.5 %collective-permute-start.3 = (bf16[1,512,384]{2,1,0:T(8,128)(2,1)S(1)}, bf16[1,512,384]{2,1,0:T(8,128)(2,1)S(1)}, u32[]{:S(2)}, u32[]{:S(2)}) collective-permute-start(bf16[1,512,384]{2,1,0:T(8,128)(2,1)S(1)} %bitcast.37), channel_id=1, source_target_pairs={{0,64},{1,65},{2,66},{3,67},{64,0},{65,1},{66,2},{67,3},{4,68},{5,... | collective-permute-start | bytes 1179656 | tf_op jit(solution)/shard_map/ppermute | solution.py:250
  161.3 65.0 %collective-permute-start.7 = (f32[1,256]{1,0:T(1,128)S(1)}, f32[1,256]{1,0:T(1,128)S(1)}, u32[]{:S(2)}, u32[]{:S(2)}) collective-permute-start(f32[1,256]{1,0:T(1,128)S(1)} %get-tuple-element.20), channel_id=1, source_target_pairs={{3,0},{0,1},{1,2},{2,3},{7,4},{4,5},{5,6},{6,7},{11,8},{8,9},{9,10... | collective-permute-start | bytes 3080 | tf_op jit(solution)/shard_map/ppermute | solution.py:242
  161.3 65.0 %collective-permute-start.8 = (f32[1,256]{1,0:T(1,128)S(1)}, f32[1,256]{1,0:T(1,128)S(1)}, u32[]{:S(2)}, u32[]{:S(2)}) collective-permute-start(f32[1,256]{1,0:T(1,128)S(1)} %get-tuple-element.21), channel_id=1, source_target_pairs={{1,0},{2,1},{3,2},{0,3},{5,4},{6,5},{7,6},{4,7},{9,8},{10,9},{11,1... | collective-permute-start | bytes 3080 | tf_op jit(solution)/shard_map/ppermute | solution.py:242
  226.4 1.6 copy-start.4
  261.9 3.8 %collective-permute-start.10 = (bf16[16,256]{1,0:T(8,128)(2,1)S(1)}, bf16[16,256]{1,0:T(8,128)(2,1)S(1)}, u32[]{:S(2)}, u32[]{:S(2)}) collective-permute-start(bf16[16,256]{1,0:T(8,128)(2,1)S(1)} %get-tuple-element.12), channel_id=1, source_target_pairs={{1,64},{2,65},{3,66},{0,67},{65,0},{66,1},{67,2},{64,3},{5,68},{6,... | collective-permute-start | bytes 24584 | tf_op jit(solution)/shard_map/ppermute | solution.py:250
  264.9 4.3 %collective-permute-start.11 = (bf16[16,256]{1,0:T(8,128)(2,1)S(1)}, bf16[16,256]{1,0:T(8,128)(2,1)S(1)}, u32[]{:S(2)}, u32[]{:S(2)}) collective-permute-start(bf16[16,256]{1,0:T(8,128)(2,1)S(1)} %get-tuple-element.13), channel_id=1, source_target_pairs={{3,64},{0,65},{1,66},{2,67},{67,0},{64,1},{65,2},{66,3},{7,68},{4,... | collective-permute-start | bytes 24584 | tf_op jit(solution)/shard_map/ppermute | solution.py:250
  264.9 4.3 %collective-permute-start.9 = (bf16[16,512]{1,0:T(8,128)(2,1)S(1)}, bf16[16,512]{1,0:T(8,128)(2,1)S(1)}, u32[]{:S(2)}, u32[]{:S(2)}) collective-permute-start(bf16[16,512]{1,0:T(8,128)(2,1)S(1)} %slice.54), channel_id=1, source_target_pairs={{0,64},{1,65},{2,66},{3,67},{64,0},{65,1},{66,2},{67,3},{4,68},{5,... | collective-permute-start | bytes 49160 | tf_op jit(solution)/shard_map/ppermute | solution.py:250
Sparse Core Ops, SparseCore 0:
  59.5 72.3 all-gather.4
  153.5 90.2 all-gather.6

commit v4 on v2

v4 whole, which is shorter than its diff:
```python
import functools

import jax
import jax.numpy as jnp
from jax import lax
from jax.experimental import pallas as pl
from jax.experimental.pallas import tpu as pltpu
from jax.sharding import PartitionSpec as P

HD = 128
POOL = 64
HDIM = 8192
BLK = 128
PACK = 3 * BLK + 16

epsilon = 1e-06
MIB = 1 << 20


def dot(a, b, dims=((1,), (0,))):
    return lax.dot_general(a, b, (dims, ((), ())), preferred_element_type=jnp.float32)


def split(x):
    high = x.astype(jnp.bfloat16)
    return high, (x - high.astype(jnp.float32)).astype(jnp.bfloat16)


def in_hbm(x):
    return pltpu.with_memory_space_constraint(x, pltpu.HBM)


def pack_kernel(queries_ref, keys_ref, values_ref, docs_ref, out_ref):
    docs = jnp.broadcast_to(docs_ref[...].astype(jnp.float32), (PACK - 3 * BLK, BLK))
    docs = docs.astype(out_ref.dtype)
    for head in range(out_ref.shape[0]):
        columns = slice(head * HD, (head + 1) * HD)
        out_ref[head, 0:BLK, :] = queries_ref[:, columns]
        out_ref[head, BLK : 2 * BLK, :] = keys_ref[:, columns]
        out_ref[head, 2 * BLK : 3 * BLK, :] = values_ref[:, columns]
        out_ref[head, 3 * BLK : PACK, :] = docs


def pack(queries, keys, values, docs):
    heads = queries.shape[1] // HD
    return pl.pallas_call(
        pack_kernel,
        out_shape=jax.ShapeDtypeStruct((heads, PACK, HD), jnp.bfloat16),
        compiler_params=pltpu.CompilerParams(vmem_limit_bytes=12 * MIB),
    )(*[in_hbm(x) for x in (queries, keys, values)], docs)


def attend_kernel(packed_ref, prior_ref, gain_ref, out_ref):
    groups, per_group = out_ref.shape[0], packed_ref.shape[0] // out_ref.shape[0]
    row = lax.broadcasted_iota(jnp.int32, (BLK, BLK), 0)
    col = lax.broadcasted_iota(jnp.int32, (BLK, BLK), 1)
    causal = col <= row
    gain = gain_ref[...]
    state = prior_ref[...]
    last = jnp.zeros((BLK, BLK), jnp.float32)
    for group in range(groups):
        for member in range(per_group):
            block = group * per_group + member
            queries = packed_ref[block, 0:BLK, :]
            keys = packed_ref[block, BLK : 2 * BLK, :]
            values = packed_ref[block, 2 * BLK : 3 * BLK, :]
            along = jnp.broadcast_to(
                packed_ref[block, 3 * BLK : PACK, :].astype(jnp.float32)[0:1, :], (BLK, BLK)
            )
            down = along.T
            scores = dot(queries, keys, ((1,), (1,)))
            scores = jnp.where(causal & (along == down), scores, 0.0)
            high, low = split(scores)
            intra = dot(high, values) + dot(low, values)
            high, low = split(state)
            inter = dot(queries, high) + dot(queries, low)
            attended = jnp.where(down == last, inter, 0.0) + intra
            rows = slice(member * BLK, (member + 1) * BLK)
            out_ref[group, rows, :] = (attended * gain).astype(out_ref.dtype)
            newest = jnp.broadcast_to(along[:, BLK - 1 :], (BLK, BLK))
            chosen = jnp.where(down == newest, keys.astype(jnp.float32), 0.0)
            summary = dot(chosen.astype(jnp.bfloat16), values, ((0,), (0,)))
            state = jnp.where(last == newest, state, 0.0) + summary
            last = newest


def attend(packed, prior, gain, groups):
    rows = packed.shape[0] * BLK // groups
    return pl.pallas_call(
        attend_kernel,
        out_shape=jax.ShapeDtypeStruct((groups, rows, HD), jnp.bfloat16),
        compiler_params=pltpu.CompilerParams(vmem_limit_bytes=12 * MIB),
    )(packed, prior, gain)


def project_kernel(steps, final, *refs):
    source, inverse_ref, w0, w1, w2, w3 = refs[:6]
    count = 4 * len(steps)
    blocks = refs[6 : 6 + count]
    rest = refs[6 + count :]
    if final:
        acc_ref, square_ref, residual_ref, out_ref, acc, square = rest
        acc[...] = acc_ref[...]
        square[...] = square_ref[...]
    else:
        acc, square = rest
        acc[...] = jnp.zeros_like(acc)
        square[...] = jnp.zeros_like(square)

    def add(i, carry):
        across = pl.ds(pl.multiple_of(i * BLK, BLK), BLK)
        for n, step in enumerate(steps):
            for c in range(4):
                here = slice(c * BLK, (c + 1) * BLK)
                part = source[(c * 4 + step) * 4 + i]
                rows = pl.ds(pl.multiple_of(part * HD, HD), HD)
                a = blocks[n * 4 + c][across, :]
                w = jnp.concatenate([w[rows, :] for w in (w0, w1, w2, w3)], axis=0)
                acc[here, :] += dot(a, w)
                wide = a.astype(jnp.float32)
                wide = wide * wide * inverse_ref[pl.ds(part, 1), :]
                squares = square[here, :]
                for j in range(4):
                    squares += wide[:, j * HD : (j + 1) * HD]
                square[here, :] = squares
        return carry

    lax.fori_loop(0, 4, add, 0)
    if final:
        mean = jnp.sum(square[...], axis=1, keepdims=True) / HDIM
        scaled = acc[...] * lax.rsqrt(mean + epsilon)
        out_ref[...] = (residual_ref[...].astype(jnp.float32) + scaled).astype(out_ref.dtype)


def project(source, inverse, weights, rings, residual):
    rows, columns = residual.shape
    sums = [
        jax.ShapeDtypeStruct((rows, columns), jnp.float32),
        jax.ShapeDtypeStruct((rows, HD), jnp.float32),
    ]
    smem, vmem = pl.BlockSpec(memory_space=pltpu.SMEM), pl.BlockSpec(memory_space=pltpu.VMEM)

    def blocks(steps):
        return [rings[c][step] for step in steps for c in range(4)]

    early = [0, 1, 2]
    acc, square = pl.pallas_call(
        functools.partial(project_kernel, early, False),
        in_specs=[smem] + [vmem] * (5 + 4 * len(early)),
        out_specs=[vmem] * 2,
        out_shape=sums,
        compiler_params=pltpu.CompilerParams(vmem_limit_bytes=18 * MIB),
    )(source, inverse, *weights, *blocks(early))
    return pl.pallas_call(
        functools.partial(project_kernel, [3], True),
        in_specs=[smem] + [vmem] * (5 + 4 + 3),
        out_specs=vmem,
        out_shape=jax.ShapeDtypeStruct((rows, columns), jnp.bfloat16),
        scratch_shapes=[pltpu.VMEM(x.shape, x.dtype) for x in sums],
        compiler_params=pltpu.CompilerParams(vmem_limit_bytes=18 * MIB),
    )(source, inverse, *weights, *blocks([3]), acc, square, residual)


def encode_kernel(steps, first, final, *refs):
    source, e0, e1, e2 = refs[:4]
    count = 4 * len(steps)
    blocks = refs[4 : 4 + count]
    rest = refs[4 + count :]
    if final:
        acc_ref, bias_ref, out_ref, acc = rest
    elif first:
        (acc,) = rest
        acc_ref = None
    else:
        acc_ref, acc = rest
    rows, depth = blocks[0].shape[0] // 4, blocks[0].shape[1]
    acc[...] = jnp.zeros_like(acc) if first else acc_ref[...]

    def add(i, carry):
        across = pl.ds(pl.multiple_of(i * rows, BLK), rows)
        for c in range(4):
            here = slice(c * rows, (c + 1) * rows)
            start = 0
            for e in (e0, e1, e2):
                there = slice(start, start + e.shape[1])
                total = acc[here, there]
                for n, step in enumerate(steps):
                    part = source[(c * 4 + step) * 4 + i]
                    columns = pl.ds(pl.multiple_of(part * depth, BLK), depth)
                    total += dot(blocks[n * 4 + c][across, :], e[columns, :])
                acc[here, there] = total
                start += e.shape[1]
        return carry

    lax.fori_loop(0, 4, add, 0)
    if final:
        for i in range(out_ref.shape[0] // 8):
            pools = []
            for j in range(8 * i, 8 * i + 8):
                latent = jnp.maximum(acc[j * POOL : (j + 1) * POOL, :] + bias_ref[...], 0.0)
                pools.append(jnp.sum(latent, axis=0, keepdims=True) * (1.0 / POOL))
            out_ref[8 * i : 8 * i + 8, :] = jnp.concatenate(pools, axis=0)


def encode(source, encoders, rings, bias):
    rows = rings[0][0].shape[0]
    width = bias.shape[1]
    acc_shape = jax.ShapeDtypeStruct((rows, width), jnp.float32)
    smem, vmem = pl.BlockSpec(memory_space=pltpu.SMEM), pl.BlockSpec(memory_space=pltpu.VMEM)

    def blocks(steps):
        return [rings[c][step] for step in steps for c in range(4)]

    acc = None
    for steps in ([0, 1], [2]):
        acc = pl.pallas_call(
            functools.partial(encode_kernel, steps, acc is None, False),
            in_specs=[smem] + [vmem] * (3 + 4 * len(steps) + (acc is not None)),
            out_specs=vmem,
            out_shape=acc_shape,
            compiler_params=pltpu.CompilerParams(vmem_limit_bytes=28 * MIB),
        )(source, *encoders, *blocks(steps), *([] if acc is None else [acc]))
    return pl.pallas_call(
        functools.partial(encode_kernel, [3], False, True),
        in_specs=[smem] + [vmem] * (3 + 4 + 2),
        out_specs=vmem,
        out_shape=jax.ShapeDtypeStruct((rows // POOL, width), jnp.float32),
        scratch_shapes=[pltpu.VMEM(acc_shape.shape, acc_shape.dtype)],
        compiler_params=pltpu.CompilerParams(vmem_limit_bytes=28 * MIB),
    )(source, *encoders, *blocks([3]), acc, bias)


SIDE = 4
ROUTES = ((("y", 1), ("z", 1)), (("y", -1), ("z", -1)), (("z", 1), ("y", 1)), (("z", -1), ("y", -1)))


def moved(x, axis, by):
    pairs = []
    for z in range(SIDE):
        for y in range(SIDE):
            to = (z, (y + by) % SIDE) if axis == "y" else ((z + by) % SIDE, y)
            pairs.append((z * SIDE + y, to[0] * SIDE + to[1]))
    return lax.ppermute(x, "seq", pairs)


def sources(place):
    z, y = place // SIDE, place % SIDE
    table = []
    for (axis, by), (_, by_second) in ROUTES:
        for second in range(SIDE):
            for first in range(SIDE):
                back = (first * by, second * by_second)
                back_y, back_z = back if axis == "y" else back[::-1]
                table.append((z - back_z) % SIDE * SIDE + (y - back_y) % SIDE)
    return jnp.stack(table).astype(jnp.int32)


def ring_gather(quarters):
    lines = [[q] for q in quarters]
    for _ in range(SIDE - 1):
        for line, ((axis, by), _) in zip(lines, ROUTES):
            line.append(moved(line[-1], axis, by))
    rings = [[jnp.concatenate(line, axis=0)] for line in lines]
    for _ in range(SIDE - 1):
        for ring, (_, (axis, by)) in zip(rings, ROUTES):
            ring.append(moved(ring[-1], axis, by))
    return rings


def local(
    query_vectors,
    key_vectors,
    value_vectors,
    prior_state,
    doc_ids,
    norm_gain,
    residual,
    out_weight,
    enc_weight,
    enc_bias,
):
    groups, sections = lax.axis_size("head"), lax.axis_size("section")
    group, place = lax.axis_index("head"), lax.axis_index("seq")

    def from_head(x, by):
        return lax.ppermute(x, "head", [((i + by) % groups, i) for i in range(groups)])

    def from_section(x, by):
        pairs = []
        for s in range(sections):
            for i in range(groups):
                target = (s + 1) % sections
                pairs.append((s * groups + (i + by) % groups, target * groups + i))
        return lax.ppermute(x, ("section", "head"), pairs)

    packed = pack(query_vectors[0], key_vectors[0], value_vectors[0], doc_ids)
    weight = out_weight[0]
    after, before = from_head(weight, 1), from_head(weight, -1)
    gains = [norm_gain] + [from_head(norm_gain, k) for k in range(1, groups)]
    inverse = jnp.concatenate([(1.0 / (g * g)).reshape(-1, HD) for g in gains], axis=1)
    half = enc_weight.shape[2] // 2
    bias = jnp.concatenate(
        [enc_bias, from_head(enc_bias[:, :half], -1), from_head(enc_bias[:, half:], 1)], axis=1
    )
    source = sources(place)

    packed = lax.all_to_all(packed, "seq", 0, 0, tiled=True)
    prior = lax.dynamic_index_in_dim(prior_state[0], place, 0, False)
    gain = lax.dynamic_slice_in_dim(norm_gain, place * HD, HD, 1)
    attended = attend(packed, prior, gain, groups)
    attended, after, before, inverse, bias = lax.optimization_barrier(
        (attended, after, before, inverse, bias)
    )

    middle = weight.shape[0] // 2
    across = [from_head(after[:middle], 1), from_head(before[middle:], -1)]
    own = lax.all_to_all(attended, "head", 0, 0, tiled=True)
    own = jnp.concatenate(
        [
            lax.dynamic_index_in_dim(own, (group + k) % groups, 0, False)
            for k in range(groups)
        ],
        axis=1,
    )
    own, first_half = lax.optimization_barrier((own, enc_weight[0][:, :half]))
    from_before = from_head(first_half, -1)
    rings = ring_gather([own[c * BLK : (c + 1) * BLK] for c in range(4)])
    weights = [weight, after, jnp.concatenate(across, axis=0), before]
    layer_out = project(source, inverse, weights, rings, residual[0])

    layer_out, from_before, second_half = lax.optimization_barrier(
        (layer_out, from_before, enc_weight[0][:, half:])
    )
    from_after = from_head(second_half, 1)
    opposite = from_head(layer_out, 2)
    rows = layer_out.shape[0] // 2
    rings = ring_gather([layer_out[:rows], layer_out[rows:], opposite[:rows], opposite[rows:]])
    pooled = encode(source, [enc_weight[0], from_before, from_after], rings, bias)
    pooled = pooled.astype(jnp.bfloat16)
    pools = pooled.shape[0] // 2
    mine = from_section(pooled[:, : 2 * half], 0)
    after = from_section(pooled[:, 2 * half : 3 * half], 1)
    before = from_section(pooled[:, 3 * half :], -1)
    turned = [
        mine[:pools],
        jnp.concatenate([after[:pools], before[pools:]], axis=1),
        mine[pools:],
        jnp.concatenate([after[pools:], before[:pools]], axis=1),
    ]
    turned = jnp.stack(turned)
    monitor = jnp.concatenate(
        [
            lax.dynamic_index_in_dim(turned, (i - group) % groups, 0, False)
            for i in range(groups)
        ],
        axis=0,
    )
    return (from_section(layer_out[None], 0), monitor[None])


def solution(mesh):
    return jax.shard_map(
        local,
        mesh=mesh,
        in_specs=(
            P("section", "seq", "head"),
            P("section", "seq", "head"),
            P("section", "seq", "head"),
            P("section", "head", None, None),
            P("section", "seq"),
            P("section", "head"),
            P("section", "head", "seq"),
            P("section", "head", "seq"),
            P("section", None, ("seq", "head")),
            P("section", ("seq", "head")),
        ),
        out_specs=(P("section", "head", "seq"), P("section", None, ("seq", "head"))),
        check_vma=False,
    )
```

time: 308 us -> 309 us (level)
  starting transfers between devices: 30.2 us -> 103 us
  waiting for transfers between devices: 201 us -> 136 us
  Pallas kernels: 27.1 us -> 44.1 us
  between operations: 14.3 us -> 1.3 us
  local copies, waits for them, and re-layouts: 31.9 us -> 22 us
    ppermute x0 -> x48, starting transfers between devices: none -> 59.8 us  [moved(): return lax.ppermute(x, 'seq', pairs)]
    ppermute x8 -> x12, waiting for transfers between devices: 136 us -> 82.6 us  [from_head(): lax.ppermute(x, 'head', [((i + by) % groups, i) for i in range(groups)])]
    ppermute x0 -> x48, waiting for transfers between devices: none -> 48.9 us  [moved(): return lax.ppermute(x, 'seq', pairs)]
    all_gather x2 -> x0, waiting for transfers between devices: 30.4 us -> none  [the longest x1 25 us: local(): features = lax.all_gather(both, 'seq', axis=1, tiled=True)]
    all_to_all x1, waiting for transfers between devices: 23.1 us -> 0.01 us  [local(): packed = lax.all_to_all(packed, 'seq', 0, 0, tiled=True)]
    pallas_call x2 -> x5, Pallas kernels: 22.6 us -> 36.9 us  [the longest x2 18.7 us: encode(): pl.pallas_call(functools.partial(encode_kernel, steps, acc is None, False...]
    unnamed x43 -> x54, local copies, waits for them, and re-layouts: 26.9 us -> 13.2 us
    ppermute x4, starting transfers between devices: 7.02 us -> 19.8 us  [from_section(): return lax.ppermute(x, ('section', 'head'), pairs)]
  transfers between devices with their start and end apart: 16 -> 66, of which waited for: 11 -> 26; matrix products, arithmetic and copies ran while one was open for 1% -> 3% of each run, Pallas kernels for 5% -> 14%
where the time goes in v4:
time: 309 us; the launch traced here: 308 us
  waiting for transfers between devices  136 us (44%)
  starting transfers between devices  103 us (33%)
  Pallas kernels  44.1 us (14%)
  local copies, waits for them, and re-layouts  22 us (7%)
    ppermute x12, waiting for transfers between devices, from_head(): lax.ppermute(x, 'head', [((i + by) % groups, i) for i in range(groups)])  82.6 us
    ppermute x48, starting transfers between devices, moved(): return lax.ppermute(x, 'seq', pairs)  59.8 us
    ppermute x48, waiting for transfers between devices, moved(): return lax.ppermute(x, 'seq', pairs)  48.9 us
    ppermute x4, starting transfers between devices, from_section(): return lax.ppermute(x, ('section', 'head'), pairs)  19.8 us
    pallas_call x2, Pallas kernels, encode(): pl.pallas_call(functools.partial(encode_kernel, steps, acc is None, False...  18.7 us
    unnamed x54, local copies, waits for them, and re-layouts  13.2 us
    ppermute x12, starting transfers between devices, from_head(): lax.ppermute(x, 'head', [((i + by) % groups, i) for i in range(groups)])  12.3 us
    all_to_all x1, starting transfers between devices, local(): packed = lax.all_to_all(packed, 'seq', 0, 0, tiled=True)  7.94 us
  transfers between devices with their start and end apart: 66, of which 26 were waited for; matrix products, arithmetic and copies ran while one was open for 3% of the time, Pallas kernels for 14%

profile of v4, /device:TPU:1, one launch (start us, length us, event | category | flops | bytes accessed | tf_op | source)
XLA Modules:
  0.0 308.3 jit_solution(5526120911749029318)
XLA Ops:
  0.6 3.4 %collective-permute-start = (bf16[2048,384]{1,0:T(8,128)(2,1)}, bf16[2048,384]{1,0:T(8,128)(2,1)S(1)}, u32[]{:S(2)}, u32[]{:S(2)}) collective-permute-start(bf16[2048,384]{1,0:T(8,128)(2,1)} %bitcast.76), channel_id=1, source_target_pairs={{1,0},{2,1},{3,2},{0,3},{5,4},{6,5},{7,6},{4,7},{9,8},{10,9},{11,1... | collective-permute-start | bytes 4718600 | tf_op jit(solution)/shard_map/ppermute | solution.py:286
  4.7 1.6 shard_map.113
  6.3 1.2 copy-done.2
  7.5 7.9 %all-to-all-start = ((bf16[16,400,128]{2,1,0:T(8,128)(2,1)}), bf16[16,400,128]{2,1,0:T(8,128)(2,1)}, u32[]{:S(2)}, u32[]{:S(2)}) async-start(bf16[16,400,128]{2,1,0:T(8,128)(2,1)} %copy-done.2), calls=%async_computation | async-start | bytes 3276800 | tf_op jit(solution)/shard_map/all_to_all | solution.py:307
  15.7 2.6 collective-permute-start.6
  18.3 1.4 collective-permute-start.2
  19.8 20.7 %collective-permute-done.5 = f32[1,256]{1,0:T(1,128)S(1)} collective-permute-done((f32[1,256]{1,0:T(1,128)S(1)}, f32[1,256]{1,0:T(1,128)S(1)}, u32[]{:S(2)}, u32[]{:S(2)}) %collective-permute-start.5) | collective-permute-done | bytes 1056 | tf_op jit(solution)/shard_map/ppermute | solution.py:286
  40.6 3.9 %collective-permute-done.3 = f32[1,2048]{1,0:T(1,128)S(1)} collective-permute-done((f32[1,2048]{1,0:T(1,128)S(1)}, f32[1,2048]{1,0:T(1,128)S(1)}, u32[]{:S(2)}, u32[]{:S(2)}) %collective-permute-start.3) | collective-permute-done | bytes 8224 | tf_op jit(solution)/shard_map/ppermute | solution.py:286
  44.6 5.6 %shard_map.114 = bf16[4,512,128]{2,1,0:T(8,128)(2,1)} custom-call(bf16[16,400,128]{2,1,0:T(8,128)(2,1)} %all-to-all-done.packed_ref, f32[128,128]{1,0:T(8,128)S(1)} %dynamic-slice_bitcast_fusion.4.prior_ref, f32[1,128]{1,0:T(1,128)S(1)} %constant_dynamic-slice_fusion.gain_ref), custom_call_target="tpu_custom_call" | custom-call | tf_op jit(solution)/shard_map/pallas_call | solution.py:89
  50.2 3.5 %all-to-all-start.1 = ((bf16[4,512,128]{2,1,0:T(8,128)(2,1)}), bf16[4,512,128]{2,1,0:T(8,128)(2,1)S(1)}, u32[]{:S(2)}, u32[]{:S(2)}) async-start(bf16[4,512,128]{2,1,0:T(8,128)(2,1)} %shard_map.114), calls=%async_computation.1 | async-start | bytes 1048576 | tf_op jit(solution)/shard_map/all_to_all | solution.py:317
  53.7 5.8 %fusion = (bf16[6144,256]{1,0:T(8,128)(2,1)}, bf16[6144,256]{1,0:T(8,128)(2,1)}) fusion(bf16[6144,512]{1,0:T(8,128)(2,1)} %bitcast.70), kind=kLoop, calls=%fused_computation.33 | loop fusion | bytes 12582912 | tf_op jit(solution)/shard_map/slice | solution.py:332
  59.5 1.1 all-to-all-done.1
  61.1 3.8 %collective-permute-start.27 = (bf16[128,512]{1,0:T(8,128)(2,1)S(1)}, bf16[128,512]{1,0:T(8,128)(2,1)S(1)}, u32[]{:S(2)}, u32[]{:S(2)}) collective-permute-start(bf16[128,512]{1,0:T(8,128)(2,1)S(1)} %get-tuple-element.28), channel_id=1, source_target_pairs={{0,48},{4,52},{8,56},{12,60},{16,0},{20,4},{24,8},{28,12},{32,16},... | collective-permute-start | bytes 393224 | tf_op jit(solution)/shard_map/ppermute | solution.py:243
  65.0 2.7 collective-permute-start.15
  67.7 2.7 collective-permute-start.28
  70.5 1.2 slice.72
  71.7 2.4 collective-permute-start.7
  74.2 2.7 collective-permute-start.16
  76.9 2.7 collective-permute-done.22
  81.5 3.6 %collective-permute-done.10 = bf16[128,512]{1,0:T(8,128)(2,1)S(1)} collective-permute-done((bf16[128,512]{1,0:T(8,128)(2,1)S(1)}, bf16[128,512]{1,0:T(8,128)(2,1)S(1)}, u32[]{:S(2)}, u32[]{:S(2)}) %collective-permute-start.10) | collective-permute-done | bytes 131104 | tf_op jit(solution)/shard_map/ppermute | solution.py:243
  85.0 1.9 collective-permute-start.17
  86.9 3.5 %collective-permute-done.23 = bf16[128,512]{1,0:T(8,128)(2,1)S(1)} collective-permute-done((bf16[128,512]{1,0:T(8,128)(2,1)S(1)}, bf16[128,512]{1,0:T(8,128)(2,1)S(1)}, u32[]{:S(2)}, u32[]{:S(2)}) %collective-permute-start.23) | collective-permute-done | bytes 131104 | tf_op jit(solution)/shard_map/ppermute | solution.py:243
  90.5 2.7 collective-permute-start.30
  93.3 2.6 collective-permute-done.11
  96.2 48.2 %collective-permute-done.8 = bf16[1024,384]{1,0:T(8,128)(2,1)S(1)} collective-permute-done((bf16[1024,384]{1,0:T(8,128)(2,1)S(1)}, bf16[1024,384]{1,0:T(8,128)(2,1)S(1)}, u32[]{:S(2)}, u32[]{:S(2)}) %collective-permute-start.8) | collective-permute-done | bytes 786464 | tf_op jit(solution)/shard_map/ppermute | solution.py:286
  144.4 1.6 collective-permute-start.12
  146.9 2.7 collective-permute-start.31
  151.2 2.1 collective-permute-start.19
  154.2 1.2 collective-permute-done.12.refs_10_
  156.2 3.0 collective-permute-start.32
  160.0 3.1 collective-permute-start.20
  163.0 3.4 %collective-permute-done.13.refs_14_ = bf16[512,512]{1,0:T(8,128)(2,1)} collective-permute-done((bf16[512,512]{1,0:T(8,128)(2,1)S(1)}, bf16[512,512]{1,0:T(8,128)(2,1)}, u32[]{:S(2)}, u32[]{:S(2)}) %collective-permute-start.13) | collective-permute-done | bytes 524320 | tf_op jit(solution)/shard_map/ppermute | solution.py:243
  166.6 1.4 constant_dynamic-update-slice_fusion.1
  168.0 1.3 constant_dynamic-update-slice_fusion.refs_4_
  171.4 1.0 copy-done.15
  172.5 1.0 copy-done.17
  173.5 6.2 %shard_map.115 = (f32[512,384]{1,0:T(8,128)S(1)}, f32[512,128]{1,0:T(8,128)S(1)}) custom-call(s32[64]{0:T(128)S(1)} %stack.175.refs_0_, f32[16,512]{1,0:T(8,128)S(1)} %pad_maximum_fusion.9.refs_1_, bf16[2048,384]{1,0:T(8,128)(2,1)S(1)} %bitcast.78, bf16[2048,384]{1,0:T(8,128)(2,1)S(1)} %collective-permute-done.refs_3_, ...), custom_call_target="tpu_custom_call" | custom-call | tf_op jit(solution)/shard_map/pallas_call | solution.py:147
  179.8 4.2 %shard_map.116 = bf16[512,384]{1,0:T(8,128)(2,1)S(1)} custom-call(s32[64]{0:T(128)S(1)} %stack.175.refs_0_, f32[16,512]{1,0:T(8,128)S(1)} %pad_maximum_fusion.9.refs_1_, bf16[2048,384]{1,0:T(8,128)(2,1)S(1)} %bitcast.79, bf16[2048,384]{1,0:T(8,128)(2,1)S(1)} %collective-permute-done.refs_3_, bf16[2048,384]{1,0:T(8,128)(2,1)S(1)} %constant_dynamic-update-slice_fusion.refs_4_, ...), custom_call_target="tpu_custom_call" | custom-call | tf_op jit(solution)/shard_map/pallas_call | solution.py:154
  184.0 1.9 collective-permute-start.48
  186.0 2.8 collective-permute-start.42
  188.8 3.4 %collective-permute-done.48 = bf16[512,384]{1,0:T(8,128)(2,1)S(1)} collective-permute-done((bf16[512,384]{1,0:T(8,128)(2,1)S(1)}, bf16[512,384]{1,0:T(8,128)(2,1)S(1)}, u32[]{:S(2)}, u32[]{:S(2)}) %collective-permute-start.48) | collective-permute-done | bytes 393248 | tf_op jit(solution)/shard_map/ppermute | solution.py:286
  192.2 2.7 collective-permute-start.55
  195.0 2.4 collective-permute-start.43
  197.6 3.4 %collective-permute-start.56 = (bf16[256,384]{1,0:T(8,128)(2,1)S(1)}, bf16[256,384]{1,0:T(8,128)(2,1)S(1)}, u32[]{:S(2)}, u32[]{:S(2)}) collective-permute-start(bf16[256,384]{1,0:T(8,128)(2,1)S(1)} %collective-permute-done.55), channel_id=1, source_target_pairs={{0,48},{4,52},{8,56},{12,60},{16,0},{20,4},{24,8},{28,12},{32,16},... | collective-permute-start | bytes 589832 | tf_op jit(solution)/shard_map/ppermute | solution.py:243
  201.4 3.4 %collective-permute-start.44 = (bf16[256,384]{1,0:T(8,128)(2,1)S(1)}, bf16[256,384]{1,0:T(8,128)(2,1)S(1)}, u32[]{:S(2)}, u32[]{:S(2)}) collective-permute-start(bf16[256,384]{1,0:T(8,128)(2,1)S(1)} %collective-permute-done.43), channel_id=1, source_target_pairs={{0,12},{4,0},{8,4},{12,8},{16,28},{20,16},{24,20},{28,24},{32,44},... | collective-permute-start | bytes 589832 | tf_op jit(solution)/shard_map/ppermute | solution.py:243
  204.9 2.9 collective-permute-start.57
  207.9 2.6 collective-permute-done.50
  210.8 2.5 collective-permute-start.58
  213.3 3.3 %collective-permute-done.51 = bf16[256,384]{1,0:T(8,128)(2,1)S(1)} collective-permute-done((bf16[256,384]{1,0:T(8,128)(2,1)S(1)}, bf16[256,384]{1,0:T(8,128)(2,1)S(1)}, u32[]{:S(2)}, u32[]{:S(2)}) %collective-permute-start.51) | collective-permute-done | bytes 196640 | tf_op jit(solution)/shard_map/ppermute | solution.py:243
  216.8 4.4 %collective-permute-done.45.refs_9_ = bf16[1024,384]{1,0:T(8,128)(2,1)S(1)} collective-permute-done((bf16[1024,384]{1,0:T(8,128)(2,1)S(1)}, bf16[1024,384]{1,0:T(8,128)(2,1)S(1)}, u32[]{:S(2)}, u32[]{:S(2)}) %collective-permute-start.45) | collective-permute-done | bytes 786464 | tf_op jit(solution)/shard_map/ppermute | solution.py:243
  221.1 3.2 %collective-permute-start.46 = (bf16[1024,384]{1,0:T(8,128)(2,1)S(1)}, bf16[1024,384]{1,0:T(8,128)(2,1)S(1)}, u32[]{:S(2)}, u32[]{:S(2)}) collective-permute-start(bf16[1024,384]{1,0:T(8,128)(2,1)S(1)} %collective-permute-done.45.refs_9_), channel_id=1, source_target_pairs={{0,48},{4,52},{8,56},{12,60},{16,0},{20,4},{24,8},{28,12},{32,16},... | collective-permute-start | bytes 2359304 | tf_op jit(solution)/shard_map/ppermute | solution.py:243
  224.3 2.8 collective-permute-done.39.refs_8_
  227.6 3.2 %collective-permute-done.52.refs_10_ = bf16[1024,384]{1,0:T(8,128)(2,1)S(1)} collective-permute-done((bf16[1024,384]{1,0:T(8,128)(2,1)S(1)}, bf16[1024,384]{1,0:T(8,128)(2,1)S(1)}, u32[]{:S(2)}, u32[]{:S(2)}) %collective-permute-start.52) | collective-permute-done | bytes 786464 | tf_op jit(solution)/shard_map/ppermute | solution.py:243
  230.8 10.3 %collective-permute-done.46.refs_5_ = bf16[1024,384]{1,0:T(8,128)(2,1)S(1)} collective-permute-done((bf16[1024,384]{1,0:T(8,128)(2,1)S(1)}, bf16[1024,384]{1,0:T(8,128)(2,1)S(1)}, u32[]{:S(2)}, u32[]{:S(2)}) %collective-permute-start.46) | collective-permute-done | bytes 786464 | tf_op jit(solution)/shard_map/ppermute | solution.py:243
  241.0 3.4 %collective-permute-start.47 = (bf16[1024,384]{1,0:T(8,128)(2,1)S(1)}, bf16[1024,384]{1,0:T(8,128)(2,1)S(1)}, u32[]{:S(2)}, u32[]{:S(2)}) collective-permute-start(bf16[1024,384]{1,0:T(8,128)(2,1)S(1)} %collective-permute-done.46.refs_5_), channel_id=1, source_target_pairs={{0,48},{4,52},{8,56},{12,60},{16,0},{20,4},{24,8},{28,12},{32,16},... | collective-permute-start | bytes 2359304 | tf_op jit(solution)/shard_map/ppermute | solution.py:243
  244.4 3.5 %collective-permute-done.40.refs_4_ = bf16[1024,384]{1,0:T(8,128)(2,1)S(1)} collective-permute-done((bf16[1024,384]{1,0:T(8,128)(2,1)S(1)}, bf16[1024,384]{1,0:T(8,128)(2,1)S(1)}, u32[]{:S(2)}, u32[]{:S(2)}) %collective-permute-start.40) | collective-permute-done | bytes 786464 | tf_op jit(solution)/shard_map/ppermute | solution.py:243
  249.4 6.2 %collective-permute-done.35.refs_3_ = bf16[6144,256]{1,0:T(8,128)(2,1)S(1)} collective-permute-done((bf16[6144,256]{1,0:T(8,128)(2,1)S(1)}, bf16[6144,256]{1,0:T(8,128)(2,1)S(1)}, u32[]{:S(2)}, u32[]{:S(2)}) %collective-permute-start.35) | collective-permute-done | bytes 3145760 | tf_op jit(solution)/shard_map/ppermute | solution.py:286
  255.6 15.5 %collective-permute-start.34 = (bf16[1,512,384]{2,1,0:T(8,128)(2,1)S(1)}, bf16[1,512,384]{2,1,0:T(8,128)(2,1)}, u32[]{:S(2)}, u32[]{:S(2)}) collective-permute-start(bf16[1,512,384]{2,1,0:T(8,128)(2,1)S(1)} %bitcast.80), channel_id=1, source_target_pairs={{0,64},{1,65},{2,66},{3,67},{64,0},{65,1},{66,2},{67,3},{4,68},{5,... | collective-permute-start | bytes 1179656 | tf_op jit(solution)/shard_map/ppermute | solution.py:294
  271.1 11.5 %shard_map.117.refs_8_ = f32[1024,1024]{1,0:T(8,128)S(1)} custom-call(s32[64]{0:T(128)S(1)} %stack.175.refs_0_, bf16[6144,512]{1,0:T(8,128)(2,1)S(1)} %bitcast.73, bf16[6144,256]{1,0:T(8,128)(2,1)} %collective-permute-done.33.refs_2_, bf16[6144,256]{1,0:T(8,128)(2,1)S(1)} %collective-permute-done.35.refs_3_, bf16[1024,384]{1,0:T(8,128)(2,1)S(1)} %pad_maximum_fusion.refs_4_, ...), custom_call_target="tpu_custom_call" | custom-call | tf_op jit(solution)/shard_map/pallas_call | solution.py:216
  282.6 7.2 %shard_map.118.refs_8_ = f32[1024,1024]{1,0:T(8,128)S(1)} custom-call(s32[64]{0:T(128)S(1)} %stack.175.refs_0_, bf16[6144,512]{1,0:T(8,128)(2,1)S(1)} %bitcast.74, bf16[6144,256]{1,0:T(8,128)(2,1)} %collective-permute-done.33.refs_2_, bf16[6144,256]{1,0:T(8,128)(2,1)S(1)} %collective-permute-done.35.refs_3_, ...), custom_call_target="tpu_custom_call" | custom-call | tf_op jit(solution)/shard_map/pallas_call | solution.py:216
  289.9 7.8 %shard_map.119 = f32[16,1024]{1,0:T(8,128)S(1)} custom-call(s32[64]{0:T(128)S(1)} %stack.175.refs_0_, bf16[6144,512]{1,0:T(8,128)(2,1)S(1)} %bitcast.75, bf16[6144,256]{1,0:T(8,128)(2,1)} %collective-permute-done.33.refs_2_, bf16[6144,256]{1,0:T(8,128)(2,1)S(1)} %collective-permute-done.35.refs_3_, bf16[1024,384]{1,0:T(8,128)(2,1)S(1)} %collective-permute-done.41.refs_4_, ...), custom_call_target="tpu_custom_call" | custom-call | tf_op jit(solution)/shard_map/pallas_call | solution.py:223
  297.7 3.8 %collective-permute-start.62 = (bf16[16,256]{1,0:T(8,128)(2,1)S(1)}, bf16[16,256]{1,0:T(8,128)(2,1)S(1)}, u32[]{:S(2)}, u32[]{:S(2)}) collective-permute-start(bf16[16,256]{1,0:T(8,128)(2,1)S(1)} %get-tuple-element.44), channel_id=1, source_target_pairs={{1,64},{2,65},{3,66},{0,67},{65,0},{66,1},{67,2},{64,3},{5,68},{6,... | collective-permute-start | bytes 24584 | tf_op jit(solution)/shard_map/ppermute | solution.py:294
  302.3 3.6 %collective-permute-done.63 = bf16[16,256]{1,0:T(8,128)(2,1)S(1)} collective-permute-done((bf16[16,256]{1,0:T(8,128)(2,1)S(1)}, bf16[16,256]{1,0:T(8,128)(2,1)S(1)}, u32[]{:S(2)}, u32[]{:S(2)}) %collective-permute-start.63) | collective-permute-done | bytes 8224 | tf_op jit(solution)/shard_map/ppermute | solution.py:294
  306.5 1.8 copy.14
  (167 shorter events, 16.1 us)
Async XLA Ops:
  0.6 49.5 %collective-permute-start = (bf16[2048,384]{1,0:T(8,128)(2,1)}, bf16[2048,384]{1,0:T(8,128)(2,1)S(1)}, u32[]{:S(2)}, u32[]{:S(2)}) collective-permute-start(bf16[2048,384]{1,0:T(8,128)(2,1)} %bitcast.76), channel_id=1, source_target_pairs={{1,0},{2,1},{3,2},{0,3},{5,4},{6,5},{7,6},{4,7},{9,8},{10,9},{11,1... | collective-permute-start | bytes 4718600 | tf_op jit(solution)/shard_map/ppermute | solution.py:286
  4.0 46.2 %collective-permute-start.1 = (bf16[2048,384]{1,0:T(8,128)(2,1)}, bf16[2048,384]{1,0:T(8,128)(2,1)}, u32[]{:S(2)}, u32[]{:S(2)}) collective-permute-start(bf16[2048,384]{1,0:T(8,128)(2,1)} %bitcast.77), channel_id=1, source_target_pairs={{3,0},{0,1},{1,2},{2,3},{7,4},{4,5},{5,6},{6,7},{11,8},{8,9},{9,10... | collective-permute-start | bytes 4718600 | tf_op jit(solution)/shard_map/ppermute | solution.py:286
  7.5 37.1 %all-to-all-start = ((bf16[16,400,128]{2,1,0:T(8,128)(2,1)}), bf16[16,400,128]{2,1,0:T(8,128)(2,1)}, u32[]{:S(2)}, u32[]{:S(2)}) async-start(bf16[16,400,128]{2,1,0:T(8,128)(2,1)} %copy-done.2), calls=%async_computation | async-start | bytes 3276800 | tf_op jit(solution)/shard_map/all_to_all | solution.py:307
  15.5 25.0 %collective-permute-start.5 = (f32[1,256]{1,0:T(1,128)S(1)}, f32[1,256]{1,0:T(1,128)S(1)}, u32[]{:S(2)}, u32[]{:S(2)}) collective-permute-start(f32[1,256]{1,0:T(1,128)S(1)} %get-tuple-element.52), channel_id=1, source_target_pairs={{3,0},{0,1},{1,2},{2,3},{7,4},{4,5},{5,6},{6,7},{11,8},{8,9},{9,10... | collective-permute-start | bytes 3080 | tf_op jit(solution)/shard_map/ppermute | solution.py:286
  15.7 24.8 %collective-permute-start.6 = (f32[1,256]{1,0:T(1,128)S(1)}, f32[1,256]{1,0:T(1,128)S(1)}, u32[]{:S(2)}, u32[]{:S(2)}) collective-permute-start(f32[1,256]{1,0:T(1,128)S(1)} %get-tuple-element.53), channel_id=1, source_target_pairs={{1,0},{2,1},{3,2},{0,3},{5,4},{6,5},{7,6},{4,7},{9,8},{10,9},{11,1... | collective-permute-start | bytes 3080 | tf_op jit(solution)/shard_map/ppermute | solution.py:286
  18.3 22.2 %collective-permute-start.2 = (f32[1,2048]{1,0:T(1,128)S(1)}, f32[1,2048]{1,0:T(1,128)S(1)}, u32[]{:S(2)}, u32[]{:S(2)}) collective-permute-start(f32[1,2048]{1,0:T(1,128)S(1)} %copy-done.22), channel_id=1, source_target_pairs={{1,0},{2,1},{3,2},{0,3},{5,4},{6,5},{7,6},{4,7},{9,8},{10,9},{11,1... | collective-permute-start | bytes 24584 | tf_op jit(solution)/shard_map/ppermute | solution.py:286
  50.2 10.4 %all-to-all-start.1 = ((bf16[4,512,128]{2,1,0:T(8,128)(2,1)}), bf16[4,512,128]{2,1,0:T(8,128)(2,1)S(1)}, u32[]{:S(2)}, u32[]{:S(2)}) async-start(bf16[4,512,128]{2,1,0:T(8,128)(2,1)} %shard_map.114), calls=%async_computation.1 | async-start | bytes 1048576 | tf_op jit(solution)/shard_map/all_to_all | solution.py:317
  60.7 123.3 %collective-permute-start.33 = (bf16[6144,256]{1,0:T(8,128)(2,1)}, bf16[6144,256]{1,0:T(8,128)(2,1)}, u32[]{:S(2)}, u32[]{:S(2)}) collective-permute-start(bf16[6144,256]{1,0:T(8,128)(2,1)} %get-tuple-element.21), channel_id=1, source_target_pairs={{3,0},{0,1},{1,2},{2,3},{7,4},{4,5},{5,6},{6,7},{11,8},{8,9},{9,10... | collective-permute-start | bytes 9437192 | tf_op jit(solution)/shard_map/ppermute | solution.py:286
  61.1 6.6 %collective-permute-start.27 = (bf16[128,512]{1,0:T(8,128)(2,1)S(1)}, bf16[128,512]{1,0:T(8,128)(2,1)S(1)}, u32[]{:S(2)}, u32[]{:S(2)}) collective-permute-start(bf16[128,512]{1,0:T(8,128)(2,1)S(1)} %get-tuple-element.28), channel_id=1, source_target_pairs={{0,48},{4,52},{8,56},{12,60},{16,0},{20,4},{24,8},{28,12},{32,16},... | collective-permute-start | bytes 393224 | tf_op jit(solution)/shard_map/ppermute | solution.py:243
  65.0 6.7 %collective-permute-start.21 = (bf16[128,512]{1,0:T(8,128)(2,1)S(1)}, bf16[128,512]{1,0:T(8,128)(2,1)S(1)}, u32[]{:S(2)}, u32[]{:S(2)}) collective-permute-start(bf16[128,512]{1,0:T(8,128)(2,1)S(1)} %get-tuple-element.29), channel_id=1, source_target_pairs={{0,16},{4,20},{8,24},{12,28},{16,32},{20,36},{24,40},{28,44},{32,4... | collective-permute-start | bytes 393224 | tf_op jit(solution)/shard_map/ppermute | solution.py:243
  65.0 9.1 %collective-permute-start.15 = (bf16[128,512]{1,0:T(8,128)(2,1)S(1)}, bf16[128,512]{1,0:T(8,128)(2,1)S(1)}, u32[]{:S(2)}, u32[]{:S(2)}) collective-permute-start(bf16[128,512]{1,0:T(8,128)(2,1)S(1)} %get-tuple-element.30), channel_id=1, source_target_pairs={{0,12},{4,0},{8,4},{12,8},{16,28},{20,16},{24,20},{28,24},{32,44},... | collective-permute-start | bytes 393224 | tf_op jit(solution)/shard_map/ppermute | solution.py:243
  67.7 6.4 %collective-permute-start.9 = (bf16[128,512]{1,0:T(8,128)(2,1)S(1)}, bf16[128,512]{1,0:T(8,128)(2,1)S(1)}, u32[]{:S(2)}, u32[]{:S(2)}) collective-permute-start(bf16[128,512]{1,0:T(8,128)(2,1)S(1)} %get-tuple-element.31), channel_id=1, source_target_pairs={{0,4},{4,8},{8,12},{12,0},{16,20},{20,24},{24,28},{28,16},{32,36},... | collective-permute-start | bytes 393224 | tf_op jit(solution)/shard_map/ppermute | solution.py:243
  67.7 6.5 %collective-permute-start.28 = (bf16[128,512]{1,0:T(8,128)(2,1)S(1)}, bf16[128,512]{1,0:T(8,128)(2,1)S(1)}, u32[]{:S(2)}, u32[]{:S(2)}) collective-permute-start(bf16[128,512]{1,0:T(8,128)(2,1)S(1)} %collective-permute-done.27), channel_id=1, source_target_pairs={{0,48},{4,52},{8,56},{12,60},{16,0},{20,4},{24,8},{28,12},{32,16},... | collective-permute-start | bytes 393224 | tf_op jit(solution)/shard_map/ppermute | solution.py:243
  71.7 24.2 %collective-permute-start.7 = (bf16[1024,384]{1,0:T(8,128)(2,1)S(1)}, bf16[1024,384]{1,0:T(8,128)(2,1)}, u32[]{:S(2)}, u32[]{:S(2)}) collective-permute-start(bf16[1024,384]{1,0:T(8,128)(2,1)S(1)} %slice.71), channel_id=1, source_target_pairs={{1,0},{2,1},{3,2},{0,3},{5,4},{6,5},{7,6},{4,7},{9,8},{10,9},{11,1... | collective-permute-start | bytes 2359304 | tf_op jit(solution)/shard_map/ppermute | solution.py:286
  74.1 70.4 %collective-permute-start.8 = (bf16[1024,384]{1,0:T(8,128)(2,1)S(1)}, bf16[1024,384]{1,0:T(8,128)(2,1)S(1)}, u32[]{:S(2)}, u32[]{:S(2)}) collective-permute-start(bf16[1024,384]{1,0:T(8,128)(2,1)S(1)} %slice.72), channel_id=1, source_target_pairs={{3,0},{0,1},{1,2},{2,3},{7,4},{4,5},{5,6},{6,7},{11,8},{8,9},{9,10... | collective-permute-start | bytes 2359304 | tf_op jit(solution)/shard_map/ppermute | solution.py:286
  74.1 5.5 %collective-permute-start.22 = (bf16[128,512]{1,0:T(8,128)(2,1)S(1)}, bf16[128,512]{1,0:T(8,128)(2,1)S(1)}, u32[]{:S(2)}, u32[]{:S(2)}) collective-permute-start(bf16[128,512]{1,0:T(8,128)(2,1)S(1)} %collective-permute-done.21), channel_id=1, source_target_pairs={{0,16},{4,20},{8,24},{12,28},{16,32},{20,36},{24,40},{28,44},{32,4... | collective-permute-start | bytes 393224 | tf_op jit(solution)/shard_map/ppermute | solution.py:243
  74.2 6.3 %collective-permute-start.16 = (bf16[128,512]{1,0:T(8,128)(2,1)S(1)}, bf16[128,512]{1,0:T(8,128)(2,1)S(1)}, u32[]{:S(2)}, u32[]{:S(2)}) collective-permute-start(bf16[128,512]{1,0:T(8,128)(2,1)S(1)} %collective-permute-done.15), channel_id=1, source_target_pairs={{0,12},{4,0},{8,4},{12,8},{16,28},{20,16},{24,20},{28,24},{32,44},... | collective-permute-start | bytes 393224 | tf_op jit(solution)/shard_map/ppermute | solution.py:243
  79.6 5.4 %collective-permute-start.10 = (bf16[128,512]{1,0:T(8,128)(2,1)S(1)}, bf16[128,512]{1,0:T(8,128)(2,1)S(1)}, u32[]{:S(2)}, u32[]{:S(2)}) collective-permute-start(bf16[128,512]{1,0:T(8,128)(2,1)S(1)} %collective-permute-done.9), channel_id=1, source_target_pairs={{0,4},{4,8},{8,12},{12,0},{16,20},{20,24},{24,28},{28,16},{32,36},... | collective-permute-start | bytes 393224 | tf_op jit(solution)/shard_map/ppermute | solution.py:243
  80.5 4.5 %collective-permute-start.29 = (bf16[128,512]{1,0:T(8,128)(2,1)S(1)}, bf16[128,512]{1,0:T(8,128)(2,1)S(1)}, u32[]{:S(2)}, u32[]{:S(2)}) collective-permute-start(bf16[128,512]{1,0:T(8,128)(2,1)S(1)} %collective-permute-done.28), channel_id=1, source_target_pairs={{0,48},{4,52},{8,56},{12,60},{16,0},{20,4},{24,8},{28,12},{32,16},... | collective-permute-start | bytes 393224 | tf_op jit(solution)/shard_map/ppermute | solution.py:243
  85.0 5.4 %collective-permute-start.23 = (bf16[128,512]{1,0:T(8,128)(2,1)S(1)}, bf16[128,512]{1,0:T(8,128)(2,1)S(1)}, u32[]{:S(2)}, u32[]{:S(2)}) collective-permute-start(bf16[128,512]{1,0:T(8,128)(2,1)S(1)} %collective-permute-done.22), channel_id=1, source_target_pairs={{0,16},{4,20},{8,24},{12,28},{16,32},{20,36},{24,40},{28,44},{32,4... | collective-permute-start | bytes 393224 | tf_op jit(solution)/shard_map/ppermute | solution.py:243
  85.0 5.5 %collective-permute-start.17 = (bf16[128,512]{1,0:T(8,128)(2,1)S(1)}, bf16[128,512]{1,0:T(8,128)(2,1)S(1)}, u32[]{:S(2)}, u32[]{:S(2)}) collective-permute-start(bf16[128,512]{1,0:T(8,128)(2,1)S(1)} %collective-permute-done.16), channel_id=1, source_target_pairs={{0,12},{4,0},{8,4},{12,8},{16,28},{20,16},{24,20},{28,24},{32,44},... | collective-permute-start | bytes 393224 | tf_op jit(solution)/shard_map/ppermute | solution.py:243
  90.4 5.4 %collective-permute-start.11 = (bf16[128,512]{1,0:T(8,128)(2,1)S(1)}, bf16[128,512]{1,0:T(8,128)(2,1)S(1)}, u32[]{:S(2)}, u32[]{:S(2)}) collective-permute-start(bf16[128,512]{1,0:T(8,128)(2,1)S(1)} %collective-permute-done.10), channel_id=1, source_target_pairs={{0,4},{4,8},{8,12},{12,0},{16,20},{20,24},{24,28},{28,16},{32,36},... | collective-permute-start | bytes 393224 | tf_op jit(solution)/shard_map/ppermute | solution.py:243
  90.5 56.4 %collective-permute-start.30 = (bf16[512,512]{1,0:T(8,128)(2,1)S(1)}, bf16[512,512]{1,0:T(8,128)(2,1)S(1)}, u32[]{:S(2)}, u32[]{:S(2)}) collective-permute-start(bf16[512,512]{1,0:T(8,128)(2,1)S(1)} %pad_maximum_fusion.8.refs_9_), channel_id=1, source_target_pairs={{0,12},{4,0},{8,4},{12,8},{16,28},{20,16},{24,20},{28,24},{32,44},... | collective-permute-start | bytes 1572872 | tf_op jit(solution)/shard_map/ppermute | solution.py:243
  95.9 54.5 %collective-permute-start.24 = (bf16[512,512]{1,0:T(8,128)(2,1)S(1)}, bf16[512,512]{1,0:T(8,128)(2,1)S(1)}, u32[]{:S(2)}, u32[]{:S(2)}) collective-permute-start(bf16[512,512]{1,0:T(8,128)(2,1)S(1)} %pad_maximum_fusion.7.refs_8_), channel_id=1, source_target_pairs={{0,4},{4,8},{8,12},{12,0},{16,20},{20,24},{24,28},{28,16},{32,36},... | collective-permute-start | bytes 1572872 | tf_op jit(solution)/shard_map/ppermute | solution.py:243
  95.9 55.3 %collective-permute-start.18 = (bf16[512,512]{1,0:T(8,128)(2,1)S(1)}, bf16[512,512]{1,0:T(8,128)(2,1)S(1)}, u32[]{:S(2)}, u32[]{:S(2)}) collective-permute-start(bf16[512,512]{1,0:T(8,128)(2,1)S(1)} %pad_maximum_fusion.6.refs_7_), channel_id=1, source_target_pairs={{0,48},{4,52},{8,56},{12,60},{16,0},{20,4},{24,8},{28,12},{32,16},... | collective-permute-start | bytes 1572872 | tf_op jit(solution)/shard_map/ppermute | solution.py:243
  144.4 10.9 %collective-permute-start.12 = (bf16[512,512]{1,0:T(8,128)(2,1)S(1)}, bf16[512,512]{1,0:T(8,128)(2,1)S(1)}, u32[]{:S(2)}, u32[]{:S(2)}) collective-permute-start(bf16[512,512]{1,0:T(8,128)(2,1)S(1)} %pad_maximum_fusion.5.refs_6_), channel_id=1, source_target_pairs={{0,16},{4,20},{8,24},{12,28},{16,32},{20,36},{24,40},{28,44},{32,4... | collective-permute-start | bytes 1572872 | tf_op jit(solution)/shard_map/ppermute | solution.py:243
  146.9 9.3 %collective-permute-start.31 = (bf16[512,512]{1,0:T(8,128)(2,1)S(1)}, bf16[512,512]{1,0:T(8,128)(2,1)}, u32[]{:S(2)}, u32[]{:S(2)}) collective-permute-start(bf16[512,512]{1,0:T(8,128)(2,1)S(1)} %collective-permute-done.30.refs_13_), channel_id=1, source_target_pairs={{0,12},{4,0},{8,4},{12,8},{16,28},{20,16},{24,20},{28,24},{32,44},... | collective-permute-start | bytes 1572872 | tf_op jit(solution)/shard_map/ppermute | solution.py:243
  150.4 9.5 %collective-permute-start.25 = (bf16[512,512]{1,0:T(8,128)(2,1)S(1)}, bf16[512,512]{1,0:T(8,128)(2,1)}, u32[]{:S(2)}, u32[]{:S(2)}) collective-permute-start(bf16[512,512]{1,0:T(8,128)(2,1)S(1)} %collective-permute-done.24.refs_12_), channel_id=1, source_target_pairs={{0,4},{4,8},{8,12},{12,0},{16,20},{20,24},{24,28},{28,16},{32,36},... | collective-permute-start | bytes 1572872 | tf_op jit(solution)/shard_map/ppermute | solution.py:243
  151.2 8.7 %collective-permute-start.19 = (bf16[512,512]{1,0:T(8,128)(2,1)S(1)}, bf16[512,512]{1,0:T(8,128)(2,1)}, u32[]{:S(2)}, u32[]{:S(2)}) collective-permute-start(bf16[512,512]{1,0:T(8,128)(2,1)S(1)} %collective-permute-done.18.refs_11_), channel_id=1, source_target_pairs={{0,48},{4,52},{8,56},{12,60},{16,0},{20,4},{24,8},{28,12},{32,16},... | collective-permute-start | bytes 1572872 | tf_op jit(solution)/shard_map/ppermute | solution.py:243
  155.4 11.0 %collective-permute-start.13 = (bf16[512,512]{1,0:T(8,128)(2,1)S(1)}, bf16[512,512]{1,0:T(8,128)(2,1)}, u32[]{:S(2)}, u32[]{:S(2)}) collective-permute-start(bf16[512,512]{1,0:T(8,128)(2,1)S(1)} %collective-permute-done.12.refs_10_), channel_id=1, source_target_pairs={{0,16},{4,20},{8,24},{12,28},{16,32},{20,36},{24,40},{28,44},{32,4... | collective-permute-start | bytes 1572872 | tf_op jit(solution)/shard_map/ppermute | solution.py:243
  156.2 23.5 %collective-permute-start.32 = (bf16[512,512]{1,0:T(8,128)(2,1)}, bf16[512,512]{1,0:T(8,128)(2,1)}, u32[]{:S(2)}, u32[]{:S(2)}) collective-permute-start(bf16[512,512]{1,0:T(8,128)(2,1)} %collective-permute-done.31.refs_17_), channel_id=1, source_target_pairs={{0,12},{4,0},{8,4},{12,8},{16,28},{20,16},{24,20},{28,24},{32,44},... | collective-permute-start | bytes 1572872 | tf_op jit(solution)/shard_map/ppermute | solution.py:243
  160.0 19.7 %collective-permute-start.26 = (bf16[512,512]{1,0:T(8,128)(2,1)}, bf16[512,512]{1,0:T(8,128)(2,1)}, u32[]{:S(2)}, u32[]{:S(2)}) collective-permute-start(bf16[512,512]{1,0:T(8,128)(2,1)} %collective-permute-done.25.refs_16_), channel_id=1, source_target_pairs={{0,4},{4,8},{8,12},{12,0},{16,20},{20,24},{24,28},{28,16},{32,36},... | collective-permute-start | bytes 1572872 | tf_op jit(solution)/shard_map/ppermute | solution.py:243
  160.0 19.7 %collective-permute-start.20 = (bf16[512,512]{1,0:T(8,128)(2,1)}, bf16[512,512]{1,0:T(8,128)(2,1)}, u32[]{:S(2)}, u32[]{:S(2)}) collective-permute-start(bf16[512,512]{1,0:T(8,128)(2,1)} %collective-permute-done.19.refs_15_), channel_id=1, source_target_pairs={{0,48},{4,52},{8,56},{12,60},{16,0},{20,4},{24,8},{28,12},{32,16},... | collective-permute-start | bytes 1572872 | tf_op jit(solution)/shard_map/ppermute | solution.py:243
  166.4 13.3 %collective-permute-start.14 = (bf16[512,512]{1,0:T(8,128)(2,1)}, bf16[512,512]{1,0:T(8,128)(2,1)}, u32[]{:S(2)}, u32[]{:S(2)}) collective-permute-start(bf16[512,512]{1,0:T(8,128)(2,1)} %collective-permute-done.13.refs_14_), channel_id=1, source_target_pairs={{0,16},{4,20},{8,24},{12,28},{16,32},{20,36},{24,40},{28,44},{32,4... | collective-permute-start | bytes 1572872 | tf_op jit(solution)/shard_map/ppermute | solution.py:243
  184.0 8.2 %collective-permute-start.48 = (bf16[512,384]{1,0:T(8,128)(2,1)S(1)}, bf16[512,384]{1,0:T(8,128)(2,1)S(1)}, u32[]{:S(2)}, u32[]{:S(2)}) collective-permute-start(bf16[512,384]{1,0:T(8,128)(2,1)S(1)} %shard_map.116), channel_id=1, source_target_pairs={{2,0},{3,1},{0,2},{1,3},{6,4},{7,5},{4,6},{5,7},{10,8},{11,9},{8,1... | collective-permute-start | bytes 1179656 | tf_op jit(solution)/shard_map/ppermute | solution.py:286
  186.0 9.0 %collective-permute-start.42 = (bf16[256,384]{1,0:T(8,128)(2,1)S(1)}, bf16[256,384]{1,0:T(8,128)(2,1)S(1)}, u32[]{:S(2)}, u32[]{:S(2)}) collective-permute-start(bf16[256,384]{1,0:T(8,128)(2,1)S(1)} %get-tuple-element.38), channel_id=1, source_target_pairs={{0,12},{4,0},{8,4},{12,8},{16,28},{20,16},{24,20},{28,24},{32,44},... | collective-permute-start | bytes 589832 | tf_op jit(solution)/shard_map/ppermute | solution.py:243
  188.8 8.6 %collective-permute-start.36 = (bf16[256,384]{1,0:T(8,128)(2,1)S(1)}, bf16[256,384]{1,0:T(8,128)(2,1)S(1)}, u32[]{:S(2)}, u32[]{:S(2)}) collective-permute-start(bf16[256,384]{1,0:T(8,128)(2,1)S(1)} %get-tuple-element.39), channel_id=1, source_target_pairs={{0,4},{4,8},{8,12},{12,0},{16,20},{20,24},{24,28},{28,16},{32,36},... | collective-permute-start | bytes 589832 | tf_op jit(solution)/shard_map/ppermute | solution.py:243
  188.8 66.8 %collective-permute-start.35 = (bf16[6144,256]{1,0:T(8,128)(2,1)S(1)}, bf16[6144,256]{1,0:T(8,128)(2,1)S(1)}, u32[]{:S(2)}, u32[]{:S(2)}) collective-permute-start(bf16[6144,256]{1,0:T(8,128)(2,1)S(1)} %copy-done.20), channel_id=1, source_target_pairs={{1,0},{2,1},{3,2},{0,3},{5,4},{6,5},{7,6},{4,7},{9,8},{10,9},{11,1... | collective-permute-start | bytes 9437192 | tf_op jit(solution)/shard_map/ppermute | solution.py:286
  192.2 5.3 %collective-permute-start.55 = (bf16[256,384]{1,0:T(8,128)(2,1)S(1)}, bf16[256,384]{1,0:T(8,128)(2,1)S(1)}, u32[]{:S(2)}, u32[]{:S(2)}) collective-permute-start(bf16[256,384]{1,0:T(8,128)(2,1)S(1)} %get-tuple-element.36), channel_id=1, source_target_pairs={{0,48},{4,52},{8,56},{12,60},{16,0},{20,4},{24,8},{28,12},{32,16},... | collective-permute-start | bytes 589832 | tf_op jit(solution)/shard_map/ppermute | solution.py:243
  195.0 6.4 %collective-permute-start.43 = (bf16[256,384]{1,0:T(8,128)(2,1)S(1)}, bf16[256,384]{1,0:T(8,128)(2,1)S(1)}, u32[]{:S(2)}, u32[]{:S(2)}) collective-permute-start(bf16[256,384]{1,0:T(8,128)(2,1)S(1)} %collective-permute-done.42), channel_id=1, source_target_pairs={{0,12},{4,0},{8,4},{12,8},{16,28},{20,16},{24,20},{28,24},{32,44},... | collective-permute-start | bytes 589832 | tf_op jit(solution)/shard_map/ppermute | solution.py:243
  197.4 7.4 %collective-permute-start.49 = (bf16[256,384]{1,0:T(8,128)(2,1)S(1)}, bf16[256,384]{1,0:T(8,128)(2,1)S(1)}, u32[]{:S(2)}, u32[]{:S(2)}) collective-permute-start(bf16[256,384]{1,0:T(8,128)(2,1)S(1)} %get-tuple-element.37), channel_id=1, source_target_pairs={{0,16},{4,20},{8,24},{12,28},{16,32},{20,36},{24,40},{28,44},{32,4... | collective-permute-start | bytes 589832 | tf_op jit(solution)/shard_map/ppermute | solution.py:243
  197.4 7.4 %collective-permute-start.37 = (bf16[256,384]{1,0:T(8,128)(2,1)S(1)}, bf16[256,384]{1,0:T(8,128)(2,1)S(1)}, u32[]{:S(2)}, u32[]{:S(2)}) collective-permute-start(bf16[256,384]{1,0:T(8,128)(2,1)S(1)} %collective-permute-done.36), channel_id=1, source_target_pairs={{0,4},{4,8},{8,12},{12,0},{16,20},{20,24},{24,28},{28,16},{32,36},... | collective-permute-start | bytes 589832 | tf_op jit(solution)/shard_map/ppermute | solution.py:243
  197.6 7.3 %collective-permute-start.56 = (bf16[256,384]{1,0:T(8,128)(2,1)S(1)}, bf16[256,384]{1,0:T(8,128)(2,1)S(1)}, u32[]{:S(2)}, u32[]{:S(2)}) collective-permute-start(bf16[256,384]{1,0:T(8,128)(2,1)S(1)} %collective-permute-done.55), channel_id=1, source_target_pairs={{0,48},{4,52},{8,56},{12,60},{16,0},{20,4},{24,8},{28,12},{32,16},... | collective-permute-start | bytes 589832 | tf_op jit(solution)/shard_map/ppermute | solution.py:243
  201.4 6.4 %collective-permute-start.44 = (bf16[256,384]{1,0:T(8,128)(2,1)S(1)}, bf16[256,384]{1,0:T(8,128)(2,1)S(1)}, u32[]{:S(2)}, u32[]{:S(2)}) collective-permute-start(bf16[256,384]{1,0:T(8,128)(2,1)S(1)} %collective-permute-done.43), channel_id=1, source_target_pairs={{0,12},{4,0},{8,4},{12,8},{16,28},{20,16},{24,20},{28,24},{32,44},... | collective-permute-start | bytes 589832 | tf_op jit(solution)/shard_map/ppermute | solution.py:243
  204.8 5.7 %collective-permute-start.50 = (bf16[256,384]{1,0:T(8,128)(2,1)S(1)}, bf16[256,384]{1,0:T(8,128)(2,1)S(1)}, u32[]{:S(2)}, u32[]{:S(2)}) collective-permute-start(bf16[256,384]{1,0:T(8,128)(2,1)S(1)} %collective-permute-done.49), channel_id=1, source_target_pairs={{0,16},{4,20},{8,24},{12,28},{16,32},{20,36},{24,40},{28,44},{32,4... | collective-permute-start | bytes 589832 | tf_op jit(solution)/shard_map/ppermute | solution.py:243
  204.8 5.8 %collective-permute-start.38 = (bf16[256,384]{1,0:T(8,128)(2,1)S(1)}, bf16[256,384]{1,0:T(8,128)(2,1)S(1)}, u32[]{:S(2)}, u32[]{:S(2)}) collective-permute-start(bf16[256,384]{1,0:T(8,128)(2,1)S(1)} %collective-permute-done.37), channel_id=1, source_target_pairs={{0,4},{4,8},{8,12},{12,0},{16,20},{20,24},{24,28},{28,16},{32,36},... | collective-permute-start | bytes 589832 | tf_op jit(solution)/shard_map/ppermute | solution.py:243
  204.9 5.9 %collective-permute-start.57 = (bf16[256,384]{1,0:T(8,128)(2,1)S(1)}, bf16[256,384]{1,0:T(8,128)(2,1)S(1)}, u32[]{:S(2)}, u32[]{:S(2)}) collective-permute-start(bf16[256,384]{1,0:T(8,128)(2,1)S(1)} %collective-permute-done.56), channel_id=1, source_target_pairs={{0,48},{4,52},{8,56},{12,60},{16,0},{20,4},{24,8},{28,12},{32,16},... | collective-permute-start | bytes 589832 | tf_op jit(solution)/shard_map/ppermute | solution.py:243
  207.8 13.3 %collective-permute-start.45 = (bf16[1024,384]{1,0:T(8,128)(2,1)S(1)}, bf16[1024,384]{1,0:T(8,128)(2,1)S(1)}, u32[]{:S(2)}, u32[]{:S(2)}) collective-permute-start(bf16[1024,384]{1,0:T(8,128)(2,1)S(1)} %pad_maximum_fusion.1.refs_5_), channel_id=1, source_target_pairs={{0,48},{4,52},{8,56},{12,60},{16,0},{20,4},{24,8},{28,12},{32,16},... | collective-permute-start | bytes 2359304 | tf_op jit(solution)/shard_map/ppermute | solution.py:243
  210.5 6.1 %collective-permute-start.51 = (bf16[256,384]{1,0:T(8,128)(2,1)S(1)}, bf16[256,384]{1,0:T(8,128)(2,1)S(1)}, u32[]{:S(2)}, u32[]{:S(2)}) collective-permute-start(bf16[256,384]{1,0:T(8,128)(2,1)S(1)} %collective-permute-done.50), channel_id=1, source_target_pairs={{0,16},{4,20},{8,24},{12,28},{16,32},{20,36},{24,40},{28,44},{32,4... | collective-permute-start | bytes 589832 | tf_op jit(solution)/shard_map/ppermute | solution.py:243
  210.6 16.5 %collective-permute-start.39 = (bf16[1024,384]{1,0:T(8,128)(2,1)S(1)}, bf16[1024,384]{1,0:T(8,128)(2,1)S(1)}, u32[]{:S(2)}, u32[]{:S(2)}) collective-permute-start(bf16[1024,384]{1,0:T(8,128)(2,1)S(1)} %pad_maximum_fusion.refs_4_), channel_id=1, source_target_pairs={{0,16},{4,20},{8,24},{12,28},{16,32},{20,36},{24,40},{28,44},{32,4... | collective-permute-start | bytes 2359304 | tf_op jit(solution)/shard_map/ppermute | solution.py:243
  210.8 16.3 %collective-permute-start.58 = (bf16[1024,384]{1,0:T(8,128)(2,1)S(1)}, bf16[1024,384]{1,0:T(8,128)(2,1)S(1)}, u32[]{:S(2)}, u32[]{:S(2)}) collective-permute-start(bf16[1024,384]{1,0:T(8,128)(2,1)S(1)} %pad_maximum_fusion.3.refs_7_), channel_id=1, source_target_pairs={{0,12},{4,0},{8,4},{12,8},{16,28},{20,16},{24,20},{28,24},{32,44},... | collective-permute-start | bytes 2359304 | tf_op jit(solution)/shard_map/ppermute | solution.py:243
  216.7 14.1 %collective-permute-start.52 = (bf16[1024,384]{1,0:T(8,128)(2,1)S(1)}, bf16[1024,384]{1,0:T(8,128)(2,1)S(1)}, u32[]{:S(2)}, u32[]{:S(2)}) collective-permute-start(bf16[1024,384]{1,0:T(8,128)(2,1)S(1)} %pad_maximum_fusion.2.refs_6_), channel_id=1, source_target_pairs={{0,4},{4,8},{8,12},{12,0},{16,20},{20,24},{24,28},{28,16},{32,36},... | collective-permute-start | bytes 2359304 | tf_op jit(solution)/shard_map/ppermute | solution.py:243
  221.1 19.9 %collective-permute-start.46 = (bf16[1024,384]{1,0:T(8,128)(2,1)S(1)}, bf16[1024,384]{1,0:T(8,128)(2,1)S(1)}, u32[]{:S(2)}, u32[]{:S(2)}) collective-permute-start(bf16[1024,384]{1,0:T(8,128)(2,1)S(1)} %collective-permute-done.45.refs_9_), channel_id=1, source_target_pairs={{0,48},{4,52},{8,56},{12,60},{16,0},{20,4},{24,8},{28,12},{32,16},... | collective-permute-start | bytes 2359304 | tf_op jit(solution)/shard_map/ppermute | solution.py:243
  227.1 20.8 %collective-permute-start.40 = (bf16[1024,384]{1,0:T(8,128)(2,1)S(1)}, bf16[1024,384]{1,0:T(8,128)(2,1)S(1)}, u32[]{:S(2)}, u32[]{:S(2)}) collective-permute-start(bf16[1024,384]{1,0:T(8,128)(2,1)S(1)} %collective-permute-done.39.refs_8_), channel_id=1, source_target_pairs={{0,16},{4,20},{8,24},{12,28},{16,32},{20,36},{24,40},{28,44},{32,4... | collective-permute-start | bytes 2359304 | tf_op jit(solution)/shard_map/ppermute | solution.py:243
  227.1 20.8 %collective-permute-start.59 = (bf16[1024,384]{1,0:T(8,128)(2,1)S(1)}, bf16[1024,384]{1,0:T(8,128)(2,1)S(1)}, u32[]{:S(2)}, u32[]{:S(2)}) collective-permute-start(bf16[1024,384]{1,0:T(8,128)(2,1)S(1)} %collective-permute-done.58.refs_11_), channel_id=1, source_target_pairs={{0,12},{4,0},{8,4},{12,8},{16,28},{20,16},{24,20},{28,24},{32,44},... | collective-permute-start | bytes 2359304 | tf_op jit(solution)/shard_map/ppermute | solution.py:243
  230.8 18.2 %collective-permute-start.53 = (bf16[1024,384]{1,0:T(8,128)(2,1)S(1)}, bf16[1024,384]{1,0:T(8,128)(2,1)S(1)}, u32[]{:S(2)}, u32[]{:S(2)}) collective-permute-start(bf16[1024,384]{1,0:T(8,128)(2,1)S(1)} %collective-permute-done.52.refs_10_), channel_id=1, source_target_pairs={{0,4},{4,8},{8,12},{12,0},{16,20},{20,24},{24,28},{28,16},{32,36},... | collective-permute-start | bytes 2359304 | tf_op jit(solution)/shard_map/ppermute | solution.py:243
  241.0 48.8 %collective-permute-start.47 = (bf16[1024,384]{1,0:T(8,128)(2,1)S(1)}, bf16[1024,384]{1,0:T(8,128)(2,1)S(1)}, u32[]{:S(2)}, u32[]{:S(2)}) collective-permute-start(bf16[1024,384]{1,0:T(8,128)(2,1)S(1)} %collective-permute-done.46.refs_5_), channel_id=1, source_target_pairs={{0,48},{4,52},{8,56},{12,60},{16,0},{20,4},{24,8},{28,12},{32,16},... | collective-permute-start | bytes 2359304 | tf_op jit(solution)/shard_map/ppermute | solution.py:243
  247.9 41.9 %collective-permute-start.41 = (bf16[1024,384]{1,0:T(8,128)(2,1)S(1)}, bf16[1024,384]{1,0:T(8,128)(2,1)S(1)}, u32[]{:S(2)}, u32[]{:S(2)}) collective-permute-start(bf16[1024,384]{1,0:T(8,128)(2,1)S(1)} %collective-permute-done.40.refs_4_), channel_id=1, source_target_pairs={{0,16},{4,20},{8,24},{12,28},{16,32},{20,36},{24,40},{28,44},{32,4... | collective-permute-start | bytes 2359304 | tf_op jit(solution)/shard_map/ppermute | solution.py:243
  247.9 41.9 %collective-permute-start.60 = (bf16[1024,384]{1,0:T(8,128)(2,1)S(1)}, bf16[1024,384]{1,0:T(8,128)(2,1)S(1)}, u32[]{:S(2)}, u32[]{:S(2)}) collective-permute-start(bf16[1024,384]{1,0:T(8,128)(2,1)S(1)} %collective-permute-done.59.refs_7_), channel_id=1, source_target_pairs={{0,12},{4,0},{8,4},{12,8},{16,28},{20,16},{24,20},{28,24},{32,44},... | collective-permute-start | bytes 2359304 | tf_op jit(solution)/shard_map/ppermute | solution.py:243
  248.9 40.9 %collective-permute-start.54 = (bf16[1024,384]{1,0:T(8,128)(2,1)S(1)}, bf16[1024,384]{1,0:T(8,128)(2,1)S(1)}, u32[]{:S(2)}, u32[]{:S(2)}) collective-permute-start(bf16[1024,384]{1,0:T(8,128)(2,1)S(1)} %collective-permute-done.53.refs_6_), channel_id=1, source_target_pairs={{0,4},{4,8},{8,12},{12,0},{16,20},{20,24},{24,28},{28,16},{32,36},... | collective-permute-start | bytes 2359304 | tf_op jit(solution)/shard_map/ppermute | solution.py:243
  255.6 45.9 %collective-permute-start.34 = (bf16[1,512,384]{2,1,0:T(8,128)(2,1)S(1)}, bf16[1,512,384]{2,1,0:T(8,128)(2,1)}, u32[]{:S(2)}, u32[]{:S(2)}) collective-permute-start(bf16[1,512,384]{2,1,0:T(8,128)(2,1)S(1)} %bitcast.80), channel_id=1, source_target_pairs={{0,64},{1,65},{2,66},{3,67},{64,0},{65,1},{66,2},{67,3},{4,68},{5,... | collective-permute-start | bytes 1179656 | tf_op jit(solution)/shard_map/ppermute | solution.py:294
  297.7 4.6 %collective-permute-start.62 = (bf16[16,256]{1,0:T(8,128)(2,1)S(1)}, bf16[16,256]{1,0:T(8,128)(2,1)S(1)}, u32[]{:S(2)}, u32[]{:S(2)}) collective-permute-start(bf16[16,256]{1,0:T(8,128)(2,1)S(1)} %get-tuple-element.44), channel_id=1, source_target_pairs={{1,64},{2,65},{3,66},{0,67},{65,0},{66,1},{67,2},{64,3},{5,68},{6,... | collective-permute-start | bytes 24584 | tf_op jit(solution)/shard_map/ppermute | solution.py:294
  301.5 4.4 %collective-permute-start.63 = (bf16[16,256]{1,0:T(8,128)(2,1)S(1)}, bf16[16,256]{1,0:T(8,128)(2,1)S(1)}, u32[]{:S(2)}, u32[]{:S(2)}) collective-permute-start(bf16[16,256]{1,0:T(8,128)(2,1)S(1)} %get-tuple-element.45), channel_id=1, source_target_pairs={{3,64},{0,65},{1,66},{2,67},{67,0},{64,1},{65,2},{66,3},{7,68},{4,... | collective-permute-start | bytes 24584 | tf_op jit(solution)/shard_map/ppermute | solution.py:294
  301.5 4.4 %collective-permute-start.61 = (bf16[16,512]{1,0:T(8,128)(2,1)S(1)}, bf16[16,512]{1,0:T(8,128)(2,1)S(1)}, u32[]{:S(2)}, u32[]{:S(2)}) collective-permute-start(bf16[16,512]{1,0:T(8,128)(2,1)S(1)} %slice.96), channel_id=1, source_target_pairs={{0,64},{1,65},{2,66},{3,67},{64,0},{65,1},{66,2},{67,3},{4,68},{5,... | collective-permute-start | bytes 49160 | tf_op jit(solution)/shard_map/ppermute | solution.py:294
  (28 other events, 463.6 us)

commit v5 on v4

--- a/solution.py
+++ b/solution.py
@@ -93,11 +93,35 @@
     )(packed, prior, gain)
 
 
-def project_kernel(steps, final, *refs):
-    source, inverse_ref, w0, w1, w2, w3 = refs[:6]
-    count = 4 * len(steps)
-    blocks = refs[6 : 6 + count]
-    rest = refs[6 + count :]
+def listed(gathered, steps):
+    arrays, layout = [], []
+    for step in steps:
+        for half, parts in enumerate(gathered):
+            first = 0
+            for array in parts[step]:
+                count = 4 * array.shape[0] // parts[0][0].shape[0]
+                arrays.append(array)
+                layout.append((half, step, first, count))
+                first += count
+    return arrays, layout
+
+
+def each_part(source, layout, blocks, rows, body):
+    for (half, step, first, count), block in zip(layout, blocks):
+
+        def one(i, carry, half=half, step=step, first=first, block=block):
+            part = source[(half * 4 + step) * 4 + first + i]
+            across = pl.ds(pl.multiple_of(i * rows, BLK), rows)
+            body(slice(half * rows, (half + 1) * rows), part, block[across, :], step)
+            return carry
+
+        lax.fori_loop(0, count, one, 0)
+
+
+def project_kernel(layout, final, *refs):
+    source, inverse_ref, w0, w1, w2, w3, w4 = refs[:7]
+    blocks = refs[7 : 7 + len(layout)]
+    rest = refs[7 + len(layout) :]
     if final:
         acc_ref, square_ref, residual_ref, out_ref, acc, square = rest
         acc[...] = acc_ref[...]
@@ -106,93 +130,83 @@
         acc, square = rest
         acc[...] = jnp.zeros_like(acc)
         square[...] = jnp.zeros_like(square)
-
-    def add(i, carry):
-        across = pl.ds(pl.multiple_of(i * BLK, BLK), BLK)
-        for n, step in enumerate(steps):
-            for c in range(4):
-                here = slice(c * BLK, (c + 1) * BLK)
-                part = source[(c * 4 + step) * 4 + i]
-                rows = pl.ds(pl.multiple_of(part * HD, HD), HD)
-                a = blocks[n * 4 + c][across, :]
-                w = jnp.concatenate([w[rows, :] for w in (w0, w1, w2, w3)], axis=0)
-                acc[here, :] += dot(a, w)
-                wide = a.astype(jnp.float32)
-                wide = wide * wide * inverse_ref[pl.ds(part, 1), :]
-                squares = square[here, :]
-                for j in range(4):
-                    squares += wide[:, j * HD : (j + 1) * HD]
-                square[here, :] = squares
-        return carry
-
-    lax.fori_loop(0, 4, add, 0)
+    middle = w2.shape[0] // HD
+
+    def body(here, part, a, step):
+        rows = pl.ds(pl.multiple_of(part * HD, HD), HD)
+        inner = pl.ds(pl.multiple_of(lax.rem(part, middle) * HD, HD), HD)
+        lower = (part < middle).astype(jnp.float32)
+        far = w2[inner, :].astype(jnp.float32) * lower
+        far = far + w3[inner, :].astype(jnp.float32) * (1.0 - lower)
+        w = jnp.concatenate([w0[rows, :], w1[rows, :], far.astype(w0.dtype), w4[rows, :]], axis=0)
+        acc[here, :] += dot(a, w)
+        wide = a.astype(jnp.float32)
+        wide = wide * wide * inverse_ref[pl.ds(part, 1), :]
+        squares = square[here, :]
+        for j in range(a.shape[1] // HD):
+            squares += wide[:, j * HD : (j + 1) * HD]
+        square[here, :] = squares
+
+    each_part(source, layout, blocks, acc.shape[0] // 2, body)
     if final:
         mean = jnp.sum(square[...], axis=1, keepdims=True) / HDIM
         scaled = acc[...] * lax.rsqrt(mean + epsilon)
         out_ref[...] = (residual_ref[...].astype(jnp.float32) + scaled).astype(out_ref.dtype)
 
 
-def project(source, inverse, weights, rings, residual):
+def project(source, inverse, weights, gathered, residual):
     rows, columns = residual.shape
     sums = [
         jax.ShapeDtypeStruct((rows, columns), jnp.float32),
         jax.ShapeDtypeStruct((rows, HD), jnp.float32),
     ]
     smem, vmem = pl.BlockSpec(memory_space=pltpu.SMEM), pl.BlockSpec(memory_space=pltpu.VMEM)
-
-    def blocks(steps):
-        return [rings[c][step] for step in steps for c in range(4)]
-
-    early = [0, 1, 2]
+    arrays, layout = listed(gathered, [0, 1, 2])
     acc, square = pl.pallas_call(
-        functools.partial(project_kernel, early, False),
-        in_specs=[smem] + [vmem] * (5 + 4 * len(early)),
+        functools.partial(project_kernel, layout, False),
+        in_specs=[smem] + [vmem] * (6 + len(arrays)),
         out_specs=[vmem] * 2,
         out_shape=sums,
         compiler_params=pltpu.CompilerParams(vmem_limit_bytes=18 * MIB),
-    )(source, inverse, *weights, *blocks(early))
+    )(source, inverse, *weights, *arrays)
+    arrays, layout = listed(gathered, [3])
     return pl.pallas_call(
-        functools.partial(project_kernel, [3], True),
-        in_specs=[smem] + [vmem] * (5 + 4 + 3),
+        functools.partial(project_kernel, layout, True),
+        in_specs=[smem] + [vmem] * (6 + len(arrays) + 3),
         out_specs=vmem,
         out_shape=jax.ShapeDtypeStruct((rows, columns), jnp.bfloat16),
         scratch_shapes=[pltpu.VMEM(x.shape, x.dtype) for x in sums],
         compiler_params=pltpu.CompilerParams(vmem_limit_bytes=18 * MIB),
-    )(source, inverse, *weights, *blocks([3]), acc, square, residual)
-
-
-def encode_kernel(steps, first, final, *refs):
-    source, e0, e1, e2 = refs[:4]
-    count = 4 * len(steps)
-    blocks = refs[4 : 4 + count]
-    rest = refs[4 + count :]
+    )(source, inverse, *weights, *arrays, acc, square, residual)
+
+
+def encode_kernel(layout, late, first, final, *refs):
+    source, *encoders = refs[: 3 if first else 4]
+    used = 1 + len(encoders)
+    blocks = refs[used : used + len(layout)]
+    rest = refs[used + len(layout) :]
     if final:
         acc_ref, bias_ref, out_ref, acc = rest
     elif first:
         (acc,) = rest
-        acc_ref = None
     else:
         acc_ref, acc = rest
-    rows, depth = blocks[0].shape[0] // 4, blocks[0].shape[1]
-    acc[...] = jnp.zeros_like(acc) if first else acc_ref[...]
-
-    def add(i, carry):
-        across = pl.ds(pl.multiple_of(i * rows, BLK), rows)
-        for c in range(4):
-            here = slice(c * rows, (c + 1) * rows)
-            start = 0
-            for e in (e0, e1, e2):
-                there = slice(start, start + e.shape[1])
-                total = acc[here, there]
-                for n, step in enumerate(steps):
-                    part = source[(c * 4 + step) * 4 + i]
-                    columns = pl.ds(pl.multiple_of(part * depth, BLK), depth)
-                    total += dot(blocks[n * 4 + c][across, :], e[columns, :])
-                acc[here, there] = total
-                start += e.shape[1]
-        return carry
-
-    lax.fori_loop(0, 4, add, 0)
+    if first:
+        acc[...] = jnp.zeros_like(acc)
+    else:
+        acc[...] = acc_ref[...]
+    depth = blocks[0].shape[1]
+
+    def body(here, part, a, step):
+        columns = pl.ds(pl.multiple_of(part * depth, BLK), depth)
+        start = 0
+        for n, e in enumerate(encoders):
+            there = slice(start, start + e.shape[1])
+            if step not in late or n == 2:
+                acc[here, there] += dot(a, e[columns, :])
+            start += e.shape[1]
+
+    each_part(source, layout, blocks, acc.shape[0] // 2, body)
     if final:
         for i in range(out_ref.shape[0] // 8):
             pools = []
@@ -202,36 +216,45 @@
             out_ref[8 * i : 8 * i + 8, :] = jnp.concatenate(pools, axis=0)
 
 
-def encode(source, encoders, rings, bias):
-    rows = rings[0][0].shape[0]
-    width = bias.shape[1]
-    acc_shape = jax.ShapeDtypeStruct((rows, width), jnp.float32)
+def encode_own(source, encoders, gathered, bias):
+    rows = gathered[0][0][0].shape[0] // 2
     smem, vmem = pl.BlockSpec(memory_space=pltpu.SMEM), pl.BlockSpec(memory_space=pltpu.VMEM)
-
-    def blocks(steps):
-        return [rings[c][step] for step in steps for c in range(4)]
-
-    acc = None
-    for steps in ([0, 1], [2]):
-        acc = pl.pallas_call(
-            functools.partial(encode_kernel, steps, acc is None, False),
-            in_specs=[smem] + [vmem] * (3 + 4 * len(steps) + (acc is not None)),
-            out_specs=vmem,
-            out_shape=acc_shape,
-            compiler_params=pltpu.CompilerParams(vmem_limit_bytes=28 * MIB),
-        )(source, *encoders, *blocks(steps), *([] if acc is None else [acc]))
+    arrays, layout = listed(gathered, [0])
     return pl.pallas_call(
-        functools.partial(encode_kernel, [3], False, True),
-        in_specs=[smem] + [vmem] * (3 + 4 + 2),
+        functools.partial(encode_kernel, layout, (), True, False),
+        in_specs=[smem] + [vmem] * (2 + len(arrays)),
         out_specs=vmem,
-        out_shape=jax.ShapeDtypeStruct((rows // POOL, width), jnp.float32),
-        scratch_shapes=[pltpu.VMEM(acc_shape.shape, acc_shape.dtype)],
-        compiler_params=pltpu.CompilerParams(vmem_limit_bytes=28 * MIB),
-    )(source, *encoders, *blocks([3]), acc, bias)
+        out_shape=jax.ShapeDtypeStruct((rows, bias.shape[1]), jnp.float32),
+        compiler_params=pltpu.CompilerParams(vmem_limit_bytes=30 * MIB),
+    )(source, *encoders[:2], *arrays)
+
+
+def encode(source, encoders, gathered, acc, bias):
+    smem, vmem = pl.BlockSpec(memory_space=pltpu.SMEM), pl.BlockSpec(memory_space=pltpu.VMEM)
+    params = pltpu.CompilerParams(vmem_limit_bytes=30 * MIB)
+    shape = jax.ShapeDtypeStruct(acc.shape, acc.dtype)
+    arrays, layout = listed(gathered, [0, 1, 2])
+    acc = pl.pallas_call(
+        functools.partial(encode_kernel, layout, (0,), False, False),
+        in_specs=[smem] + [vmem] * (3 + len(arrays) + 1),
+        out_specs=vmem,
+        out_shape=shape,
+        compiler_params=params,
+    )(source, *encoders, *arrays, acc)
+    arrays, layout = listed(gathered, [3])
+    return pl.pallas_call(
+        functools.partial(encode_kernel, layout, (), False, True),
+        in_specs=[smem] + [vmem] * (3 + len(arrays) + 2),
+        out_specs=vmem,
+        out_shape=jax.ShapeDtypeStruct((acc.shape[0] // POOL, acc.shape[1]), jnp.float32),
+        scratch_shapes=[pltpu.VMEM(acc.shape, acc.dtype)],
+        compiler_params=params,
+    )(source, *encoders, *arrays, acc, bias)
 
 
 SIDE = 4
-ROUTES = ((("y", 1), ("z", 1)), (("y", -1), ("z", -1)), (("z", 1), ("y", 1)), (("z", -1), ("y", -1)))
+AXES = (("y", "z"), ("z", "y"))
+HOPS = (0, 1, -1, 2)
 
 
 def moved(x, axis, by):
@@ -246,25 +269,29 @@
 def sources(place):
     z, y = place // SIDE, place % SIDE
     table = []
-    for (axis, by), (_, by_second) in ROUTES:
-        for second in range(SIDE):
-            for first in range(SIDE):
-                back = (first * by, second * by_second)
-                back_y, back_z = back if axis == "y" else back[::-1]
+    for axis, _ in AXES:
+        for second in HOPS:
+            for first in HOPS:
+                back_y, back_z = (first, second) if axis == "y" else (second, first)
                 table.append((z - back_z) % SIDE * SIDE + (y - back_y) % SIDE)
     return jnp.stack(table).astype(jnp.int32)
 
 
-def ring_gather(quarters):
-    lines = [[q] for q in quarters]
-    for _ in range(SIDE - 1):
-        for line, ((axis, by), _) in zip(lines, ROUTES):
-            line.append(moved(line[-1], axis, by))
-    rings = [[jnp.concatenate(line, axis=0)] for line in lines]
-    for _ in range(SIDE - 1):
-        for ring, (_, (axis, by)) in zip(rings, ROUTES):
-            ring.append(moved(ring[-1], axis, by))
-    return rings
+def lines(halves):
+    return [[half] + [moved(half, axis, by) for by in HOPS[1:]] for half, (axis, _) in zip(halves, AXES)]
+
+
+def near(joined):
+    return [(moved(x, axis, 1), moved(x, axis, -1)) for x, (_, axis) in zip(joined, AXES)]
+
+
+def planes(joined, beside):
+    out = []
+    for x, (up, down), (_, axis) in zip(joined, beside, AXES):
+        middle = x.shape[0] // 2
+        across = (moved(up[:middle], axis, 1), moved(down[middle:], axis, -1))
+        out.append(((x,), (up,), (down,), across))
+    return out
 
 
 def local(
@@ -295,7 +322,11 @@
 
     packed = pack(query_vectors[0], key_vectors[0], value_vectors[0], doc_ids)
     weight = out_weight[0]
-    after, before = from_head(weight, 1), from_head(weight, -1)
+    middle = weight.shape[0] // 2
+    after_upper, before_lower = from_head(weight[:middle], 1), from_head(weight[middle:], -1)
+    after_upper, before_lower, rest = lax.optimization_barrier((after_upper, before_lower, weight))
+    across = [from_head(after_upper, 1), from_head(before_lower, -1)]
+    after_lower, before_upper = from_head(rest[middle:], 1), from_head(rest[:middle], -1)
     gains = [norm_gain] + [from_head(norm_gain, k) for k in range(1, groups)]
     inverse = jnp.concatenate([(1.0 / (g * g)).reshape(-1, HD) for g in gains], axis=1)
     half = enc_weight.shape[2] // 2
@@ -308,12 +339,10 @@
     prior = lax.dynamic_index_in_dim(prior_state[0], place, 0, False)
     gain = lax.dynamic_slice_in_dim(norm_gain, place * HD, HD, 1)
     attended = attend(packed, prior, gain, groups)
-    attended, after, before, inverse, bias = lax.optimization_barrier(
-        (attended, after, before, inverse, bias)
-    )
-
-    middle = weight.shape[0] // 2
-    across = [from_head(after[:middle], 1), from_head(before[middle:], -1)]
+    attended, after_lower, before_upper, inverse, bias = lax.optimization_barrier(
+        (attended, after_lower, before_upper, inverse, bias)
+    )
+
     own = lax.all_to_all(attended, "head", 0, 0, tiled=True)
     own = jnp.concatenate(
         [
@@ -322,20 +351,29 @@
         ],
         axis=1,
     )
-    own, first_half = lax.optimization_barrier((own, enc_weight[0][:, :half]))
+    own, across, first_half = lax.optimization_barrier((own, across, enc_weight[0][:, :half]))
     from_before = from_head(first_half, -1)
-    rings = ring_gather([own[c * BLK : (c + 1) * BLK] for c in range(4)])
-    weights = [weight, after, jnp.concatenate(across, axis=0), before]
-    layer_out = project(source, inverse, weights, rings, residual[0])
+    rows = own.shape[0] // 2
+    joined = [jnp.concatenate(line, axis=0) for line in lines([own[:rows], own[rows:]])]
+    weights = [
+        weight,
+        jnp.concatenate([after_upper, after_lower], axis=0),
+        *across,
+        jnp.concatenate([before_upper, before_lower], axis=0),
+    ]
+    layer_out = project(source, inverse, weights, planes(joined, near(joined)), residual[0])
 
     layer_out, from_before, second_half = lax.optimization_barrier(
         (layer_out, from_before, enc_weight[0][:, half:])
     )
     from_after = from_head(second_half, 1)
     opposite = from_head(layer_out, 2)
-    rows = layer_out.shape[0] // 2
-    rings = ring_gather([layer_out[:rows], layer_out[rows:], opposite[:rows], opposite[rows:]])
-    pooled = encode(source, [enc_weight[0], from_before, from_after], rings, bias)
+    joined = [jnp.concatenate(line, axis=0) for line in lines([layer_out, opposite])]
+    beside = near(joined)
+    encoders = [enc_weight[0], from_before, from_after]
+    acc = encode_own(source, encoders, [((x,),) for x in joined], bias)
+    beside, acc = lax.optimization_barrier((beside, acc))
+    pooled = encode(source, encoders, planes(joined, beside), acc, bias)
     pooled = pooled.astype(jnp.bfloat16)
     pools = pooled.shape[0] // 2
     mine = from_section(pooled[:, : 2 * half], 0)

time: 309 us -> 266 us (0.86)
  waiting for transfers between devices: 136 us -> 107 us
  starting transfers between devices: 103 us -> 76 us
  Pallas kernels: 44.1 us -> 55 us
    ppermute x12 -> x14, waiting for transfers between devices: 82.6 us -> 28.2 us  [from_head(): lax.ppermute(x, 'head', [((i + by) % groups, i) for i in range(groups)])]
    ppermute x48 -> x28, starting transfers between devices: 59.8 us -> 40.1 us  [moved(): return lax.ppermute(x, 'seq', pairs)]
    ppermute x48 -> x28, waiting for transfers between devices: 48.9 us -> 63.2 us  [moved(): return lax.ppermute(x, 'seq', pairs)]
    ppermute x4, starting transfers between devices: 19.8 us -> 7.59 us  [from_section(): return lax.ppermute(x, ('section', 'head'), pairs)]
    pallas_call x5, Pallas kernels: 36.9 us -> 47.8 us  [the longest x1 17.7 us: encode(): pl.pallas_call(functools.partial(encode_kernel, layout, (0,), False, Fals...]
    all_to_all x1, waiting for transfers between devices: 1.06 us -> 11.8 us  [local(): own = lax.all_to_all(attended, 'head', 0, 0, tiled=True)]
    slice x5 -> x11, local copies, waits for them, and re-layouts: 1.41 us -> 9.24 us  [the longest x8 6.46 us: planes(): across = (moved(up[:middle], axis, 1), moved(down[middle:], axis, -1))]
    unnamed x54 -> x47, local copies, waits for them, and re-layouts: 13.2 us -> 6.39 us
  transfers between devices with their start and end apart: 66 -> 48, of which waited for: 26 -> 18; matrix products, arithmetic and copies ran while one was open for 3% -> 8% of each run, Pallas kernels for 14% -> 20%
where the time goes in v5:
time: 266 us
  waiting for transfers between devices  107 us (40%)
  starting transfers between devices  76 us (29%)
  Pallas kernels  55 us (21%)
  local copies, waits for them, and re-layouts  24.6 us (9%)
    ppermute x28, waiting for transfers between devices, moved(): return lax.ppermute(x, 'seq', pairs)  63.2 us
    ppermute x28, starting transfers between devices, moved(): return lax.ppermute(x, 'seq', pairs)  40.1 us
    ppermute x14, waiting for transfers between devices, from_head(): lax.ppermute(x, 'head', [((i + by) % groups, i) for i in range(groups)])  28.2 us
    pallas_call x1, Pallas kernels, encode(): pl.pallas_call(functools.partial(encode_kernel, layout, (0,), False, Fals...  17.7 us
    ppermute x14, starting transfers between devices, from_head(): lax.ppermute(x, 'head', [((i + by) % groups, i) for i in range(groups)])  16 us
    all_to_all x1, waiting for transfers between devices, local(): own = lax.all_to_all(attended, 'head', 0, 0, tiled=True)  11.8 us
    pallas_call x1, Pallas kernels, project(): pl.pallas_call(functools.partial(project_kernel, layout, False), in_specs...  10.2 us
    all_to_all x1, starting transfers between devices, local(): packed = lax.all_to_all(packed, 'seq', 0, 0, tiled=True)  8.77 us
  transfers between devices with their start and end apart: 48, of which 18 were waited for; matrix products, arithmetic and copies ran while one was open for 8% of the time, Pallas kernels for 20%

profile of v5, /device:TPU:1, one launch (start us, length us, event | category | flops | bytes accessed | tf_op | source)
XLA Modules:
  0.0 265.7 jit_solution(16915649748254938812)
XLA Ops:
  1.4 1.6 shard_map.113
  3.0 1.2 copy-done.5
  4.2 8.8 %all-to-all-start = ((bf16[16,400,128]{2,1,0:T(8,128)(2,1)}), bf16[16,400,128]{2,1,0:T(8,128)(2,1)}, u32[]{:S(2)}, u32[]{:S(2)}) async-start(bf16[16,400,128]{2,1,0:T(8,128)(2,1)} %copy-done.5), calls=%async_computation | async-start | bytes 3276800 | tf_op jit(solution)/shard_map/all_to_all | solution.py:338
  13.0 1.3 slice_bitcast_fusion
  14.3 2.5 collective-permute-start
  17.0 2.5 collective-permute-start.8
  19.6 1.4 collective-permute-start.4
  21.1 15.1 %collective-permute-done.7 = f32[1,256]{1,0:T(1,128)S(1)} collective-permute-done((f32[1,256]{1,0:T(1,128)S(1)}, f32[1,256]{1,0:T(1,128)S(1)}, u32[]{:S(2)}, u32[]{:S(2)}) %collective-permute-start.7) | collective-permute-done | bytes 1056 | tf_op jit(solution)/shard_map/ppermute | solution.py:313
  36.3 1.4 fusion.1
  37.7 2.7 collective-permute-start.2
  40.4 1.5 collective-permute-start.10
  41.9 1.3 collective-permute-start.9
  43.2 5.5 %shard_map.114 = bf16[4,512,128]{2,1,0:T(8,128)(2,1)} custom-call(bf16[16,400,128]{2,1,0:T(8,128)(2,1)} %all-to-all-done.packed_ref, f32[128,128]{1,0:T(8,128)S(1)} %dynamic-slice_bitcast_fusion.4.prior_ref, f32[1,128]{1,0:T(1,128)S(1)} %constant_dynamic-slice_fusion.gain_ref), custom_call_target="tpu_custom_call" | custom-call | tf_op jit(solution)/shard_map/pallas_call | solution.py:89
  48.8 7.0 %collective-permute-done.2 = bf16[1024,384]{1,0:T(8,128)(2,1)} collective-permute-done((bf16[1024,384]{1,0:T(8,128)(2,1)}, bf16[1024,384]{1,0:T(8,128)(2,1)}, u32[]{:S(2)}, u32[]{:S(2)}) %collective-permute-start.2) | collective-permute-done | bytes 786464 | tf_op jit(solution)/shard_map/ppermute | solution.py:313
  55.8 2.4 collective-permute-done.3
  58.2 3.5 %all-to-all-start.1 = ((bf16[4,512,128]{2,1,0:T(8,128)(2,1)}), bf16[4,512,128]{2,1,0:T(8,128)(2,1)S(1)}, u32[]{:S(2)}, u32[]{:S(2)}) async-start(bf16[4,512,128]{2,1,0:T(8,128)(2,1)} %shard_map.114), calls=%async_computation.1 | async-start | bytes 1048576 | tf_op jit(solution)/shard_map/all_to_all | solution.py:346
  61.7 5.9 %fusion = (bf16[6144,256]{1,0:T(8,128)(2,1)}, bf16[6144,256]{1,0:T(8,128)(2,1)}) fusion(bf16[6144,512]{1,0:T(8,128)(2,1)} %bitcast.59), kind=kLoop, calls=%fused_computation.39 | loop fusion | bytes 12582912 | tf_op jit(solution)/shard_map/slice | solution.py:367
  67.6 11.8 %all-to-all-done.1 = bf16[4,512,128]{2,1,0:T(8,128)(2,1)S(1)} async-done(((bf16[4,512,128]{2,1,0:T(8,128)(2,1)}), bf16[4,512,128]{2,1,0:T(8,128)(2,1)S(1)}, u32[]{:S(2)}, u32[]{:S(2)}) %all-to-all-start.1) | async-done | bytes 524320 | tf_op jit(solution)/shard_map/all_to_all | solution.py:346
  80.4 1.9 collective-permute-start.19
  82.3 1.1 collective-permute-start.20
  83.4 1.2 collective-permute-start.11
  84.6 1.5 collective-permute-done.18
  86.1 2.0 collective-permute-start.12
  89.6 1.2 collective-permute-start.21
  90.8 1.5 collective-permute-start.23
  92.3 1.9 collective-permute-done.12
  94.2 1.5 collective-permute-done.13
  95.7 1.0 pad_maximum_fusion.refs_7_
  96.7 5.5 %collective-permute-start.16 = (bf16[1024,512]{1,0:T(8,128)(2,1)}, bf16[1024,512]{1,0:T(8,128)(2,1)}, u32[]{:S(2)}, u32[]{:S(2)}) collective-permute-start(bf16[1024,512]{1,0:T(8,128)(2,1)} %pad_maximum_fusion.refs_7_), channel_id=1, source_target_pairs={{0,48},{4,52},{8,56},{12,60},{16,0},{20,4},{24,8},{28,12},{32,16},... | collective-permute-start | bytes 3145736 | tf_op jit(solution)/shard_map/ppermute | solution.py:266
  102.4 18.2 %collective-permute-done.21.refs_10_ = bf16[1024,512]{1,0:T(8,128)(2,1)} collective-permute-done((bf16[1024,512]{1,0:T(8,128)(2,1)S(1)}, bf16[1024,512]{1,0:T(8,128)(2,1)}, u32[]{:S(2)}, u32[]{:S(2)}) %collective-permute-start.21) | collective-permute-done | bytes 1048608 | tf_op jit(solution)/shard_map/ppermute | solution.py:266
  120.5 1.1 slice.119
  121.7 1.1 slice.120
  122.9 2.7 %collective-permute-start.24 = (bf16[512,512]{1,0:T(8,128)(2,1)S(1)}, bf16[512,512]{1,0:T(8,128)(2,1)S(1)}, u32[]{:S(2)}, u32[]{:S(2)}) collective-permute-start(bf16[512,512]{1,0:T(8,128)(2,1)S(1)} %slice.120), channel_id=1, source_target_pairs={{0,12},{4,0},{8,4},{12,8},{16,28},{20,16},{24,20},{28,24},{32,44},... | collective-permute-start | bytes 1572872 | tf_op jit(solution)/shard_map/ppermute | solution.py:266
  125.5 1.1 slice.117
  126.7 1.1 slice.118
  127.8 2.7 %collective-permute-start.17 = (bf16[512,512]{1,0:T(8,128)(2,1)S(1)}, bf16[512,512]{1,0:T(8,128)(2,1)S(1)}, u32[]{:S(2)}, u32[]{:S(2)}) collective-permute-start(bf16[512,512]{1,0:T(8,128)(2,1)S(1)} %slice.118), channel_id=1, source_target_pairs={{0,48},{4,52},{8,56},{12,60},{16,0},{20,4},{24,8},{28,12},{32,16},... | collective-permute-start | bytes 1572872 | tf_op jit(solution)/shard_map/ppermute | solution.py:266
  130.6 1.2 constant_dynamic-update-slice_fusion.3
  131.8 1.4 constant_dynamic-update-slice_fusion.2.refs_6_
  133.2 1.3 constant_dynamic-update-slice_fusion.refs_3_
  134.5 10.2 %shard_map.115 = (f32[512,384]{1,0:T(8,128)S(1)}, f32[512,128]{1,0:T(8,128)S(1)}) custom-call(s32[32]{0:T(128)S(1)} %stack.98.refs_0_, f32[16,512]{1,0:T(8,128)S(1)} %pad_maximum_fusion.3.refs_1_, bf16[2048,384]{1,0:T(8,128)(2,1)S(1)} %bitcast.68, bf16[2048,384]{1,0:T(8,128)(2,1)S(1)} %constant_dynamic-update-slice_fusion.refs_3_, ...), custom_call_target="tpu_custom_call" | custom-call | tf_op jit(solution)/shard_map/pallas_call | solution.py:165
  144.8 4.7 %shard_map.116 = bf16[512,384]{1,0:T(8,128)(2,1)} custom-call(s32[32]{0:T(128)S(1)} %stack.98.refs_0_, f32[16,512]{1,0:T(8,128)S(1)} %pad_maximum_fusion.3.refs_1_, bf16[2048,384]{1,0:T(8,128)(2,1)S(1)} %bitcast.69, bf16[2048,384]{1,0:T(8,128)(2,1)S(1)} %constant_dynamic-update-slice_fusion.refs_3_, bf16[1024,384]{1,0:T(8,128)(2,1)} %collective-permute-done.9.refs_4_, ...), custom_call_target="tpu_custom_call" | custom-call | tf_op jit(solution)/shard_map/pallas_call | solution.py:173
  149.6 2.8 %collective-permute-start.33 = (bf16[512,384]{1,0:T(8,128)(2,1)}, bf16[512,384]{1,0:T(8,128)(2,1)S(1)}, u32[]{:S(2)}, u32[]{:S(2)}) collective-permute-start(bf16[512,384]{1,0:T(8,128)(2,1)} %shard_map.116), channel_id=1, source_target_pairs={{2,0},{3,1},{0,2},{1,3},{6,4},{7,5},{4,6},{5,7},{10,8},{11,9},{8,1... | collective-permute-start | bytes 1179656 | tf_op jit(solution)/shard_map/ppermute | solution.py:313
  152.3 2.7 %collective-permute-start.29 = (bf16[512,384]{1,0:T(8,128)(2,1)}, bf16[512,384]{1,0:T(8,128)(2,1)S(1)}, u32[]{:S(2)}, u32[]{:S(2)}) collective-permute-start(bf16[512,384]{1,0:T(8,128)(2,1)} %shard_map.116), channel_id=1, source_target_pairs={{0,12},{4,0},{8,4},{12,8},{16,28},{20,16},{24,20},{28,24},{32,44},... | collective-permute-start | bytes 1179656 | tf_op jit(solution)/shard_map/ppermute | solution.py:266
  155.0 1.0 collective-permute-start.27
  156.1 1.0 constant_dynamic-update-slice_fusion.7
  157.9 4.8 %collective-permute-done.28 = bf16[512,384]{1,0:T(8,128)(2,1)S(1)} collective-permute-done((bf16[512,384]{1,0:T(8,128)(2,1)}, bf16[512,384]{1,0:T(8,128)(2,1)S(1)}, u32[]{:S(2)}, u32[]{:S(2)}) %collective-permute-start.28) | collective-permute-done | bytes 393248 | tf_op jit(solution)/shard_map/ppermute | solution.py:266
  162.8 4.4 %collective-permute-start.35 = (bf16[512,384]{1,0:T(8,128)(2,1)S(1)}, bf16[512,384]{1,0:T(8,128)(2,1)S(1)}, u32[]{:S(2)}, u32[]{:S(2)}) collective-permute-start(bf16[512,384]{1,0:T(8,128)(2,1)S(1)} %collective-permute-done.33), channel_id=1, source_target_pairs={{0,48},{4,52},{8,56},{12,60},{16,0},{20,4},{24,8},{28,12},{32,16},... | collective-permute-start | bytes 1179656 | tf_op jit(solution)/shard_map/ppermute | solution.py:266
  168.2 2.2 collective-permute-start.32
  170.4 5.7 %collective-permute-done.35 = bf16[512,384]{1,0:T(8,128)(2,1)S(1)} collective-permute-done((bf16[512,384]{1,0:T(8,128)(2,1)S(1)}, bf16[512,384]{1,0:T(8,128)(2,1)S(1)}, u32[]{:S(2)}, u32[]{:S(2)}) %collective-permute-start.35) | collective-permute-done | bytes 393248 | tf_op jit(solution)/shard_map/ppermute | solution.py:266
  176.3 2.7 %collective-permute-start.38 = (bf16[2048,384]{1,0:T(8,128)(2,1)S(1)}, bf16[2048,384]{1,0:T(8,128)(2,1)S(1)}, u32[]{:S(2)}, u32[]{:S(2)}) collective-permute-start(bf16[2048,384]{1,0:T(8,128)(2,1)S(1)} %constant_dynamic-update-slice_fusion.8.refs_4_.refs_5_), channel_id=1, source_target_pairs={{0,12},{4,0},{8,4},{12,8},{16,28},{20,16},{24,20},{28,24},{32,44},... | collective-permute-start | bytes 4718600 | tf_op jit(solution)/shard_map/ppermute | solution.py:266
  179.0 6.8 %shard_map.117.refs_10_ = f32[1024,1024]{1,0:T(8,128)S(1)} custom-call(s32[32]{0:T(128)S(1)} %stack.98.refs_0_, bf16[6144,512]{1,0:T(8,128)(2,1)S(1)} %bitcast.63, bf16[6144,256]{1,0:T(8,128)(2,1)} %collective-permute-done.25.refs_2_, bf16[2048,384]{1,0:T(8,128)(2,1)S(1)} %constant_dynamic-update-slice_fusion.4.refs_3_.refs_4_, ...), custom_call_target="tpu_custom_call" | custom-call | tf_op jit(solution)/shard_map/pallas_call | solution.py:223
  185.8 25.2 %collective-permute-done.31.refs_6_ = bf16[2048,384]{1,0:T(8,128)(2,1)S(1)} collective-permute-done((bf16[2048,384]{1,0:T(8,128)(2,1)S(1)}, bf16[2048,384]{1,0:T(8,128)(2,1)S(1)}, u32[]{:S(2)}, u32[]{:S(2)}) %collective-permute-start.31) | collective-permute-done | bytes 1572896 | tf_op jit(solution)/shard_map/ppermute | solution.py:266
  211.0 3.2 %collective-permute-done.32.refs_8_ = bf16[2048,384]{1,0:T(8,128)(2,1)S(1)} collective-permute-done((bf16[2048,384]{1,0:T(8,128)(2,1)S(1)}, bf16[2048,384]{1,0:T(8,128)(2,1)S(1)}, u32[]{:S(2)}, u32[]{:S(2)}) %collective-permute-start.32) | collective-permute-done | bytes 1572896 | tf_op jit(solution)/shard_map/ppermute | solution.py:266
  214.3 1.0 collective-permute-start.39
  215.3 2.8 %collective-permute-start.40 = (bf16[1024,384]{1,0:T(8,128)(2,1)S(1)}, bf16[1024,384]{1,0:T(8,128)(2,1)S(1)}, u32[]{:S(2)}, u32[]{:S(2)}) collective-permute-start(bf16[1024,384]{1,0:T(8,128)(2,1)S(1)} %slice.104), channel_id=1, source_target_pairs={{0,48},{4,52},{8,56},{12,60},{16,0},{20,4},{24,8},{28,12},{32,16},... | collective-permute-start | bytes 2359304 | tf_op jit(solution)/shard_map/ppermute | solution.py:266
  218.1 1.0 slice.105
  220.1 2.7 %collective-permute-start.42 = (bf16[1024,384]{1,0:T(8,128)(2,1)}, bf16[1024,384]{1,0:T(8,128)(2,1)S(1)}, u32[]{:S(2)}, u32[]{:S(2)}) collective-permute-start(bf16[1024,384]{1,0:T(8,128)(2,1)} %slice.106), channel_id=1, source_target_pairs={{0,12},{4,0},{8,4},{12,8},{16,28},{20,16},{24,20},{28,24},{32,44},... | collective-permute-start | bytes 2359304 | tf_op jit(solution)/shard_map/ppermute | solution.py:266
  222.7 2.8 %collective-permute-done.27.refs_3_ = bf16[6144,256]{1,0:T(8,128)(2,1)S(1)} collective-permute-done((bf16[6144,256]{1,0:T(8,128)(2,1)S(1)}, bf16[6144,256]{1,0:T(8,128)(2,1)S(1)}, u32[]{:S(2)}, u32[]{:S(2)}) %collective-permute-start.27) | collective-permute-done | bytes 3145760 | tf_op jit(solution)/shard_map/ppermute | solution.py:313
  225.6 4.6 %collective-permute-start.26 = (bf16[1,512,384]{2,1,0:T(8,128)(2,1)}, bf16[1,512,384]{2,1,0:T(8,128)(2,1)}, u32[]{:S(2)}, u32[]{:S(2)}) collective-permute-start(bf16[1,512,384]{2,1,0:T(8,128)(2,1)} %bitcast.33), channel_id=1, source_target_pairs={{0,64},{1,65},{2,66},{3,67},{64,0},{65,1},{66,2},{67,3},{4,68},{5,... | collective-permute-start | bytes 1179656 | tf_op jit(solution)/shard_map/ppermute | solution.py:321
  230.2 17.7 %shard_map.118.refs_8_ = f32[1024,1024]{1,0:T(8,128)S(1)} custom-call(s32[32]{0:T(128)S(1)} %stack.98.refs_0_, bf16[6144,512]{1,0:T(8,128)(2,1)} %bitcast.60, bf16[6144,256]{1,0:T(8,128)(2,1)} %collective-permute-done.25.refs_2_, bf16[6144,256]{1,0:T(8,128)(2,1)S(1)} %collective-permute-done.27.refs_3_, bf16[2048,384]{1,0:T(8,128)(2,1)S(1)} %copy-done.4, ...), custom_call_target="tpu_custom_call" | custom-call | tf_op jit(solution)/shard_map/pallas_call | solution.py:237
  248.0 8.5 %shard_map.119 = f32[16,1024]{1,0:T(8,128)S(1)} custom-call(s32[32]{0:T(128)S(1)} %stack.98.refs_0_, bf16[6144,512]{1,0:T(8,128)(2,1)S(1)} %bitcast.66, bf16[6144,256]{1,0:T(8,128)(2,1)} %collective-permute-done.25.refs_2_, bf16[6144,256]{1,0:T(8,128)(2,1)S(1)} %collective-permute-done.27.refs_3_, bf16[1024,384]{1,0:T(8,128)(2,1)S(1)} %collective-permute-done.39.refs_4_, ...), custom_call_target="tpu_custom_call" | custom-call | tf_op jit(solution)/shard_map/pallas_call | solution.py:245
  256.5 2.5 collective-permute-start.44
  259.8 3.5 %collective-permute-done.45 = bf16[16,256]{1,0:T(8,128)(2,1)S(1)} collective-permute-done((bf16[16,256]{1,0:T(8,128)(2,1)S(1)}, bf16[16,256]{1,0:T(8,128)(2,1)S(1)}, u32[]{:S(2)}, u32[]{:S(2)}) %collective-permute-start.45) | collective-permute-done | bytes 8224 | tf_op jit(solution)/shard_map/ppermute | solution.py:321
  264.0 1.8 copy.21
  (128 shorter events, 8.7 us)
Async XLA Ops:
  0.6 20.4 %copy-start = (f32[1,16,128,128]{3,2,1,0:T(8,128)S(1)}, f32[1,16,128,128]{3,2,1,0:T(8,128)}, u32[]{:S(2)}) copy-start(f32[1,16,128,128]{3,2,1,0:T(8,128)} %param.13) | copy-start | bytes 3145732
  4.2 8.8 %copy-start.2 = (bf16[1,2048,384]{2,1,0:T(8,128)(2,1)S(1)}, bf16[1,2048,384]{2,1,0:T(8,128)(2,1)}, u32[]{:S(2)}) copy-start(bf16[1,2048,384]{2,1,0:T(8,128)(2,1)} %param.17) | copy-start | bytes 4718596
  4.2 39.0 %all-to-all-start = ((bf16[16,400,128]{2,1,0:T(8,128)(2,1)}), bf16[16,400,128]{2,1,0:T(8,128)(2,1)}, u32[]{:S(2)}, u32[]{:S(2)}) async-start(bf16[16,400,128]{2,1,0:T(8,128)(2,1)} %copy-done.5), calls=%async_computation | async-start | bytes 3276800 | tf_op jit(solution)/shard_map/all_to_all | solution.py:338
  13.0 3.8 %copy-start.14 = (f32[1,512]{1,0:T(1,128)S(1)}, f32[1,512]{1,0:T(1,128)}, u32[]{:S(2)}) copy-start(f32[1,512]{1,0:T(1,128)} %param.19) | copy-start | bytes 6148
  13.0 6.6 %copy-start.13 = (f32[1,2048]{1,0:T(1,128)S(1)}, f32[1,2048]{1,0:T(1,128)}, u32[]{:S(2)}) copy-start(f32[1,2048]{1,0:T(1,128)} %param.15) | copy-start | bytes 24580
  14.3 21.9 %collective-permute-start = (bf16[1024,384]{1,0:T(8,128)(2,1)}, bf16[1024,384]{1,0:T(8,128)(2,1)S(1)}, u32[]{:S(2)}, u32[]{:S(2)}) collective-permute-start(bf16[1024,384]{1,0:T(8,128)(2,1)} %get-tuple-element.51), channel_id=1, source_target_pairs={{1,0},{2,1},{3,2},{0,3},{5,4},{6,5},{7,6},{4,7},{9,8},{10,9},{11,1... | collective-permute-start | bytes 2359304 | tf_op jit(solution)/shard_map/ppermute | solution.py:313
  16.8 19.4 %collective-permute-start.1 = (bf16[1024,384]{1,0:T(8,128)(2,1)}, bf16[1024,384]{1,0:T(8,128)(2,1)}, u32[]{:S(2)}, u32[]{:S(2)}) collective-permute-start(bf16[1024,384]{1,0:T(8,128)(2,1)} %get-tuple-element.50), channel_id=1, source_target_pairs={{3,0},{0,1},{1,2},{2,3},{7,4},{4,5},{5,6},{6,7},{11,8},{8,9},{9,10... | collective-permute-start | bytes 2359304 | tf_op jit(solution)/shard_map/ppermute | solution.py:313
  16.8 19.3 %collective-permute-start.7 = (f32[1,256]{1,0:T(1,128)S(1)}, f32[1,256]{1,0:T(1,128)S(1)}, u32[]{:S(2)}, u32[]{:S(2)}) collective-permute-start(f32[1,256]{1,0:T(1,128)S(1)} %get-tuple-element.70), channel_id=1, source_target_pairs={{3,0},{0,1},{1,2},{2,3},{7,4},{4,5},{5,6},{6,7},{11,8},{8,9},{9,10... | collective-permute-start | bytes 3080 | tf_op jit(solution)/shard_map/ppermute | solution.py:313
  17.0 19.1 %collective-permute-start.8 = (f32[1,256]{1,0:T(1,128)S(1)}, f32[1,256]{1,0:T(1,128)S(1)}, u32[]{:S(2)}, u32[]{:S(2)}) collective-permute-start(f32[1,256]{1,0:T(1,128)S(1)} %get-tuple-element.71), channel_id=1, source_target_pairs={{1,0},{2,1},{3,2},{0,3},{5,4},{6,5},{7,6},{4,7},{9,8},{10,9},{11,1... | collective-permute-start | bytes 3080 | tf_op jit(solution)/shard_map/ppermute | solution.py:313
  19.6 16.6 %collective-permute-start.4 = (f32[1,2048]{1,0:T(1,128)S(1)}, f32[1,2048]{1,0:T(1,128)S(1)}, u32[]{:S(2)}, u32[]{:S(2)}) collective-permute-start(f32[1,2048]{1,0:T(1,128)S(1)} %copy-done.13), channel_id=1, source_target_pairs={{1,0},{2,1},{3,2},{0,3},{5,4},{6,5},{7,6},{4,7},{9,8},{10,9},{11,1... | collective-permute-start | bytes 24584 | tf_op jit(solution)/shard_map/ppermute | solution.py:313
  36.2 4.2 %collective-permute-start.5 = (f32[1,2048]{1,0:T(1,128)S(1)}, f32[1,2048]{1,0:T(1,128)S(1)}, u32[]{:S(2)}, u32[]{:S(2)}) collective-permute-start(f32[1,2048]{1,0:T(1,128)S(1)} %copy-done.13), channel_id=1, source_target_pairs={{2,0},{3,1},{0,2},{1,3},{6,4},{7,5},{4,6},{5,7},{10,8},{11,9},{8,1... | collective-permute-start | bytes 24584 | tf_op jit(solution)/shard_map/ppermute | solution.py:313
  36.2 4.2 %collective-permute-start.6 = (f32[1,2048]{1,0:T(1,128)S(1)}, f32[1,2048]{1,0:T(1,128)S(1)}, u32[]{:S(2)}, u32[]{:S(2)}) collective-permute-start(f32[1,2048]{1,0:T(1,128)S(1)} %copy-done.13), channel_id=1, source_target_pairs={{3,0},{0,1},{1,2},{2,3},{7,4},{4,5},{5,6},{6,7},{11,8},{8,9},{9,10... | collective-permute-start | bytes 24584 | tf_op jit(solution)/shard_map/ppermute | solution.py:313
  36.2 4.2 %copy-start.11 = (bf16[1024,384]{1,0:T(8,128)(2,1)}, bf16[1024,384]{1,0:T(8,128)(2,1)S(1)}, u32[]{:S(2)}) copy-start(bf16[1024,384]{1,0:T(8,128)(2,1)S(1)} %collective-permute-done) | copy-start | bytes 2359300
  37.7 18.1 %collective-permute-start.2 = (bf16[1024,384]{1,0:T(8,128)(2,1)}, bf16[1024,384]{1,0:T(8,128)(2,1)}, u32[]{:S(2)}, u32[]{:S(2)}) collective-permute-start(bf16[1024,384]{1,0:T(8,128)(2,1)} %get-tuple-element.49), channel_id=1, source_target_pairs={{1,0},{2,1},{3,2},{0,3},{5,4},{6,5},{7,6},{4,7},{9,8},{10,9},{11,1... | collective-permute-start | bytes 2359304 | tf_op jit(solution)/shard_map/ppermute | solution.py:313
  40.3 17.8 %collective-permute-start.3 = (bf16[1024,384]{1,0:T(8,128)(2,1)}, bf16[1024,384]{1,0:T(8,128)(2,1)}, u32[]{:S(2)}, u32[]{:S(2)}) collective-permute-start(bf16[1024,384]{1,0:T(8,128)(2,1)} %get-tuple-element.48), channel_id=1, source_target_pairs={{3,0},{0,1},{1,2},{2,3},{7,4},{4,5},{5,6},{6,7},{11,8},{8,9},{9,10... | collective-permute-start | bytes 2359304 | tf_op jit(solution)/shard_map/ppermute | solution.py:313
  40.4 39.0 %collective-permute-start.10 = (bf16[1024,384]{1,0:T(8,128)(2,1)}, bf16[1024,384]{1,0:T(8,128)(2,1)S(1)}, u32[]{:S(2)}, u32[]{:S(2)}) collective-permute-start(bf16[1024,384]{1,0:T(8,128)(2,1)} %collective-permute-done.1), channel_id=1, source_target_pairs={{3,0},{0,1},{1,2},{2,3},{7,4},{4,5},{5,6},{6,7},{11,8},{8,9},{9,10... | collective-permute-start | bytes 2359304 | tf_op jit(solution)/shard_map/ppermute | solution.py:313
  41.9 37.5 %collective-permute-start.9 = (bf16[1024,384]{1,0:T(8,128)(2,1)}, bf16[1024,384]{1,0:T(8,128)(2,1)}, u32[]{:S(2)}, u32[]{:S(2)}) collective-permute-start(bf16[1024,384]{1,0:T(8,128)(2,1)} %copy-done.11), channel_id=1, source_target_pairs={{1,0},{2,1},{3,2},{0,3},{5,4},{6,5},{7,6},{4,7},{9,8},{10,9},{11,1... | collective-permute-start | bytes 2359304 | tf_op jit(solution)/shard_map/ppermute | solution.py:313
  58.2 21.2 %all-to-all-start.1 = ((bf16[4,512,128]{2,1,0:T(8,128)(2,1)}), bf16[4,512,128]{2,1,0:T(8,128)(2,1)S(1)}, u32[]{:S(2)}, u32[]{:S(2)}) async-start(bf16[4,512,128]{2,1,0:T(8,128)(2,1)} %shard_map.114), calls=%async_computation.1 | async-start | bytes 1048576 | tf_op jit(solution)/shard_map/all_to_all | solution.py:346
  79.5 70.1 %collective-permute-start.25 = (bf16[6144,256]{1,0:T(8,128)(2,1)}, bf16[6144,256]{1,0:T(8,128)(2,1)}, u32[]{:S(2)}, u32[]{:S(2)}) collective-permute-start(bf16[6144,256]{1,0:T(8,128)(2,1)} %get-tuple-element.36), channel_id=1, source_target_pairs={{3,0},{0,1},{1,2},{2,3},{7,4},{4,5},{5,6},{6,7},{11,8},{8,9},{9,10... | collective-permute-start | bytes 9437192 | tf_op jit(solution)/shard_map/ppermute | solution.py:313
  79.6 6.5 %collective-permute-start.18 = (bf16[256,512]{1,0:T(8,128)(2,1)S(1)}, bf16[256,512]{1,0:T(8,128)(2,1)S(1)}, u32[]{:S(2)}, u32[]{:S(2)}) collective-permute-start(bf16[256,512]{1,0:T(8,128)(2,1)S(1)} %get-tuple-element.52), channel_id=1, source_target_pairs={{0,16},{4,20},{8,24},{12,28},{16,32},{20,36},{24,40},{28,44},{32,4... | collective-permute-start | bytes 786440 | tf_op jit(solution)/shard_map/ppermute | solution.py:266
  80.4 8.0 %collective-permute-start.19 = (bf16[256,512]{1,0:T(8,128)(2,1)S(1)}, bf16[256,512]{1,0:T(8,128)(2,1)S(1)}, u32[]{:S(2)}, u32[]{:S(2)}) collective-permute-start(bf16[256,512]{1,0:T(8,128)(2,1)S(1)} %get-tuple-element.52), channel_id=1, source_target_pairs={{0,48},{4,52},{8,56},{12,60},{16,0},{20,4},{24,8},{28,12},{32,16},... | collective-permute-start | bytes 786440 | tf_op jit(solution)/shard_map/ppermute | solution.py:266
  82.3 7.1 %collective-permute-start.20 = (bf16[256,512]{1,0:T(8,128)(2,1)S(1)}, bf16[256,512]{1,0:T(8,128)(2,1)S(1)}, u32[]{:S(2)}, u32[]{:S(2)}) collective-permute-start(bf16[256,512]{1,0:T(8,128)(2,1)S(1)} %get-tuple-element.52), channel_id=1, source_target_pairs={{0,32},{4,36},{8,40},{12,44},{16,48},{20,52},{24,56},{28,60},{32,0... | collective-permute-start | bytes 786440 | tf_op jit(solution)/shard_map/ppermute | solution.py:266
  83.4 7.4 %collective-permute-start.11 = (bf16[256,512]{1,0:T(8,128)(2,1)S(1)}, bf16[256,512]{1,0:T(8,128)(2,1)S(1)}, u32[]{:S(2)}, u32[]{:S(2)}) collective-permute-start(bf16[256,512]{1,0:T(8,128)(2,1)S(1)} %get-tuple-element.53), channel_id=1, source_target_pairs={{0,4},{4,8},{8,12},{12,0},{16,20},{20,24},{24,28},{28,16},{32,36},... | collective-permute-start | bytes 786440 | tf_op jit(solution)/shard_map/ppermute | solution.py:266
  86.1 8.1 %collective-permute-start.12 = (bf16[256,512]{1,0:T(8,128)(2,1)S(1)}, bf16[256,512]{1,0:T(8,128)(2,1)S(1)}, u32[]{:S(2)}, u32[]{:S(2)}) collective-permute-start(bf16[256,512]{1,0:T(8,128)(2,1)S(1)} %get-tuple-element.53), channel_id=1, source_target_pairs={{0,12},{4,0},{8,4},{12,8},{16,28},{20,16},{24,20},{28,24},{32,44},... | collective-permute-start | bytes 786440 | tf_op jit(solution)/shard_map/ppermute | solution.py:266
  88.5 7.2 %collective-permute-start.13 = (bf16[256,512]{1,0:T(8,128)(2,1)S(1)}, bf16[256,512]{1,0:T(8,128)(2,1)S(1)}, u32[]{:S(2)}, u32[]{:S(2)}) collective-permute-start(bf16[256,512]{1,0:T(8,128)(2,1)S(1)} %get-tuple-element.53), channel_id=1, source_target_pairs={{0,8},{4,12},{8,0},{12,4},{16,24},{20,28},{24,16},{28,20},{32,40},... | collective-permute-start | bytes 786440 | tf_op jit(solution)/shard_map/ppermute | solution.py:266
  89.5 32.1 %copy-start.6 = (bf16[1024,512]{1,0:T(8,128)(2,1)}, bf16[1024,512]{1,0:T(8,128)(2,1)S(1)}, u32[]{:S(2)}) copy-start(bf16[1024,512]{1,0:T(8,128)(2,1)S(1)} %pad_maximum_fusion.1.refs_8_) | copy-start | bytes 3145732
  89.6 31.0 %collective-permute-start.21 = (bf16[1024,512]{1,0:T(8,128)(2,1)S(1)}, bf16[1024,512]{1,0:T(8,128)(2,1)}, u32[]{:S(2)}, u32[]{:S(2)}) collective-permute-start(bf16[1024,512]{1,0:T(8,128)(2,1)S(1)} %pad_maximum_fusion.1.refs_8_), channel_id=1, source_target_pairs={{0,4},{4,8},{8,12},{12,0},{16,20},{20,24},{24,28},{28,16},{32,36},... | collective-permute-start | bytes 3145736 | tf_op jit(solution)/shard_map/ppermute | solution.py:266
  90.8 30.9 %collective-permute-start.23 = (bf16[1024,512]{1,0:T(8,128)(2,1)S(1)}, bf16[1024,512]{1,0:T(8,128)(2,1)}, u32[]{:S(2)}, u32[]{:S(2)}) collective-permute-start(bf16[1024,512]{1,0:T(8,128)(2,1)S(1)} %pad_maximum_fusion.1.refs_8_), channel_id=1, source_target_pairs={{0,12},{4,0},{8,4},{12,8},{16,28},{20,16},{24,20},{28,24},{32,44},... | collective-permute-start | bytes 3145736 | tf_op jit(solution)/shard_map/ppermute | solution.py:266
  96.7 28.8 %collective-permute-start.14 = (bf16[1024,512]{1,0:T(8,128)(2,1)}, bf16[1024,512]{1,0:T(8,128)(2,1)}, u32[]{:S(2)}, u32[]{:S(2)}) collective-permute-start(bf16[1024,512]{1,0:T(8,128)(2,1)} %pad_maximum_fusion.refs_7_), channel_id=1, source_target_pairs={{0,16},{4,20},{8,24},{12,28},{16,32},{20,36},{24,40},{28,44},{32,4... | collective-permute-start | bytes 3145736 | tf_op jit(solution)/shard_map/ppermute | solution.py:266
  96.7 30.0 %collective-permute-start.16 = (bf16[1024,512]{1,0:T(8,128)(2,1)}, bf16[1024,512]{1,0:T(8,128)(2,1)}, u32[]{:S(2)}, u32[]{:S(2)}) collective-permute-start(bf16[1024,512]{1,0:T(8,128)(2,1)} %pad_maximum_fusion.refs_7_), channel_id=1, source_target_pairs={{0,48},{4,52},{8,56},{12,60},{16,0},{20,4},{24,8},{28,12},{32,16},... | collective-permute-start | bytes 3145736 | tf_op jit(solution)/shard_map/ppermute | solution.py:266
  121.6 8.9 %copy-start.12 = (bf16[1024,384]{1,0:T(8,128)(2,1)S(1)}, bf16[1024,384]{1,0:T(8,128)(2,1)}, u32[]{:S(2)}) copy-start(bf16[1024,384]{1,0:T(8,128)(2,1)} %copy-done.11) | copy-start | bytes 2359300
  121.6 23.1 %collective-permute-start.22 = (bf16[512,512]{1,0:T(8,128)(2,1)S(1)}, bf16[512,512]{1,0:T(8,128)(2,1)S(1)}, u32[]{:S(2)}, u32[]{:S(2)}) collective-permute-start(bf16[512,512]{1,0:T(8,128)(2,1)S(1)} %slice.119), channel_id=1, source_target_pairs={{0,4},{4,8},{8,12},{12,0},{16,20},{20,24},{24,28},{28,16},{32,36},... | collective-permute-start | bytes 1572872 | tf_op jit(solution)/shard_map/ppermute | solution.py:266
  122.9 21.9 %collective-permute-start.24 = (bf16[512,512]{1,0:T(8,128)(2,1)S(1)}, bf16[512,512]{1,0:T(8,128)(2,1)S(1)}, u32[]{:S(2)}, u32[]{:S(2)}) collective-permute-start(bf16[512,512]{1,0:T(8,128)(2,1)S(1)} %slice.120), channel_id=1, source_target_pairs={{0,12},{4,0},{8,4},{12,8},{16,28},{20,16},{24,20},{28,24},{32,44},... | collective-permute-start | bytes 1572872 | tf_op jit(solution)/shard_map/ppermute | solution.py:266
  126.6 18.2 %collective-permute-start.15 = (bf16[512,512]{1,0:T(8,128)(2,1)S(1)}, bf16[512,512]{1,0:T(8,128)(2,1)S(1)}, u32[]{:S(2)}, u32[]{:S(2)}) collective-permute-start(bf16[512,512]{1,0:T(8,128)(2,1)S(1)} %slice.117), channel_id=1, source_target_pairs={{0,16},{4,20},{8,24},{12,28},{16,32},{20,36},{24,40},{28,44},{32,4... | collective-permute-start | bytes 1572872 | tf_op jit(solution)/shard_map/ppermute | solution.py:266
  127.8 17.0 %collective-permute-start.17 = (bf16[512,512]{1,0:T(8,128)(2,1)S(1)}, bf16[512,512]{1,0:T(8,128)(2,1)S(1)}, u32[]{:S(2)}, u32[]{:S(2)}) collective-permute-start(bf16[512,512]{1,0:T(8,128)(2,1)S(1)} %slice.118), channel_id=1, source_target_pairs={{0,48},{4,52},{8,56},{12,60},{16,0},{20,4},{24,8},{28,12},{32,16},... | collective-permute-start | bytes 1572872 | tf_op jit(solution)/shard_map/ppermute | solution.py:266
  134.5 10.3 %copy-start.8 = (bf16[1,512,384]{2,1,0:T(8,128)(2,1)S(1)}, bf16[1,512,384]{2,1,0:T(8,128)(2,1)}, u32[]{:S(2)}) copy-start(bf16[1,512,384]{2,1,0:T(8,128)(2,1)} %param.16) | copy-start | bytes 1179652
  134.5 44.5 %slice-start = ((s8[6291456]{0:T(1024)(128)(4,1)}), s8[4194304]{0:T(1024)(128)(4,1)S(1)}, s32[]{:S(2)}) async-start(s8[6291456]{0:T(1024)(128)(4,1)} %bitcast.61), calls=%async_computation.2 | async-start | bytes 8388608
  144.8 10.2 %copy-start.10 = (bf16[6144,256]{1,0:T(8,128)(2,1)S(1)}, bf16[6144,256]{1,0:T(8,128)(2,1)}, u32[]{:S(2)}) copy-start(bf16[6144,256]{1,0:T(8,128)(2,1)} %get-tuple-element.39) | copy-start | bytes 9437188
  144.8 34.2 %slice-start.1 = ((s8[6291456]{0:T(1024)(128)(4,1)}), s8[2097152]{0:T(1024)(128)(4,1)S(1)}, s32[]{:S(2)}) async-start(s8[6291456]{0:T(1024)(128)(4,1)} %bitcast.61), calls=%async_computation.3 | async-start | bytes 4194304
  149.6 8.3 %collective-permute-start.33 = (bf16[512,384]{1,0:T(8,128)(2,1)}, bf16[512,384]{1,0:T(8,128)(2,1)S(1)}, u32[]{:S(2)}, u32[]{:S(2)}) collective-permute-start(bf16[512,384]{1,0:T(8,128)(2,1)} %shard_map.116), channel_id=1, source_target_pairs={{2,0},{3,1},{0,2},{1,3},{6,4},{7,5},{4,6},{5,7},{10,8},{11,9},{8,1... | collective-permute-start | bytes 1179656 | tf_op jit(solution)/shard_map/ppermute | solution.py:313
  152.3 10.4 %collective-permute-start.28 = (bf16[512,384]{1,0:T(8,128)(2,1)}, bf16[512,384]{1,0:T(8,128)(2,1)S(1)}, u32[]{:S(2)}, u32[]{:S(2)}) collective-permute-start(bf16[512,384]{1,0:T(8,128)(2,1)} %shard_map.116), channel_id=1, source_target_pairs={{0,4},{4,8},{8,12},{12,0},{16,20},{20,24},{24,28},{28,16},{32,36},... | collective-permute-start | bytes 1179656 | tf_op jit(solution)/shard_map/ppermute | solution.py:266
  152.3 14.9 %collective-permute-start.29 = (bf16[512,384]{1,0:T(8,128)(2,1)}, bf16[512,384]{1,0:T(8,128)(2,1)S(1)}, u32[]{:S(2)}, u32[]{:S(2)}) collective-permute-start(bf16[512,384]{1,0:T(8,128)(2,1)} %shard_map.116), channel_id=1, source_target_pairs={{0,12},{4,0},{8,4},{12,8},{16,28},{20,16},{24,20},{28,24},{32,44},... | collective-permute-start | bytes 1179656 | tf_op jit(solution)/shard_map/ppermute | solution.py:266
  155.0 12.4 %collective-permute-start.30 = (bf16[512,384]{1,0:T(8,128)(2,1)}, bf16[512,384]{1,0:T(8,128)(2,1)S(1)}, u32[]{:S(2)}, u32[]{:S(2)}) collective-permute-start(bf16[512,384]{1,0:T(8,128)(2,1)} %shard_map.116), channel_id=1, source_target_pairs={{0,8},{4,12},{8,0},{12,4},{16,24},{20,28},{24,16},{28,20},{32,40},... | collective-permute-start | bytes 1179656 | tf_op jit(solution)/shard_map/ppermute | solution.py:266
  155.0 70.6 %collective-permute-start.27 = (bf16[6144,256]{1,0:T(8,128)(2,1)S(1)}, bf16[6144,256]{1,0:T(8,128)(2,1)S(1)}, u32[]{:S(2)}, u32[]{:S(2)}) collective-permute-start(bf16[6144,256]{1,0:T(8,128)(2,1)S(1)} %copy-done.10), channel_id=1, source_target_pairs={{1,0},{2,1},{3,2},{0,3},{5,4},{6,5},{7,6},{4,7},{9,8},{10,9},{11,1... | collective-permute-start | bytes 9437192 | tf_op jit(solution)/shard_map/ppermute | solution.py:313
  157.9 10.3 %collective-permute-start.34 = (bf16[512,384]{1,0:T(8,128)(2,1)S(1)}, bf16[512,384]{1,0:T(8,128)(2,1)S(1)}, u32[]{:S(2)}, u32[]{:S(2)}) collective-permute-start(bf16[512,384]{1,0:T(8,128)(2,1)S(1)} %collective-permute-done.33), channel_id=1, source_target_pairs={{0,16},{4,20},{8,24},{12,28},{16,32},{20,36},{24,40},{28,44},{32,4... | collective-permute-start | bytes 1179656 | tf_op jit(solution)/shard_map/ppermute | solution.py:266
  162.8 13.3 %collective-permute-start.35 = (bf16[512,384]{1,0:T(8,128)(2,1)S(1)}, bf16[512,384]{1,0:T(8,128)(2,1)S(1)}, u32[]{:S(2)}, u32[]{:S(2)}) collective-permute-start(bf16[512,384]{1,0:T(8,128)(2,1)S(1)} %collective-permute-done.33), channel_id=1, source_target_pairs={{0,48},{4,52},{8,56},{12,60},{16,0},{20,4},{24,8},{28,12},{32,16},... | collective-permute-start | bytes 1179656 | tf_op jit(solution)/shard_map/ppermute | solution.py:266
  167.2 8.9 %collective-permute-start.36 = (bf16[512,384]{1,0:T(8,128)(2,1)S(1)}, bf16[512,384]{1,0:T(8,128)(2,1)S(1)}, u32[]{:S(2)}, u32[]{:S(2)}) collective-permute-start(bf16[512,384]{1,0:T(8,128)(2,1)S(1)} %collective-permute-done.33), channel_id=1, source_target_pairs={{0,32},{4,36},{8,40},{12,44},{16,48},{20,52},{24,56},{28,60},{32,0... | collective-permute-start | bytes 1179656 | tf_op jit(solution)/shard_map/ppermute | solution.py:266
  167.5 11.5 %copy-start.3 = (bf16[2048,384]{1,0:T(8,128)(2,1)}, bf16[2048,384]{1,0:T(8,128)(2,1)S(1)}, u32[]{:S(2)}) copy-start(bf16[2048,384]{1,0:T(8,128)(2,1)S(1)} %constant_dynamic-update-slice_fusion.4.refs_3_.refs_4_) | copy-start | bytes 4718596
  167.5 43.5 %collective-permute-start.31 = (bf16[2048,384]{1,0:T(8,128)(2,1)S(1)}, bf16[2048,384]{1,0:T(8,128)(2,1)S(1)}, u32[]{:S(2)}, u32[]{:S(2)}) collective-permute-start(bf16[2048,384]{1,0:T(8,128)(2,1)S(1)} %constant_dynamic-update-slice_fusion.4.refs_3_.refs_4_), channel_id=1, source_target_pairs={{0,16},{4,20},{8,24},{12,28},{16,32},{20,36},{24,40},{28,44},{32,4... | collective-permute-start | bytes 4718600 | tf_op jit(solution)/shard_map/ppermute | solution.py:266
  168.2 46.0 %collective-permute-start.32 = (bf16[2048,384]{1,0:T(8,128)(2,1)S(1)}, bf16[2048,384]{1,0:T(8,128)(2,1)S(1)}, u32[]{:S(2)}, u32[]{:S(2)}) collective-permute-start(bf16[2048,384]{1,0:T(8,128)(2,1)S(1)} %constant_dynamic-update-slice_fusion.4.refs_3_.refs_4_), channel_id=1, source_target_pairs={{0,48},{4,52},{8,56},{12,60},{16,0},{20,4},{24,8},{28,12},{32,16},... | collective-permute-start | bytes 4718600 | tf_op jit(solution)/shard_map/ppermute | solution.py:266
  176.2 37.9 %collective-permute-start.37 = (bf16[2048,384]{1,0:T(8,128)(2,1)S(1)}, bf16[2048,384]{1,0:T(8,128)(2,1)S(1)}, u32[]{:S(2)}, u32[]{:S(2)}) collective-permute-start(bf16[2048,384]{1,0:T(8,128)(2,1)S(1)} %constant_dynamic-update-slice_fusion.8.refs_4_.refs_5_), channel_id=1, source_target_pairs={{0,4},{4,8},{8,12},{12,0},{16,20},{20,24},{24,28},{28,16},{32,36},... | collective-permute-start | bytes 4718600 | tf_op jit(solution)/shard_map/ppermute | solution.py:266
  176.3 37.8 %collective-permute-start.38 = (bf16[2048,384]{1,0:T(8,128)(2,1)S(1)}, bf16[2048,384]{1,0:T(8,128)(2,1)S(1)}, u32[]{:S(2)}, u32[]{:S(2)}) collective-permute-start(bf16[2048,384]{1,0:T(8,128)(2,1)S(1)} %constant_dynamic-update-slice_fusion.8.refs_4_.refs_5_), channel_id=1, source_target_pairs={{0,12},{4,0},{8,4},{12,8},{16,28},{20,16},{24,20},{28,24},{32,44},... | collective-permute-start | bytes 4718600 | tf_op jit(solution)/shard_map/ppermute | solution.py:266
  214.3 33.6 %collective-permute-start.39 = (bf16[1024,384]{1,0:T(8,128)(2,1)S(1)}, bf16[1024,384]{1,0:T(8,128)(2,1)S(1)}, u32[]{:S(2)}, u32[]{:S(2)}) collective-permute-start(bf16[1024,384]{1,0:T(8,128)(2,1)S(1)} %slice.103), channel_id=1, source_target_pairs={{0,16},{4,20},{8,24},{12,28},{16,32},{20,36},{24,40},{28,44},{32,4... | collective-permute-start | bytes 2359304 | tf_op jit(solution)/shard_map/ppermute | solution.py:266
  215.3 14.9 %copy-start.4 = (bf16[2048,384]{1,0:T(8,128)(2,1)S(1)}, bf16[2048,384]{1,0:T(8,128)(2,1)}, u32[]{:S(2)}) copy-start(bf16[2048,384]{1,0:T(8,128)(2,1)} %copy-done.3) | copy-start | bytes 4718596
  215.3 32.6 %collective-permute-start.40 = (bf16[1024,384]{1,0:T(8,128)(2,1)S(1)}, bf16[1024,384]{1,0:T(8,128)(2,1)S(1)}, u32[]{:S(2)}, u32[]{:S(2)}) collective-permute-start(bf16[1024,384]{1,0:T(8,128)(2,1)S(1)} %slice.104), channel_id=1, source_target_pairs={{0,48},{4,52},{8,56},{12,60},{16,0},{20,4},{24,8},{28,12},{32,16},... | collective-permute-start | bytes 2359304 | tf_op jit(solution)/shard_map/ppermute | solution.py:266
  219.1 28.8 %collective-permute-start.41 = (bf16[1024,384]{1,0:T(8,128)(2,1)}, bf16[1024,384]{1,0:T(8,128)(2,1)S(1)}, u32[]{:S(2)}, u32[]{:S(2)}) collective-permute-start(bf16[1024,384]{1,0:T(8,128)(2,1)} %slice.105), channel_id=1, source_target_pairs={{0,4},{4,8},{8,12},{12,0},{16,20},{20,24},{24,28},{28,16},{32,36},... | collective-permute-start | bytes 2359304 | tf_op jit(solution)/shard_map/ppermute | solution.py:266
  220.1 27.8 %collective-permute-start.42 = (bf16[1024,384]{1,0:T(8,128)(2,1)}, bf16[1024,384]{1,0:T(8,128)(2,1)S(1)}, u32[]{:S(2)}, u32[]{:S(2)}) collective-permute-start(bf16[1024,384]{1,0:T(8,128)(2,1)} %slice.106), channel_id=1, source_target_pairs={{0,12},{4,0},{8,4},{12,8},{16,28},{20,16},{24,20},{28,24},{32,44},... | collective-permute-start | bytes 2359304 | tf_op jit(solution)/shard_map/ppermute | solution.py:266
  225.6 22.3 %slice-start.2 = ((s8[6291456]{0:T(1024)(128)(4,1)}), s8[4194304]{0:T(1024)(128)(4,1)S(1)}, s32[]{:S(2)}) async-start(s8[6291456]{0:T(1024)(128)(4,1)} %bitcast.64), calls=%async_computation.4 | async-start | bytes 8388608
  225.6 22.3 %slice-start.3 = ((s8[6291456]{0:T(1024)(128)(4,1)}), s8[2097152]{0:T(1024)(128)(4,1)S(1)}, s32[]{:S(2)}) async-start(s8[6291456]{0:T(1024)(128)(4,1)} %bitcast.64), calls=%async_computation.5 | async-start | bytes 4194304
  225.6 33.4 %collective-permute-start.26 = (bf16[1,512,384]{2,1,0:T(8,128)(2,1)}, bf16[1,512,384]{2,1,0:T(8,128)(2,1)}, u32[]{:S(2)}, u32[]{:S(2)}) collective-permute-start(bf16[1,512,384]{2,1,0:T(8,128)(2,1)} %bitcast.33), channel_id=1, source_target_pairs={{0,64},{1,65},{2,66},{3,67},{64,0},{65,1},{66,2},{67,3},{4,68},{5,... | collective-permute-start | bytes 1179656 | tf_op jit(solution)/shard_map/ppermute | solution.py:321
  248.0 17.8 %copy-start.1 = (f32[1,16,128,128]{3,2,1,0:T(8,128)S(1)}, f32[1,16,128,128]{3,2,1,0:T(8,128)}, u32[]{:S(2)}) copy-start(f32[1,16,128,128]{3,2,1,0:T(8,128)} %param.13) | copy-start | bytes 3145732
  256.5 3.3 %collective-permute-start.44 = (bf16[16,256]{1,0:T(8,128)(2,1)S(1)}, bf16[16,256]{1,0:T(8,128)(2,1)S(1)}, u32[]{:S(2)}, u32[]{:S(2)}) collective-permute-start(bf16[16,256]{1,0:T(8,128)(2,1)S(1)} %get-tuple-element.62), channel_id=1, source_target_pairs={{1,64},{2,65},{3,66},{0,67},{65,0},{66,1},{67,2},{64,3},{5,68},{6,... | collective-permute-start | bytes 24584 | tf_op jit(solution)/shard_map/ppermute | solution.py:321
  259.0 4.3 %collective-permute-start.45 = (bf16[16,256]{1,0:T(8,128)(2,1)S(1)}, bf16[16,256]{1,0:T(8,128)(2,1)S(1)}, u32[]{:S(2)}, u32[]{:S(2)}) collective-permute-start(bf16[16,256]{1,0:T(8,128)(2,1)S(1)} %get-tuple-element.63), channel_id=1, source_target_pairs={{3,64},{0,65},{1,66},{2,67},{67,0},{64,1},{65,2},{66,3},{7,68},{4,... | collective-permute-start | bytes 24584 | tf_op jit(solution)/shard_map/ppermute | solution.py:321
  259.0 4.3 %collective-permute-start.43 = (bf16[16,512]{1,0:T(8,128)(2,1)S(1)}, bf16[16,512]{1,0:T(8,128)(2,1)S(1)}, u32[]{:S(2)}, u32[]{:S(2)}) collective-permute-start(bf16[16,512]{1,0:T(8,128)(2,1)S(1)} %slice.122), channel_id=1, source_target_pairs={{0,64},{1,65},{2,66},{3,67},{64,0},{65,1},{66,2},{67,3},{4,68},{5,... | collective-permute-start | bytes 49160 | tf_op jit(solution)/shard_map/ppermute | solution.py:321
  (3 other events, 4.6 us)

commit v6 on v5

--- a/solution.py
+++ b/solution.py
@@ -94,34 +94,51 @@
 
 
 def listed(gathered, steps):
-    arrays, layout = [], []
-    for step in steps:
-        for half, parts in enumerate(gathered):
-            first = 0
-            for array in parts[step]:
-                count = 4 * array.shape[0] // parts[0][0].shape[0]
-                arrays.append(array)
-                layout.append((half, step, first, count))
-                first += count
-    return arrays, layout
-
-
-def each_part(source, layout, blocks, rows, body):
-    for (half, step, first, count), block in zip(layout, blocks):
-
-        def one(i, carry, half=half, step=step, first=first, block=block):
-            part = source[(half * 4 + step) * 4 + first + i]
-            across = pl.ds(pl.multiple_of(i * rows, BLK), rows)
-            body(slice(half * rows, (half + 1) * rows), part, block[across, :], step)
-            return carry
-
-        lax.fori_loop(0, count, one, 0)
-
-
-def project_kernel(layout, final, *refs):
+    return [array for step in steps for parts in gathered for array in parts[step]]
+
+
+def stream(source, step, arrays, rows, buffer, sems, fetch, fetched, body):
+    total = sum(array.shape[0] // rows for array in arrays)
+    count = total // len(arrays)
+
+    def place(n):
+        half = lax.rem(lax.div(n, 4), 2)
+        row = half * 4 + step + lax.div(n, 8)
+        return half, source[row * 4 + lax.rem(n, 4)]
+
+    def start(n, slot):
+        for r, array in enumerate(arrays):
+
+            @pl.when(lax.div(n, count) == r)
+            def _():
+                across = pl.ds(pl.multiple_of(lax.rem(n, count) * rows, BLK), rows)
+                pltpu.make_async_copy(array.at[across, :], buffer.at[slot], sems.at[slot, 0]).start()
+
+        fetch(place(n)[1], slot)
+
+    start(0, 0)
+
+    def one(n, carry):
+        slot = lax.rem(n, 2)
+
+        @pl.when(n + 1 < total)
+        def _():
+            start(n + 1, 1 - slot)
+
+        first = pl.ds(0, rows)
+        pltpu.make_async_copy(arrays[0].at[first, :], buffer.at[slot], sems.at[slot, 0]).wait()
+        half, part = place(n)
+        fetched(slot)
+        body(pl.ds(pl.multiple_of(half * rows, BLK), rows), part, slot)
+        return carry
+
+    lax.fori_loop(0, total, one, 0)
+
+
+def project_kernel(count, step, final, *refs):
     source, inverse_ref, w0, w1, w2, w3, w4 = refs[:7]
-    blocks = refs[7 : 7 + len(layout)]
-    rest = refs[7 + len(layout) :]
+    blocks = refs[7 : 7 + count]
+    *rest, buffer, w_buffer, sems = refs[7 + count :]
     if final:
         acc_ref, square_ref, residual_ref, out_ref, acc, square = rest
         acc[...] = acc_ref[...]
@@ -132,14 +149,30 @@
         square[...] = jnp.zeros_like(square)
     middle = w2.shape[0] // HD
 
-    def body(here, part, a, step):
-        rows = pl.ds(pl.multiple_of(part * HD, HD), HD)
-        inner = pl.ds(pl.multiple_of(lax.rem(part, middle) * HD, HD), HD)
-        lower = (part < middle).astype(jnp.float32)
-        far = w2[inner, :].astype(jnp.float32) * lower
-        far = far + w3[inner, :].astype(jnp.float32) * (1.0 - lower)
-        w = jnp.concatenate([w0[rows, :], w1[rows, :], far.astype(w0.dtype), w4[rows, :]], axis=0)
-        acc[here, :] += dot(a, w)
+    def copy(ref, block, k, slot):
+        rows = pl.ds(pl.multiple_of(block * HD, HD), HD)
+        there = w_buffer.at[slot, k * HD : (k + 1) * HD, :]
+        return pltpu.make_async_copy(ref.at[rows, :], there, sems.at[slot, 1 + k])
+
+    def fetch(part, slot):
+        for k, w in ((0, w0), (1, w1), (3, w4)):
+            copy(w, part, k, slot).start()
+
+        @pl.when(part < middle)
+        def _():
+            copy(w2, part, 2, slot).start()
+
+        @pl.when(part >= middle)
+        def _():
+            copy(w3, part - middle, 2, slot).start()
+
+    def fetched(slot):
+        for k in range(4):
+            copy(w0, 0, k, slot).wait()
+
+    def body(here, part, slot):
+        a = buffer[slot]
+        acc[here, :] += dot(a, w_buffer[slot])
         wide = a.astype(jnp.float32)
         wide = wide * wide * inverse_ref[pl.ds(part, 1), :]
         squares = square[here, :]
@@ -147,66 +180,96 @@
             squares += wide[:, j * HD : (j + 1) * HD]
         square[here, :] = squares
 
-    each_part(source, layout, blocks, acc.shape[0] // 2, body)
+    stream(source, step, blocks, buffer.shape[1], buffer, sems, fetch, fetched, body)
     if final:
         mean = jnp.sum(square[...], axis=1, keepdims=True) / HDIM
         scaled = acc[...] * lax.rsqrt(mean + epsilon)
         out_ref[...] = (residual_ref[...].astype(jnp.float32) + scaled).astype(out_ref.dtype)
 
 
+SMEM, VMEM, HBM, ANY = (
+    pl.BlockSpec(memory_space=x) for x in (pltpu.SMEM, pltpu.VMEM, pltpu.HBM, pl.ANY)
+)
+
+
 def project(source, inverse, weights, gathered, residual):
     rows, columns = residual.shape
+    depth = gathered[0][0][0].shape[1]
     sums = [
         jax.ShapeDtypeStruct((rows, columns), jnp.float32),
         jax.ShapeDtypeStruct((rows, HD), jnp.float32),
     ]
-    smem, vmem = pl.BlockSpec(memory_space=pltpu.SMEM), pl.BlockSpec(memory_space=pltpu.VMEM)
-    arrays, layout = listed(gathered, [0, 1, 2])
+    slots = [
+        pltpu.VMEM((2, rows // 2, depth), jnp.bfloat16),
+        pltpu.VMEM((2, depth, columns), jnp.bfloat16),
+        pltpu.SemaphoreType.DMA((2, 5)),
+    ]
+    params = pltpu.CompilerParams(vmem_limit_bytes=12 * MIB)
+    weights = [in_hbm(w) for w in weights]
+    arrays = listed(gathered, [0, 1, 2])
     acc, square = pl.pallas_call(
-        functools.partial(project_kernel, layout, False),
-        in_specs=[smem] + [vmem] * (6 + len(arrays)),
-        out_specs=[vmem] * 2,
+        functools.partial(project_kernel, len(arrays), 0, False),
+        in_specs=[SMEM, VMEM] + [HBM] * 5 + [ANY] * len(arrays),
+        out_specs=[VMEM] * 2,
         out_shape=sums,
-        compiler_params=pltpu.CompilerParams(vmem_limit_bytes=18 * MIB),
+        scratch_shapes=slots,
+        compiler_params=params,
     )(source, inverse, *weights, *arrays)
-    arrays, layout = listed(gathered, [3])
+    arrays = listed(gathered, [3])
     return pl.pallas_call(
-        functools.partial(project_kernel, layout, True),
-        in_specs=[smem] + [vmem] * (6 + len(arrays) + 3),
-        out_specs=vmem,
+        functools.partial(project_kernel, len(arrays), 3, True),
+        in_specs=[SMEM, VMEM] + [HBM] * 5 + [ANY] * len(arrays) + [VMEM] * 3,
+        out_specs=VMEM,
         out_shape=jax.ShapeDtypeStruct((rows, columns), jnp.bfloat16),
-        scratch_shapes=[pltpu.VMEM(x.shape, x.dtype) for x in sums],
-        compiler_params=pltpu.CompilerParams(vmem_limit_bytes=18 * MIB),
+        scratch_shapes=[pltpu.VMEM(x.shape, x.dtype) for x in sums] + slots,
+        compiler_params=params,
     )(source, inverse, *weights, *arrays, acc, square, residual)
 
 
-def encode_kernel(layout, late, first, final, *refs):
-    source, *encoders = refs[: 3 if first else 4]
-    used = 1 + len(encoders)
-    blocks = refs[used : used + len(layout)]
-    rest = refs[used + len(layout) :]
+def encode_kernel(encoder_count, count, step, late, final, *refs):
+    source, *encoders = refs[: 1 + encoder_count]
+    blocks = refs[1 + encoder_count : 1 + encoder_count + count]
+    *rest, buffer, e_buffer, sems = refs[1 + encoder_count + count :]
     if final:
         acc_ref, bias_ref, out_ref, acc = rest
-    elif first:
+    elif encoder_count == 2:
         (acc,) = rest
+        acc_ref = None
     else:
         acc_ref, acc = rest
-    if first:
-        acc[...] = jnp.zeros_like(acc)
+    acc[...] = jnp.zeros_like(acc) if acc_ref is None else acc_ref[...]
+    depth = e_buffer.shape[1]
+    starts = [sum(e.shape[1] for e in encoders[:n]) for n in range(encoder_count)]
+
+    def run(step, blocks, used):
+        def there(n):
+            return slice(starts[n], starts[n] + encoders[n].shape[1])
+
+        def copy(n, part, slot):
+            rows = pl.ds(pl.multiple_of(part * depth, BLK), depth)
+            to = e_buffer.at[slot, :, there(n)]
+            return pltpu.make_async_copy(encoders[n].at[rows, :], to, sems.at[slot, 1 + n])
+
+        def fetch(part, slot):
+            for n in used:
+                copy(n, part, slot).start()
+
+        def fetched(slot):
+            for n in used:
+                copy(n, 0, slot).wait()
+
+        def body(here, part, slot):
+            across = slice(starts[used[0]], there(used[-1]).stop)
+            acc[here, across] += dot(buffer[slot], e_buffer[slot, :, across])
+
+        stream(source, step, blocks, buffer.shape[1], buffer, sems, fetch, fetched, body)
+
+    every = list(range(encoder_count))
+    if late:
+        run(step, blocks[:late], every[-1:])
+        run(step + 1, blocks[late:], every)
     else:
-        acc[...] = acc_ref[...]
-    depth = blocks[0].shape[1]
-
-    def body(here, part, a, step):
-        columns = pl.ds(pl.multiple_of(part * depth, BLK), depth)
-        start = 0
-        for n, e in enumerate(encoders):
-            there = slice(start, start + e.shape[1])
-            if step not in late or n == 2:
-                acc[here, there] += dot(a, e[columns, :])
-            start += e.shape[1]
-
-    each_part(source, layout, blocks, acc.shape[0] // 2, body)
+        run(step, blocks, every)
     if final:
         for i in range(out_ref.shape[0] // 8):
             pools = []
@@ -216,40 +279,25 @@
             out_ref[8 * i : 8 * i + 8, :] = jnp.concatenate(pools, axis=0)
 
 
-def encode_own(source, encoders, gathered, bias):
-    rows = gathered[0][0][0].shape[0] // 2
-    smem, vmem = pl.BlockSpec(memory_space=pltpu.SMEM), pl.BlockSpec(memory_space=pltpu.VMEM)
-    arrays, layout = listed(gathered, [0])
+def encode(source, encoders, arrays, step, late=0, acc=None, bias=None):
+    rows, depth = arrays[0].shape[0] // (4 if bias is None else 2), arrays[0].shape[1]
+    width = 4 * encoders[1].shape[1]
+    shape = jax.ShapeDtypeStruct((2 * rows, width), jnp.float32)
+    final = bias is not None
+    extra = [x for x in (acc, bias) if x is not None]
+    slots = [
+        pltpu.VMEM((2, rows, depth), jnp.bfloat16),
+        pltpu.VMEM((2, depth, width), jnp.bfloat16),
+        pltpu.SemaphoreType.DMA((2, 4)),
+    ]
     return pl.pallas_call(
-        functools.partial(encode_kernel, layout, (), True, False),
-        in_specs=[smem] + [vmem] * (2 + len(arrays)),
-        out_specs=vmem,
-        out_shape=jax.ShapeDtypeStruct((rows, bias.shape[1]), jnp.float32),
-        compiler_params=pltpu.CompilerParams(vmem_limit_bytes=30 * MIB),
-    )(source, *encoders[:2], *arrays)
-
-
-def encode(source, encoders, gathered, acc, bias):
-    smem, vmem = pl.BlockSpec(memory_space=pltpu.SMEM), pl.BlockSpec(memory_space=pltpu.VMEM)
-    params = pltpu.CompilerParams(vmem_limit_bytes=30 * MIB)
-    shape = jax.ShapeDtypeStruct(acc.shape, acc.dtype)
-    arrays, layout = listed(gathered, [0, 1, 2])
-    acc = pl.pallas_call(
-        functools.partial(encode_kernel, layout, (0,), False, False),
-        in_specs=[smem] + [vmem] * (3 + len(arrays) + 1),
-        out_specs=vmem,
-        out_shape=shape,
-        compiler_params=params,
-    )(source, *encoders, *arrays, acc)
-    arrays, layout = listed(gathered, [3])
-    return pl.pallas_call(
-        functools.partial(encode_kernel, layout, (), False, True),
-        in_specs=[smem] + [vmem] * (3 + len(arrays) + 2),
-        out_specs=vmem,
-        out_shape=jax.ShapeDtypeStruct((acc.shape[0] // POOL, acc.shape[1]), jnp.float32),
-        scratch_shapes=[pltpu.VMEM(acc.shape, acc.dtype)],
-        compiler_params=params,
-    )(source, *encoders, *arrays, acc, bias)
+        functools.partial(encode_kernel, len(encoders), len(arrays), step, late, final),
+        in_specs=[SMEM] + [HBM] * len(encoders) + [ANY] * len(arrays) + [VMEM] * len(extra),
+        out_specs=VMEM,
+        out_shape=jax.ShapeDtypeStruct((2 * rows // POOL, width), jnp.float32) if final else shape,
+        scratch_shapes=([pltpu.VMEM(shape.shape, shape.dtype)] if final else []) + slots,
+        compiler_params=pltpu.CompilerParams(vmem_limit_bytes=18 * MIB),
+    )(source, *[in_hbm(x) for x in encoders], *arrays, *extra)
 
 
 SIDE = 4
@@ -323,10 +371,7 @@
     packed = pack(query_vectors[0], key_vectors[0], value_vectors[0], doc_ids)
     weight = out_weight[0]
     middle = weight.shape[0] // 2
-    after_upper, before_lower = from_head(weight[:middle], 1), from_head(weight[middle:], -1)
-    after_upper, before_lower, rest = lax.optimization_barrier((after_upper, before_lower, weight))
-    across = [from_head(after_upper, 1), from_head(before_lower, -1)]
-    after_lower, before_upper = from_head(rest[middle:], 1), from_head(rest[:middle], -1)
+    after, before = from_head(weight, 1), from_head(weight, -1)
     gains = [norm_gain] + [from_head(norm_gain, k) for k in range(1, groups)]
     inverse = jnp.concatenate([(1.0 / (g * g)).reshape(-1, HD) for g in gains], axis=1)
     half = enc_weight.shape[2] // 2
@@ -339,9 +384,10 @@
     prior = lax.dynamic_index_in_dim(prior_state[0], place, 0, False)
     gain = lax.dynamic_slice_in_dim(norm_gain, place * HD, HD, 1)
     attended = attend(packed, prior, gain, groups)
-    attended, after_lower, before_upper, inverse, bias = lax.optimization_barrier(
-        (attended, after_lower, before_upper, inverse, bias)
-    )
+    attended, after, before, inverse, bias = lax.optimization_barrier(
+        (attended, after, before, inverse, bias)
+    )
+    across = [from_head(after[:middle], 1), from_head(before[middle:], -1)]
 
     own = lax.all_to_all(attended, "head", 0, 0, tiled=True)
     own = jnp.concatenate(
@@ -355,12 +401,7 @@
     from_before = from_head(first_half, -1)
     rows = own.shape[0] // 2
     joined = [jnp.concatenate(line, axis=0) for line in lines([own[:rows], own[rows:]])]
-    weights = [
-        weight,
-        jnp.concatenate([after_upper, after_lower], axis=0),
-        *across,
-        jnp.concatenate([before_upper, before_lower], axis=0),
-    ]
+    weights = [weight, after, *across, before]
     layer_out = project(source, inverse, weights, planes(joined, near(joined)), residual[0])
 
     layer_out, from_before, second_half = lax.optimization_barrier(
@@ -371,9 +412,12 @@
     joined = [jnp.concatenate(line, axis=0) for line in lines([layer_out, opposite])]
     beside = near(joined)
     encoders = [enc_weight[0], from_before, from_after]
-    acc = encode_own(source, encoders, [((x,),) for x in joined], bias)
+    acc = encode(source, encoders[:2], joined, 0)
     beside, acc = lax.optimization_barrier((beside, acc))
-    pooled = encode(source, encoders, planes(joined, beside), acc, bias)
+    gathered = planes(joined, beside)
+    acc = encode(source, encoders, listed(gathered, [0, 1, 2]), 0, late=2, acc=acc)
+    acc, layer_out = lax.optimization_barrier((acc, layer_out))
+    pooled = encode(source, encoders, listed(gathered, [3]), 3, acc=acc, bias=bias)
     pooled = pooled.astype(jnp.bfloat16)
     pools = pooled.shape[0] // 2
     mine = from_section(pooled[:, : 2 * half], 0)

time: 266 us -> 285 us (1.071)
  Pallas kernels: 55 us -> 75.5 us
  waiting for transfers between devices: 107 us -> 111 us
    pallas_call x5, Pallas kernels: 47.8 us -> 69.7 us  [the longest x3 44.3 us: encode(): pl.pallas_call(functools.partial(encode_kernel, len(encoders), len(arrays...]
    ppermute x14 -> x12, waiting for transfers between devices: 28.2 us -> 47.7 us  [from_head(): lax.ppermute(x, 'head', [((i + by) % groups, i) for i in range(groups)])]
    all_to_all x1, waiting for transfers between devices: 11.8 us -> 0.01 us  [local(): own = lax.all_to_all(attended, 'head', 0, 0, tiled=True)]
    ppermute x28, waiting for transfers between devices: 63.2 us -> 59.2 us  [moved(): return lax.ppermute(x, 'seq', pairs)]
    ppermute x14 -> x12, starting transfers between devices: 16 us -> 13.2 us  [from_head(): lax.ppermute(x, 'head', [((i + by) % groups, i) for i in range(groups)])]
    unnamed x47 -> x41, local copies, waits for them, and re-layouts: 6.39 us -> 8.47 us
  transfers between devices with their start and end apart: 48 -> 46, of which waited for: 18 -> 15; matrix products, arithmetic and copies ran while one was open for 8% -> 5% of each run, Pallas kernels for 20% -> 23%
where the time goes in v6:
time: 285 us; the launch traced here: 284 us
  waiting for transfers between devices  111 us (39%)
  Pallas kernels  75.5 us (26%)
  starting transfers between devices  73.3 us (26%)
  local copies, waits for them, and re-layouts  21.9 us (8%)
    ppermute x28, waiting for transfers between devices, moved(): return lax.ppermute(x, 'seq', pairs)  59.2 us
    ppermute x12, waiting for transfers between devices, from_head(): lax.ppermute(x, 'head', [((i + by) % groups, i) for i in range(groups)])  47.7 us
    pallas_call x3, Pallas kernels, encode(): pl.pallas_call(functools.partial(encode_kernel, len(encoders), len(arrays...  44.3 us
    ppermute x28, starting transfers between devices, moved(): return lax.ppermute(x, 'seq', pairs)  40 us
    pallas_call x1, Pallas kernels, project(): pl.pallas_call(functools.partial(project_kernel, len(arrays), 0, False),...  18.2 us
    ppermute x12, starting transfers between devices, from_head(): lax.ppermute(x, 'head', [((i + by) % groups, i) for i in range(groups)])  13.2 us
    ppermute x4, starting transfers between devices, from_section(): return lax.ppermute(x, ('section', 'head'), pairs)  8.74 us
    unnamed x41, local copies, waits for them, and re-layouts  8.47 us
  transfers between devices with their start and end apart: 46, of which 15 were waited for; matrix products, arithmetic and copies ran while one was open for 5% of the time, Pallas kernels for 23%

profile of v6, /device:TPU:1, one launch (start us, length us, event | category | flops | bytes accessed | tf_op | source)
XLA Modules:
  0.0 283.5 jit_solution(9068913145535498724)
XLA Ops:
  0.6 3.4 %collective-permute-start = (bf16[2048,384]{1,0:T(8,128)(2,1)}, bf16[2048,384]{1,0:T(8,128)(2,1)}, u32[]{:S(2)}, u32[]{:S(2)}) collective-permute-start(bf16[2048,384]{1,0:T(8,128)(2,1)} %bitcast.61), channel_id=1, source_target_pairs={{1,0},{2,1},{3,2},{0,3},{5,4},{6,5},{7,6},{4,7},{9,8},{10,9},{11,1... | collective-permute-start | bytes 4718600 | tf_op jit(solution)/shard_map/ppermute | solution.py:361
  4.0 0.7 copy-done.10
  4.7 1.6 shard_map.113
  6.3 1.2 copy-done.2
  7.5 7.9 %all-to-all-start = ((bf16[16,400,128]{2,1,0:T(8,128)(2,1)}), bf16[16,400,128]{2,1,0:T(8,128)(2,1)S(1)}, u32[]{:S(2)}, u32[]{:S(2)}) async-start(bf16[16,400,128]{2,1,0:T(8,128)(2,1)} %copy-done.2), calls=%async_computation | async-start | bytes 3276800 | tf_op jit(solution)/shard_map/all_to_all | solution.py:383
  15.7 2.6 collective-permute-start.6
  18.3 1.4 collective-permute-start.2
  19.7 20.8 %collective-permute-done.5 = f32[1,256]{1,0:T(1,128)S(1)} collective-permute-done((f32[1,256]{1,0:T(1,128)S(1)}, f32[1,256]{1,0:T(1,128)S(1)}, u32[]{:S(2)}, u32[]{:S(2)}) %collective-permute-start.5) | collective-permute-done | bytes 1056 | tf_op jit(solution)/shard_map/ppermute | solution.py:361
  40.6 3.9 %collective-permute-done.3 = f32[1,2048]{1,0:T(1,128)S(1)} collective-permute-done((f32[1,2048]{1,0:T(1,128)S(1)}, f32[1,2048]{1,0:T(1,128)S(1)}, u32[]{:S(2)}, u32[]{:S(2)}) %collective-permute-start.3) | collective-permute-done | bytes 8224 | tf_op jit(solution)/shard_map/ppermute | solution.py:361
  44.6 4.2 %shard_map.114 = bf16[4,512,128]{2,1,0:T(8,128)(2,1)} custom-call(bf16[16,400,128]{2,1,0:T(8,128)(2,1)S(1)} %all-to-all-done.packed_ref, f32[128,128]{1,0:T(8,128)S(1)} %dynamic-slice_bitcast_fusion.4.prior_ref, f32[1,128]{1,0:T(1,128)S(1)} %constant_dynamic-slice_fusion.gain_ref), custom_call_target="tpu_custom_call" | custom-call | tf_op jit(solution)/shard_map/pallas_call | solution.py:89
  48.8 3.5 %all-to-all-start.1 = ((bf16[4,512,128]{2,1,0:T(8,128)(2,1)}), bf16[4,512,128]{2,1,0:T(8,128)(2,1)S(1)}, u32[]{:S(2)}, u32[]{:S(2)}) async-start(bf16[4,512,128]{2,1,0:T(8,128)(2,1)} %shard_map.114), calls=%async_computation.1 | async-start | bytes 1048576 | tf_op jit(solution)/shard_map/all_to_all | solution.py:392
  52.2 1.2 slice.77
  53.5 2.7 collective-permute-start.7
  56.2 2.1 slice.78
  58.3 5.9 %fusion = (bf16[6144,256]{1,0:T(8,128)(2,1)}, bf16[6144,256]{1,0:T(8,128)(2,1)}) fusion(bf16[6144,512]{1,0:T(8,128)(2,1)} %bitcast.57), kind=kLoop, calls=%fused_computation.33 | loop fusion | bytes 12582912 | tf_op jit(solution)/shard_map/slice | solution.py:408
  64.3 10.1 %collective-permute-done.7.refs_4_ = bf16[1024,384]{1,0:T(8,128)(2,1)S(1)} collective-permute-done((bf16[1024,384]{1,0:T(8,128)(2,1)S(1)}, bf16[1024,384]{1,0:T(8,128)(2,1)S(1)}, u32[]{:S(2)}, u32[]{:S(2)}) %collective-permute-start.7) | collective-permute-done | bytes 786464 | tf_op jit(solution)/shard_map/ppermute | solution.py:361
  74.4 2.6 collective-permute-done.8.refs_5_
  77.1 1.7 collective-permute-start.16
  78.8 2.2 collective-permute-start.17
  81.0 1.2 collective-permute-start.18
  82.2 2.7 collective-permute-start.10
  85.0 2.6 collective-permute-start.11
  88.0 2.3 collective-permute-done.18
  90.4 1.4 collective-permute-start.19
  91.7 1.5 collective-permute-start.21
  93.3 1.6 collective-permute-done.9
  95.0 1.1 collective-permute-start.12
  96.1 2.1 collective-permute-start.14
  98.2 18.7 %collective-permute-done.19.refs_10_ = bf16[1024,512]{1,0:T(8,128)(2,1)S(1)} collective-permute-done((bf16[1024,512]{1,0:T(8,128)(2,1)S(1)}, bf16[1024,512]{1,0:T(8,128)(2,1)S(1)}, u32[]{:S(2)}, u32[]{:S(2)}) %collective-permute-start.19) | collective-permute-done | bytes 1048608 | tf_op jit(solution)/shard_map/ppermute | solution.py:314
  116.9 0.8 slice.103
  117.7 1.4 collective-permute-start.20
  119.1 0.9 slice.104
  120.0 1.3 collective-permute-start.22
  121.3 0.9 slice.101
  122.2 2.9 %collective-permute-start.13 = (bf16[512,512]{1,0:T(8,128)(2,1)}, bf16[512,512]{1,0:T(8,128)(2,1)}, u32[]{:S(2)}, u32[]{:S(2)}) collective-permute-start(bf16[512,512]{1,0:T(8,128)(2,1)} %slice.101), channel_id=1, source_target_pairs={{0,16},{4,20},{8,24},{12,28},{16,32},{20,36},{24,40},{28,44},{32,4... | collective-permute-start | bytes 1572872 | tf_op jit(solution)/shard_map/ppermute | solution.py:314
  125.1 0.9 slice.102
  126.2 1.8 collective-permute-start.15
  128.1 1.2 copy-done.4
  129.4 1.2 copy-done.6
  130.6 1.2 copy-done.8
  131.8 18.2 %shard_map.115 = (f32[512,384]{1,0:T(8,128)S(1)}, f32[512,128]{1,0:T(8,128)S(1)}) custom-call(s32[32]{0:T(128)S(1)} %stack.98.refs_0_, f32[16,512]{1,0:T(8,128)S(1)} %pad_maximum_fusion.3.refs_1_, bf16[2048,384]{1,0:T(8,128)(2,1)} %bitcast.63, bf16[2048,384]{1,0:T(8,128)(2,1)} %collective-permute-done.refs_3_, bf16[1024,384]{1,0:T(8,128)(2,1)} %copy-done.12, ...), custom_call_target="tpu_custom_call" | custom-call | tf_op jit(solution)/shard_map/pallas_call | solution.py:210
  150.1 7.2 %shard_map.116 = bf16[512,384]{1,0:T(8,128)(2,1)S(1)} custom-call(s32[32]{0:T(128)S(1)} %stack.98.refs_0_, f32[16,512]{1,0:T(8,128)S(1)} %pad_maximum_fusion.3.refs_1_, bf16[2048,384]{1,0:T(8,128)(2,1)} %bitcast.64, bf16[2048,384]{1,0:T(8,128)(2,1)} %collective-permute-done.refs_3_, bf16[1024,384]{1,0:T(8,128)(2,1)} %copy-done.12, ...), custom_call_target="tpu_custom_call" | custom-call | tf_op jit(solution)/shard_map/pallas_call | solution.py:219
  157.3 1.9 collective-permute-start.28
  159.1 2.7 collective-permute-start.26
  162.0 1.0 collective-permute-start.24
  163.1 2.4 collective-permute-done.28
  165.5 6.4 %collective-permute-done.25 = bf16[512,384]{1,0:T(8,128)(2,1)S(1)} collective-permute-done((bf16[512,384]{1,0:T(8,128)(2,1)S(1)}, bf16[512,384]{1,0:T(8,128)(2,1)S(1)}, u32[]{:S(2)}, u32[]{:S(2)}) %collective-permute-start.25) | collective-permute-done | bytes 393248 | tf_op jit(solution)/shard_map/ppermute | solution.py:314
  172.6 1.2 collective-permute-start.32
  173.8 2.5 collective-permute-start.33
  176.3 2.5 collective-permute-done.30
  178.9 4.6 %collective-permute-done.31 = bf16[512,384]{1,0:T(8,128)(2,1)S(1)} collective-permute-done((bf16[512,384]{1,0:T(8,128)(2,1)S(1)}, bf16[512,384]{1,0:T(8,128)(2,1)S(1)}, u32[]{:S(2)}, u32[]{:S(2)}) %collective-permute-start.31) | collective-permute-done | bytes 393248 | tf_op jit(solution)/shard_map/ppermute | solution.py:314
  183.6 2.7 collective-permute-start.35
  186.3 9.1 %shard_map.117.refs_10_ = f32[1024,1024]{1,0:T(8,128)S(1)} custom-call(s32[32]{0:T(128)S(1)} %stack.98.refs_0_, bf16[6144,512]{1,0:T(8,128)(2,1)} %bitcast.58, bf16[6144,256]{1,0:T(8,128)(2,1)} %collective-permute-done.23.refs_2_, bf16[2048,384]{1,0:T(8,128)(2,1)S(1)} %constant_dynamic-update-slice_fusion.refs_3_.refs_4_, ...), custom_call_target="tpu_custom_call" | custom-call | tf_op jit(solution)/shard_map/pallas_call | solution.py:293
  195.4 23.1 %collective-permute-done.32.refs_6_ = bf16[2048,384]{1,0:T(8,128)(2,1)S(1)} collective-permute-done((bf16[2048,384]{1,0:T(8,128)(2,1)S(1)}, bf16[2048,384]{1,0:T(8,128)(2,1)S(1)}, u32[]{:S(2)}, u32[]{:S(2)}) %collective-permute-start.32) | collective-permute-done | bytes 1572896 | tf_op jit(solution)/shard_map/ppermute | solution.py:314
  218.7 2.7 collective-permute-start.38
  221.7 2.9 %collective-permute-start.40 = (bf16[1024,384]{1,0:T(8,128)(2,1)S(1)}, bf16[1024,384]{1,0:T(8,128)(2,1)S(1)}, u32[]{:S(2)}, u32[]{:S(2)}) collective-permute-start(bf16[1024,384]{1,0:T(8,128)(2,1)S(1)} %slice.90), channel_id=1, source_target_pairs={{0,12},{4,0},{8,4},{12,8},{16,28},{20,16},{24,20},{28,24},{32,44},... | collective-permute-start | bytes 2359304 | tf_op jit(solution)/shard_map/ppermute | solution.py:314
  224.6 7.8 %collective-permute-done.24.refs_3_ = bf16[6144,256]{1,0:T(8,128)(2,1)S(1)} collective-permute-done((bf16[6144,256]{1,0:T(8,128)(2,1)S(1)}, bf16[6144,256]{1,0:T(8,128)(2,1)S(1)}, u32[]{:S(2)}, u32[]{:S(2)}) %collective-permute-start.24) | collective-permute-done | bytes 3145760 | tf_op jit(solution)/shard_map/ppermute | solution.py:361
  232.5 1.6 copy-done.11
  234.1 24.6 %shard_map.118.refs_8_ = f32[1024,1024]{1,0:T(8,128)S(1)} custom-call(s32[32]{0:T(128)S(1)} %stack.98.refs_0_, bf16[6144,512]{1,0:T(8,128)(2,1)} %bitcast.59, bf16[6144,256]{1,0:T(8,128)(2,1)} %collective-permute-done.23.refs_2_, bf16[6144,256]{1,0:T(8,128)(2,1)} %copy-done.11, bf16[2048,384]{1,0:T(8,128)(2,1)S(1)} %constant_dynamic-update-slice_fusion.refs_3_.refs_4_, ...), custom_call_target="tpu_custom_call" | custom-call | tf_op jit(solution)/shard_map/pallas_call | solution.py:293
  258.8 10.6 %shard_map.119 = f32[16,1024]{1,0:T(8,128)S(1)} custom-call(s32[32]{0:T(128)S(1)} %stack.98.refs_0_, bf16[6144,512]{1,0:T(8,128)(2,1)} %bitcast.60, bf16[6144,256]{1,0:T(8,128)(2,1)} %collective-permute-done.23.refs_2_, bf16[6144,256]{1,0:T(8,128)(2,1)} %copy-done.11, bf16[1024,384]{1,0:T(8,128)(2,1)S(1)} %collective-permute-done.37.refs_4_, ...), custom_call_target="tpu_custom_call" | custom-call | tf_op jit(solution)/shard_map/pallas_call | solution.py:293
  269.4 8.2 %collective-permute-start.42 = (bf16[16,256]{1,0:T(8,128)(2,1)S(1)}, bf16[16,256]{1,0:T(8,128)(2,1)S(1)}, u32[]{:S(2)}, u32[]{:S(2)}) collective-permute-start(bf16[16,256]{1,0:T(8,128)(2,1)S(1)} %get-tuple-element.56), channel_id=1, source_target_pairs={{1,64},{2,65},{3,66},{0,67},{65,0},{66,1},{67,2},{64,3},{5,68},{6,... | collective-permute-start | bytes 24584 | tf_op jit(solution)/shard_map/ppermute | solution.py:369
  278.5 3.6 %collective-permute-done.43 = bf16[16,256]{1,0:T(8,128)(2,1)S(1)} collective-permute-done((bf16[16,256]{1,0:T(8,128)(2,1)S(1)}, bf16[16,256]{1,0:T(8,128)(2,1)S(1)}, u32[]{:S(2)}, u32[]{:S(2)}) %collective-permute-start.43) | collective-permute-done | bytes 8224 | tf_op jit(solution)/shard_map/ppermute | solution.py:369
  282.1 0.6 maximum_bitcast_fusion
  282.8 0.7 copy.19
  (114 shorter events, 4.1 us)
Async XLA Ops:
  0.6 19.0 %copy-start = (f32[1,16,128,128]{3,2,1,0:T(8,128)S(1)}, f32[1,16,128,128]{3,2,1,0:T(8,128)}, u32[]{:S(2)}) copy-start(f32[1,16,128,128]{3,2,1,0:T(8,128)} %param.13) | copy-start | bytes 3145732
  0.6 48.1 %collective-permute-start = (bf16[2048,384]{1,0:T(8,128)(2,1)}, bf16[2048,384]{1,0:T(8,128)(2,1)}, u32[]{:S(2)}, u32[]{:S(2)}) collective-permute-start(bf16[2048,384]{1,0:T(8,128)(2,1)} %bitcast.61), channel_id=1, source_target_pairs={{1,0},{2,1},{3,2},{0,3},{5,4},{6,5},{7,6},{4,7},{9,8},{10,9},{11,1... | collective-permute-start | bytes 4718600 | tf_op jit(solution)/shard_map/ppermute | solution.py:361
  4.0 44.7 %collective-permute-start.1 = (bf16[2048,384]{1,0:T(8,128)(2,1)}, bf16[2048,384]{1,0:T(8,128)(2,1)}, u32[]{:S(2)}, u32[]{:S(2)}) collective-permute-start(bf16[2048,384]{1,0:T(8,128)(2,1)} %bitcast.62), channel_id=1, source_target_pairs={{3,0},{0,1},{1,2},{2,3},{7,4},{4,5},{5,6},{6,7},{11,8},{8,9},{9,10... | collective-permute-start | bytes 4718600 | tf_op jit(solution)/shard_map/ppermute | solution.py:361
  4.0 0.7 copy-start.10
  6.3 1.2 copy-start.2
  7.5 7.9 %copy-start.16 = (f32[1,512]{1,0:T(1,128)S(1)}, f32[1,512]{1,0:T(1,128)}, u32[]{:S(2)}) copy-start(f32[1,512]{1,0:T(1,128)} %param.19) | copy-start | bytes 6148
  7.5 10.8 %copy-start.15 = (f32[1,2048]{1,0:T(1,128)S(1)}, f32[1,2048]{1,0:T(1,128)}, u32[]{:S(2)}) copy-start(f32[1,2048]{1,0:T(1,128)} %param.15) | copy-start | bytes 24580
  7.5 37.1 %all-to-all-start = ((bf16[16,400,128]{2,1,0:T(8,128)(2,1)}), bf16[16,400,128]{2,1,0:T(8,128)(2,1)S(1)}, u32[]{:S(2)}, u32[]{:S(2)}) async-start(bf16[16,400,128]{2,1,0:T(8,128)(2,1)} %copy-done.2), calls=%async_computation | async-start | bytes 3276800 | tf_op jit(solution)/shard_map/all_to_all | solution.py:383
  15.4 25.1 %collective-permute-start.5 = (f32[1,256]{1,0:T(1,128)S(1)}, f32[1,256]{1,0:T(1,128)S(1)}, u32[]{:S(2)}, u32[]{:S(2)}) collective-permute-start(f32[1,256]{1,0:T(1,128)S(1)} %get-tuple-element.64), channel_id=1, source_target_pairs={{3,0},{0,1},{1,2},{2,3},{7,4},{4,5},{5,6},{6,7},{11,8},{8,9},{9,10... | collective-permute-start | bytes 3080 | tf_op jit(solution)/shard_map/ppermute | solution.py:361
  15.7 24.8 %collective-permute-start.6 = (f32[1,256]{1,0:T(1,128)S(1)}, f32[1,256]{1,0:T(1,128)S(1)}, u32[]{:S(2)}, u32[]{:S(2)}) collective-permute-start(f32[1,256]{1,0:T(1,128)S(1)} %get-tuple-element.65), channel_id=1, source_target_pairs={{1,0},{2,1},{3,2},{0,3},{5,4},{6,5},{7,6},{4,7},{9,8},{10,9},{11,1... | collective-permute-start | bytes 3080 | tf_op jit(solution)/shard_map/ppermute | solution.py:361
  18.3 22.3 %collective-permute-start.2 = (f32[1,2048]{1,0:T(1,128)S(1)}, f32[1,2048]{1,0:T(1,128)S(1)}, u32[]{:S(2)}, u32[]{:S(2)}) collective-permute-start(f32[1,2048]{1,0:T(1,128)S(1)} %copy-done.15), channel_id=1, source_target_pairs={{1,0},{2,1},{3,2},{0,3},{5,4},{6,5},{7,6},{4,7},{9,8},{10,9},{11,1... | collective-permute-start | bytes 24584 | tf_op jit(solution)/shard_map/ppermute | solution.py:361
  40.5 4.0 %collective-permute-start.3 = (f32[1,2048]{1,0:T(1,128)S(1)}, f32[1,2048]{1,0:T(1,128)S(1)}, u32[]{:S(2)}, u32[]{:S(2)}) collective-permute-start(f32[1,2048]{1,0:T(1,128)S(1)} %copy-done.15), channel_id=1, source_target_pairs={{2,0},{3,1},{0,2},{1,3},{6,4},{7,5},{4,6},{5,7},{10,8},{11,9},{8,1... | collective-permute-start | bytes 24584 | tf_op jit(solution)/shard_map/ppermute | solution.py:361
  40.5 4.0 %collective-permute-start.4 = (f32[1,2048]{1,0:T(1,128)S(1)}, f32[1,2048]{1,0:T(1,128)S(1)}, u32[]{:S(2)}, u32[]{:S(2)}) collective-permute-start(f32[1,2048]{1,0:T(1,128)S(1)} %copy-done.15), channel_id=1, source_target_pairs={{3,0},{0,1},{1,2},{2,3},{7,4},{4,5},{5,6},{6,7},{11,8},{8,9},{9,10... | collective-permute-start | bytes 24584 | tf_op jit(solution)/shard_map/ppermute | solution.py:361
  48.8 15.4 %all-to-all-start.1 = ((bf16[4,512,128]{2,1,0:T(8,128)(2,1)}), bf16[4,512,128]{2,1,0:T(8,128)(2,1)S(1)}, u32[]{:S(2)}, u32[]{:S(2)}) async-start(bf16[4,512,128]{2,1,0:T(8,128)(2,1)} %shard_map.114), calls=%async_computation.1 | async-start | bytes 1048576 | tf_op jit(solution)/shard_map/all_to_all | solution.py:392
  53.5 20.9 %collective-permute-start.7 = (bf16[1024,384]{1,0:T(8,128)(2,1)S(1)}, bf16[1024,384]{1,0:T(8,128)(2,1)S(1)}, u32[]{:S(2)}, u32[]{:S(2)}) collective-permute-start(bf16[1024,384]{1,0:T(8,128)(2,1)S(1)} %slice.77), channel_id=1, source_target_pairs={{1,0},{2,1},{3,2},{0,3},{5,4},{6,5},{7,6},{4,7},{9,8},{10,9},{11,1... | collective-permute-start | bytes 2359304 | tf_op jit(solution)/shard_map/ppermute | solution.py:361
  58.3 18.8 %collective-permute-start.8 = (bf16[1024,384]{1,0:T(8,128)(2,1)}, bf16[1024,384]{1,0:T(8,128)(2,1)S(1)}, u32[]{:S(2)}, u32[]{:S(2)}) collective-permute-start(bf16[1024,384]{1,0:T(8,128)(2,1)} %slice.78), channel_id=1, source_target_pairs={{3,0},{0,1},{1,2},{2,3},{7,4},{4,5},{5,6},{6,7},{11,8},{8,9},{9,10... | collective-permute-start | bytes 2359304 | tf_op jit(solution)/shard_map/ppermute | solution.py:361
  74.4 15.9 %copy-start.12 = (bf16[1024,384]{1,0:T(8,128)(2,1)}, bf16[1024,384]{1,0:T(8,128)(2,1)S(1)}, u32[]{:S(2)}) copy-start(bf16[1024,384]{1,0:T(8,128)(2,1)S(1)} %collective-permute-done.7.refs_4_) | copy-start | bytes 2359300
  77.0 11.0 %copy-start.13 = (bf16[1024,384]{1,0:T(8,128)(2,1)}, bf16[1024,384]{1,0:T(8,128)(2,1)S(1)}, u32[]{:S(2)}) copy-start(bf16[1024,384]{1,0:T(8,128)(2,1)S(1)} %collective-permute-done.8.refs_5_) | copy-start | bytes 2359300
  77.0 80.2 %collective-permute-start.23 = (bf16[6144,256]{1,0:T(8,128)(2,1)}, bf16[6144,256]{1,0:T(8,128)(2,1)}, u32[]{:S(2)}, u32[]{:S(2)}) collective-permute-start(bf16[6144,256]{1,0:T(8,128)(2,1)} %get-tuple-element.32), channel_id=1, source_target_pairs={{3,0},{0,1},{1,2},{2,3},{7,4},{4,5},{5,6},{6,7},{11,8},{8,9},{9,10... | collective-permute-start | bytes 9437192 | tf_op jit(solution)/shard_map/ppermute | solution.py:361
  77.1 7.9 %collective-permute-start.16 = (bf16[256,512]{1,0:T(8,128)(2,1)S(1)}, bf16[256,512]{1,0:T(8,128)(2,1)S(1)}, u32[]{:S(2)}, u32[]{:S(2)}) collective-permute-start(bf16[256,512]{1,0:T(8,128)(2,1)S(1)} %get-tuple-element.46), channel_id=1, source_target_pairs={{0,16},{4,20},{8,24},{12,28},{16,32},{20,36},{24,40},{28,44},{32,4... | collective-permute-start | bytes 786440 | tf_op jit(solution)/shard_map/ppermute | solution.py:314
  78.8 8.8 %collective-permute-start.17 = (bf16[256,512]{1,0:T(8,128)(2,1)S(1)}, bf16[256,512]{1,0:T(8,128)(2,1)S(1)}, u32[]{:S(2)}, u32[]{:S(2)}) collective-permute-start(bf16[256,512]{1,0:T(8,128)(2,1)S(1)} %get-tuple-element.46), channel_id=1, source_target_pairs={{0,48},{4,52},{8,56},{12,60},{16,0},{20,4},{24,8},{28,12},{32,16},... | collective-permute-start | bytes 786440 | tf_op jit(solution)/shard_map/ppermute | solution.py:314
  81.0 9.3 %collective-permute-start.18 = (bf16[256,512]{1,0:T(8,128)(2,1)S(1)}, bf16[256,512]{1,0:T(8,128)(2,1)S(1)}, u32[]{:S(2)}, u32[]{:S(2)}) collective-permute-start(bf16[256,512]{1,0:T(8,128)(2,1)S(1)} %get-tuple-element.46), channel_id=1, source_target_pairs={{0,32},{4,36},{8,40},{12,44},{16,48},{20,52},{24,56},{28,60},{32,0... | collective-permute-start | bytes 786440 | tf_op jit(solution)/shard_map/ppermute | solution.py:314
  82.2 9.5 %collective-permute-start.10 = (bf16[256,512]{1,0:T(8,128)(2,1)S(1)}, bf16[256,512]{1,0:T(8,128)(2,1)S(1)}, u32[]{:S(2)}, u32[]{:S(2)}) collective-permute-start(bf16[256,512]{1,0:T(8,128)(2,1)S(1)} %get-tuple-element.47), channel_id=1, source_target_pairs={{0,12},{4,0},{8,4},{12,8},{16,28},{20,16},{24,20},{28,24},{32,44},... | collective-permute-start | bytes 786440 | tf_op jit(solution)/shard_map/ppermute | solution.py:314
  85.0 8.3 %collective-permute-start.11 = (bf16[256,512]{1,0:T(8,128)(2,1)S(1)}, bf16[256,512]{1,0:T(8,128)(2,1)S(1)}, u32[]{:S(2)}, u32[]{:S(2)}) collective-permute-start(bf16[256,512]{1,0:T(8,128)(2,1)S(1)} %get-tuple-element.47), channel_id=1, source_target_pairs={{0,8},{4,12},{8,0},{12,4},{16,24},{20,28},{24,16},{28,20},{32,40},... | collective-permute-start | bytes 786440 | tf_op jit(solution)/shard_map/ppermute | solution.py:314
  87.6 7.3 %collective-permute-start.9 = (bf16[256,512]{1,0:T(8,128)(2,1)S(1)}, bf16[256,512]{1,0:T(8,128)(2,1)S(1)}, u32[]{:S(2)}, u32[]{:S(2)}) collective-permute-start(bf16[256,512]{1,0:T(8,128)(2,1)S(1)} %get-tuple-element.47), channel_id=1, source_target_pairs={{0,4},{4,8},{8,12},{12,0},{16,20},{20,24},{24,28},{28,16},{32,36},... | collective-permute-start | bytes 786440 | tf_op jit(solution)/shard_map/ppermute | solution.py:314
  90.4 26.5 %collective-permute-start.19 = (bf16[1024,512]{1,0:T(8,128)(2,1)S(1)}, bf16[1024,512]{1,0:T(8,128)(2,1)S(1)}, u32[]{:S(2)}, u32[]{:S(2)}) collective-permute-start(bf16[1024,512]{1,0:T(8,128)(2,1)S(1)} %pad_maximum_fusion.1.refs_8_), channel_id=1, source_target_pairs={{0,4},{4,8},{8,12},{12,0},{16,20},{20,24},{24,28},{28,16},{32,36},... | collective-permute-start | bytes 3145736 | tf_op jit(solution)/shard_map/ppermute | solution.py:314
  91.7 27.4 %collective-permute-start.21 = (bf16[1024,512]{1,0:T(8,128)(2,1)S(1)}, bf16[1024,512]{1,0:T(8,128)(2,1)S(1)}, u32[]{:S(2)}, u32[]{:S(2)}) collective-permute-start(bf16[1024,512]{1,0:T(8,128)(2,1)S(1)} %pad_maximum_fusion.1.refs_8_), channel_id=1, source_target_pairs={{0,12},{4,0},{8,4},{12,8},{16,28},{20,16},{24,20},{28,24},{32,44},... | collective-permute-start | bytes 3145736 | tf_op jit(solution)/shard_map/ppermute | solution.py:314
  95.0 26.3 %collective-permute-start.12 = (bf16[1024,512]{1,0:T(8,128)(2,1)S(1)}, bf16[1024,512]{1,0:T(8,128)(2,1)S(1)}, u32[]{:S(2)}, u32[]{:S(2)}) collective-permute-start(bf16[1024,512]{1,0:T(8,128)(2,1)S(1)} %pad_maximum_fusion.refs_7_), channel_id=1, source_target_pairs={{0,16},{4,20},{8,24},{12,28},{16,32},{20,36},{24,40},{28,44},{32,4... | collective-permute-start | bytes 3145736 | tf_op jit(solution)/shard_map/ppermute | solution.py:314
  96.1 29.0 %collective-permute-start.14 = (bf16[1024,512]{1,0:T(8,128)(2,1)S(1)}, bf16[1024,512]{1,0:T(8,128)(2,1)S(1)}, u32[]{:S(2)}, u32[]{:S(2)}) collective-permute-start(bf16[1024,512]{1,0:T(8,128)(2,1)S(1)} %pad_maximum_fusion.refs_7_), channel_id=1, source_target_pairs={{0,48},{4,52},{8,56},{12,60},{16,0},{20,4},{24,8},{28,12},{32,16},... | collective-permute-start | bytes 3145736 | tf_op jit(solution)/shard_map/ppermute | solution.py:314
  117.7 32.3 %collective-permute-start.20 = (bf16[512,512]{1,0:T(8,128)(2,1)}, bf16[512,512]{1,0:T(8,128)(2,1)}, u32[]{:S(2)}, u32[]{:S(2)}) collective-permute-start(bf16[512,512]{1,0:T(8,128)(2,1)} %slice.103), channel_id=1, source_target_pairs={{0,4},{4,8},{8,12},{12,0},{16,20},{20,24},{24,28},{28,16},{32,36},... | collective-permute-start | bytes 1572872 | tf_op jit(solution)/shard_map/ppermute | solution.py:314
  119.1 6.9 %copy-start.3 = (bf16[1024,512]{1,0:T(8,128)(2,1)}, bf16[1024,512]{1,0:T(8,128)(2,1)S(1)}, u32[]{:S(2)}) copy-start(bf16[1024,512]{1,0:T(8,128)(2,1)S(1)} %collective-permute-done.21.refs_12_) | copy-start | bytes 3145732
  120.0 30.0 %collective-permute-start.22 = (bf16[512,512]{1,0:T(8,128)(2,1)}, bf16[512,512]{1,0:T(8,128)(2,1)}, u32[]{:S(2)}, u32[]{:S(2)}) collective-permute-start(bf16[512,512]{1,0:T(8,128)(2,1)} %slice.104), channel_id=1, source_target_pairs={{0,12},{4,0},{8,4},{12,8},{16,28},{20,16},{24,20},{28,24},{32,44},... | collective-permute-start | bytes 1572872 | tf_op jit(solution)/shard_map/ppermute | solution.py:314
  121.3 3.8 %copy-start.5 = (bf16[1024,512]{1,0:T(8,128)(2,1)}, bf16[1024,512]{1,0:T(8,128)(2,1)S(1)}, u32[]{:S(2)}) copy-start(bf16[1024,512]{1,0:T(8,128)(2,1)S(1)} %collective-permute-done.12.refs_9_) | copy-start | bytes 3145732
  122.2 27.9 %collective-permute-start.13 = (bf16[512,512]{1,0:T(8,128)(2,1)}, bf16[512,512]{1,0:T(8,128)(2,1)}, u32[]{:S(2)}, u32[]{:S(2)}) collective-permute-start(bf16[512,512]{1,0:T(8,128)(2,1)} %slice.101), channel_id=1, source_target_pairs={{0,16},{4,20},{8,24},{12,28},{16,32},{20,36},{24,40},{28,44},{32,4... | collective-permute-start | bytes 1572872 | tf_op jit(solution)/shard_map/ppermute | solution.py:314
  125.1 1.1 copy-start.7
  126.2 23.8 %collective-permute-start.15 = (bf16[512,512]{1,0:T(8,128)(2,1)}, bf16[512,512]{1,0:T(8,128)(2,1)}, u32[]{:S(2)}, u32[]{:S(2)}) collective-permute-start(bf16[512,512]{1,0:T(8,128)(2,1)} %slice.102), channel_id=1, source_target_pairs={{0,48},{4,52},{8,56},{12,60},{16,0},{20,4},{24,8},{28,12},{32,16},... | collective-permute-start | bytes 1572872 | tf_op jit(solution)/shard_map/ppermute | solution.py:314
  128.1 1.2 copy-start.4
  129.4 1.2 copy-start.6
  130.6 1.2 copy-start.8
  131.8 18.2 %copy-start.9 = (bf16[1,512,384]{2,1,0:T(8,128)(2,1)S(1)}, bf16[1,512,384]{2,1,0:T(8,128)(2,1)}, u32[]{:S(2)}) copy-start(bf16[1,512,384]{2,1,0:T(8,128)(2,1)} %param.16) | copy-start | bytes 1179652
  150.1 12.0 %copy-start.14 = (bf16[6144,256]{1,0:T(8,128)(2,1)S(1)}, bf16[6144,256]{1,0:T(8,128)(2,1)}, u32[]{:S(2)}) copy-start(bf16[6144,256]{1,0:T(8,128)(2,1)} %get-tuple-element.34) | copy-start | bytes 9437188
  157.3 8.2 %collective-permute-start.28 = (bf16[512,384]{1,0:T(8,128)(2,1)S(1)}, bf16[512,384]{1,0:T(8,128)(2,1)S(1)}, u32[]{:S(2)}, u32[]{:S(2)}) collective-permute-start(bf16[512,384]{1,0:T(8,128)(2,1)S(1)} %shard_map.116), channel_id=1, source_target_pairs={{2,0},{3,1},{0,2},{1,3},{6,4},{7,5},{4,6},{5,7},{10,8},{11,9},{8,1... | collective-permute-start | bytes 1179656 | tf_op jit(solution)/shard_map/ppermute | solution.py:361
  159.1 12.8 %collective-permute-start.25 = (bf16[512,384]{1,0:T(8,128)(2,1)S(1)}, bf16[512,384]{1,0:T(8,128)(2,1)S(1)}, u32[]{:S(2)}, u32[]{:S(2)}) collective-permute-start(bf16[512,384]{1,0:T(8,128)(2,1)S(1)} %shard_map.116), channel_id=1, source_target_pairs={{0,4},{4,8},{8,12},{12,0},{16,20},{20,24},{24,28},{28,16},{32,36},... | collective-permute-start | bytes 1179656 | tf_op jit(solution)/shard_map/ppermute | solution.py:314
  159.1 12.9 %collective-permute-start.26 = (bf16[512,384]{1,0:T(8,128)(2,1)S(1)}, bf16[512,384]{1,0:T(8,128)(2,1)S(1)}, u32[]{:S(2)}, u32[]{:S(2)}) collective-permute-start(bf16[512,384]{1,0:T(8,128)(2,1)S(1)} %shard_map.116), channel_id=1, source_target_pairs={{0,12},{4,0},{8,4},{12,8},{16,28},{20,16},{24,20},{28,24},{32,44},... | collective-permute-start | bytes 1179656 | tf_op jit(solution)/shard_map/ppermute | solution.py:314
  161.8 10.7 %collective-permute-start.27 = (bf16[512,384]{1,0:T(8,128)(2,1)S(1)}, bf16[512,384]{1,0:T(8,128)(2,1)S(1)}, u32[]{:S(2)}, u32[]{:S(2)}) collective-permute-start(bf16[512,384]{1,0:T(8,128)(2,1)S(1)} %shard_map.116), channel_id=1, source_target_pairs={{0,8},{4,12},{8,0},{12,4},{16,24},{20,28},{24,16},{28,20},{32,40},... | collective-permute-start | bytes 1179656 | tf_op jit(solution)/shard_map/ppermute | solution.py:314
  162.0 70.5 %collective-permute-start.24 = (bf16[6144,256]{1,0:T(8,128)(2,1)S(1)}, bf16[6144,256]{1,0:T(8,128)(2,1)S(1)}, u32[]{:S(2)}, u32[]{:S(2)}) collective-permute-start(bf16[6144,256]{1,0:T(8,128)(2,1)S(1)} %copy-done.14), channel_id=1, source_target_pairs={{1,0},{2,1},{3,2},{0,3},{5,4},{6,5},{7,6},{4,7},{9,8},{10,9},{11,1... | collective-permute-start | bytes 9437192 | tf_op jit(solution)/shard_map/ppermute | solution.py:361
  165.5 8.3 %collective-permute-start.29 = (bf16[512,384]{1,0:T(8,128)(2,1)S(1)}, bf16[512,384]{1,0:T(8,128)(2,1)S(1)}, u32[]{:S(2)}, u32[]{:S(2)}) collective-permute-start(bf16[512,384]{1,0:T(8,128)(2,1)S(1)} %collective-permute-done.28), channel_id=1, source_target_pairs={{0,16},{4,20},{8,24},{12,28},{16,32},{20,36},{24,40},{28,44},{32,4... | collective-permute-start | bytes 1179656 | tf_op jit(solution)/shard_map/ppermute | solution.py:314
  171.9 6.9 %collective-permute-start.30 = (bf16[512,384]{1,0:T(8,128)(2,1)S(1)}, bf16[512,384]{1,0:T(8,128)(2,1)S(1)}, u32[]{:S(2)}, u32[]{:S(2)}) collective-permute-start(bf16[512,384]{1,0:T(8,128)(2,1)S(1)} %collective-permute-done.28), channel_id=1, source_target_pairs={{0,48},{4,52},{8,56},{12,60},{16,0},{20,4},{24,8},{28,12},{32,16},... | collective-permute-start | bytes 1179656 | tf_op jit(solution)/shard_map/ppermute | solution.py:314
  172.0 11.5 %collective-permute-start.31 = (bf16[512,384]{1,0:T(8,128)(2,1)S(1)}, bf16[512,384]{1,0:T(8,128)(2,1)S(1)}, u32[]{:S(2)}, u32[]{:S(2)}) collective-permute-start(bf16[512,384]{1,0:T(8,128)(2,1)S(1)} %collective-permute-done.28), channel_id=1, source_target_pairs={{0,32},{4,36},{8,40},{12,44},{16,48},{20,52},{24,56},{28,60},{32,0... | collective-permute-start | bytes 1179656 | tf_op jit(solution)/shard_map/ppermute | solution.py:314
  172.6 45.8 %collective-permute-start.32 = (bf16[2048,384]{1,0:T(8,128)(2,1)S(1)}, bf16[2048,384]{1,0:T(8,128)(2,1)S(1)}, u32[]{:S(2)}, u32[]{:S(2)}) collective-permute-start(bf16[2048,384]{1,0:T(8,128)(2,1)S(1)} %constant_dynamic-update-slice_fusion.refs_3_.refs_4_), channel_id=1, source_target_pairs={{0,16},{4,20},{8,24},{12,28},{16,32},{20,36},{24,40},{28,44},{32,4... | collective-permute-start | bytes 4718600 | tf_op jit(solution)/shard_map/ppermute | solution.py:314
  173.8 44.6 %collective-permute-start.33 = (bf16[2048,384]{1,0:T(8,128)(2,1)S(1)}, bf16[2048,384]{1,0:T(8,128)(2,1)S(1)}, u32[]{:S(2)}, u32[]{:S(2)}) collective-permute-start(bf16[2048,384]{1,0:T(8,128)(2,1)S(1)} %constant_dynamic-update-slice_fusion.refs_3_.refs_4_), channel_id=1, source_target_pairs={{0,48},{4,52},{8,56},{12,60},{16,0},{20,4},{24,8},{28,12},{32,16},... | collective-permute-start | bytes 4718600 | tf_op jit(solution)/shard_map/ppermute | solution.py:314
  183.5 34.9 %collective-permute-start.34 = (bf16[2048,384]{1,0:T(8,128)(2,1)S(1)}, bf16[2048,384]{1,0:T(8,128)(2,1)S(1)}, u32[]{:S(2)}, u32[]{:S(2)}) collective-permute-start(bf16[2048,384]{1,0:T(8,128)(2,1)S(1)} %constant_dynamic-update-slice_fusion.4.refs_4_.refs_5_), channel_id=1, source_target_pairs={{0,4},{4,8},{8,12},{12,0},{16,20},{20,24},{24,28},{28,16},{32,36},... | collective-permute-start | bytes 4718600 | tf_op jit(solution)/shard_map/ppermute | solution.py:314
  183.6 34.8 %collective-permute-start.35 = (bf16[2048,384]{1,0:T(8,128)(2,1)S(1)}, bf16[2048,384]{1,0:T(8,128)(2,1)S(1)}, u32[]{:S(2)}, u32[]{:S(2)}) collective-permute-start(bf16[2048,384]{1,0:T(8,128)(2,1)S(1)} %constant_dynamic-update-slice_fusion.4.refs_4_.refs_5_), channel_id=1, source_target_pairs={{0,12},{4,0},{8,4},{12,8},{16,28},{20,16},{24,20},{28,24},{32,44},... | collective-permute-start | bytes 4718600 | tf_op jit(solution)/shard_map/ppermute | solution.py:314
  218.5 40.2 %collective-permute-start.37 = (bf16[1024,384]{1,0:T(8,128)(2,1)S(1)}, bf16[1024,384]{1,0:T(8,128)(2,1)S(1)}, u32[]{:S(2)}, u32[]{:S(2)}) collective-permute-start(bf16[1024,384]{1,0:T(8,128)(2,1)S(1)} %slice.87), channel_id=1, source_target_pairs={{0,16},{4,20},{8,24},{12,28},{16,32},{20,36},{24,40},{28,44},{32,4... | collective-permute-start | bytes 2359304 | tf_op jit(solution)/shard_map/ppermute | solution.py:314
  218.7 40.0 %collective-permute-start.38 = (bf16[1024,384]{1,0:T(8,128)(2,1)S(1)}, bf16[1024,384]{1,0:T(8,128)(2,1)S(1)}, u32[]{:S(2)}, u32[]{:S(2)}) collective-permute-start(bf16[1024,384]{1,0:T(8,128)(2,1)S(1)} %slice.88), channel_id=1, source_target_pairs={{0,48},{4,52},{8,56},{12,60},{16,0},{20,4},{24,8},{28,12},{32,16},... | collective-permute-start | bytes 2359304 | tf_op jit(solution)/shard_map/ppermute | solution.py:314
  221.5 37.2 %collective-permute-start.39 = (bf16[1024,384]{1,0:T(8,128)(2,1)S(1)}, bf16[1024,384]{1,0:T(8,128)(2,1)S(1)}, u32[]{:S(2)}, u32[]{:S(2)}) collective-permute-start(bf16[1024,384]{1,0:T(8,128)(2,1)S(1)} %slice.89), channel_id=1, source_target_pairs={{0,4},{4,8},{8,12},{12,0},{16,20},{20,24},{24,28},{28,16},{32,36},... | collective-permute-start | bytes 2359304 | tf_op jit(solution)/shard_map/ppermute | solution.py:314
  221.7 37.1 %collective-permute-start.40 = (bf16[1024,384]{1,0:T(8,128)(2,1)S(1)}, bf16[1024,384]{1,0:T(8,128)(2,1)S(1)}, u32[]{:S(2)}, u32[]{:S(2)}) collective-permute-start(bf16[1024,384]{1,0:T(8,128)(2,1)S(1)} %slice.90), channel_id=1, source_target_pairs={{0,12},{4,0},{8,4},{12,8},{16,28},{20,16},{24,20},{28,24},{32,44},... | collective-permute-start | bytes 2359304 | tf_op jit(solution)/shard_map/ppermute | solution.py:314
  232.5 1.6 copy-start.11
  258.8 24.7 %copy-start.1 = (f32[1,16,128,128]{3,2,1,0:T(8,128)S(1)}, f32[1,16,128,128]{3,2,1,0:T(8,128)}, u32[]{:S(2)}) copy-start(f32[1,16,128,128]{3,2,1,0:T(8,128)} %param.13) | copy-start | bytes 3145732
  269.4 9.0 %collective-permute-start.42 = (bf16[16,256]{1,0:T(8,128)(2,1)S(1)}, bf16[16,256]{1,0:T(8,128)(2,1)S(1)}, u32[]{:S(2)}, u32[]{:S(2)}) collective-permute-start(bf16[16,256]{1,0:T(8,128)(2,1)S(1)} %get-tuple-element.56), channel_id=1, source_target_pairs={{1,64},{2,65},{3,66},{0,67},{65,0},{66,1},{67,2},{64,3},{5,68},{6,... | collective-permute-start | bytes 24584 | tf_op jit(solution)/shard_map/ppermute | solution.py:369
  277.7 5.1 %collective-permute-start.36 = (bf16[1,512,384]{2,1,0:T(8,128)(2,1)S(1)}, bf16[1,512,384]{2,1,0:T(8,128)(2,1)S(1)}, u32[]{:S(2)}, u32[]{:S(2)}) collective-permute-start(bf16[1,512,384]{2,1,0:T(8,128)(2,1)S(1)} %bitcast.55), channel_id=1, source_target_pairs={{0,64},{1,65},{2,66},{3,67},{64,0},{65,1},{66,2},{67,3},{4,68},{5,... | collective-permute-start | bytes 1179656 | tf_op jit(solution)/shard_map/ppermute | solution.py:369
  277.7 4.4 %collective-permute-start.43 = (bf16[16,256]{1,0:T(8,128)(2,1)S(1)}, bf16[16,256]{1,0:T(8,128)(2,1)S(1)}, u32[]{:S(2)}, u32[]{:S(2)}) collective-permute-start(bf16[16,256]{1,0:T(8,128)(2,1)S(1)} %get-tuple-element.57), channel_id=1, source_target_pairs={{3,64},{0,65},{1,66},{2,67},{67,0},{64,1},{65,2},{66,3},{7,68},{4,... | collective-permute-start | bytes 24584 | tf_op jit(solution)/shard_map/ppermute | solution.py:369
  277.7 4.4 %collective-permute-start.41 = (bf16[16,512]{1,0:T(8,128)(2,1)S(1)}, bf16[16,512]{1,0:T(8,128)(2,1)S(1)}, u32[]{:S(2)}, u32[]{:S(2)}) collective-permute-start(bf16[16,512]{1,0:T(8,128)(2,1)S(1)} %slice.106), channel_id=1, source_target_pairs={{0,64},{1,65},{2,66},{3,67},{64,0},{65,1},{66,2},{67,3},{4,68},{5,... | collective-permute-start | bytes 49160 | tf_op jit(solution)/shard_map/ppermute | solution.py:369

commit v7 on v6

--- a/solution.py
+++ b/solution.py
@@ -93,6 +93,9 @@
     )(packed, prior, gain)
 
 
+SLOTS = 4
+
+
 def listed(gathered, steps):
     return [array for step in steps for parts in gathered for array in parts[step]]
 
@@ -116,14 +119,15 @@
 
         fetch(place(n)[1], slot)
 
-    start(0, 0)
+    for n in range(SLOTS - 1):
+        start(n, n)
 
     def one(n, carry):
-        slot = lax.rem(n, 2)
-
-        @pl.when(n + 1 < total)
+        slot = lax.rem(n, SLOTS)
+
+        @pl.when(n + SLOTS - 1 < total)
         def _():
-            start(n + 1, 1 - slot)
+            start(n + SLOTS - 1, lax.rem(n + SLOTS - 1, SLOTS))
 
         first = pl.ds(0, rows)
         pltpu.make_async_copy(arrays[0].at[first, :], buffer.at[slot], sems.at[slot, 0]).wait()
@@ -200,9 +204,9 @@
         jax.ShapeDtypeStruct((rows, HD), jnp.float32),
     ]
     slots = [
-        pltpu.VMEM((2, rows // 2, depth), jnp.bfloat16),
-        pltpu.VMEM((2, depth, columns), jnp.bfloat16),
-        pltpu.SemaphoreType.DMA((2, 5)),
+        pltpu.VMEM((SLOTS, rows // 2, depth), jnp.bfloat16),
+        pltpu.VMEM((SLOTS, depth, columns), jnp.bfloat16),
+        pltpu.SemaphoreType.DMA((SLOTS, 5)),
     ]
     params = pltpu.CompilerParams(vmem_limit_bytes=12 * MIB)
     weights = [in_hbm(w) for w in weights]
@@ -286,9 +290,9 @@
     final = bias is not None
     extra = [x for x in (acc, bias) if x is not None]
     slots = [
-        pltpu.VMEM((2, rows, depth), jnp.bfloat16),
-        pltpu.VMEM((2, depth, width), jnp.bfloat16),
-        pltpu.SemaphoreType.DMA((2, 4)),
+        pltpu.VMEM((SLOTS, rows, depth), jnp.bfloat16),
+        pltpu.VMEM((SLOTS, depth, width), jnp.bfloat16),
+        pltpu.SemaphoreType.DMA((SLOTS, 4)),
     ]
     return pl.pallas_call(
         functools.partial(encode_kernel, len(encoders), len(arrays), step, late, final),
@@ -360,13 +364,16 @@
     def from_head(x, by):
         return lax.ppermute(x, "head", [((i + by) % groups, i) for i in range(groups)])
 
-    def from_section(x, by):
-        pairs = []
+    def paired(shift):
+        pairs = [((i + shift) % groups, (i + 1 + shift) % groups) for i in range(0, groups, 2)]
+        return [pair for a, b in pairs for pair in ((a, b), (b, a))]
+
+    def from_section(x, pairs=None):
+        both = []
         for s in range(sections):
-            for i in range(groups):
-                target = (s + 1) % sections
-                pairs.append((s * groups + (i + by) % groups, target * groups + i))
-        return lax.ppermute(x, ("section", "head"), pairs)
+            for a, b in pairs or [(i, i) for i in range(groups)]:
+                both.append((s * groups + a, (s + 1) % sections * groups + b))
+        return lax.ppermute(x, ("section", "head"), both)
 
     packed = pack(query_vectors[0], key_vectors[0], value_vectors[0], doc_ids)
     weight = out_weight[0]
@@ -375,19 +382,29 @@
     gains = [norm_gain] + [from_head(norm_gain, k) for k in range(1, groups)]
     inverse = jnp.concatenate([(1.0 / (g * g)).reshape(-1, HD) for g in gains], axis=1)
     half = enc_weight.shape[2] // 2
+    odd = group % 2
+
+    def halves(x):
+        return [lax.dynamic_slice_in_dim(x, n * half, half, 1) for n in (odd, 1 - odd)]
+
+    first_bias, second_bias = halves(enc_bias)
     bias = jnp.concatenate(
-        [enc_bias, from_head(enc_bias[:, :half], -1), from_head(enc_bias[:, half:], 1)], axis=1
+        [
+            enc_bias,
+            lax.ppermute(first_bias, "head", paired(0)),
+            lax.ppermute(second_bias, "head", paired(1)),
+        ],
+        axis=1,
     )
     source = sources(place)
 
     packed = lax.all_to_all(packed, "seq", 0, 0, tiled=True)
+    packed, after, before, inverse, bias = lax.optimization_barrier(
+        (packed, after, before, inverse, bias)
+    )
     prior = lax.dynamic_index_in_dim(prior_state[0], place, 0, False)
     gain = lax.dynamic_slice_in_dim(norm_gain, place * HD, HD, 1)
     attended = attend(packed, prior, gain, groups)
-    attended, after, before, inverse, bias = lax.optimization_barrier(
-        (attended, after, before, inverse, bias)
-    )
-    across = [from_head(after[:middle], 1), from_head(before[middle:], -1)]
 
     own = lax.all_to_all(attended, "head", 0, 0, tiled=True)
     own = jnp.concatenate(
@@ -397,32 +414,41 @@
         ],
         axis=1,
     )
-    own, across, first_half = lax.optimization_barrier((own, across, enc_weight[0][:, :half]))
-    from_before = from_head(first_half, -1)
+    own, *parts = lax.optimization_barrier((own, after[:middle], before[middle:]))
+    across = [from_head(parts[0], 1), from_head(parts[1], -1)]
     rows = own.shape[0] // 2
     joined = [jnp.concatenate(line, axis=0) for line in lines([own[:rows], own[rows:]])]
+    first, second = halves(enc_weight[0])
+    _, across, first, second = lax.optimization_barrier((joined, across, first, second))
+    first = lax.ppermute(first, "head", paired(0))
+    second = lax.all_to_all(
+        jnp.broadcast_to(second[None], (2, *second.shape)),
+        "head",
+        0,
+        0,
+        axis_index_groups=[[(i + 1) % groups, (i + 2) % groups] for i in range(0, groups, 2)],
+        tiled=True,
+    )
+    second = lax.dynamic_index_in_dim(second, odd, 0, False)
     weights = [weight, after, *across, before]
     layer_out = project(source, inverse, weights, planes(joined, near(joined)), residual[0])
-
-    layer_out, from_before, second_half = lax.optimization_barrier(
-        (layer_out, from_before, enc_weight[0][:, half:])
-    )
-    from_after = from_head(second_half, 1)
     opposite = from_head(layer_out, 2)
     joined = [jnp.concatenate(line, axis=0) for line in lines([layer_out, opposite])]
+    joined, first = lax.optimization_barrier((joined, first))
     beside = near(joined)
-    encoders = [enc_weight[0], from_before, from_after]
-    acc = encode(source, encoders[:2], joined, 0)
-    beside, acc = lax.optimization_barrier((beside, acc))
+    acc = encode(source, [enc_weight[0], first], joined, 0)
+    beside, acc, second = lax.optimization_barrier((beside, acc, second))
+    encoders = [enc_weight[0], first, second]
     gathered = planes(joined, beside)
     acc = encode(source, encoders, listed(gathered, [0, 1, 2]), 0, late=2, acc=acc)
     acc, layer_out = lax.optimization_barrier((acc, layer_out))
     pooled = encode(source, encoders, listed(gathered, [3]), 3, acc=acc, bias=bias)
     pooled = pooled.astype(jnp.bfloat16)
     pools = pooled.shape[0] // 2
-    mine = from_section(pooled[:, : 2 * half], 0)
-    after = from_section(pooled[:, 2 * half : 3 * half], 1)
-    before = from_section(pooled[:, 3 * half :], -1)
+    mine = from_section(pooled[:, : 2 * half])
+    first = from_section(pooled[:, 2 * half : 3 * half], paired(0))
+    second = from_section(pooled[:, 3 * half :], paired(1))
+    after, before = jnp.where(odd, second, first), jnp.where(odd, first, second)
     turned = [
         mine[:pools],
         jnp.concatenate([after[:pools], before[pools:]], axis=1),
@@ -437,7 +463,7 @@
         ],
         axis=0,
     )
-    return (from_section(layer_out[None], 0), monitor[None])
+    return (from_section(layer_out[None]), monitor[None])
 
 
 def solution(mesh):

time: 285 us -> 267 us (0.937)
  waiting for transfers between devices: 111 us -> 84.1 us
  Pallas kernels: 75.5 us -> 57 us
  starting transfers between devices: 73.3 us -> 88.5 us
  local copies, waits for them, and re-layouts: 21.9 us -> 33.5 us
    ppermute x28, waiting for transfers between devices: 59.2 us -> 26.6 us  [moved(): return lax.ppermute(x, 'seq', pairs)]
    ppermute x4 -> x7, waiting for transfers between devices: 3.89 us -> 21.1 us  [the longest x1 18.3 us: local(): lax.ppermute(first_bias, 'head', paired(0))]
    ppermute x12 -> x8, waiting for transfers between devices: 47.7 us -> 33.8 us  [from_head(): lax.ppermute(x, 'head', [((i + by) % groups, i) for i in range(groups)])]
    ppermute x4 -> x7, starting transfers between devices: 8.74 us -> 18.1 us  [the longest x4 15.5 us: from_section(): return lax.ppermute(x, ('section', 'head'), both)]
    pallas_call x3, Pallas kernels: 44.3 us -> 35.7 us  [encode(): pl.pallas_call(functools.partial(encode_kernel, len(encoders), len(arrays...]
    pallas_call x1, Pallas kernels: 18.2 us -> 10.7 us  [project(): pl.pallas_call(functools.partial(project_kernel, len(arrays), 0, False),...]
    slice x8, local copies, waits for them, and re-layouts: 3.87 us -> 11.3 us  [planes(): across = (moved(up[:middle], axis, 1), moved(down[middle:], axis, -1))]
    all_to_all x0 -> x1, starting transfers between devices: none -> 6.51 us  [local(): lax.all_to_all(jnp.broadcast_to(second[None], (2, *second.shape)), 'head'...]
  transfers between devices with their start and end apart: 46 -> 46, of which waited for: 15 -> 15; matrix products, arithmetic and copies ran while one was open for 5% -> 10% of each run, Pallas kernels for 23% -> 20%
where the time goes in v7:
time: 267 us; the launch traced here: 266 us
  starting transfers between devices  88.5 us (33%)
  waiting for transfers between devices  84.1 us (31%)
  Pallas kernels  57 us (21%)
  local copies, waits for them, and re-layouts  33.5 us (13%)
    ppermute x28, starting transfers between devices, moved(): return lax.ppermute(x, 'seq', pairs)  41.4 us
    pallas_call x3, Pallas kernels, encode(): pl.pallas_call(functools.partial(encode_kernel, len(encoders), len(arrays...  35.7 us
    ppermute x8, waiting for transfers between devices, from_head(): lax.ppermute(x, 'head', [((i + by) % groups, i) for i in range(groups)])  33.8 us
    ppermute x28, waiting for transfers between devices, moved(): return lax.ppermute(x, 'seq', pairs)  26.6 us
    ppermute x1, waiting for transfers between devices, local(): lax.ppermute(first_bias, 'head', paired(0))  18.3 us
    ppermute x4, starting transfers between devices, from_section(): return lax.ppermute(x, ('section', 'head'), both)  15.5 us
    slice x8, local copies, waits for them, and re-layouts, planes(): across = (moved(up[:middle], axis, 1), moved(down[middle:], axis, -1))  11.3 us
    ppermute x8, starting transfers between devices, from_head(): lax.ppermute(x, 'head', [((i + by) % groups, i) for i in range(groups)])  11.1 us
  transfers between devices with their start and end apart: 46, of which 15 were waited for; matrix products, arithmetic and copies ran while one was open for 10% of the time, Pallas kernels for 20%

profile of v7, /device:TPU:1, one launch (start us, length us, event | category | flops | bytes accessed | tf_op | source)
XLA Modules:
  0.0 265.6 jit_solution(6619445746047136334)
XLA Ops:
  0.6 3.4 %collective-permute-start = (bf16[2048,384]{1,0:T(8,128)(2,1)}, bf16[2048,384]{1,0:T(8,128)(2,1)}, u32[]{:S(2)}, u32[]{:S(2)}) collective-permute-start(bf16[2048,384]{1,0:T(8,128)(2,1)} %bitcast.66), channel_id=1, source_target_pairs={{1,0},{2,1},{3,2},{0,3},{5,4},{6,5},{7,6},{4,7},{9,8},{10,9},{11,1... | collective-permute-start | bytes 4718600 | tf_op jit(solution)/shard_map/ppermute | solution.py:365
  4.9 2.5 collective-permute-start.6
  8.1 1.6 shard_map.113
  9.7 1.2 copy-done.4
  10.9 7.9 %all-to-all-start = ((bf16[16,400,128]{2,1,0:T(8,128)(2,1)}), bf16[16,400,128]{2,1,0:T(8,128)(2,1)S(1)}, u32[]{:S(2)}, u32[]{:S(2)}) async-start(bf16[16,400,128]{2,1,0:T(8,128)(2,1)} %copy-done.4), calls=%async_computation | async-start | bytes 3276800 | tf_op jit(solution)/shard_map/all_to_all | solution.py:401
  19.2 18.3 %collective-permute-done.5 = f32[1,256]{1,0:T(1,128)S(1)} collective-permute-done((f32[1,256]{1,0:T(1,128)S(1)}, f32[1,256]{1,0:T(1,128)S(1)}, u32[]{:S(2)}, u32[]{:S(2)}) %collective-permute-start.5) | collective-permute-done | bytes 1056 | tf_op jit(solution)/shard_map/ppermute | solution.py:394
  37.4 2.4 collective-permute-start.3
  40.6 1.0 collective-permute-done.3
  41.6 2.7 collective-permute-done.4
  44.3 4.1 %shard_map.114 = bf16[4,512,128]{2,1,0:T(8,128)(2,1)} custom-call(bf16[16,400,128]{2,1,0:T(8,128)(2,1)S(1)} %all-to-all-done.packed_ref, f32[128,128]{1,0:T(8,128)S(1)} %dynamic-slice_bitcast_fusion.7.prior_ref, f32[1,128]{1,0:T(1,128)S(1)} %constant_dynamic-slice_fusion.gain_ref), custom_call_target="tpu_custom_call" | custom-call | tf_op jit(solution)/shard_map/pallas_call | solution.py:89
  48.4 3.5 %all-to-all-start.1 = ((bf16[4,512,128]{2,1,0:T(8,128)(2,1)}), bf16[4,512,128]{2,1,0:T(8,128)(2,1)S(1)}, u32[]{:S(2)}, u32[]{:S(2)}) async-start(bf16[4,512,128]{2,1,0:T(8,128)(2,1)} %shard_map.114), calls=%async_computation.1 | async-start | bytes 1048576 | tf_op jit(solution)/shard_map/all_to_all | solution.py:409
  51.9 2.1 slice.63
  54.0 2.1 slice.64
  56.1 2.6 all-to-all-done.1
  58.9 1.7 collective-permute-start.10
  60.6 2.2 collective-permute-start.11
  62.8 1.2 collective-permute-start.12
  64.1 1.3 collective-permute-start.7
  65.3 1.4 collective-permute-start.8
  66.8 2.6 collective-permute-start.9
  71.6 4.9 %dynamic-slice_bitcast_fusion.1 = (bf16[6144,256]{1,0:T(8,128)(2,1)S(1)}, bf16[6144,256]{1,0:T(8,128)(2,1)}) fusion(bf16[1,6144,512]{2,1,0:T(8,128)(2,1)} %param.18, s32[]{:T(128)S(6)} %select_n.260, s32[]{:T(128)S(6)} %select_n.259), kind=kLoop, calls=%fused_computation.1 | loop fusion | bytes 12582920 | tf_op jit(solution)/shard_map/dynamic_slice | solution.py:388
  76.7 4.2 %collective-permute-done.13.refs_4_ = bf16[1024,384]{1,0:T(8,128)(2,1)S(1)} collective-permute-done((bf16[1024,384]{1,0:T(8,128)(2,1)}, bf16[1024,384]{1,0:T(8,128)(2,1)S(1)}, u32[]{:S(2)}, u32[]{:S(2)}) %collective-permute-start.13) | collective-permute-done | bytes 786464 | tf_op jit(solution)/shard_map/ppermute | solution.py:365
  80.9 3.8 %collective-permute-done.14.refs_5_ = bf16[1024,384]{1,0:T(8,128)(2,1)S(1)} collective-permute-done((bf16[1024,384]{1,0:T(8,128)(2,1)}, bf16[1024,384]{1,0:T(8,128)(2,1)S(1)}, u32[]{:S(2)}, u32[]{:S(2)}) %collective-permute-start.14) | collective-permute-done | bytes 786464 | tf_op jit(solution)/shard_map/ppermute | solution.py:365
  84.7 2.3 collective-permute-start.19
  87.0 2.3 collective-permute-start.21
  89.5 2.4 collective-permute-start.17
  91.9 3.1 %broadcast_in_dim.12 = bf16[2,6144,256]{2,1,0:T(8,128)(2,1)} broadcast(bf16[6144,256]{1,0:T(8,128)(2,1)S(1)} %get-tuple-element.42), dimensions={1,2} | broadcast | bytes 9437184 | tf_op jit(solution)/shard_map/broadcast_in_dim | solution.py:425
  95.0 6.5 %all-to-all-start.2 = ((bf16[2,6144,256]{2,1,0:T(8,128)(2,1)}), bf16[2,6144,256]{2,1,0:T(8,128)(2,1)}, u32[]{:S(2)}, u32[]{:S(2)}) async-start(bf16[2,6144,256]{2,1,0:T(8,128)(2,1)} %broadcast_in_dim.12), calls=%async_computation.2 | async-start | bytes 12582912 | tf_op jit(solution)/shard_map/all_to_all | solution.py:424
  101.5 1.5 collective-permute-done.19.refs_10_
  104.6 1.9 slice.87
  106.4 2.5 collective-permute-start.22
  108.9 1.9 slice.84
  111.7 1.9 slice.85
  113.5 1.8 collective-permute-start.18
  115.4 10.7 %shard_map.115 = (f32[512,384]{1,0:T(8,128)S(1)}, f32[512,128]{1,0:T(8,128)S(1)}) custom-call(s32[32]{0:T(128)S(1)} %stack.98.refs_0_, f32[16,512]{1,0:T(8,128)S(1)} %pad_maximum_fusion.5.refs_1_, bf16[2048,384]{1,0:T(8,128)(2,1)} %bitcast.68, bf16[2048,384]{1,0:T(8,128)(2,1)} %collective-permute-done.refs_3_, bf16[1024,384]{1,0:T(8,128)(2,1)} %copy-done.9, ...), custom_call_target="tpu_custom_call" | custom-call | tf_op jit(solution)/shard_map/pallas_call | solution.py:214
  127.0 4.9 %shard_map.116 = bf16[512,384]{1,0:T(8,128)(2,1)S(1)} custom-call(s32[32]{0:T(128)S(1)} %stack.98.refs_0_, f32[16,512]{1,0:T(8,128)S(1)} %copy-done.7, bf16[2048,384]{1,0:T(8,128)(2,1)} %bitcast.69, bf16[2048,384]{1,0:T(8,128)(2,1)} %collective-permute-done.refs_3_, bf16[1024,384]{1,0:T(8,128)(2,1)} %copy-done.9, bf16[1024,384]{1,0:T(8,128)(2,1)} %copy-done.10, ...), custom_call_target="tpu_custom_call" | custom-call | tf_op jit(solution)/shard_map/pallas_call | solution.py:223
  131.8 3.8 %collective-permute-start.26 = (bf16[512,384]{1,0:T(8,128)(2,1)S(1)}, bf16[512,384]{1,0:T(8,128)(2,1)S(1)}, u32[]{:S(2)}, u32[]{:S(2)}) collective-permute-start(bf16[512,384]{1,0:T(8,128)(2,1)S(1)} %shard_map.116), channel_id=1, source_target_pairs={{2,0},{3,1},{0,2},{1,3},{6,4},{7,5},{4,6},{5,7},{10,8},{11,9},{8,1... | collective-permute-start | bytes 1179656 | tf_op jit(solution)/shard_map/ppermute | solution.py:365
  135.6 2.7 %collective-permute-start.24 = (bf16[512,384]{1,0:T(8,128)(2,1)S(1)}, bf16[512,384]{1,0:T(8,128)(2,1)S(1)}, u32[]{:S(2)}, u32[]{:S(2)}) collective-permute-start(bf16[512,384]{1,0:T(8,128)(2,1)S(1)} %shard_map.116), channel_id=1, source_target_pairs={{0,12},{4,0},{8,4},{12,8},{16,28},{20,16},{24,20},{28,24},{32,44},... | collective-permute-start | bytes 1179656 | tf_op jit(solution)/shard_map/ppermute | solution.py:318
  138.3 22.1 %collective-permute-done.26 = bf16[512,384]{1,0:T(8,128)(2,1)S(1)} collective-permute-done((bf16[512,384]{1,0:T(8,128)(2,1)S(1)}, bf16[512,384]{1,0:T(8,128)(2,1)S(1)}, u32[]{:S(2)}, u32[]{:S(2)}) %collective-permute-start.26) | collective-permute-done | bytes 393248 | tf_op jit(solution)/shard_map/ppermute | solution.py:365
  161.2 2.0 collective-permute-start.28
  164.3 4.4 %collective-permute-done.27 = bf16[512,384]{1,0:T(8,128)(2,1)S(1)} collective-permute-done((bf16[512,384]{1,0:T(8,128)(2,1)S(1)}, bf16[512,384]{1,0:T(8,128)(2,1)S(1)}, u32[]{:S(2)}, u32[]{:S(2)}) %collective-permute-start.27) | collective-permute-done | bytes 393248 | tf_op jit(solution)/shard_map/ppermute | solution.py:318
  168.7 3.4 %collective-permute-done.28 = bf16[512,384]{1,0:T(8,128)(2,1)S(1)} collective-permute-done((bf16[512,384]{1,0:T(8,128)(2,1)S(1)}, bf16[512,384]{1,0:T(8,128)(2,1)S(1)}, u32[]{:S(2)}, u32[]{:S(2)}) %collective-permute-start.28) | collective-permute-done | bytes 393248 | tf_op jit(solution)/shard_map/ppermute | solution.py:318
  172.1 2.5 collective-permute-done.29
  174.8 1.1 collective-permute-start.31
  175.8 1.7 collective-permute-start.32
  177.5 1.3 collective-permute-start.33
  178.8 1.4 collective-permute-start.34
  180.2 7.7 %shard_map.117.refs_10_ = f32[1024,1024]{1,0:T(8,128)S(1)} custom-call(s32[32]{0:T(128)S(1)} %stack.98.refs_0_, bf16[6144,512]{1,0:T(8,128)(2,1)} %bitcast.63, bf16[6144,256]{1,0:T(8,128)(2,1)} %collective-permute-done.30.refs_2_, bf16[2048,384]{1,0:T(8,128)(2,1)S(1)} %pad_maximum_fusion.refs_3_.refs_4_, bf16[2048,384]{1,0:T(8,128)(2,1)S(1)} %pad_maximum_fusion.1.refs_4_.refs_5_), custom_call_target="tpu_custom_call" | custom-call | tf_op jit(solution)/shard_map/pallas_call | solution.py:297
  188.0 1.9 copy-done.2
  189.9 3.8 %dynamic-slice_bitcast_fusion.refs_3_ = bf16[6144,256]{1,0:T(8,128)(2,1)} fusion(bf16[2,6144,256]{2,1,0:T(8,128)(2,1)} %all-to-all-done.2, s32[]{:T(128)S(6)} %select_n.271), kind=kLoop, calls=%fused_computation | loop fusion | bytes 6291460 | tf_op jit(solution)/shard_map/jit(dynamic_index_in_dim)/squeeze | solution.py:432
  193.7 13.7 %collective-permute-done.31.refs_6_ = bf16[2048,384]{1,0:T(8,128)(2,1)} collective-permute-done((bf16[2048,384]{1,0:T(8,128)(2,1)S(1)}, bf16[2048,384]{1,0:T(8,128)(2,1)}, u32[]{:S(2)}, u32[]{:S(2)}) %collective-permute-start.31) | collective-permute-done | bytes 1572896 | tf_op jit(solution)/shard_map/ppermute | solution.py:318
  207.5 1.2 slice.71
  208.7 1.8 collective-permute-start.36
  210.5 1.2 slice.72
  211.8 1.3 collective-permute-start.37
  213.1 1.2 slice.73
  214.3 1.4 collective-permute-start.38
  215.7 1.2 slice.74
  216.9 1.5 collective-permute-start.39
  218.4 18.5 %shard_map.118.refs_8_ = f32[1024,1024]{1,0:T(8,128)S(1)} custom-call(s32[32]{0:T(128)S(1)} %stack.98.refs_0_, bf16[6144,512]{1,0:T(8,128)(2,1)} %bitcast.64, bf16[6144,256]{1,0:T(8,128)(2,1)} %collective-permute-done.30.refs_2_, bf16[6144,256]{1,0:T(8,128)(2,1)} %dynamic-slice_bitcast_fusion.refs_3_, bf16[2048,384]{1,0:T(8,128)(2,1)S(1)} %pad_maximum_fusion.refs_3_.refs_4_, ...), custom_call_target="tpu_custom_call" | custom-call | tf_op jit(solution)/shard_map/pallas_call | solution.py:297
  236.9 13.3 %collective-permute-start.35 = (bf16[1,512,384]{2,1,0:T(8,128)(2,1)S(1)}, bf16[1,512,384]{2,1,0:T(8,128)(2,1)S(1)}, u32[]{:S(2)}, u32[]{:S(2)}) collective-permute-start(bf16[1,512,384]{2,1,0:T(8,128)(2,1)S(1)} %bitcast.61), channel_id=1, source_target_pairs={{0,64},{1,65},{2,66},{3,67},{64,0},{65,1},{66,2},{67,3},{4,68},{5,... | collective-permute-start | bytes 1179656 | tf_op jit(solution)/shard_map/ppermute | solution.py:376
  250.2 9.5 %shard_map.119 = f32[16,1024]{1,0:T(8,128)S(1)} custom-call(s32[32]{0:T(128)S(1)} %stack.98.refs_0_, bf16[6144,512]{1,0:T(8,128)(2,1)} %bitcast.65, bf16[6144,256]{1,0:T(8,128)(2,1)} %collective-permute-done.30.refs_2_, bf16[6144,256]{1,0:T(8,128)(2,1)} %dynamic-slice_bitcast_fusion.refs_3_, bf16[1024,384]{1,0:T(8,128)(2,1)S(1)} %collective-permute-done.36.refs_4_, ...), custom_call_target="tpu_custom_call" | custom-call | tf_op jit(solution)/shard_map/pallas_call | solution.py:297
  260.6 1.3 collective-permute-start.42
  261.9 2.2 collective-permute-done.41
  (103 shorter events, 13.0 us)
Async XLA Ops:
  0.6 18.5 %copy-start = (f32[1,16,128,128]{3,2,1,0:T(8,128)S(1)}, f32[1,16,128,128]{3,2,1,0:T(8,128)}, u32[]{:S(2)}) copy-start(f32[1,16,128,128]{3,2,1,0:T(8,128)} %param.13) | copy-start | bytes 3145732
  0.6 43.6 %collective-permute-start = (bf16[2048,384]{1,0:T(8,128)(2,1)}, bf16[2048,384]{1,0:T(8,128)(2,1)}, u32[]{:S(2)}, u32[]{:S(2)}) collective-permute-start(bf16[2048,384]{1,0:T(8,128)(2,1)} %bitcast.66), channel_id=1, source_target_pairs={{1,0},{2,1},{3,2},{0,3},{5,4},{6,5},{7,6},{4,7},{9,8},{10,9},{11,1... | collective-permute-start | bytes 4718600 | tf_op jit(solution)/shard_map/ppermute | solution.py:365
  4.0 40.3 %collective-permute-start.1 = (bf16[2048,384]{1,0:T(8,128)(2,1)}, bf16[2048,384]{1,0:T(8,128)(2,1)}, u32[]{:S(2)}, u32[]{:S(2)}) collective-permute-start(bf16[2048,384]{1,0:T(8,128)(2,1)} %bitcast.67), channel_id=1, source_target_pairs={{3,0},{0,1},{1,2},{2,3},{7,4},{4,5},{5,6},{6,7},{11,8},{8,9},{9,10... | collective-permute-start | bytes 4718600 | tf_op jit(solution)/shard_map/ppermute | solution.py:365
  4.7 32.7 %collective-permute-start.5 = (f32[1,256]{1,0:T(1,128)S(1)}, f32[1,256]{1,0:T(1,128)S(1)}, u32[]{:S(2)}, u32[]{:S(2)}) collective-permute-start(f32[1,256]{1,0:T(1,128)S(1)} %get-tuple-element.74), channel_id=1, source_target_pairs={{0,1},{1,0},{2,3},{3,2},{4,5},{5,4},{6,7},{7,6},{8,9},{9,8},{10,11... | collective-permute-start | bytes 3080 | tf_op jit(solution)/shard_map/ppermute | solution.py:394
  4.9 35.6 %collective-permute-start.6 = (f32[1,256]{1,0:T(1,128)S(1)}, f32[1,256]{1,0:T(1,128)S(1)}, u32[]{:S(2)}, u32[]{:S(2)}) collective-permute-start(f32[1,256]{1,0:T(1,128)S(1)} %get-tuple-element.75), channel_id=1, source_target_pairs={{1,2},{2,1},{3,0},{0,3},{5,6},{6,5},{7,4},{4,7},{9,10},{10,9},{11,... | collective-permute-start | bytes 3080 | tf_op jit(solution)/shard_map/ppermute | solution.py:395
  7.4 0.7 copy-start.8
  9.7 1.2 copy-start.4
  10.9 7.9 %copy-start.11 = (f32[1,2048]{1,0:T(1,128)S(1)}, f32[1,2048]{1,0:T(1,128)}, u32[]{:S(2)}) copy-start(f32[1,2048]{1,0:T(1,128)} %param.15) | copy-start | bytes 24580
  10.9 29.6 %copy-start.12 = (f32[1,512]{1,0:T(1,128)S(1)}, f32[1,512]{1,0:T(1,128)}, u32[]{:S(2)}) copy-start(f32[1,512]{1,0:T(1,128)} %param.19) | copy-start | bytes 6148
  10.9 33.4 %all-to-all-start = ((bf16[16,400,128]{2,1,0:T(8,128)(2,1)}), bf16[16,400,128]{2,1,0:T(8,128)(2,1)S(1)}, u32[]{:S(2)}, u32[]{:S(2)}) async-start(bf16[16,400,128]{2,1,0:T(8,128)(2,1)} %copy-done.4), calls=%async_computation | async-start | bytes 3276800 | tf_op jit(solution)/shard_map/all_to_all | solution.py:401
  18.8 21.7 %collective-permute-start.2 = (f32[1,2048]{1,0:T(1,128)S(1)}, f32[1,2048]{1,0:T(1,128)S(1)}, u32[]{:S(2)}, u32[]{:S(2)}) collective-permute-start(f32[1,2048]{1,0:T(1,128)S(1)} %copy-done.11), channel_id=1, source_target_pairs={{1,0},{2,1},{3,2},{0,3},{5,4},{6,5},{7,6},{4,7},{9,8},{10,9},{11,1... | collective-permute-start | bytes 24584 | tf_op jit(solution)/shard_map/ppermute | solution.py:365
  37.4 4.1 %collective-permute-start.3 = (f32[1,2048]{1,0:T(1,128)S(1)}, f32[1,2048]{1,0:T(1,128)S(1)}, u32[]{:S(2)}, u32[]{:S(2)}) collective-permute-start(f32[1,2048]{1,0:T(1,128)S(1)} %copy-done.11), channel_id=1, source_target_pairs={{2,0},{3,1},{0,2},{1,3},{6,4},{7,5},{4,6},{5,7},{10,8},{11,9},{8,1... | collective-permute-start | bytes 24584 | tf_op jit(solution)/shard_map/ppermute | solution.py:365
  40.5 3.7 %collective-permute-start.4 = (f32[1,2048]{1,0:T(1,128)S(1)}, f32[1,2048]{1,0:T(1,128)S(1)}, u32[]{:S(2)}, u32[]{:S(2)}) collective-permute-start(f32[1,2048]{1,0:T(1,128)S(1)} %copy-done.11), channel_id=1, source_target_pairs={{3,0},{0,1},{1,2},{2,3},{7,4},{4,5},{5,6},{6,7},{11,8},{8,9},{9,10... | collective-permute-start | bytes 24584 | tf_op jit(solution)/shard_map/ppermute | solution.py:365
  44.3 71.2 %copy-start.6 = (f32[16,512]{1,0:T(8,128)}, f32[16,512]{1,0:T(8,128)S(1)}, u32[]{:S(2)}) copy-start(f32[16,512]{1,0:T(8,128)S(1)} %pad_maximum_fusion.5.refs_1_) | copy-start | bytes 98308
  48.4 10.4 %all-to-all-start.1 = ((bf16[4,512,128]{2,1,0:T(8,128)(2,1)}), bf16[4,512,128]{2,1,0:T(8,128)(2,1)S(1)}, u32[]{:S(2)}, u32[]{:S(2)}) async-start(bf16[4,512,128]{2,1,0:T(8,128)(2,1)} %shard_map.114), calls=%async_computation.1 | async-start | bytes 1048576 | tf_op jit(solution)/shard_map/all_to_all | solution.py:409
  58.9 7.9 %collective-permute-start.10 = (bf16[256,512]{1,0:T(8,128)(2,1)S(1)}, bf16[256,512]{1,0:T(8,128)(2,1)S(1)}, u32[]{:S(2)}, u32[]{:S(2)}) collective-permute-start(bf16[256,512]{1,0:T(8,128)(2,1)S(1)} %get-tuple-element.54), channel_id=1, source_target_pairs={{0,16},{4,20},{8,24},{12,28},{16,32},{20,36},{24,40},{28,44},{32,4... | collective-permute-start | bytes 786440 | tf_op jit(solution)/shard_map/ppermute | solution.py:318
  60.6 8.8 %collective-permute-start.11 = (bf16[256,512]{1,0:T(8,128)(2,1)S(1)}, bf16[256,512]{1,0:T(8,128)(2,1)S(1)}, u32[]{:S(2)}, u32[]{:S(2)}) collective-permute-start(bf16[256,512]{1,0:T(8,128)(2,1)S(1)} %get-tuple-element.54), channel_id=1, source_target_pairs={{0,48},{4,52},{8,56},{12,60},{16,0},{20,4},{24,8},{28,12},{32,16},... | collective-permute-start | bytes 786440 | tf_op jit(solution)/shard_map/ppermute | solution.py:318
  62.8 8.5 %collective-permute-start.12 = (bf16[256,512]{1,0:T(8,128)(2,1)S(1)}, bf16[256,512]{1,0:T(8,128)(2,1)S(1)}, u32[]{:S(2)}, u32[]{:S(2)}) collective-permute-start(bf16[256,512]{1,0:T(8,128)(2,1)S(1)} %get-tuple-element.54), channel_id=1, source_target_pairs={{0,32},{4,36},{8,40},{12,44},{16,48},{20,52},{24,56},{28,60},{32,0... | collective-permute-start | bytes 786440 | tf_op jit(solution)/shard_map/ppermute | solution.py:318
  64.1 12.5 %collective-permute-start.7 = (bf16[256,512]{1,0:T(8,128)(2,1)S(1)}, bf16[256,512]{1,0:T(8,128)(2,1)S(1)}, u32[]{:S(2)}, u32[]{:S(2)}) collective-permute-start(bf16[256,512]{1,0:T(8,128)(2,1)S(1)} %get-tuple-element.55), channel_id=1, source_target_pairs={{0,4},{4,8},{8,12},{12,0},{16,20},{20,24},{24,28},{28,16},{32,36},... | collective-permute-start | bytes 786440 | tf_op jit(solution)/shard_map/ppermute | solution.py:318
  65.3 11.2 %collective-permute-start.8 = (bf16[256,512]{1,0:T(8,128)(2,1)S(1)}, bf16[256,512]{1,0:T(8,128)(2,1)S(1)}, u32[]{:S(2)}, u32[]{:S(2)}) collective-permute-start(bf16[256,512]{1,0:T(8,128)(2,1)S(1)} %get-tuple-element.55), channel_id=1, source_target_pairs={{0,12},{4,0},{8,4},{12,8},{16,28},{20,16},{24,20},{28,24},{32,44},... | collective-permute-start | bytes 786440 | tf_op jit(solution)/shard_map/ppermute | solution.py:318
  66.8 9.8 %collective-permute-start.9 = (bf16[256,512]{1,0:T(8,128)(2,1)S(1)}, bf16[256,512]{1,0:T(8,128)(2,1)S(1)}, u32[]{:S(2)}, u32[]{:S(2)}) collective-permute-start(bf16[256,512]{1,0:T(8,128)(2,1)S(1)} %get-tuple-element.55), channel_id=1, source_target_pairs={{0,8},{4,12},{8,0},{12,4},{16,24},{20,28},{24,16},{28,20},{32,40},... | collective-permute-start | bytes 786440 | tf_op jit(solution)/shard_map/ppermute | solution.py:318
  69.4 11.5 %collective-permute-start.13 = (bf16[1024,384]{1,0:T(8,128)(2,1)}, bf16[1024,384]{1,0:T(8,128)(2,1)S(1)}, u32[]{:S(2)}, u32[]{:S(2)}) collective-permute-start(bf16[1024,384]{1,0:T(8,128)(2,1)} %slice.63), channel_id=1, source_target_pairs={{1,0},{2,1},{3,2},{0,3},{5,4},{6,5},{7,6},{4,7},{9,8},{10,9},{11,1... | collective-permute-start | bytes 2359304 | tf_op jit(solution)/shard_map/ppermute | solution.py:365
  71.3 13.4 %collective-permute-start.14 = (bf16[1024,384]{1,0:T(8,128)(2,1)}, bf16[1024,384]{1,0:T(8,128)(2,1)S(1)}, u32[]{:S(2)}, u32[]{:S(2)}) collective-permute-start(bf16[1024,384]{1,0:T(8,128)(2,1)} %slice.64), channel_id=1, source_target_pairs={{3,0},{0,1},{1,2},{2,3},{7,4},{4,5},{5,6},{6,7},{11,8},{8,9},{9,10... | collective-permute-start | bytes 2359304 | tf_op jit(solution)/shard_map/ppermute | solution.py:365
  80.9 3.8 %copy-start.9 = (bf16[1024,384]{1,0:T(8,128)(2,1)}, bf16[1024,384]{1,0:T(8,128)(2,1)S(1)}, u32[]{:S(2)}) copy-start(bf16[1024,384]{1,0:T(8,128)(2,1)S(1)} %collective-permute-done.13.refs_4_) | copy-start | bytes 2359300
  84.7 4.5 %copy-start.10 = (bf16[1024,384]{1,0:T(8,128)(2,1)}, bf16[1024,384]{1,0:T(8,128)(2,1)S(1)}, u32[]{:S(2)}) copy-start(bf16[1024,384]{1,0:T(8,128)(2,1)S(1)} %collective-permute-done.14.refs_5_) | copy-start | bytes 2359300
  84.7 90.0 %collective-permute-start.30 = (bf16[6144,256]{1,0:T(8,128)(2,1)}, bf16[6144,256]{1,0:T(8,128)(2,1)}, u32[]{:S(2)}, u32[]{:S(2)}) collective-permute-start(bf16[6144,256]{1,0:T(8,128)(2,1)} %get-tuple-element.38), channel_id=1, source_target_pairs={{0,1},{1,0},{2,3},{3,2},{4,5},{5,4},{6,7},{7,6},{8,9},{9,8},{10,11... | collective-permute-start | bytes 9437192 | tf_op jit(solution)/shard_map/ppermute | solution.py:423
  84.7 18.3 %collective-permute-start.19 = (bf16[1024,512]{1,0:T(8,128)(2,1)S(1)}, bf16[1024,512]{1,0:T(8,128)(2,1)S(1)}, u32[]{:S(2)}, u32[]{:S(2)}) collective-permute-start(bf16[1024,512]{1,0:T(8,128)(2,1)S(1)} %pad_maximum_fusion.3.refs_8_), channel_id=1, source_target_pairs={{0,4},{4,8},{8,12},{12,0},{16,20},{20,24},{24,28},{28,16},{32,36},... | collective-permute-start | bytes 3145736 | tf_op jit(solution)/shard_map/ppermute | solution.py:318
  87.0 17.6 %collective-permute-start.21 = (bf16[1024,512]{1,0:T(8,128)(2,1)S(1)}, bf16[1024,512]{1,0:T(8,128)(2,1)}, u32[]{:S(2)}, u32[]{:S(2)}) collective-permute-start(bf16[1024,512]{1,0:T(8,128)(2,1)S(1)} %pad_maximum_fusion.3.refs_8_), channel_id=1, source_target_pairs={{0,12},{4,0},{8,4},{12,8},{16,28},{20,16},{24,20},{28,24},{32,44},... | collective-permute-start | bytes 3145736 | tf_op jit(solution)/shard_map/ppermute | solution.py:318
  89.2 19.7 %collective-permute-start.15 = (bf16[1024,512]{1,0:T(8,128)(2,1)S(1)}, bf16[1024,512]{1,0:T(8,128)(2,1)}, u32[]{:S(2)}, u32[]{:S(2)}) collective-permute-start(bf16[1024,512]{1,0:T(8,128)(2,1)S(1)} %pad_maximum_fusion.2.refs_7_), channel_id=1, source_target_pairs={{0,16},{4,20},{8,24},{12,28},{16,32},{20,36},{24,40},{28,44},{32,4... | collective-permute-start | bytes 3145736 | tf_op jit(solution)/shard_map/ppermute | solution.py:318
  89.5 22.1 %collective-permute-start.17 = (bf16[1024,512]{1,0:T(8,128)(2,1)S(1)}, bf16[1024,512]{1,0:T(8,128)(2,1)}, u32[]{:S(2)}, u32[]{:S(2)}) collective-permute-start(bf16[1024,512]{1,0:T(8,128)(2,1)S(1)} %pad_maximum_fusion.2.refs_7_), channel_id=1, source_target_pairs={{0,48},{4,52},{8,56},{12,60},{16,0},{20,4},{24,8},{28,12},{32,16},... | collective-permute-start | bytes 3145736 | tf_op jit(solution)/shard_map/ppermute | solution.py:318
  95.0 94.9 %all-to-all-start.2 = ((bf16[2,6144,256]{2,1,0:T(8,128)(2,1)}), bf16[2,6144,256]{2,1,0:T(8,128)(2,1)}, u32[]{:S(2)}, u32[]{:S(2)}) async-start(bf16[2,6144,256]{2,1,0:T(8,128)(2,1)} %broadcast_in_dim.12), calls=%async_computation.2 | async-start | bytes 12582912 | tf_op jit(solution)/shard_map/all_to_all | solution.py:424
  103.9 22.3 %collective-permute-start.20 = (bf16[512,512]{1,0:T(8,128)(2,1)}, bf16[512,512]{1,0:T(8,128)(2,1)}, u32[]{:S(2)}, u32[]{:S(2)}) collective-permute-start(bf16[512,512]{1,0:T(8,128)(2,1)} %slice.86), channel_id=1, source_target_pairs={{0,4},{4,8},{8,12},{12,0},{16,20},{20,24},{24,28},{28,16},{32,36},... | collective-permute-start | bytes 1572872 | tf_op jit(solution)/shard_map/ppermute | solution.py:318
  106.4 19.7 %collective-permute-start.22 = (bf16[512,512]{1,0:T(8,128)(2,1)}, bf16[512,512]{1,0:T(8,128)(2,1)}, u32[]{:S(2)}, u32[]{:S(2)}) collective-permute-start(bf16[512,512]{1,0:T(8,128)(2,1)} %slice.87), channel_id=1, source_target_pairs={{0,12},{4,0},{8,4},{12,8},{16,28},{20,16},{24,20},{28,24},{32,44},... | collective-permute-start | bytes 1572872 | tf_op jit(solution)/shard_map/ppermute | solution.py:318
  110.8 15.4 %collective-permute-start.16 = (bf16[512,512]{1,0:T(8,128)(2,1)}, bf16[512,512]{1,0:T(8,128)(2,1)}, u32[]{:S(2)}, u32[]{:S(2)}) collective-permute-start(bf16[512,512]{1,0:T(8,128)(2,1)} %slice.84), channel_id=1, source_target_pairs={{0,16},{4,20},{8,24},{12,28},{16,32},{20,36},{24,40},{28,44},{32,4... | collective-permute-start | bytes 1572872 | tf_op jit(solution)/shard_map/ppermute | solution.py:318
  113.5 12.7 %collective-permute-start.18 = (bf16[512,512]{1,0:T(8,128)(2,1)}, bf16[512,512]{1,0:T(8,128)(2,1)}, u32[]{:S(2)}, u32[]{:S(2)}) collective-permute-start(bf16[512,512]{1,0:T(8,128)(2,1)} %slice.85), channel_id=1, source_target_pairs={{0,48},{4,52},{8,56},{12,60},{16,0},{20,4},{24,8},{28,12},{32,16},... | collective-permute-start | bytes 1572872 | tf_op jit(solution)/shard_map/ppermute | solution.py:318
  115.4 10.8 %copy-start.5 = (bf16[1,512,384]{2,1,0:T(8,128)(2,1)S(1)}, bf16[1,512,384]{2,1,0:T(8,128)(2,1)}, u32[]{:S(2)}) copy-start(bf16[1,512,384]{2,1,0:T(8,128)(2,1)} %param.16) | copy-start | bytes 1179652
  126.2 0.8 copy-start.7
  131.8 28.6 %collective-permute-start.26 = (bf16[512,384]{1,0:T(8,128)(2,1)S(1)}, bf16[512,384]{1,0:T(8,128)(2,1)S(1)}, u32[]{:S(2)}, u32[]{:S(2)}) collective-permute-start(bf16[512,384]{1,0:T(8,128)(2,1)S(1)} %shard_map.116), channel_id=1, source_target_pairs={{2,0},{3,1},{0,2},{1,3},{6,4},{7,5},{4,6},{5,7},{10,8},{11,9},{8,1... | collective-permute-start | bytes 1179656 | tf_op jit(solution)/shard_map/ppermute | solution.py:365
  135.6 25.5 %collective-permute-start.23 = (bf16[512,384]{1,0:T(8,128)(2,1)S(1)}, bf16[512,384]{1,0:T(8,128)(2,1)S(1)}, u32[]{:S(2)}, u32[]{:S(2)}) collective-permute-start(bf16[512,384]{1,0:T(8,128)(2,1)S(1)} %shard_map.116), channel_id=1, source_target_pairs={{0,4},{4,8},{8,12},{12,0},{16,20},{20,24},{24,28},{28,16},{32,36},... | collective-permute-start | bytes 1179656 | tf_op jit(solution)/shard_map/ppermute | solution.py:318
  135.6 27.5 %collective-permute-start.24 = (bf16[512,384]{1,0:T(8,128)(2,1)S(1)}, bf16[512,384]{1,0:T(8,128)(2,1)S(1)}, u32[]{:S(2)}, u32[]{:S(2)}) collective-permute-start(bf16[512,384]{1,0:T(8,128)(2,1)S(1)} %shard_map.116), channel_id=1, source_target_pairs={{0,12},{4,0},{8,4},{12,8},{16,28},{20,16},{24,20},{28,24},{32,44},... | collective-permute-start | bytes 1179656 | tf_op jit(solution)/shard_map/ppermute | solution.py:318
  138.3 25.8 %collective-permute-start.25 = (bf16[512,384]{1,0:T(8,128)(2,1)S(1)}, bf16[512,384]{1,0:T(8,128)(2,1)S(1)}, u32[]{:S(2)}, u32[]{:S(2)}) collective-permute-start(bf16[512,384]{1,0:T(8,128)(2,1)S(1)} %shard_map.116), channel_id=1, source_target_pairs={{0,8},{4,12},{8,0},{12,4},{16,24},{20,28},{24,16},{28,20},{32,40},... | collective-permute-start | bytes 1179656 | tf_op jit(solution)/shard_map/ppermute | solution.py:318
  160.5 8.2 %collective-permute-start.27 = (bf16[512,384]{1,0:T(8,128)(2,1)S(1)}, bf16[512,384]{1,0:T(8,128)(2,1)S(1)}, u32[]{:S(2)}, u32[]{:S(2)}) collective-permute-start(bf16[512,384]{1,0:T(8,128)(2,1)S(1)} %collective-permute-done.26), channel_id=1, source_target_pairs={{0,16},{4,20},{8,24},{12,28},{16,32},{20,36},{24,40},{28,44},{32,4... | collective-permute-start | bytes 1179656 | tf_op jit(solution)/shard_map/ppermute | solution.py:318
  161.2 10.9 %collective-permute-start.28 = (bf16[512,384]{1,0:T(8,128)(2,1)S(1)}, bf16[512,384]{1,0:T(8,128)(2,1)S(1)}, u32[]{:S(2)}, u32[]{:S(2)}) collective-permute-start(bf16[512,384]{1,0:T(8,128)(2,1)S(1)} %collective-permute-done.26), channel_id=1, source_target_pairs={{0,48},{4,52},{8,56},{12,60},{16,0},{20,4},{24,8},{28,12},{32,16},... | collective-permute-start | bytes 1179656 | tf_op jit(solution)/shard_map/ppermute | solution.py:318
  163.1 11.4 %collective-permute-start.29 = (bf16[512,384]{1,0:T(8,128)(2,1)S(1)}, bf16[512,384]{1,0:T(8,128)(2,1)S(1)}, u32[]{:S(2)}, u32[]{:S(2)}) collective-permute-start(bf16[512,384]{1,0:T(8,128)(2,1)S(1)} %collective-permute-done.26), channel_id=1, source_target_pairs={{0,32},{4,36},{8,40},{12,44},{16,48},{20,52},{24,56},{28,60},{32,0... | collective-permute-start | bytes 1179656 | tf_op jit(solution)/shard_map/ppermute | solution.py:318
  174.8 32.7 %collective-permute-start.31 = (bf16[2048,384]{1,0:T(8,128)(2,1)S(1)}, bf16[2048,384]{1,0:T(8,128)(2,1)}, u32[]{:S(2)}, u32[]{:S(2)}) collective-permute-start(bf16[2048,384]{1,0:T(8,128)(2,1)S(1)} %pad_maximum_fusion.refs_3_.refs_4_), channel_id=1, source_target_pairs={{0,16},{4,20},{8,24},{12,28},{16,32},{20,36},{24,40},{28,44},{32,4... | collective-permute-start | bytes 4718600 | tf_op jit(solution)/shard_map/ppermute | solution.py:318
  175.8 31.7 %collective-permute-start.32 = (bf16[2048,384]{1,0:T(8,128)(2,1)S(1)}, bf16[2048,384]{1,0:T(8,128)(2,1)}, u32[]{:S(2)}, u32[]{:S(2)}) collective-permute-start(bf16[2048,384]{1,0:T(8,128)(2,1)S(1)} %pad_maximum_fusion.refs_3_.refs_4_), channel_id=1, source_target_pairs={{0,48},{4,52},{8,56},{12,60},{16,0},{20,4},{24,8},{28,12},{32,16},... | collective-permute-start | bytes 4718600 | tf_op jit(solution)/shard_map/ppermute | solution.py:318
  177.5 30.0 %collective-permute-start.33 = (bf16[2048,384]{1,0:T(8,128)(2,1)S(1)}, bf16[2048,384]{1,0:T(8,128)(2,1)}, u32[]{:S(2)}, u32[]{:S(2)}) collective-permute-start(bf16[2048,384]{1,0:T(8,128)(2,1)S(1)} %pad_maximum_fusion.1.refs_4_.refs_5_), channel_id=1, source_target_pairs={{0,4},{4,8},{8,12},{12,0},{16,20},{20,24},{24,28},{28,16},{32,36},... | collective-permute-start | bytes 4718600 | tf_op jit(solution)/shard_map/ppermute | solution.py:318
  178.8 28.7 %collective-permute-start.34 = (bf16[2048,384]{1,0:T(8,128)(2,1)S(1)}, bf16[2048,384]{1,0:T(8,128)(2,1)}, u32[]{:S(2)}, u32[]{:S(2)}) collective-permute-start(bf16[2048,384]{1,0:T(8,128)(2,1)S(1)} %pad_maximum_fusion.1.refs_4_.refs_5_), channel_id=1, source_target_pairs={{0,12},{4,0},{8,4},{12,8},{16,28},{20,16},{24,20},{28,24},{32,44},... | collective-permute-start | bytes 4718600 | tf_op jit(solution)/shard_map/ppermute | solution.py:318
  188.0 1.9 copy-start.2
  208.7 9.7 %copy-start.3 = (f32[1024,1024]{1,0:T(8,128)S(1)}, f32[1024,1024]{1,0:T(8,128)}, u32[]{:S(2)}) copy-start(f32[1024,1024]{1,0:T(8,128)} %copy-done.2) | copy-start | bytes 12582916
  208.7 41.5 %collective-permute-start.36 = (bf16[1024,384]{1,0:T(8,128)(2,1)S(1)}, bf16[1024,384]{1,0:T(8,128)(2,1)S(1)}, u32[]{:S(2)}, u32[]{:S(2)}) collective-permute-start(bf16[1024,384]{1,0:T(8,128)(2,1)S(1)} %slice.71), channel_id=1, source_target_pairs={{0,16},{4,20},{8,24},{12,28},{16,32},{20,36},{24,40},{28,44},{32,4... | collective-permute-start | bytes 2359304 | tf_op jit(solution)/shard_map/ppermute | solution.py:318
  211.8 38.4 %collective-permute-start.37 = (bf16[1024,384]{1,0:T(8,128)(2,1)S(1)}, bf16[1024,384]{1,0:T(8,128)(2,1)S(1)}, u32[]{:S(2)}, u32[]{:S(2)}) collective-permute-start(bf16[1024,384]{1,0:T(8,128)(2,1)S(1)} %slice.72), channel_id=1, source_target_pairs={{0,48},{4,52},{8,56},{12,60},{16,0},{20,4},{24,8},{28,12},{32,16},... | collective-permute-start | bytes 2359304 | tf_op jit(solution)/shard_map/ppermute | solution.py:318
  214.3 35.9 %collective-permute-start.38 = (bf16[1024,384]{1,0:T(8,128)(2,1)S(1)}, bf16[1024,384]{1,0:T(8,128)(2,1)S(1)}, u32[]{:S(2)}, u32[]{:S(2)}) collective-permute-start(bf16[1024,384]{1,0:T(8,128)(2,1)S(1)} %slice.73), channel_id=1, source_target_pairs={{0,4},{4,8},{8,12},{12,0},{16,20},{20,24},{24,28},{28,16},{32,36},... | collective-permute-start | bytes 2359304 | tf_op jit(solution)/shard_map/ppermute | solution.py:318
  216.9 33.3 %collective-permute-start.39 = (bf16[1024,384]{1,0:T(8,128)(2,1)S(1)}, bf16[1024,384]{1,0:T(8,128)(2,1)S(1)}, u32[]{:S(2)}, u32[]{:S(2)}) collective-permute-start(bf16[1024,384]{1,0:T(8,128)(2,1)S(1)} %slice.74), channel_id=1, source_target_pairs={{0,12},{4,0},{8,4},{12,8},{16,28},{20,16},{24,20},{28,24},{32,44},... | collective-permute-start | bytes 2359304 | tf_op jit(solution)/shard_map/ppermute | solution.py:318
  236.9 25.0 %collective-permute-start.35 = (bf16[1,512,384]{2,1,0:T(8,128)(2,1)S(1)}, bf16[1,512,384]{2,1,0:T(8,128)(2,1)S(1)}, u32[]{:S(2)}, u32[]{:S(2)}) collective-permute-start(bf16[1,512,384]{2,1,0:T(8,128)(2,1)S(1)} %bitcast.61), channel_id=1, source_target_pairs={{0,64},{1,65},{2,66},{3,67},{64,0},{65,1},{66,2},{67,3},{4,68},{5,... | collective-permute-start | bytes 1179656 | tf_op jit(solution)/shard_map/ppermute | solution.py:376
  250.2 15.4 %copy-start.1 = (f32[1,16,128,128]{3,2,1,0:T(8,128)S(1)}, f32[1,16,128,128]{3,2,1,0:T(8,128)}, u32[]{:S(2)}) copy-start(f32[1,16,128,128]{3,2,1,0:T(8,128)} %param.13) | copy-start | bytes 3145732
  259.7 4.4 %collective-permute-start.41 = (bf16[16,256]{1,0:T(8,128)(2,1)S(1)}, bf16[16,256]{1,0:T(8,128)(2,1)S(1)}, u32[]{:S(2)}, u32[]{:S(2)}) collective-permute-start(bf16[16,256]{1,0:T(8,128)(2,1)S(1)} %get-tuple-element.64), channel_id=1, source_target_pairs={{1,66},{2,65},{3,64},{0,67},{65,2},{66,1},{67,0},{64,3},{5,70},{6,... | collective-permute-start | bytes 24584 | tf_op jit(solution)/shard_map/ppermute | solution.py:376
  260.6 3.5 %collective-permute-start.42 = (bf16[16,256]{1,0:T(8,128)(2,1)S(1)}, bf16[16,256]{1,0:T(8,128)(2,1)S(1)}, u32[]{:S(2)}, u32[]{:S(2)}) collective-permute-start(bf16[16,256]{1,0:T(8,128)(2,1)S(1)} %get-tuple-element.65), channel_id=1, source_target_pairs={{0,65},{1,64},{2,67},{3,66},{64,1},{65,0},{66,3},{67,2},{4,69},{5,... | collective-permute-start | bytes 24584 | tf_op jit(solution)/shard_map/ppermute | solution.py:376
  261.9 2.3 collective-permute-start.40

commit v8 on v7

--- a/solution.py
+++ b/solution.py
@@ -93,50 +93,62 @@
     )(packed, prior, gain)
 
 
-SLOTS = 4
+SLOTS = 2
 
 
 def listed(gathered, steps):
     return [array for step in steps for parts in gathered for array in parts[step]]
 
 
-def stream(source, step, arrays, rows, buffer, sems, fetch, fetched, body):
-    total = sum(array.shape[0] // rows for array in arrays)
-    count = total // len(arrays)
-
-    def place(n):
-        half = lax.rem(lax.div(n, 4), 2)
-        row = half * 4 + step + lax.div(n, 8)
-        return half, source[row * 4 + lax.rem(n, 4)]
-
-    def start(n, slot):
-        for r, array in enumerate(arrays):
-
-            @pl.when(lax.div(n, count) == r)
+def units(arrays, step, rows):
+    parts = [(array, i * rows) for array in arrays for i in range(array.shape[0] // rows)]
+    return [(step + n // 8, n // 4 % 2, parts[n : n + 4]) for n in range(0, len(parts), 4)]
+
+
+def stream(source, work, buffer, sems, fetch, bodies):
+    rows, depth = buffer.shape[1], buffer.shape[2] // 4
+
+    def copies(n):
+        slot, out = n % SLOTS, []
+        for i, (array, first) in enumerate(work[n][2]):
+            there = buffer.at[slot, :, i * depth : (i + 1) * depth]
+            here = array.at[first : first + rows, :]
+            out.append(pltpu.make_async_copy(here, there, sems.at[slot, 0, i]))
+        return out
+
+    def start(n):
+        for copy in copies(n):
+            copy.start()
+        for i in range(4):
+            fetch(source[(work[n][1] * 4 + work[n][0]) * 4 + i], i, n, True)
+
+    def one(n, body):
+        for m in range(1, len(work)):
+            pl.when(n + 1 == m)(functools.partial(start, m))
+        for m in range(len(work)):
+
+            @pl.when(n == m)
             def _():
-                across = pl.ds(pl.multiple_of(lax.rem(n, count) * rows, BLK), rows)
-                pltpu.make_async_copy(array.at[across, :], buffer.at[slot], sems.at[slot, 0]).start()
-
-        fetch(place(n)[1], slot)
-
-    for n in range(SLOTS - 1):
-        start(n, n)
-
-    def one(n, carry):
-        slot = lax.rem(n, SLOTS)
-
-        @pl.when(n + SLOTS - 1 < total)
-        def _():
-            start(n + SLOTS - 1, lax.rem(n + SLOTS - 1, SLOTS))
-
-        first = pl.ds(0, rows)
-        pltpu.make_async_copy(arrays[0].at[first, :], buffer.at[slot], sems.at[slot, 0]).wait()
-        half, part = place(n)
-        fetched(slot)
-        body(pl.ds(pl.multiple_of(half * rows, BLK), rows), part, slot)
-        return carry
-
-    lax.fori_loop(0, total, one, 0)
+                for copy in copies(m):
+                    copy.wait()
+                for i in range(4):
+                    fetch(0, i, m, False)
+
+        half = lax.rem(n, 2)
+        row = (half * 4 + work[0][0] + lax.div(n, 2)) * 4
+        here = pl.ds(pl.multiple_of(half * rows, BLK), rows)
+        body(here, lax.rem(n, SLOTS), [source[row + i] for i in range(4)])
+
+    start(0)
+    begin = 0
+    for count, body in bodies:
+
+        def step(n, carry, body=body):
+            one(n, body)
+            return carry
+
+        lax.fori_loop(begin, begin + count, step, 0)
+        begin += count
 
 
 def project_kernel(count, step, final, *refs):
@@ -151,40 +163,43 @@
         acc, square = rest
         acc[...] = jnp.zeros_like(acc)
         square[...] = jnp.zeros_like(square)
-    middle = w2.shape[0] // HD
-
-    def copy(ref, block, k, slot):
-        rows = pl.ds(pl.multiple_of(block * HD, HD), HD)
-        there = w_buffer.at[slot, k * HD : (k + 1) * HD, :]
-        return pltpu.make_async_copy(ref.at[rows, :], there, sems.at[slot, 1 + k])
-
-    def fetch(part, slot):
+    middle, rows = w2.shape[0] // HD, buffer.shape[1]
+
+    def copy(ref, block, i, k, slot):
+        here = pl.ds(pl.multiple_of(block * HD, HD), HD)
+        there = w_buffer.at[slot, (4 * i + k) * HD : (4 * i + k + 1) * HD, :]
+        return pltpu.make_async_copy(ref.at[here, :], there, sems.at[slot, 1 + k, i])
+
+    def fetch(part, i, n, begin):
+        slot = n % SLOTS
+        if not begin:
+            for k in range(4):
+                copy(w0, 0, i, k, slot).wait()
+            return
         for k, w in ((0, w0), (1, w1), (3, w4)):
-            copy(w, part, k, slot).start()
+            copy(w, part, i, k, slot).start()
 
         @pl.when(part < middle)
         def _():
-            copy(w2, part, 2, slot).start()
+            copy(w2, part, i, 2, slot).start()
 
         @pl.when(part >= middle)
         def _():
-            copy(w3, part - middle, 2, slot).start()
-
-    def fetched(slot):
-        for k in range(4):
-            copy(w0, 0, k, slot).wait()
-
-    def body(here, part, slot):
-        a = buffer[slot]
-        acc[here, :] += dot(a, w_buffer[slot])
-        wide = a.astype(jnp.float32)
-        wide = wide * wide * inverse_ref[pl.ds(part, 1), :]
+            copy(w3, part - middle, i, 2, slot).start()
+
+    def body(here, slot, parts):
+        acc[here, :] += dot(buffer[slot], w_buffer[slot])
         squares = square[here, :]
-        for j in range(a.shape[1] // HD):
-            squares += wide[:, j * HD : (j + 1) * HD]
+        width = buffer.shape[2] // 4
+        for i, part in enumerate(parts):
+            scale = inverse_ref[pl.ds(part, 1), :]
+            for j in range(0, width, HD):
+                wide = buffer[slot, :, i * width + j : i * width + j + HD].astype(jnp.float32)
+                squares += wide * wide * scale[:, j : j + HD]
         square[here, :] = squares
 
-    stream(source, step, blocks, buffer.shape[1], buffer, sems, fetch, fetched, body)
+    work = units(blocks, step, rows)
+    stream(source, work, buffer, sems, fetch, [(len(work), body)])
     if final:
         mean = jnp.sum(square[...], axis=1, keepdims=True) / HDIM
         scaled = acc[...] * lax.rsqrt(mean + epsilon)
@@ -204,9 +219,9 @@
         jax.ShapeDtypeStruct((rows, HD), jnp.float32),
     ]
     slots = [
-        pltpu.VMEM((SLOTS, rows // 2, depth), jnp.bfloat16),
-        pltpu.VMEM((SLOTS, depth, columns), jnp.bfloat16),
-        pltpu.SemaphoreType.DMA((SLOTS, 5)),
+        pltpu.VMEM((SLOTS, rows // 2, 4 * depth), jnp.bfloat16),
+        pltpu.VMEM((SLOTS, 4 * depth, columns), jnp.bfloat16),
+        pltpu.SemaphoreType.DMA((SLOTS, 5, 4)),
     ]
     params = pltpu.CompilerParams(vmem_limit_bytes=12 * MIB)
     weights = [in_hbm(w) for w in weights]
@@ -242,38 +257,29 @@
     else:
         acc_ref, acc = rest
     acc[...] = jnp.zeros_like(acc) if acc_ref is None else acc_ref[...]
-    depth = e_buffer.shape[1]
-    starts = [sum(e.shape[1] for e in encoders[:n]) for n in range(encoder_count)]
-
-    def run(step, blocks, used):
-        def there(n):
-            return slice(starts[n], starts[n] + encoders[n].shape[1])
-
-        def copy(n, part, slot):
-            rows = pl.ds(pl.multiple_of(part * depth, BLK), depth)
-            to = e_buffer.at[slot, :, there(n)]
-            return pltpu.make_async_copy(encoders[n].at[rows, :], to, sems.at[slot, 1 + n])
-
-        def fetch(part, slot):
-            for n in used:
-                copy(n, part, slot).start()
-
-        def fetched(slot):
-            for n in used:
-                copy(n, 0, slot).wait()
-
-        def body(here, part, slot):
-            across = slice(starts[used[0]], there(used[-1]).stop)
-            acc[here, across] += dot(buffer[slot], e_buffer[slot, :, across])
-
-        stream(source, step, blocks, buffer.shape[1], buffer, sems, fetch, fetched, body)
-
+    rows, depth = buffer.shape[1], buffer.shape[2] // 4
+    starts = [sum(e.shape[1] for e in encoders[:n]) for n in range(encoder_count + 1)]
     every = list(range(encoder_count))
+    work = [(*unit, every[-1:]) for unit in units(blocks[:late], step, rows)]
+    work += [(*unit, every) for unit in units(blocks[late:], step + (late > 0), rows)]
+
+    def fetch(part, i, n, begin):
+        slot = n % SLOTS
+        for k in work[n][3]:
+            here = pl.ds(pl.multiple_of(part * depth, BLK), depth)
+            to = e_buffer.at[slot, i * depth : (i + 1) * depth, starts[k] : starts[k + 1]]
+            copy = pltpu.make_async_copy(encoders[k].at[here, :], to, sems.at[slot, 1 + k, i])
+            copy.start() if begin else copy.wait()
+
+    def body(used, here, slot, parts):
+        across = slice(starts[used[0]], starts[used[-1] + 1])
+        acc[here, across] += dot(buffer[slot], e_buffer[slot, :, across])
+
+    ahead = len(units(blocks[:late], step, rows))
+    bodies = [(len(work) - ahead, functools.partial(body, every))]
     if late:
-        run(step, blocks[:late], every[-1:])
-        run(step + 1, blocks[late:], every)
-    else:
-        run(step, blocks, every)
+        bodies.insert(0, (ahead, functools.partial(body, every[-1:])))
+    stream(source, work, buffer, sems, fetch, bodies)
     if final:
         for i in range(out_ref.shape[0] // 8):
             pools = []
@@ -290,9 +296,9 @@
     final = bias is not None
     extra = [x for x in (acc, bias) if x is not None]
     slots = [
-        pltpu.VMEM((SLOTS, rows, depth), jnp.bfloat16),
-        pltpu.VMEM((SLOTS, depth, width), jnp.bfloat16),
-        pltpu.SemaphoreType.DMA((SLOTS, 4)),
+        pltpu.VMEM((SLOTS, rows, 4 * depth), jnp.bfloat16),
+        pltpu.VMEM((SLOTS, 4 * depth, width), jnp.bfloat16),
+        pltpu.SemaphoreType.DMA((SLOTS, 4, 4)),
     ]
     return pl.pallas_call(
         functools.partial(encode_kernel, len(encoders), len(arrays), step, late, final),
@@ -300,7 +306,7 @@
         out_specs=VMEM,
         out_shape=jax.ShapeDtypeStruct((2 * rows // POOL, width), jnp.float32) if final else shape,
         scratch_shapes=([pltpu.VMEM(shape.shape, shape.dtype)] if final else []) + slots,
-        compiler_params=pltpu.CompilerParams(vmem_limit_bytes=18 * MIB),
+        compiler_params=pltpu.CompilerParams(vmem_limit_bytes=24 * MIB),
     )(source, *[in_hbm(x) for x in encoders], *arrays, *extra)
 
 
@@ -399,9 +405,11 @@
     source = sources(place)
 
     packed = lax.all_to_all(packed, "seq", 0, 0, tiled=True)
-    packed, after, before, inverse, bias = lax.optimization_barrier(
-        (packed, after, before, inverse, bias)
-    )
+    first, second = halves(enc_weight[0])
+    packed, after, before, inverse, bias, first = lax.optimization_barrier(
+        (packed, after, before, inverse, bias, first)
+    )
+    first = lax.ppermute(first, "head", paired(0))
     prior = lax.dynamic_index_in_dim(prior_state[0], place, 0, False)
     gain = lax.dynamic_slice_in_dim(norm_gain, place * HD, HD, 1)
     attended = attend(packed, prior, gain, groups)
@@ -418,9 +426,7 @@
     across = [from_head(parts[0], 1), from_head(parts[1], -1)]
     rows = own.shape[0] // 2
     joined = [jnp.concatenate(line, axis=0) for line in lines([own[:rows], own[rows:]])]
-    first, second = halves(enc_weight[0])
-    _, across, first, second = lax.optimization_barrier((joined, across, first, second))
-    first = lax.ppermute(first, "head", paired(0))
+    _, second = lax.optimization_barrier((joined, second))
     second = lax.all_to_all(
         jnp.broadcast_to(second[None], (2, *second.shape)),
         "head",
@@ -432,9 +438,9 @@
     second = lax.dynamic_index_in_dim(second, odd, 0, False)
     weights = [weight, after, *across, before]
     layer_out = project(source, inverse, weights, planes(joined, near(joined)), residual[0])
+    layer_out, first = lax.optimization_barrier((layer_out, first))
     opposite = from_head(layer_out, 2)
     joined = [jnp.concatenate(line, axis=0) for line in lines([layer_out, opposite])]
-    joined, first = lax.optimization_barrier((joined, first))
     beside = near(joined)
     acc = encode(source, [enc_weight[0], first], joined, 0)
     beside, acc, second = lax.optimization_barrier((beside, acc, second))

time: 267 us -> 268 us (level)
  waiting for transfers between devices: 84.1 us -> 105 us
  Pallas kernels: 57 us -> 47.6 us
  starting transfers between devices: 88.5 us -> 79.6 us
    ppermute x28, waiting for transfers between devices: 26.6 us -> 62.8 us  [moved(): return lax.ppermute(x, 'seq', pairs)]
    ppermute x8, waiting for transfers between devices: 33.8 us -> 19.2 us  [from_head(): lax.ppermute(x, 'head', [((i + by) % groups, i) for i in range(groups)])]
    pallas_call x3, Pallas kernels: 35.7 us -> 26.4 us  [encode(): pl.pallas_call(functools.partial(encode_kernel, len(encoders), len(arrays...]
    ppermute x4, starting transfers between devices: 15.5 us -> 6.35 us  [from_section(): return lax.ppermute(x, ('section', 'head'), both)]
    all_to_all x1, waiting for transfers between devices: 0.01 us -> 6.86 us  [local(): lax.all_to_all(jnp.broadcast_to(second[None], (2, *second.shape)), 'head'...]
    ppermute x1, waiting for transfers between devices: 18.3 us -> 12.4 us  [local(): lax.ppermute(first_bias, 'head', paired(0))]
  transfers between devices with their start and end apart: 46 -> 46, of which waited for: 15 -> 18; matrix products, arithmetic and copies ran while one was open for 10% -> 11% of each run, Pallas kernels for 20% -> 16%
where the time goes in v8:
time: 268 us; the launch traced here: 267 us
  waiting for transfers between devices  105 us (39%)
  starting transfers between devices  79.6 us (30%)
  Pallas kernels  47.6 us (18%)
  local copies, waits for them, and re-layouts  33.1 us (12%)
    ppermute x28, waiting for transfers between devices, moved(): return lax.ppermute(x, 'seq', pairs)  62.8 us
    ppermute x28, starting transfers between devices, moved(): return lax.ppermute(x, 'seq', pairs)  39.1 us
    pallas_call x3, Pallas kernels, encode(): pl.pallas_call(functools.partial(encode_kernel, len(encoders), len(arrays...  26.4 us
    ppermute x8, waiting for transfers between devices, from_head(): lax.ppermute(x, 'head', [((i + by) % groups, i) for i in range(groups)])  19.2 us
    ppermute x1, waiting for transfers between devices, local(): lax.ppermute(first_bias, 'head', paired(0))  12.4 us
    slice x8, local copies, waits for them, and re-layouts, planes(): across = (moved(up[:middle], axis, 1), moved(down[middle:], axis, -1))  11.3 us
    pallas_call x1, Pallas kernels, project(): pl.pallas_call(functools.partial(project_kernel, len(arrays), 0, False),...  10.5 us
    ppermute x8, starting transfers between devices, from_head(): lax.ppermute(x, 'head', [((i + by) % groups, i) for i in range(groups)])  9.81 us
  transfers between devices with their start and end apart: 46, of which 18 were waited for; matrix products, arithmetic and copies ran while one was open for 11% of the time, Pallas kernels for 16%

profile of v8, /device:TPU:1, one launch (start us, length us, event | category | flops | bytes accessed | tf_op | source)
XLA Modules:
  0.0 267.0 jit_solution(2109996004706682973)
XLA Ops:
  0.6 3.4 %collective-permute-start = (bf16[2048,384]{1,0:T(8,128)(2,1)}, bf16[2048,384]{1,0:T(8,128)(2,1)}, u32[]{:S(2)}, u32[]{:S(2)}) collective-permute-start(bf16[2048,384]{1,0:T(8,128)(2,1)} %bitcast.66), channel_id=1, source_target_pairs={{1,0},{2,1},{3,2},{0,3},{5,4},{6,5},{7,6},{4,7},{9,8},{10,9},{11,1... | collective-permute-start | bytes 4718600 | tf_op jit(solution)/shard_map/ppermute | solution.py:371
  4.9 2.5 collective-permute-start.6
  8.1 1.6 shard_map.113
  10.9 7.9 %all-to-all-start = ((bf16[16,400,128]{2,1,0:T(8,128)(2,1)}), bf16[16,400,128]{2,1,0:T(8,128)(2,1)S(1)}, u32[]{:S(2)}, u32[]{:S(2)}) async-start(bf16[16,400,128]{2,1,0:T(8,128)(2,1)} %copy-done.2), calls=%async_computation | async-start | bytes 3276800 | tf_op jit(solution)/shard_map/all_to_all | solution.py:407
  19.1 5.9 %dynamic-slice_bitcast_fusion.1 = (bf16[6144,256]{1,0:T(8,128)(2,1)}, bf16[6144,256]{1,0:T(8,128)(2,1)}) fusion(bf16[1,6144,512]{2,1,0:T(8,128)(2,1)} %param.18, s32[]{:T(128)S(6)} %select_n.260, s32[]{:T(128)S(6)} %select_n.259), kind=kLoop, calls=%fused_computation.1 | loop fusion | bytes 12582920 | tf_op jit(solution)/shard_map/dynamic_slice | solution.py:394
  25.0 12.4 %collective-permute-done.5 = f32[1,256]{1,0:T(1,128)S(1)} collective-permute-done((f32[1,256]{1,0:T(1,128)S(1)}, f32[1,256]{1,0:T(1,128)S(1)}, u32[]{:S(2)}, u32[]{:S(2)}) %collective-permute-start.5) | collective-permute-done | bytes 1056 | tf_op jit(solution)/shard_map/ppermute | solution.py:400
  37.4 2.4 collective-permute-start.3
  41.6 2.7 collective-permute-done.4
  44.3 4.1 %shard_map.114 = bf16[4,512,128]{2,1,0:T(8,128)(2,1)} custom-call(bf16[16,400,128]{2,1,0:T(8,128)(2,1)S(1)} %all-to-all-done.packed_ref, f32[128,128]{1,0:T(8,128)S(1)} %dynamic-slice_bitcast_fusion.7.prior_ref, f32[1,128]{1,0:T(1,128)S(1)} %constant_dynamic-slice_fusion.gain_ref), custom_call_target="tpu_custom_call" | custom-call | tf_op jit(solution)/shard_map/pallas_call | solution.py:89
  48.4 3.5 %all-to-all-start.1 = ((bf16[4,512,128]{2,1,0:T(8,128)(2,1)}), bf16[4,512,128]{2,1,0:T(8,128)(2,1)S(1)}, u32[]{:S(2)}, u32[]{:S(2)}) async-start(bf16[4,512,128]{2,1,0:T(8,128)(2,1)} %shard_map.114), calls=%async_computation.1 | async-start | bytes 1048576 | tf_op jit(solution)/shard_map/all_to_all | solution.py:417
  51.9 2.1 slice.63
  54.1 2.1 slice.64
  56.2 1.4 collective-permute-start.23
  57.5 1.3 all-to-all-done.1
  58.9 1.7 collective-permute-start.16
  60.6 2.2 collective-permute-start.17
  62.8 1.2 collective-permute-start.18
  64.1 2.5 collective-permute-done.16
  66.5 2.4 collective-permute-done.17
  69.0 1.6 collective-permute-done.18
  70.7 1.4 collective-permute-start.19
  72.1 1.5 collective-permute-start.21
  73.6 1.4 collective-permute-start.10
  75.3 20.4 %collective-permute-done.10 = bf16[256,512]{1,0:T(8,128)(2,1)S(1)} collective-permute-done((bf16[256,512]{1,0:T(8,128)(2,1)S(1)}, bf16[256,512]{1,0:T(8,128)(2,1)S(1)}, u32[]{:S(2)}, u32[]{:S(2)}) %collective-permute-start.10) | collective-permute-done | bytes 262176 | tf_op jit(solution)/shard_map/ppermute | solution.py:324
  95.7 1.3 collective-permute-start.9
  97.0 8.3 %collective-permute-done.9 = bf16[256,512]{1,0:T(8,128)(2,1)S(1)} collective-permute-done((bf16[256,512]{1,0:T(8,128)(2,1)S(1)}, bf16[256,512]{1,0:T(8,128)(2,1)S(1)}, u32[]{:S(2)}, u32[]{:S(2)}) %collective-permute-start.9) | collective-permute-done | bytes 262176 | tf_op jit(solution)/shard_map/ppermute | solution.py:324
  105.4 2.7 collective-permute-start.14
  108.1 1.5 collective-permute-start.8
  109.5 3.1 %broadcast_in_dim.12 = bf16[2,6144,256]{2,1,0:T(8,128)(2,1)} broadcast(bf16[6144,256]{1,0:T(8,128)(2,1)S(1)} %copy-done.7), dimensions={1,2} | broadcast | bytes 9437184 | tf_op jit(solution)/shard_map/broadcast_in_dim | solution.py:431
  112.6 8.9 %all-to-all-start.2 = ((bf16[2,6144,256]{2,1,0:T(8,128)(2,1)}), bf16[2,6144,256]{2,1,0:T(8,128)(2,1)}, u32[]{:S(2)}, u32[]{:S(2)}) async-start(bf16[2,6144,256]{2,1,0:T(8,128)(2,1)} %broadcast_in_dim.12), calls=%async_computation.2 | async-start | bytes 12582912 | tf_op jit(solution)/shard_map/all_to_all | solution.py:430
  122.4 1.9 slice.87
  124.2 1.9 slice.84
  126.1 2.7 %collective-permute-start.22 = (bf16[512,512]{1,0:T(8,128)(2,1)}, bf16[512,512]{1,0:T(8,128)(2,1)}, u32[]{:S(2)}, u32[]{:S(2)}) collective-permute-start(bf16[512,512]{1,0:T(8,128)(2,1)} %slice.87), channel_id=1, source_target_pairs={{0,12},{4,0},{8,4},{12,8},{16,28},{20,16},{24,20},{28,24},{32,44},... | collective-permute-start | bytes 1572872 | tf_op jit(solution)/shard_map/ppermute | solution.py:324
  128.8 1.9 slice.85
  130.7 12.7 %collective-permute-done.7.refs_4_ = bf16[1024,384]{1,0:T(8,128)(2,1)} collective-permute-done((bf16[1024,384]{1,0:T(8,128)(2,1)}, bf16[1024,384]{1,0:T(8,128)(2,1)}, u32[]{:S(2)}, u32[]{:S(2)}) %collective-permute-start.7) | collective-permute-done | bytes 786464 | tf_op jit(solution)/shard_map/ppermute | solution.py:371
  143.4 1.6 collective-permute-start.13
  145.0 2.1 collective-permute-start.15
  147.3 10.5 %shard_map.115 = (f32[512,384]{1,0:T(8,128)S(1)}, f32[512,128]{1,0:T(8,128)S(1)}) custom-call(s32[32]{0:T(128)S(1)} %stack.98.refs_0_, f32[16,512]{1,0:T(8,128)S(1)} %pad_maximum_fusion.3.refs_1_, bf16[2048,384]{1,0:T(8,128)(2,1)} %bitcast.68, bf16[2048,384]{1,0:T(8,128)(2,1)} %collective-permute-done.refs_3_, ...), custom_call_target="tpu_custom_call" | custom-call | tf_op jit(solution)/shard_map/pallas_call | solution.py:229
  158.6 4.9 %shard_map.116 = bf16[512,384]{1,0:T(8,128)(2,1)S(1)} custom-call(s32[32]{0:T(128)S(1)} %stack.98.refs_0_, f32[16,512]{1,0:T(8,128)S(1)} %copy-done.5, bf16[2048,384]{1,0:T(8,128)(2,1)} %bitcast.69, bf16[2048,384]{1,0:T(8,128)(2,1)} %collective-permute-done.refs_3_, bf16[1024,384]{1,0:T(8,128)(2,1)} %collective-permute-done.7.refs_4_, ...), custom_call_target="tpu_custom_call" | custom-call | tf_op jit(solution)/shard_map/pallas_call | solution.py:238
  163.5 2.3 collective-permute-start.29
  165.8 1.3 collective-permute-start.24
  167.1 1.4 collective-permute-start.25
  168.5 1.6 collective-permute-start.26
  170.2 2.8 %collective-permute-done.29 = bf16[512,384]{1,0:T(8,128)(2,1)S(1)} collective-permute-done((bf16[512,384]{1,0:T(8,128)(2,1)S(1)}, bf16[512,384]{1,0:T(8,128)(2,1)S(1)}, u32[]{:S(2)}, u32[]{:S(2)}) %collective-permute-start.29) | collective-permute-done | bytes 393248 | tf_op jit(solution)/shard_map/ppermute | solution.py:371
  173.1 2.7 %collective-permute-start.31 = (bf16[512,384]{1,0:T(8,128)(2,1)S(1)}, bf16[512,384]{1,0:T(8,128)(2,1)S(1)}, u32[]{:S(2)}, u32[]{:S(2)}) collective-permute-start(bf16[512,384]{1,0:T(8,128)(2,1)S(1)} %collective-permute-done.29), channel_id=1, source_target_pairs={{0,48},{4,52},{8,56},{12,60},{16,0},{20,4},{24,8},{28,12},{32,16},... | collective-permute-start | bytes 1179656 | tf_op jit(solution)/shard_map/ppermute | solution.py:324
  175.9 8.1 %collective-permute-done.26 = bf16[512,384]{1,0:T(8,128)(2,1)S(1)} collective-permute-done((bf16[512,384]{1,0:T(8,128)(2,1)S(1)}, bf16[512,384]{1,0:T(8,128)(2,1)S(1)}, u32[]{:S(2)}, u32[]{:S(2)}) %collective-permute-start.26) | collective-permute-done | bytes 393248 | tf_op jit(solution)/shard_map/ppermute | solution.py:324
  184.2 2.7 collective-permute-start.28
  187.0 1.3 collective-permute-done.32
  188.4 1.4 collective-permute-start.33
  189.8 1.5 collective-permute-start.34
  191.3 6.9 %all-to-all-done.2 = bf16[2,6144,256]{2,1,0:T(8,128)(2,1)} async-done(((bf16[2,6144,256]{2,1,0:T(8,128)(2,1)}), bf16[2,6144,256]{2,1,0:T(8,128)(2,1)}, u32[]{:S(2)}, u32[]{:S(2)}) %all-to-all-start.2) | async-done | bytes 6291488 | tf_op jit(solution)/shard_map/all_to_all | solution.py:430
  198.1 3.8 %dynamic-slice_bitcast_fusion.refs_3_ = bf16[6144,256]{1,0:T(8,128)(2,1)} fusion(bf16[2,6144,256]{2,1,0:T(8,128)(2,1)} %all-to-all-done.2, s32[]{:T(128)S(6)} %select_n.271), kind=kLoop, calls=%fused_computation | loop fusion | bytes 6291460 | tf_op jit(solution)/shard_map/jit(dynamic_index_in_dim)/squeeze | solution.py:438
  201.9 5.7 %shard_map.117.refs_10_ = f32[1024,1024]{1,0:T(8,128)S(1)} custom-call(s32[32]{0:T(128)S(1)} %stack.98.refs_0_, bf16[6144,512]{1,0:T(8,128)(2,1)} %bitcast.63, bf16[6144,256]{1,0:T(8,128)(2,1)} %collective-permute-done.23.refs_2_, bf16[2048,384]{1,0:T(8,128)(2,1)S(1)} %constant_dynamic-update-slice_fusion.refs_3_.refs_4_, ...), custom_call_target="tpu_custom_call" | custom-call | tf_op jit(solution)/shard_map/pallas_call | solution.py:303
  207.7 18.2 %collective-permute-done.27.refs_6_ = bf16[2048,384]{1,0:T(8,128)(2,1)} collective-permute-done((bf16[2048,384]{1,0:T(8,128)(2,1)S(1)}, bf16[2048,384]{1,0:T(8,128)(2,1)}, u32[]{:S(2)}, u32[]{:S(2)}) %collective-permute-start.27) | collective-permute-done | bytes 1572896 | tf_op jit(solution)/shard_map/ppermute | solution.py:324
  225.9 1.2 slice.71
  227.4 1.2 slice.72
  228.6 3.0 %collective-permute-start.37 = (bf16[1024,384]{1,0:T(8,128)(2,1)S(1)}, bf16[1024,384]{1,0:T(8,128)(2,1)S(1)}, u32[]{:S(2)}, u32[]{:S(2)}) collective-permute-start(bf16[1024,384]{1,0:T(8,128)(2,1)S(1)} %slice.72), channel_id=1, source_target_pairs={{0,48},{4,52},{8,56},{12,60},{16,0},{20,4},{24,8},{28,12},{32,16},... | collective-permute-start | bytes 2359304 | tf_op jit(solution)/shard_map/ppermute | solution.py:324
  232.8 1.3 collective-permute-start.38
  235.4 1.5 collective-permute-start.39
  236.9 13.4 %shard_map.118.refs_8_ = f32[1024,1024]{1,0:T(8,128)S(1)} custom-call(s32[32]{0:T(128)S(1)} %stack.98.refs_0_, bf16[6144,512]{1,0:T(8,128)(2,1)} %bitcast.64, bf16[6144,256]{1,0:T(8,128)(2,1)} %collective-permute-done.23.refs_2_, bf16[6144,256]{1,0:T(8,128)(2,1)} %dynamic-slice_bitcast_fusion.refs_3_, ...), custom_call_target="tpu_custom_call" | custom-call | tf_op jit(solution)/shard_map/pallas_call | solution.py:303
  250.3 3.1 %collective-permute-start.35 = (bf16[1,512,384]{2,1,0:T(8,128)(2,1)S(1)}, bf16[1,512,384]{2,1,0:T(8,128)(2,1)S(1)}, u32[]{:S(2)}, u32[]{:S(2)}) collective-permute-start(bf16[1,512,384]{2,1,0:T(8,128)(2,1)S(1)} %bitcast.61), channel_id=1, source_target_pairs={{0,64},{1,65},{2,66},{3,67},{64,0},{65,1},{66,2},{67,3},{4,68},{5,... | collective-permute-start | bytes 1179656 | tf_op jit(solution)/shard_map/ppermute | solution.py:382
  253.4 7.3 %shard_map.119 = f32[16,1024]{1,0:T(8,128)S(1)} custom-call(s32[32]{0:T(128)S(1)} %stack.98.refs_0_, bf16[6144,512]{1,0:T(8,128)(2,1)} %bitcast.65, bf16[6144,256]{1,0:T(8,128)(2,1)} %collective-permute-done.23.refs_2_, bf16[6144,256]{1,0:T(8,128)(2,1)} %dynamic-slice_bitcast_fusion.refs_3_, bf16[1024,384]{1,0:T(8,128)(2,1)S(1)} %collective-permute-done.36.refs_4_, ...), custom_call_target="tpu_custom_call" | custom-call | tf_op jit(solution)/shard_map/pallas_call | solution.py:303
  260.7 1.4 collective-permute-start.41
  262.7 1.3 collective-permute-start.40
  (103 shorter events, 14.0 us)
Async XLA Ops:
  0.6 24.4 %copy-start = (f32[1,16,128,128]{3,2,1,0:T(8,128)S(1)}, f32[1,16,128,128]{3,2,1,0:T(8,128)}, u32[]{:S(2)}) copy-start(f32[1,16,128,128]{3,2,1,0:T(8,128)} %param.13) | copy-start | bytes 3145732
  0.6 43.6 %collective-permute-start = (bf16[2048,384]{1,0:T(8,128)(2,1)}, bf16[2048,384]{1,0:T(8,128)(2,1)}, u32[]{:S(2)}, u32[]{:S(2)}) collective-permute-start(bf16[2048,384]{1,0:T(8,128)(2,1)} %bitcast.66), channel_id=1, source_target_pairs={{1,0},{2,1},{3,2},{0,3},{5,4},{6,5},{7,6},{4,7},{9,8},{10,9},{11,1... | collective-permute-start | bytes 4718600 | tf_op jit(solution)/shard_map/ppermute | solution.py:371
  4.0 40.3 %collective-permute-start.1 = (bf16[2048,384]{1,0:T(8,128)(2,1)}, bf16[2048,384]{1,0:T(8,128)(2,1)}, u32[]{:S(2)}, u32[]{:S(2)}) collective-permute-start(bf16[2048,384]{1,0:T(8,128)(2,1)} %bitcast.67), channel_id=1, source_target_pairs={{3,0},{0,1},{1,2},{2,3},{7,4},{4,5},{5,6},{6,7},{11,8},{8,9},{9,10... | collective-permute-start | bytes 4718600 | tf_op jit(solution)/shard_map/ppermute | solution.py:371
  4.7 32.7 %collective-permute-start.5 = (f32[1,256]{1,0:T(1,128)S(1)}, f32[1,256]{1,0:T(1,128)S(1)}, u32[]{:S(2)}, u32[]{:S(2)}) collective-permute-start(f32[1,256]{1,0:T(1,128)S(1)} %get-tuple-element.68), channel_id=1, source_target_pairs={{0,1},{1,0},{2,3},{3,2},{4,5},{5,4},{6,7},{7,6},{8,9},{9,8},{10,11... | collective-permute-start | bytes 3080 | tf_op jit(solution)/shard_map/ppermute | solution.py:400
  4.9 35.6 %collective-permute-start.6 = (f32[1,256]{1,0:T(1,128)S(1)}, f32[1,256]{1,0:T(1,128)S(1)}, u32[]{:S(2)}, u32[]{:S(2)}) collective-permute-start(f32[1,256]{1,0:T(1,128)S(1)} %get-tuple-element.69), channel_id=1, source_target_pairs={{1,2},{2,1},{3,0},{0,3},{5,6},{6,5},{7,4},{4,7},{9,10},{10,9},{11,... | collective-permute-start | bytes 3080 | tf_op jit(solution)/shard_map/ppermute | solution.py:401
  7.4 0.7 copy-start.6
  9.7 1.2 copy-start.2
  10.9 7.9 %copy-start.8 = (f32[1,2048]{1,0:T(1,128)S(1)}, f32[1,2048]{1,0:T(1,128)}, u32[]{:S(2)}) copy-start(f32[1,2048]{1,0:T(1,128)} %param.15) | copy-start | bytes 24580
  10.9 33.4 %all-to-all-start = ((bf16[16,400,128]{2,1,0:T(8,128)(2,1)}), bf16[16,400,128]{2,1,0:T(8,128)(2,1)S(1)}, u32[]{:S(2)}, u32[]{:S(2)}) async-start(bf16[16,400,128]{2,1,0:T(8,128)(2,1)} %copy-done.2), calls=%async_computation | async-start | bytes 3276800 | tf_op jit(solution)/shard_map/all_to_all | solution.py:407
  18.8 21.7 %collective-permute-start.2 = (f32[1,2048]{1,0:T(1,128)S(1)}, f32[1,2048]{1,0:T(1,128)S(1)}, u32[]{:S(2)}, u32[]{:S(2)}) collective-permute-start(f32[1,2048]{1,0:T(1,128)S(1)} %copy-done.8), channel_id=1, source_target_pairs={{1,0},{2,1},{3,2},{0,3},{5,4},{6,5},{7,6},{4,7},{9,8},{10,9},{11,1... | collective-permute-start | bytes 24584 | tf_op jit(solution)/shard_map/ppermute | solution.py:371
  19.1 21.4 %copy-start.9 = (f32[1,512]{1,0:T(1,128)S(1)}, f32[1,512]{1,0:T(1,128)}, u32[]{:S(2)}) copy-start(f32[1,512]{1,0:T(1,128)} %param.19) | copy-start | bytes 6148
  37.4 4.1 %collective-permute-start.3 = (f32[1,2048]{1,0:T(1,128)S(1)}, f32[1,2048]{1,0:T(1,128)S(1)}, u32[]{:S(2)}, u32[]{:S(2)}) collective-permute-start(f32[1,2048]{1,0:T(1,128)S(1)} %copy-done.8), channel_id=1, source_target_pairs={{2,0},{3,1},{0,2},{1,3},{6,4},{7,5},{4,6},{5,7},{10,8},{11,9},{8,1... | collective-permute-start | bytes 24584 | tf_op jit(solution)/shard_map/ppermute | solution.py:371
  40.5 3.7 %collective-permute-start.4 = (f32[1,2048]{1,0:T(1,128)S(1)}, f32[1,2048]{1,0:T(1,128)S(1)}, u32[]{:S(2)}, u32[]{:S(2)}) collective-permute-start(f32[1,2048]{1,0:T(1,128)S(1)} %copy-done.8), channel_id=1, source_target_pairs={{3,0},{0,1},{1,2},{2,3},{7,4},{4,5},{5,6},{6,7},{11,8},{8,9},{9,10... | collective-permute-start | bytes 24584 | tf_op jit(solution)/shard_map/ppermute | solution.py:371
  44.3 103.0 %copy-start.4 = (f32[16,512]{1,0:T(8,128)}, f32[16,512]{1,0:T(8,128)S(1)}, u32[]{:S(2)}) copy-start(f32[16,512]{1,0:T(8,128)S(1)} %pad_maximum_fusion.3.refs_1_) | copy-start | bytes 98308
  48.4 10.4 %all-to-all-start.1 = ((bf16[4,512,128]{2,1,0:T(8,128)(2,1)}), bf16[4,512,128]{2,1,0:T(8,128)(2,1)S(1)}, u32[]{:S(2)}, u32[]{:S(2)}) async-start(bf16[4,512,128]{2,1,0:T(8,128)(2,1)} %shard_map.114), calls=%async_computation.1 | async-start | bytes 1048576 | tf_op jit(solution)/shard_map/all_to_all | solution.py:417
  56.2 107.4 %collective-permute-start.23 = (bf16[6144,256]{1,0:T(8,128)(2,1)}, bf16[6144,256]{1,0:T(8,128)(2,1)}, u32[]{:S(2)}, u32[]{:S(2)}) collective-permute-start(bf16[6144,256]{1,0:T(8,128)(2,1)} %get-tuple-element.33), channel_id=1, source_target_pairs={{0,1},{1,0},{2,3},{3,2},{4,5},{5,4},{6,7},{7,6},{8,9},{9,8},{10,11... | collective-permute-start | bytes 9437192 | tf_op jit(solution)/shard_map/ppermute | solution.py:412
  58.9 7.6 %collective-permute-start.16 = (bf16[256,512]{1,0:T(8,128)(2,1)S(1)}, bf16[256,512]{1,0:T(8,128)(2,1)S(1)}, u32[]{:S(2)}, u32[]{:S(2)}) collective-permute-start(bf16[256,512]{1,0:T(8,128)(2,1)S(1)} %get-tuple-element.48), channel_id=1, source_target_pairs={{0,16},{4,20},{8,24},{12,28},{16,32},{20,36},{24,40},{28,44},{32,4... | collective-permute-start | bytes 786440 | tf_op jit(solution)/shard_map/ppermute | solution.py:324
  60.6 8.3 %collective-permute-start.17 = (bf16[256,512]{1,0:T(8,128)(2,1)S(1)}, bf16[256,512]{1,0:T(8,128)(2,1)S(1)}, u32[]{:S(2)}, u32[]{:S(2)}) collective-permute-start(bf16[256,512]{1,0:T(8,128)(2,1)S(1)} %get-tuple-element.48), channel_id=1, source_target_pairs={{0,48},{4,52},{8,56},{12,60},{16,0},{20,4},{24,8},{28,12},{32,16},... | collective-permute-start | bytes 786440 | tf_op jit(solution)/shard_map/ppermute | solution.py:324
  62.8 7.8 %collective-permute-start.18 = (bf16[256,512]{1,0:T(8,128)(2,1)S(1)}, bf16[256,512]{1,0:T(8,128)(2,1)S(1)}, u32[]{:S(2)}, u32[]{:S(2)}) collective-permute-start(bf16[256,512]{1,0:T(8,128)(2,1)S(1)} %get-tuple-element.48), channel_id=1, source_target_pairs={{0,32},{4,36},{8,40},{12,44},{16,48},{20,52},{24,56},{28,60},{32,0... | collective-permute-start | bytes 786440 | tf_op jit(solution)/shard_map/ppermute | solution.py:324
  70.6 38.9 %copy-start.7 = (bf16[6144,256]{1,0:T(8,128)(2,1)S(1)}, bf16[6144,256]{1,0:T(8,128)(2,1)}, u32[]{:S(2)}) copy-start(bf16[6144,256]{1,0:T(8,128)(2,1)} %get-tuple-element.36) | copy-start | bytes 9437188
  70.7 37.4 %collective-permute-start.19 = (bf16[1024,512]{1,0:T(8,128)(2,1)S(1)}, bf16[1024,512]{1,0:T(8,128)(2,1)S(1)}, u32[]{:S(2)}, u32[]{:S(2)}) collective-permute-start(bf16[1024,512]{1,0:T(8,128)(2,1)S(1)} %pad_maximum_fusion.1.refs_8_), channel_id=1, source_target_pairs={{0,4},{4,8},{8,12},{12,0},{16,20},{20,24},{24,28},{28,16},{32,36},... | collective-permute-start | bytes 3145736 | tf_op jit(solution)/shard_map/ppermute | solution.py:324
  72.1 36.0 %collective-permute-start.21 = (bf16[1024,512]{1,0:T(8,128)(2,1)S(1)}, bf16[1024,512]{1,0:T(8,128)(2,1)}, u32[]{:S(2)}, u32[]{:S(2)}) collective-permute-start(bf16[1024,512]{1,0:T(8,128)(2,1)S(1)} %pad_maximum_fusion.1.refs_8_), channel_id=1, source_target_pairs={{0,12},{4,0},{8,4},{12,8},{16,28},{20,16},{24,20},{28,24},{32,44},... | collective-permute-start | bytes 3145736 | tf_op jit(solution)/shard_map/ppermute | solution.py:324
  73.6 22.1 %collective-permute-start.10 = (bf16[256,512]{1,0:T(8,128)(2,1)S(1)}, bf16[256,512]{1,0:T(8,128)(2,1)S(1)}, u32[]{:S(2)}, u32[]{:S(2)}) collective-permute-start(bf16[256,512]{1,0:T(8,128)(2,1)S(1)} %get-tuple-element.49), channel_id=1, source_target_pairs={{0,12},{4,0},{8,4},{12,8},{16,28},{20,16},{24,20},{28,24},{32,44},... | collective-permute-start | bytes 786440 | tf_op jit(solution)/shard_map/ppermute | solution.py:324
  75.0 22.0 %collective-permute-start.11 = (bf16[256,512]{1,0:T(8,128)(2,1)S(1)}, bf16[256,512]{1,0:T(8,128)(2,1)S(1)}, u32[]{:S(2)}, u32[]{:S(2)}) collective-permute-start(bf16[256,512]{1,0:T(8,128)(2,1)S(1)} %get-tuple-element.49), channel_id=1, source_target_pairs={{0,8},{4,12},{8,0},{12,4},{16,24},{20,28},{24,16},{28,20},{32,40},... | collective-permute-start | bytes 786440 | tf_op jit(solution)/shard_map/ppermute | solution.py:324
  95.7 9.6 %collective-permute-start.9 = (bf16[256,512]{1,0:T(8,128)(2,1)S(1)}, bf16[256,512]{1,0:T(8,128)(2,1)S(1)}, u32[]{:S(2)}, u32[]{:S(2)}) collective-permute-start(bf16[256,512]{1,0:T(8,128)(2,1)S(1)} %get-tuple-element.49), channel_id=1, source_target_pairs={{0,4},{4,8},{8,12},{12,0},{16,20},{20,24},{24,28},{28,16},{32,36},... | collective-permute-start | bytes 786440 | tf_op jit(solution)/shard_map/ppermute | solution.py:324
  105.3 18.9 %collective-permute-start.12 = (bf16[1024,512]{1,0:T(8,128)(2,1)S(1)}, bf16[1024,512]{1,0:T(8,128)(2,1)}, u32[]{:S(2)}, u32[]{:S(2)}) collective-permute-start(bf16[1024,512]{1,0:T(8,128)(2,1)S(1)} %pad_maximum_fusion.refs_7_), channel_id=1, source_target_pairs={{0,16},{4,20},{8,24},{12,28},{16,32},{20,36},{24,40},{28,44},{32,4... | collective-permute-start | bytes 3145736 | tf_op jit(solution)/shard_map/ppermute | solution.py:324
  105.4 20.7 %collective-permute-start.14 = (bf16[1024,512]{1,0:T(8,128)(2,1)S(1)}, bf16[1024,512]{1,0:T(8,128)(2,1)}, u32[]{:S(2)}, u32[]{:S(2)}) collective-permute-start(bf16[1024,512]{1,0:T(8,128)(2,1)S(1)} %pad_maximum_fusion.refs_7_), channel_id=1, source_target_pairs={{0,48},{4,52},{8,56},{12,60},{16,0},{20,4},{24,8},{28,12},{32,16},... | collective-permute-start | bytes 3145736 | tf_op jit(solution)/shard_map/ppermute | solution.py:324
  108.0 35.4 %collective-permute-start.7 = (bf16[1024,384]{1,0:T(8,128)(2,1)}, bf16[1024,384]{1,0:T(8,128)(2,1)}, u32[]{:S(2)}, u32[]{:S(2)}) collective-permute-start(bf16[1024,384]{1,0:T(8,128)(2,1)} %slice.63), channel_id=1, source_target_pairs={{1,0},{2,1},{3,2},{0,3},{5,4},{6,5},{7,6},{4,7},{9,8},{10,9},{11,1... | collective-permute-start | bytes 2359304 | tf_op jit(solution)/shard_map/ppermute | solution.py:371
  108.1 37.0 %collective-permute-start.8 = (bf16[1024,384]{1,0:T(8,128)(2,1)}, bf16[1024,384]{1,0:T(8,128)(2,1)}, u32[]{:S(2)}, u32[]{:S(2)}) collective-permute-start(bf16[1024,384]{1,0:T(8,128)(2,1)} %slice.64), channel_id=1, source_target_pairs={{3,0},{0,1},{1,2},{2,3},{7,4},{4,5},{5,6},{6,7},{11,8},{8,9},{9,10... | collective-permute-start | bytes 2359304 | tf_op jit(solution)/shard_map/ppermute | solution.py:371
  112.6 85.5 %all-to-all-start.2 = ((bf16[2,6144,256]{2,1,0:T(8,128)(2,1)}), bf16[2,6144,256]{2,1,0:T(8,128)(2,1)}, u32[]{:S(2)}, u32[]{:S(2)}) async-start(bf16[2,6144,256]{2,1,0:T(8,128)(2,1)} %broadcast_in_dim.12), calls=%async_computation.2 | async-start | bytes 12582912 | tf_op jit(solution)/shard_map/all_to_all | solution.py:430
  124.2 33.5 %collective-permute-start.20 = (bf16[512,512]{1,0:T(8,128)(2,1)}, bf16[512,512]{1,0:T(8,128)(2,1)}, u32[]{:S(2)}, u32[]{:S(2)}) collective-permute-start(bf16[512,512]{1,0:T(8,128)(2,1)} %slice.86), channel_id=1, source_target_pairs={{0,4},{4,8},{8,12},{12,0},{16,20},{20,24},{24,28},{28,16},{32,36},... | collective-permute-start | bytes 1572872 | tf_op jit(solution)/shard_map/ppermute | solution.py:324
  126.1 31.7 %collective-permute-start.22 = (bf16[512,512]{1,0:T(8,128)(2,1)}, bf16[512,512]{1,0:T(8,128)(2,1)}, u32[]{:S(2)}, u32[]{:S(2)}) collective-permute-start(bf16[512,512]{1,0:T(8,128)(2,1)} %slice.87), channel_id=1, source_target_pairs={{0,12},{4,0},{8,4},{12,8},{16,28},{20,16},{24,20},{28,24},{32,44},... | collective-permute-start | bytes 1572872 | tf_op jit(solution)/shard_map/ppermute | solution.py:324
  143.4 14.4 %collective-permute-start.13 = (bf16[512,512]{1,0:T(8,128)(2,1)}, bf16[512,512]{1,0:T(8,128)(2,1)}, u32[]{:S(2)}, u32[]{:S(2)}) collective-permute-start(bf16[512,512]{1,0:T(8,128)(2,1)} %slice.84), channel_id=1, source_target_pairs={{0,16},{4,20},{8,24},{12,28},{16,32},{20,36},{24,40},{28,44},{32,4... | collective-permute-start | bytes 1572872 | tf_op jit(solution)/shard_map/ppermute | solution.py:324
  145.0 12.8 %collective-permute-start.15 = (bf16[512,512]{1,0:T(8,128)(2,1)}, bf16[512,512]{1,0:T(8,128)(2,1)}, u32[]{:S(2)}, u32[]{:S(2)}) collective-permute-start(bf16[512,512]{1,0:T(8,128)(2,1)} %slice.85), channel_id=1, source_target_pairs={{0,48},{4,52},{8,56},{12,60},{16,0},{20,4},{24,8},{28,12},{32,16},... | collective-permute-start | bytes 1572872 | tf_op jit(solution)/shard_map/ppermute | solution.py:324
  147.3 10.5 %copy-start.3 = (bf16[1,512,384]{2,1,0:T(8,128)(2,1)S(1)}, bf16[1,512,384]{2,1,0:T(8,128)(2,1)}, u32[]{:S(2)}) copy-start(bf16[1,512,384]{2,1,0:T(8,128)(2,1)} %param.16) | copy-start | bytes 1179652
  157.8 0.8 copy-start.5
  163.5 9.5 %collective-permute-start.29 = (bf16[512,384]{1,0:T(8,128)(2,1)S(1)}, bf16[512,384]{1,0:T(8,128)(2,1)S(1)}, u32[]{:S(2)}, u32[]{:S(2)}) collective-permute-start(bf16[512,384]{1,0:T(8,128)(2,1)S(1)} %shard_map.116), channel_id=1, source_target_pairs={{2,0},{3,1},{0,2},{1,3},{6,4},{7,5},{4,6},{5,7},{10,8},{11,9},{8,1... | collective-permute-start | bytes 1179656 | tf_op jit(solution)/shard_map/ppermute | solution.py:371
  165.8 9.9 %collective-permute-start.24 = (bf16[512,384]{1,0:T(8,128)(2,1)S(1)}, bf16[512,384]{1,0:T(8,128)(2,1)S(1)}, u32[]{:S(2)}, u32[]{:S(2)}) collective-permute-start(bf16[512,384]{1,0:T(8,128)(2,1)S(1)} %shard_map.116), channel_id=1, source_target_pairs={{0,4},{4,8},{8,12},{12,0},{16,20},{20,24},{24,28},{28,16},{32,36},... | collective-permute-start | bytes 1179656 | tf_op jit(solution)/shard_map/ppermute | solution.py:324
  167.1 8.7 %collective-permute-start.25 = (bf16[512,384]{1,0:T(8,128)(2,1)S(1)}, bf16[512,384]{1,0:T(8,128)(2,1)S(1)}, u32[]{:S(2)}, u32[]{:S(2)}) collective-permute-start(bf16[512,384]{1,0:T(8,128)(2,1)S(1)} %shard_map.116), channel_id=1, source_target_pairs={{0,12},{4,0},{8,4},{12,8},{16,28},{20,16},{24,20},{28,24},{32,44},... | collective-permute-start | bytes 1179656 | tf_op jit(solution)/shard_map/ppermute | solution.py:324
  168.5 15.5 %collective-permute-start.26 = (bf16[512,384]{1,0:T(8,128)(2,1)S(1)}, bf16[512,384]{1,0:T(8,128)(2,1)S(1)}, u32[]{:S(2)}, u32[]{:S(2)}) collective-permute-start(bf16[512,384]{1,0:T(8,128)(2,1)S(1)} %shard_map.116), channel_id=1, source_target_pairs={{0,8},{4,12},{8,0},{12,4},{16,24},{20,28},{24,16},{28,20},{32,40},... | collective-permute-start | bytes 1179656 | tf_op jit(solution)/shard_map/ppermute | solution.py:324
  173.1 13.8 %collective-permute-start.30 = (bf16[512,384]{1,0:T(8,128)(2,1)S(1)}, bf16[512,384]{1,0:T(8,128)(2,1)S(1)}, u32[]{:S(2)}, u32[]{:S(2)}) collective-permute-start(bf16[512,384]{1,0:T(8,128)(2,1)S(1)} %collective-permute-done.29), channel_id=1, source_target_pairs={{0,16},{4,20},{8,24},{12,28},{16,32},{20,36},{24,40},{28,44},{32,4... | collective-permute-start | bytes 1179656 | tf_op jit(solution)/shard_map/ppermute | solution.py:324
  173.1 13.9 %collective-permute-start.31 = (bf16[512,384]{1,0:T(8,128)(2,1)S(1)}, bf16[512,384]{1,0:T(8,128)(2,1)S(1)}, u32[]{:S(2)}, u32[]{:S(2)}) collective-permute-start(bf16[512,384]{1,0:T(8,128)(2,1)S(1)} %collective-permute-done.29), channel_id=1, source_target_pairs={{0,48},{4,52},{8,56},{12,60},{16,0},{20,4},{24,8},{28,12},{32,16},... | collective-permute-start | bytes 1179656 | tf_op jit(solution)/shard_map/ppermute | solution.py:324
  175.7 12.6 %collective-permute-start.32 = (bf16[512,384]{1,0:T(8,128)(2,1)S(1)}, bf16[512,384]{1,0:T(8,128)(2,1)S(1)}, u32[]{:S(2)}, u32[]{:S(2)}) collective-permute-start(bf16[512,384]{1,0:T(8,128)(2,1)S(1)} %collective-permute-done.29), channel_id=1, source_target_pairs={{0,32},{4,36},{8,40},{12,44},{16,48},{20,52},{24,56},{28,60},{32,0... | collective-permute-start | bytes 1179656 | tf_op jit(solution)/shard_map/ppermute | solution.py:324
  184.1 41.8 %collective-permute-start.27 = (bf16[2048,384]{1,0:T(8,128)(2,1)S(1)}, bf16[2048,384]{1,0:T(8,128)(2,1)}, u32[]{:S(2)}, u32[]{:S(2)}) collective-permute-start(bf16[2048,384]{1,0:T(8,128)(2,1)S(1)} %constant_dynamic-update-slice_fusion.refs_3_.refs_4_), channel_id=1, source_target_pairs={{0,16},{4,20},{8,24},{12,28},{16,32},{20,36},{24,40},{28,44},{32,4... | collective-permute-start | bytes 4718600 | tf_op jit(solution)/shard_map/ppermute | solution.py:324
  184.2 41.7 %collective-permute-start.28 = (bf16[2048,384]{1,0:T(8,128)(2,1)S(1)}, bf16[2048,384]{1,0:T(8,128)(2,1)}, u32[]{:S(2)}, u32[]{:S(2)}) collective-permute-start(bf16[2048,384]{1,0:T(8,128)(2,1)S(1)} %constant_dynamic-update-slice_fusion.refs_3_.refs_4_), channel_id=1, source_target_pairs={{0,48},{4,52},{8,56},{12,60},{16,0},{20,4},{24,8},{28,12},{32,16},... | collective-permute-start | bytes 4718600 | tf_op jit(solution)/shard_map/ppermute | solution.py:324
  188.4 37.5 %collective-permute-start.33 = (bf16[2048,384]{1,0:T(8,128)(2,1)S(1)}, bf16[2048,384]{1,0:T(8,128)(2,1)}, u32[]{:S(2)}, u32[]{:S(2)}) collective-permute-start(bf16[2048,384]{1,0:T(8,128)(2,1)S(1)} %constant_dynamic-update-slice_fusion.4.refs_4_.refs_5_), channel_id=1, source_target_pairs={{0,4},{4,8},{8,12},{12,0},{16,20},{20,24},{24,28},{28,16},{32,36},... | collective-permute-start | bytes 4718600 | tf_op jit(solution)/shard_map/ppermute | solution.py:324
  189.8 36.1 %collective-permute-start.34 = (bf16[2048,384]{1,0:T(8,128)(2,1)S(1)}, bf16[2048,384]{1,0:T(8,128)(2,1)}, u32[]{:S(2)}, u32[]{:S(2)}) collective-permute-start(bf16[2048,384]{1,0:T(8,128)(2,1)S(1)} %constant_dynamic-update-slice_fusion.4.refs_4_.refs_5_), channel_id=1, source_target_pairs={{0,12},{4,0},{8,4},{12,8},{16,28},{20,16},{24,20},{28,24},{32,44},... | collective-permute-start | bytes 4718600 | tf_op jit(solution)/shard_map/ppermute | solution.py:324
  227.1 26.3 %collective-permute-start.36 = (bf16[1024,384]{1,0:T(8,128)(2,1)S(1)}, bf16[1024,384]{1,0:T(8,128)(2,1)S(1)}, u32[]{:S(2)}, u32[]{:S(2)}) collective-permute-start(bf16[1024,384]{1,0:T(8,128)(2,1)S(1)} %slice.71), channel_id=1, source_target_pairs={{0,16},{4,20},{8,24},{12,28},{16,32},{20,36},{24,40},{28,44},{32,4... | collective-permute-start | bytes 2359304 | tf_op jit(solution)/shard_map/ppermute | solution.py:324
  228.6 24.8 %collective-permute-start.37 = (bf16[1024,384]{1,0:T(8,128)(2,1)S(1)}, bf16[1024,384]{1,0:T(8,128)(2,1)S(1)}, u32[]{:S(2)}, u32[]{:S(2)}) collective-permute-start(bf16[1024,384]{1,0:T(8,128)(2,1)S(1)} %slice.72), channel_id=1, source_target_pairs={{0,48},{4,52},{8,56},{12,60},{16,0},{20,4},{24,8},{28,12},{32,16},... | collective-permute-start | bytes 2359304 | tf_op jit(solution)/shard_map/ppermute | solution.py:324
  232.8 20.5 %collective-permute-start.38 = (bf16[1024,384]{1,0:T(8,128)(2,1)S(1)}, bf16[1024,384]{1,0:T(8,128)(2,1)S(1)}, u32[]{:S(2)}, u32[]{:S(2)}) collective-permute-start(bf16[1024,384]{1,0:T(8,128)(2,1)S(1)} %slice.73), channel_id=1, source_target_pairs={{0,4},{4,8},{8,12},{12,0},{16,20},{20,24},{24,28},{28,16},{32,36},... | collective-permute-start | bytes 2359304 | tf_op jit(solution)/shard_map/ppermute | solution.py:324
  235.4 18.0 %collective-permute-start.39 = (bf16[1024,384]{1,0:T(8,128)(2,1)S(1)}, bf16[1024,384]{1,0:T(8,128)(2,1)S(1)}, u32[]{:S(2)}, u32[]{:S(2)}) collective-permute-start(bf16[1024,384]{1,0:T(8,128)(2,1)S(1)} %slice.74), channel_id=1, source_target_pairs={{0,12},{4,0},{8,4},{12,8},{16,28},{20,16},{24,20},{28,24},{32,44},... | collective-permute-start | bytes 2359304 | tf_op jit(solution)/shard_map/ppermute | solution.py:324
  250.3 12.4 %collective-permute-start.35 = (bf16[1,512,384]{2,1,0:T(8,128)(2,1)S(1)}, bf16[1,512,384]{2,1,0:T(8,128)(2,1)S(1)}, u32[]{:S(2)}, u32[]{:S(2)}) collective-permute-start(bf16[1,512,384]{2,1,0:T(8,128)(2,1)S(1)} %bitcast.61), channel_id=1, source_target_pairs={{0,64},{1,65},{2,66},{3,67},{64,0},{65,1},{66,2},{67,3},{4,68},{5,... | collective-permute-start | bytes 1179656 | tf_op jit(solution)/shard_map/ppermute | solution.py:382
  253.4 13.6 %copy-start.1 = (f32[1,16,128,128]{3,2,1,0:T(8,128)S(1)}, f32[1,16,128,128]{3,2,1,0:T(8,128)}, u32[]{:S(2)}) copy-start(f32[1,16,128,128]{3,2,1,0:T(8,128)} %param.13) | copy-start | bytes 3145732
  260.7 4.4 %collective-permute-start.41 = (bf16[16,256]{1,0:T(8,128)(2,1)S(1)}, bf16[16,256]{1,0:T(8,128)(2,1)S(1)}, u32[]{:S(2)}, u32[]{:S(2)}) collective-permute-start(bf16[16,256]{1,0:T(8,128)(2,1)S(1)} %get-tuple-element.58), channel_id=1, source_target_pairs={{1,66},{2,65},{3,64},{0,67},{65,2},{66,1},{67,0},{64,3},{5,70},{6,... | collective-permute-start | bytes 24584 | tf_op jit(solution)/shard_map/ppermute | solution.py:382
  262.1 3.4 %collective-permute-start.42 = (bf16[16,256]{1,0:T(8,128)(2,1)S(1)}, bf16[16,256]{1,0:T(8,128)(2,1)S(1)}, u32[]{:S(2)}, u32[]{:S(2)}) collective-permute-start(bf16[16,256]{1,0:T(8,128)(2,1)S(1)} %get-tuple-element.59), channel_id=1, source_target_pairs={{0,65},{1,64},{2,67},{3,66},{64,1},{65,0},{66,3},{67,2},{4,69},{5,... | collective-permute-start | bytes 24584 | tf_op jit(solution)/shard_map/ppermute | solution.py:382
  262.7 2.8 %collective-permute-start.40 = (bf16[16,512]{1,0:T(8,128)(2,1)S(1)}, bf16[16,512]{1,0:T(8,128)(2,1)S(1)}, u32[]{:S(2)}, u32[]{:S(2)}) collective-permute-start(bf16[16,512]{1,0:T(8,128)(2,1)S(1)} %slice.88), channel_id=1, source_target_pairs={{0,64},{1,65},{2,66},{3,67},{64,0},{65,1},{66,2},{67,3},{4,68},{5,... | collective-permute-start | bytes 49160 | tf_op jit(solution)/shard_map/ppermute | solution.py:382

commit v9 on v8

--- a/solution.py
+++ b/solution.py
@@ -422,11 +422,11 @@
         ],
         axis=1,
     )
-    own, *parts = lax.optimization_barrier((own, after[:middle], before[middle:]))
-    across = [from_head(parts[0], 1), from_head(parts[1], -1)]
+    across = [from_head(after[:middle], 1), from_head(before[middle:], -1)]
+    own, across = lax.optimization_barrier((own, across))
     rows = own.shape[0] // 2
     joined = [jnp.concatenate(line, axis=0) for line in lines([own[:rows], own[rows:]])]
-    _, second = lax.optimization_barrier((joined, second))
+    *joined, second = lax.optimization_barrier((*joined, second))
     second = lax.all_to_all(
         jnp.broadcast_to(second[None], (2, *second.shape)),
         "head",

time: 268 us -> 314 us (1.17)
  waiting for transfers between devices: 105 us -> 144 us
  starting transfers between devices: 79.6 us -> 84.2 us
    all_to_all x1, waiting for transfers between devices: 1.26 us -> 78.1 us  [local(): own = lax.all_to_all(attended, 'head', 0, 0, tiled=True)]
    ppermute x28, waiting for transfers between devices: 62.8 us -> 39.5 us  [moved(): return lax.ppermute(x, 'seq', pairs)]
    ppermute x8, waiting for transfers between devices: 19.2 us -> 5.28 us  [from_head(): lax.ppermute(x, 'head', [((i + by) % groups, i) for i in range(groups)])]
    ppermute x4, starting transfers between devices: 6.35 us -> 9.89 us  [from_section(): return lax.ppermute(x, ('section', 'head'), both)]
  transfers between devices with their start and end apart: 46 -> 46, of which waited for: 18 -> 20; matrix products, arithmetic and copies ran while one was open for 11% -> 7% of each run, Pallas kernels for 16% -> 15%
where the time goes in v9:
time: 314 us; the launch traced here: 313 us
  waiting for transfers between devices  144 us (46%)
  starting transfers between devices  84.2 us (27%)
  Pallas kernels  47.6 us (15%)
  local copies, waits for them, and re-layouts  35.2 us (11%)
    all_to_all x1, waiting for transfers between devices, local(): own = lax.all_to_all(attended, 'head', 0, 0, tiled=True)  78.1 us
    ppermute x28, waiting for transfers between devices, moved(): return lax.ppermute(x, 'seq', pairs)  39.5 us
    ppermute x28, starting transfers between devices, moved(): return lax.ppermute(x, 'seq', pairs)  39.2 us
    pallas_call x3, Pallas kernels, encode(): pl.pallas_call(functools.partial(encode_kernel, len(encoders), len(arrays...  26.4 us
    ppermute x1, waiting for transfers between devices, local(): lax.ppermute(first_bias, 'head', paired(0))  12.7 us
    ppermute x8, starting transfers between devices, from_head(): lax.ppermute(x, 'head', [((i + by) % groups, i) for i in range(groups)])  12.3 us
    slice x8, local copies, waits for them, and re-layouts, planes(): across = (moved(up[:middle], axis, 1), moved(down[middle:], axis, -1))  11.6 us
    pallas_call x1, Pallas kernels, project(): pl.pallas_call(functools.partial(project_kernel, len(arrays), 0, False),...  10.4 us
  transfers between devices with their start and end apart: 46, of which 20 were waited for; matrix products, arithmetic and copies ran while one was open for 7% of the time, Pallas kernels for 15%

profile of v9, /device:TPU:1, one launch (start us, length us, event | category | flops | bytes accessed | tf_op | source)
XLA Modules:
  0.0 312.8 jit_solution(3068677305016976233)
XLA Ops:
  0.6 2.1 collective-permute-start.1
  2.8 1.4 collective-permute-start
  4.9 1.8 collective-permute-start.6
  6.7 1.3 collective-permute-start.3
  8.7 1.6 shard_map.113
  10.4 1.2 copy-done.4
  11.6 7.9 %all-to-all-start = ((bf16[16,400,128]{2,1,0:T(8,128)(2,1)}), bf16[16,400,128]{2,1,0:T(8,128)(2,1)S(1)}, u32[]{:S(2)}, u32[]{:S(2)}) async-start(bf16[16,400,128]{2,1,0:T(8,128)(2,1)} %copy-done.4), calls=%async_computation | async-start | bytes 3276800 | tf_op jit(solution)/shard_map/all_to_all | solution.py:407
  19.5 5.9 %dynamic-slice_bitcast_fusion.1 = (bf16[6144,256]{1,0:T(8,128)(2,1)}, bf16[6144,256]{1,0:T(8,128)(2,1)}) fusion(bf16[1,6144,512]{2,1,0:T(8,128)(2,1)} %param.18, s32[]{:T(128)S(6)} %select_n.260, s32[]{:T(128)S(6)} %select_n.259), kind=kLoop, calls=%fused_computation.1 | loop fusion | bytes 12582920 | tf_op jit(solution)/shard_map/dynamic_slice | solution.py:394
  25.3 12.7 %collective-permute-done.5 = f32[1,256]{1,0:T(1,128)S(1)} collective-permute-done((f32[1,256]{1,0:T(1,128)S(1)}, f32[1,256]{1,0:T(1,128)S(1)}, u32[]{:S(2)}, u32[]{:S(2)}) %collective-permute-start.5) | collective-permute-done | bytes 1056 | tf_op jit(solution)/shard_map/ppermute | solution.py:400
  38.0 1.6 collective-permute-start.2
  40.6 3.0 collective-permute-done.4
  43.7 2.1 slice.63
  45.8 2.1 slice.64
  47.9 2.7 collective-permute-start.7
  50.7 4.1 %shard_map.114 = bf16[4,512,128]{2,1,0:T(8,128)(2,1)} custom-call(bf16[16,400,128]{2,1,0:T(8,128)(2,1)S(1)} %all-to-all-done.packed_ref, f32[128,128]{1,0:T(8,128)S(1)} %dynamic-slice_bitcast_fusion.7.prior_ref, f32[1,128]{1,0:T(1,128)S(1)} %constant_dynamic-slice_fusion.gain_ref), custom_call_target="tpu_custom_call" | custom-call | tf_op jit(solution)/shard_map/pallas_call | solution.py:89
  54.9 3.5 %all-to-all-start.1 = ((bf16[4,512,128]{2,1,0:T(8,128)(2,1)}), bf16[4,512,128]{2,1,0:T(8,128)(2,1)S(1)}, u32[]{:S(2)}, u32[]{:S(2)}) async-start(bf16[4,512,128]{2,1,0:T(8,128)(2,1)} %shard_map.114), calls=%async_computation.1 | async-start | bytes 1048576 | tf_op jit(solution)/shard_map/all_to_all | solution.py:417
  58.4 78.1 %all-to-all-done.1 = bf16[4,512,128]{2,1,0:T(8,128)(2,1)S(1)} async-done(((bf16[4,512,128]{2,1,0:T(8,128)(2,1)}), bf16[4,512,128]{2,1,0:T(8,128)(2,1)S(1)}, u32[]{:S(2)}, u32[]{:S(2)}) %all-to-all-start.1) | async-done | bytes 524320 | tf_op jit(solution)/shard_map/all_to_all | solution.py:417
  136.6 3.3 %collective-permute-start.14 = (bf16[256,512]{1,0:T(8,128)(2,1)S(1)}, bf16[256,512]{1,0:T(8,128)(2,1)S(1)}, u32[]{:S(2)}, u32[]{:S(2)}) collective-permute-start(bf16[256,512]{1,0:T(8,128)(2,1)S(1)} %get-tuple-element.52), channel_id=1, source_target_pairs={{0,32},{4,36},{8,40},{12,44},{16,48},{20,52},{24,56},{28,60},{32,0... | collective-permute-start | bytes 786440 | tf_op jit(solution)/shard_map/ppermute | solution.py:324
  141.4 2.9 collective-permute-start.11
  144.3 2.1 collective-permute-start.10
  146.4 1.8 collective-permute-done.13
  148.2 1.3 collective-permute-start.9
  150.0 1.6 collective-permute-done.10
  151.6 5.2 %collective-permute-done.9 = bf16[256,512]{1,0:T(8,128)(2,1)S(1)} collective-permute-done((bf16[256,512]{1,0:T(8,128)(2,1)S(1)}, bf16[256,512]{1,0:T(8,128)(2,1)S(1)}, u32[]{:S(2)}, u32[]{:S(2)}) %collective-permute-start.9) | collective-permute-done | bytes 262176 | tf_op jit(solution)/shard_map/ppermute | solution.py:324
  156.8 2.9 collective-permute-start.17
  159.7 1.8 collective-permute-start.21
  161.5 3.1 broadcast_in_dim.12
  164.6 9.3 %all-to-all-start.2 = ((bf16[2,6144,256]{2,1,0:T(8,128)(2,1)}), bf16[2,6144,256]{2,1,0:T(8,128)(2,1)}, u32[]{:S(2)}, u32[]{:S(2)}) async-start(bf16[2,6144,256]{2,1,0:T(8,128)(2,1)} %broadcast_in_dim.12), calls=%async_computation.2 | async-start | bytes 12582912 | tf_op jit(solution)/shard_map/all_to_all | solution.py:430
  173.9 4.0 %collective-permute-done.17.refs_11_ = bf16[1024,512]{1,0:T(8,128)(2,1)S(1)} collective-permute-done((bf16[1024,512]{1,0:T(8,128)(2,1)S(1)}, bf16[1024,512]{1,0:T(8,128)(2,1)S(1)}, u32[]{:S(2)}, u32[]{:S(2)}) %collective-permute-start.17) | collective-permute-done | bytes 1048608 | tf_op jit(solution)/shard_map/ppermute | solution.py:324
  178.8 3.5 %collective-permute-start.18 = (bf16[512,512]{1,0:T(8,128)(2,1)}, bf16[512,512]{1,0:T(8,128)(2,1)}, u32[]{:S(2)}, u32[]{:S(2)}) collective-permute-start(bf16[512,512]{1,0:T(8,128)(2,1)} %slice.85), channel_id=1, source_target_pairs={{0,48},{4,52},{8,56},{12,60},{16,0},{20,4},{24,8},{28,12},{32,16},... | collective-permute-start | bytes 1572872 | tf_op jit(solution)/shard_map/ppermute | solution.py:324
  182.3 1.9 slice.84
  184.2 1.9 slice.87
  186.0 2.4 collective-permute-start.22
  188.4 1.9 slice.86
  190.4 10.4 %shard_map.115 = (f32[512,384]{1,0:T(8,128)S(1)}, f32[512,128]{1,0:T(8,128)S(1)}) custom-call(s32[32]{0:T(128)S(1)} %stack.98.refs_0_, f32[16,512]{1,0:T(8,128)S(1)} %pad_maximum_fusion.3.refs_1_, bf16[2048,384]{1,0:T(8,128)(2,1)} %bitcast.68, bf16[2048,384]{1,0:T(8,128)(2,1)} %collective-permute-done.refs_3_, ...), custom_call_target="tpu_custom_call" | custom-call | tf_op jit(solution)/shard_map/pallas_call | solution.py:229
  201.7 4.9 %shard_map.116 = bf16[512,384]{1,0:T(8,128)(2,1)S(1)} custom-call(s32[32]{0:T(128)S(1)} %stack.98.refs_0_, f32[16,512]{1,0:T(8,128)S(1)} %copy-done.7, bf16[2048,384]{1,0:T(8,128)(2,1)} %bitcast.69, bf16[2048,384]{1,0:T(8,128)(2,1)} %collective-permute-done.refs_3_, bf16[1024,384]{1,0:T(8,128)(2,1)} %collective-permute-done.7.refs_4_, ...), custom_call_target="tpu_custom_call" | custom-call | tf_op jit(solution)/shard_map/pallas_call | solution.py:238
  206.7 3.3 %collective-permute-start.29 = (bf16[512,384]{1,0:T(8,128)(2,1)S(1)}, bf16[512,384]{1,0:T(8,128)(2,1)S(1)}, u32[]{:S(2)}, u32[]{:S(2)}) collective-permute-start(bf16[512,384]{1,0:T(8,128)(2,1)S(1)} %shard_map.116), channel_id=1, source_target_pairs={{2,0},{3,1},{0,2},{1,3},{6,4},{7,5},{4,6},{5,7},{10,8},{11,9},{8,1... | collective-permute-start | bytes 1179656 | tf_op jit(solution)/shard_map/ppermute | solution.py:371
  210.0 2.7 collective-permute-start.25
  212.7 1.2 collective-permute-start.26
  213.9 1.3 collective-permute-done.29
  215.2 1.2 collective-permute-start.32
  216.4 1.5 collective-permute-start.31
  218.6 2.7 collective-permute-done.25
  221.3 5.0 %collective-permute-done.26 = bf16[512,384]{1,0:T(8,128)(2,1)S(1)} collective-permute-done((bf16[512,384]{1,0:T(8,128)(2,1)S(1)}, bf16[512,384]{1,0:T(8,128)(2,1)S(1)}, u32[]{:S(2)}, u32[]{:S(2)}) %collective-permute-start.26) | collective-permute-done | bytes 393248 | tf_op jit(solution)/shard_map/ppermute | solution.py:324
  226.3 2.2 collective-permute-start.28
  228.6 1.2 collective-permute-done.30
  229.8 1.1 collective-permute-done.31
  231.1 2.1 collective-permute-start.34
  233.2 5.7 %shard_map.117.refs_10_ = f32[1024,1024]{1,0:T(8,128)S(1)} custom-call(s32[32]{0:T(128)S(1)} %stack.98.refs_0_, bf16[6144,512]{1,0:T(8,128)(2,1)} %bitcast.63, bf16[6144,256]{1,0:T(8,128)(2,1)} %collective-permute-done.23.refs_2_, bf16[2048,384]{1,0:T(8,128)(2,1)S(1)} %constant_dynamic-update-slice_fusion.refs_3_.refs_4_, ...), custom_call_target="tpu_custom_call" | custom-call | tf_op jit(solution)/shard_map/pallas_call | solution.py:303
  239.0 1.9 copy-done.2
  240.9 5.6 %all-to-all-done.2 = bf16[2,6144,256]{2,1,0:T(8,128)(2,1)} async-done(((bf16[2,6144,256]{2,1,0:T(8,128)(2,1)}), bf16[2,6144,256]{2,1,0:T(8,128)(2,1)}, u32[]{:S(2)}, u32[]{:S(2)}) %all-to-all-start.2) | async-done | bytes 6291488 | tf_op jit(solution)/shard_map/all_to_all | solution.py:430
  246.5 3.8 %dynamic-slice_bitcast_fusion.refs_3_ = bf16[6144,256]{1,0:T(8,128)(2,1)} fusion(bf16[2,6144,256]{2,1,0:T(8,128)(2,1)} %all-to-all-done.2, s32[]{:T(128)S(6)} %select_n.271), kind=kLoop, calls=%fused_computation | loop fusion | bytes 6291460 | tf_op jit(solution)/shard_map/jit(dynamic_index_in_dim)/squeeze | solution.py:438
  250.3 16.1 %collective-permute-done.28.refs_8_ = bf16[2048,384]{1,0:T(8,128)(2,1)} collective-permute-done((bf16[2048,384]{1,0:T(8,128)(2,1)S(1)}, bf16[2048,384]{1,0:T(8,128)(2,1)}, u32[]{:S(2)}, u32[]{:S(2)}) %collective-permute-start.28) | collective-permute-done | bytes 1572896 | tf_op jit(solution)/shard_map/ppermute | solution.py:324
  266.5 1.2 slice.74
  267.8 1.4 slice.72
  269.1 1.3 slice.73
  270.5 1.2 slice.71
  272.5 3.0 collective-permute-start.37
  275.5 2.6 collective-permute-start.39
  278.1 13.4 %shard_map.118.refs_8_ = f32[1024,1024]{1,0:T(8,128)S(1)} custom-call(s32[32]{0:T(128)S(1)} %stack.98.refs_0_, bf16[6144,512]{1,0:T(8,128)(2,1)} %bitcast.64, bf16[6144,256]{1,0:T(8,128)(2,1)} %collective-permute-done.23.refs_2_, bf16[6144,256]{1,0:T(8,128)(2,1)} %dynamic-slice_bitcast_fusion.refs_3_, ...), custom_call_target="tpu_custom_call" | custom-call | tf_op jit(solution)/shard_map/pallas_call | solution.py:303
  291.5 6.4 %collective-permute-start.35 = (bf16[1,512,384]{2,1,0:T(8,128)(2,1)S(1)}, bf16[1,512,384]{2,1,0:T(8,128)(2,1)S(1)}, u32[]{:S(2)}, u32[]{:S(2)}) collective-permute-start(bf16[1,512,384]{2,1,0:T(8,128)(2,1)S(1)} %bitcast.61), channel_id=1, source_target_pairs={{0,64},{1,65},{2,66},{3,67},{64,0},{65,1},{66,2},{67,3},{4,68},{5,... | collective-permute-start | bytes 1179656 | tf_op jit(solution)/shard_map/ppermute | solution.py:382
  297.9 7.3 %shard_map.119 = f32[16,1024]{1,0:T(8,128)S(1)} custom-call(s32[32]{0:T(128)S(1)} %stack.98.refs_0_, bf16[6144,512]{1,0:T(8,128)(2,1)} %bitcast.65, bf16[6144,256]{1,0:T(8,128)(2,1)} %collective-permute-done.23.refs_2_, bf16[6144,256]{1,0:T(8,128)(2,1)} %dynamic-slice_bitcast_fusion.refs_3_, bf16[1024,384]{1,0:T(8,128)(2,1)S(1)} %collective-permute-done.36.refs_4_, ...), custom_call_target="tpu_custom_call" | custom-call | tf_op jit(solution)/shard_map/pallas_call | solution.py:303
  305.2 3.0 collective-permute-start.41
  309.6 1.7 collective-permute-done.42
  (107 shorter events, 11.4 us)
Async XLA Ops:
  0.6 50.0 %copy-start = (f32[1,16,128,128]{3,2,1,0:T(8,128)S(1)}, f32[1,16,128,128]{3,2,1,0:T(8,128)}, u32[]{:S(2)}) copy-start(f32[1,16,128,128]{3,2,1,0:T(8,128)} %param.13) | copy-start | bytes 3145732
  0.6 43.0 %collective-permute-start.1 = (bf16[2048,384]{1,0:T(8,128)(2,1)}, bf16[2048,384]{1,0:T(8,128)(2,1)}, u32[]{:S(2)}, u32[]{:S(2)}) collective-permute-start(bf16[2048,384]{1,0:T(8,128)(2,1)} %bitcast.66), channel_id=1, source_target_pairs={{3,0},{0,1},{1,2},{2,3},{7,4},{4,5},{5,6},{6,7},{11,8},{8,9},{9,10... | collective-permute-start | bytes 4718600 | tf_op jit(solution)/shard_map/ppermute | solution.py:371
  2.8 40.9 %collective-permute-start = (bf16[2048,384]{1,0:T(8,128)(2,1)}, bf16[2048,384]{1,0:T(8,128)(2,1)}, u32[]{:S(2)}, u32[]{:S(2)}) collective-permute-start(bf16[2048,384]{1,0:T(8,128)(2,1)} %bitcast.67), channel_id=1, source_target_pairs={{1,0},{2,1},{3,2},{0,3},{5,4},{6,5},{7,6},{4,7},{9,8},{10,9},{11,1... | collective-permute-start | bytes 4718600 | tf_op jit(solution)/shard_map/ppermute | solution.py:371
  4.8 33.2 %collective-permute-start.5 = (f32[1,256]{1,0:T(1,128)S(1)}, f32[1,256]{1,0:T(1,128)S(1)}, u32[]{:S(2)}, u32[]{:S(2)}) collective-permute-start(f32[1,256]{1,0:T(1,128)S(1)} %get-tuple-element.72), channel_id=1, source_target_pairs={{0,1},{1,0},{2,3},{3,2},{4,5},{5,4},{6,7},{7,6},{8,9},{9,8},{10,11... | collective-permute-start | bytes 3080 | tf_op jit(solution)/shard_map/ppermute | solution.py:400
  4.9 34.7 %collective-permute-start.6 = (f32[1,256]{1,0:T(1,128)S(1)}, f32[1,256]{1,0:T(1,128)S(1)}, u32[]{:S(2)}, u32[]{:S(2)}) collective-permute-start(f32[1,256]{1,0:T(1,128)S(1)} %get-tuple-element.73), channel_id=1, source_target_pairs={{1,2},{2,1},{3,0},{0,3},{5,6},{6,5},{7,4},{4,7},{9,10},{10,9},{11,... | collective-permute-start | bytes 3080 | tf_op jit(solution)/shard_map/ppermute | solution.py:401
  6.7 32.9 %collective-permute-start.3 = (f32[1,2048]{1,0:T(1,128)}, f32[1,2048]{1,0:T(1,128)S(1)}, u32[]{:S(2)}, u32[]{:S(2)}) collective-permute-start(f32[1,2048]{1,0:T(1,128)} %param.15), channel_id=1, source_target_pairs={{2,0},{3,1},{0,2},{1,3},{6,4},{7,5},{4,6},{5,7},{10,8},{11,9},{8,1... | collective-permute-start | bytes 24584 | tf_op jit(solution)/shard_map/ppermute | solution.py:371
  8.1 0.7 copy-start.8
  10.4 1.2 copy-start.4
  11.6 32.1 %all-to-all-start = ((bf16[16,400,128]{2,1,0:T(8,128)(2,1)}), bf16[16,400,128]{2,1,0:T(8,128)(2,1)S(1)}, u32[]{:S(2)}, u32[]{:S(2)}) async-start(bf16[16,400,128]{2,1,0:T(8,128)(2,1)} %copy-done.4), calls=%async_computation | async-start | bytes 3276800 | tf_op jit(solution)/shard_map/all_to_all | solution.py:407
  19.4 5.9 %copy-start.10 = (f32[1,2048]{1,0:T(1,128)S(1)}, f32[1,2048]{1,0:T(1,128)}, u32[]{:S(2)}) copy-start(f32[1,2048]{1,0:T(1,128)} %param.15) | copy-start | bytes 24580
  19.5 20.2 %copy-start.11 = (f32[1,512]{1,0:T(1,128)S(1)}, f32[1,512]{1,0:T(1,128)}, u32[]{:S(2)}) copy-start(f32[1,512]{1,0:T(1,128)} %param.19) | copy-start | bytes 6148
  38.0 2.5 collective-permute-start.2
  39.6 4.0 %collective-permute-start.4 = (f32[1,2048]{1,0:T(1,128)S(1)}, f32[1,2048]{1,0:T(1,128)S(1)}, u32[]{:S(2)}, u32[]{:S(2)}) collective-permute-start(f32[1,2048]{1,0:T(1,128)S(1)} %copy-done.10), channel_id=1, source_target_pairs={{3,0},{0,1},{1,2},{2,3},{7,4},{4,5},{5,6},{6,7},{11,8},{8,9},{9,10... | collective-permute-start | bytes 24584 | tf_op jit(solution)/shard_map/ppermute | solution.py:371
  43.7 146.7 %copy-start.6 = (f32[16,512]{1,0:T(8,128)}, f32[16,512]{1,0:T(8,128)S(1)}, u32[]{:S(2)}) copy-start(f32[16,512]{1,0:T(8,128)S(1)} %pad_maximum_fusion.3.refs_1_) | copy-start | bytes 98308
  47.9 88.7 %collective-permute-start.8 = (bf16[1024,384]{1,0:T(8,128)(2,1)}, bf16[1024,384]{1,0:T(8,128)(2,1)}, u32[]{:S(2)}, u32[]{:S(2)}) collective-permute-start(bf16[1024,384]{1,0:T(8,128)(2,1)} %slice.64), channel_id=1, source_target_pairs={{3,0},{0,1},{1,2},{2,3},{7,4},{4,5},{5,6},{6,7},{11,8},{8,9},{9,10... | collective-permute-start | bytes 2359304 | tf_op jit(solution)/shard_map/ppermute | solution.py:371
  47.9 88.7 %collective-permute-start.7 = (bf16[1024,384]{1,0:T(8,128)(2,1)}, bf16[1024,384]{1,0:T(8,128)(2,1)}, u32[]{:S(2)}, u32[]{:S(2)}) collective-permute-start(bf16[1024,384]{1,0:T(8,128)(2,1)} %slice.63), channel_id=1, source_target_pairs={{1,0},{2,1},{3,2},{0,3},{5,4},{6,5},{7,6},{4,7},{9,8},{10,9},{11,1... | collective-permute-start | bytes 2359304 | tf_op jit(solution)/shard_map/ppermute | solution.py:371
  50.6 156.0 %collective-permute-start.23 = (bf16[6144,256]{1,0:T(8,128)(2,1)}, bf16[6144,256]{1,0:T(8,128)(2,1)}, u32[]{:S(2)}, u32[]{:S(2)}) collective-permute-start(bf16[6144,256]{1,0:T(8,128)(2,1)} %get-tuple-element.37), channel_id=1, source_target_pairs={{0,1},{1,0},{2,3},{3,2},{4,5},{5,4},{6,7},{7,6},{8,9},{9,8},{10,11... | collective-permute-start | bytes 9437192 | tf_op jit(solution)/shard_map/ppermute | solution.py:412
  54.9 81.6 %all-to-all-start.1 = ((bf16[4,512,128]{2,1,0:T(8,128)(2,1)}), bf16[4,512,128]{2,1,0:T(8,128)(2,1)S(1)}, u32[]{:S(2)}, u32[]{:S(2)}) async-start(bf16[4,512,128]{2,1,0:T(8,128)(2,1)} %shard_map.114), calls=%async_computation.1 | async-start | bytes 1048576 | tf_op jit(solution)/shard_map/all_to_all | solution.py:417
  136.6 7.7 %collective-permute-start.14 = (bf16[256,512]{1,0:T(8,128)(2,1)S(1)}, bf16[256,512]{1,0:T(8,128)(2,1)S(1)}, u32[]{:S(2)}, u32[]{:S(2)}) collective-permute-start(bf16[256,512]{1,0:T(8,128)(2,1)S(1)} %get-tuple-element.52), channel_id=1, source_target_pairs={{0,32},{4,36},{8,40},{12,44},{16,48},{20,52},{24,56},{28,60},{32,0... | collective-permute-start | bytes 786440 | tf_op jit(solution)/shard_map/ppermute | solution.py:324
  139.9 8.3 %collective-permute-start.13 = (bf16[256,512]{1,0:T(8,128)(2,1)S(1)}, bf16[256,512]{1,0:T(8,128)(2,1)S(1)}, u32[]{:S(2)}, u32[]{:S(2)}) collective-permute-start(bf16[256,512]{1,0:T(8,128)(2,1)S(1)} %get-tuple-element.52), channel_id=1, source_target_pairs={{0,48},{4,52},{8,56},{12,60},{16,0},{20,4},{24,8},{28,12},{32,16},... | collective-permute-start | bytes 786440 | tf_op jit(solution)/shard_map/ppermute | solution.py:324
  140.4 9.6 %collective-permute-start.12 = (bf16[256,512]{1,0:T(8,128)(2,1)S(1)}, bf16[256,512]{1,0:T(8,128)(2,1)S(1)}, u32[]{:S(2)}, u32[]{:S(2)}) collective-permute-start(bf16[256,512]{1,0:T(8,128)(2,1)S(1)} %get-tuple-element.52), channel_id=1, source_target_pairs={{0,16},{4,20},{8,24},{12,28},{16,32},{20,36},{24,40},{28,44},{32,4... | collective-permute-start | bytes 786440 | tf_op jit(solution)/shard_map/ppermute | solution.py:324
  141.4 8.6 %collective-permute-start.11 = (bf16[256,512]{1,0:T(8,128)(2,1)S(1)}, bf16[256,512]{1,0:T(8,128)(2,1)S(1)}, u32[]{:S(2)}, u32[]{:S(2)}) collective-permute-start(bf16[256,512]{1,0:T(8,128)(2,1)S(1)} %get-tuple-element.53), channel_id=1, source_target_pairs={{0,8},{4,12},{8,0},{12,4},{16,24},{20,28},{24,16},{28,20},{32,40},... | collective-permute-start | bytes 786440 | tf_op jit(solution)/shard_map/ppermute | solution.py:324
  144.3 7.3 %collective-permute-start.10 = (bf16[256,512]{1,0:T(8,128)(2,1)S(1)}, bf16[256,512]{1,0:T(8,128)(2,1)S(1)}, u32[]{:S(2)}, u32[]{:S(2)}) collective-permute-start(bf16[256,512]{1,0:T(8,128)(2,1)S(1)} %get-tuple-element.53), channel_id=1, source_target_pairs={{0,12},{4,0},{8,4},{12,8},{16,28},{20,16},{24,20},{28,24},{32,44},... | collective-permute-start | bytes 786440 | tf_op jit(solution)/shard_map/ppermute | solution.py:324
  148.2 8.5 %collective-permute-start.9 = (bf16[256,512]{1,0:T(8,128)(2,1)S(1)}, bf16[256,512]{1,0:T(8,128)(2,1)S(1)}, u32[]{:S(2)}, u32[]{:S(2)}) collective-permute-start(bf16[256,512]{1,0:T(8,128)(2,1)S(1)} %get-tuple-element.53), channel_id=1, source_target_pairs={{0,4},{4,8},{8,12},{12,0},{16,20},{20,24},{24,28},{28,16},{32,36},... | collective-permute-start | bytes 786440 | tf_op jit(solution)/shard_map/ppermute | solution.py:324
  149.9 11.6 %copy-start.9 = (bf16[6144,256]{1,0:T(8,128)(2,1)S(1)}, bf16[6144,256]{1,0:T(8,128)(2,1)}, u32[]{:S(2)}) copy-start(bf16[6144,256]{1,0:T(8,128)(2,1)} %get-tuple-element.40) | copy-start | bytes 9437188
  156.8 21.1 %collective-permute-start.17 = (bf16[1024,512]{1,0:T(8,128)(2,1)S(1)}, bf16[1024,512]{1,0:T(8,128)(2,1)S(1)}, u32[]{:S(2)}, u32[]{:S(2)}) collective-permute-start(bf16[1024,512]{1,0:T(8,128)(2,1)S(1)} %pad_maximum_fusion.refs_7_), channel_id=1, source_target_pairs={{0,48},{4,52},{8,56},{12,60},{16,0},{20,4},{24,8},{28,12},{32,16},... | collective-permute-start | bytes 3145736 | tf_op jit(solution)/shard_map/ppermute | solution.py:324
  159.7 22.6 %collective-permute-start.15 = (bf16[1024,512]{1,0:T(8,128)(2,1)S(1)}, bf16[1024,512]{1,0:T(8,128)(2,1)}, u32[]{:S(2)}, u32[]{:S(2)}) collective-permute-start(bf16[1024,512]{1,0:T(8,128)(2,1)S(1)} %pad_maximum_fusion.refs_7_), channel_id=1, source_target_pairs={{0,16},{4,20},{8,24},{12,28},{16,32},{20,36},{24,40},{28,44},{32,4... | collective-permute-start | bytes 3145736 | tf_op jit(solution)/shard_map/ppermute | solution.py:324
  159.7 24.4 %collective-permute-start.21 = (bf16[1024,512]{1,0:T(8,128)(2,1)S(1)}, bf16[1024,512]{1,0:T(8,128)(2,1)}, u32[]{:S(2)}, u32[]{:S(2)}) collective-permute-start(bf16[1024,512]{1,0:T(8,128)(2,1)S(1)} %pad_maximum_fusion.1.refs_8_), channel_id=1, source_target_pairs={{0,12},{4,0},{8,4},{12,8},{16,28},{20,16},{24,20},{28,24},{32,44},... | collective-permute-start | bytes 3145736 | tf_op jit(solution)/shard_map/ppermute | solution.py:324
  161.5 26.9 %collective-permute-start.19 = (bf16[1024,512]{1,0:T(8,128)(2,1)S(1)}, bf16[1024,512]{1,0:T(8,128)(2,1)}, u32[]{:S(2)}, u32[]{:S(2)}) collective-permute-start(bf16[1024,512]{1,0:T(8,128)(2,1)S(1)} %pad_maximum_fusion.1.refs_8_), channel_id=1, source_target_pairs={{0,4},{4,8},{8,12},{12,0},{16,20},{20,24},{24,28},{28,16},{32,36},... | collective-permute-start | bytes 3145736 | tf_op jit(solution)/shard_map/ppermute | solution.py:324
  164.6 81.9 %all-to-all-start.2 = ((bf16[2,6144,256]{2,1,0:T(8,128)(2,1)}), bf16[2,6144,256]{2,1,0:T(8,128)(2,1)}, u32[]{:S(2)}, u32[]{:S(2)}) async-start(bf16[2,6144,256]{2,1,0:T(8,128)(2,1)} %broadcast_in_dim.12), calls=%async_computation.2 | async-start | bytes 12582912 | tf_op jit(solution)/shard_map/all_to_all | solution.py:430
  178.8 22.1 %collective-permute-start.18 = (bf16[512,512]{1,0:T(8,128)(2,1)}, bf16[512,512]{1,0:T(8,128)(2,1)}, u32[]{:S(2)}, u32[]{:S(2)}) collective-permute-start(bf16[512,512]{1,0:T(8,128)(2,1)} %slice.85), channel_id=1, source_target_pairs={{0,48},{4,52},{8,56},{12,60},{16,0},{20,4},{24,8},{28,12},{32,16},... | collective-permute-start | bytes 1572872 | tf_op jit(solution)/shard_map/ppermute | solution.py:324
  184.2 16.7 %collective-permute-start.16 = (bf16[512,512]{1,0:T(8,128)(2,1)}, bf16[512,512]{1,0:T(8,128)(2,1)}, u32[]{:S(2)}, u32[]{:S(2)}) collective-permute-start(bf16[512,512]{1,0:T(8,128)(2,1)} %slice.84), channel_id=1, source_target_pairs={{0,16},{4,20},{8,24},{12,28},{16,32},{20,36},{24,40},{28,44},{32,4... | collective-permute-start | bytes 1572872 | tf_op jit(solution)/shard_map/ppermute | solution.py:324
  186.0 14.9 %collective-permute-start.22 = (bf16[512,512]{1,0:T(8,128)(2,1)}, bf16[512,512]{1,0:T(8,128)(2,1)}, u32[]{:S(2)}, u32[]{:S(2)}) collective-permute-start(bf16[512,512]{1,0:T(8,128)(2,1)} %slice.87), channel_id=1, source_target_pairs={{0,12},{4,0},{8,4},{12,8},{16,28},{20,16},{24,20},{28,24},{32,44},... | collective-permute-start | bytes 1572872 | tf_op jit(solution)/shard_map/ppermute | solution.py:324
  190.3 10.6 %collective-permute-start.20 = (bf16[512,512]{1,0:T(8,128)(2,1)}, bf16[512,512]{1,0:T(8,128)(2,1)}, u32[]{:S(2)}, u32[]{:S(2)}) collective-permute-start(bf16[512,512]{1,0:T(8,128)(2,1)} %slice.86), channel_id=1, source_target_pairs={{0,4},{4,8},{8,12},{12,0},{16,20},{20,24},{24,28},{28,16},{32,36},... | collective-permute-start | bytes 1572872 | tf_op jit(solution)/shard_map/ppermute | solution.py:324
  190.4 10.5 %copy-start.5 = (bf16[1,512,384]{2,1,0:T(8,128)(2,1)S(1)}, bf16[1,512,384]{2,1,0:T(8,128)(2,1)}, u32[]{:S(2)}) copy-start(bf16[1,512,384]{2,1,0:T(8,128)(2,1)} %param.16) | copy-start | bytes 1179652
  200.9 0.8 copy-start.7
  206.7 8.6 %collective-permute-start.29 = (bf16[512,384]{1,0:T(8,128)(2,1)S(1)}, bf16[512,384]{1,0:T(8,128)(2,1)S(1)}, u32[]{:S(2)}, u32[]{:S(2)}) collective-permute-start(bf16[512,384]{1,0:T(8,128)(2,1)S(1)} %shard_map.116), channel_id=1, source_target_pairs={{2,0},{3,1},{0,2},{1,3},{6,4},{7,5},{4,6},{5,7},{10,8},{11,9},{8,1... | collective-permute-start | bytes 1179656 | tf_op jit(solution)/shard_map/ppermute | solution.py:371
  210.0 8.3 %collective-permute-start.24 = (bf16[512,384]{1,0:T(8,128)(2,1)S(1)}, bf16[512,384]{1,0:T(8,128)(2,1)S(1)}, u32[]{:S(2)}, u32[]{:S(2)}) collective-permute-start(bf16[512,384]{1,0:T(8,128)(2,1)S(1)} %shard_map.116), channel_id=1, source_target_pairs={{0,4},{4,8},{8,12},{12,0},{16,20},{20,24},{24,28},{28,16},{32,36},... | collective-permute-start | bytes 1179656 | tf_op jit(solution)/shard_map/ppermute | solution.py:324
  210.0 11.3 %collective-permute-start.25 = (bf16[512,384]{1,0:T(8,128)(2,1)S(1)}, bf16[512,384]{1,0:T(8,128)(2,1)S(1)}, u32[]{:S(2)}, u32[]{:S(2)}) collective-permute-start(bf16[512,384]{1,0:T(8,128)(2,1)S(1)} %shard_map.116), channel_id=1, source_target_pairs={{0,12},{4,0},{8,4},{12,8},{16,28},{20,16},{24,20},{28,24},{32,44},... | collective-permute-start | bytes 1179656 | tf_op jit(solution)/shard_map/ppermute | solution.py:324
  212.7 13.6 %collective-permute-start.26 = (bf16[512,384]{1,0:T(8,128)(2,1)S(1)}, bf16[512,384]{1,0:T(8,128)(2,1)S(1)}, u32[]{:S(2)}, u32[]{:S(2)}) collective-permute-start(bf16[512,384]{1,0:T(8,128)(2,1)S(1)} %shard_map.116), channel_id=1, source_target_pairs={{0,8},{4,12},{8,0},{12,4},{16,24},{20,28},{24,16},{28,20},{32,40},... | collective-permute-start | bytes 1179656 | tf_op jit(solution)/shard_map/ppermute | solution.py:324
  215.2 15.8 %collective-permute-start.32 = (bf16[512,384]{1,0:T(8,128)(2,1)S(1)}, bf16[512,384]{1,0:T(8,128)(2,1)S(1)}, u32[]{:S(2)}, u32[]{:S(2)}) collective-permute-start(bf16[512,384]{1,0:T(8,128)(2,1)S(1)} %collective-permute-done.29), channel_id=1, source_target_pairs={{0,32},{4,36},{8,40},{12,44},{16,48},{20,52},{24,56},{28,60},{32,0... | collective-permute-start | bytes 1179656 | tf_op jit(solution)/shard_map/ppermute | solution.py:324
  216.4 14.5 %collective-permute-start.31 = (bf16[512,384]{1,0:T(8,128)(2,1)S(1)}, bf16[512,384]{1,0:T(8,128)(2,1)S(1)}, u32[]{:S(2)}, u32[]{:S(2)}) collective-permute-start(bf16[512,384]{1,0:T(8,128)(2,1)S(1)} %collective-permute-done.29), channel_id=1, source_target_pairs={{0,48},{4,52},{8,56},{12,60},{16,0},{20,4},{24,8},{28,12},{32,16},... | collective-permute-start | bytes 1179656 | tf_op jit(solution)/shard_map/ppermute | solution.py:324
  218.2 11.5 %collective-permute-start.30 = (bf16[512,384]{1,0:T(8,128)(2,1)S(1)}, bf16[512,384]{1,0:T(8,128)(2,1)S(1)}, u32[]{:S(2)}, u32[]{:S(2)}) collective-permute-start(bf16[512,384]{1,0:T(8,128)(2,1)S(1)} %collective-permute-done.29), channel_id=1, source_target_pairs={{0,16},{4,20},{8,24},{12,28},{16,32},{20,36},{24,40},{28,44},{32,4... | collective-permute-start | bytes 1179656 | tf_op jit(solution)/shard_map/ppermute | solution.py:324
  226.3 40.1 %collective-permute-start.28 = (bf16[2048,384]{1,0:T(8,128)(2,1)S(1)}, bf16[2048,384]{1,0:T(8,128)(2,1)}, u32[]{:S(2)}, u32[]{:S(2)}) collective-permute-start(bf16[2048,384]{1,0:T(8,128)(2,1)S(1)} %constant_dynamic-update-slice_fusion.refs_3_.refs_4_), channel_id=1, source_target_pairs={{0,48},{4,52},{8,56},{12,60},{16,0},{20,4},{24,8},{28,12},{32,16},... | collective-permute-start | bytes 4718600 | tf_op jit(solution)/shard_map/ppermute | solution.py:324
  228.5 38.0 %collective-permute-start.27 = (bf16[2048,384]{1,0:T(8,128)(2,1)S(1)}, bf16[2048,384]{1,0:T(8,128)(2,1)}, u32[]{:S(2)}, u32[]{:S(2)}) collective-permute-start(bf16[2048,384]{1,0:T(8,128)(2,1)S(1)} %constant_dynamic-update-slice_fusion.refs_3_.refs_4_), channel_id=1, source_target_pairs={{0,16},{4,20},{8,24},{12,28},{16,32},{20,36},{24,40},{28,44},{32,4... | collective-permute-start | bytes 4718600 | tf_op jit(solution)/shard_map/ppermute | solution.py:324
  231.1 35.4 %collective-permute-start.34 = (bf16[2048,384]{1,0:T(8,128)(2,1)S(1)}, bf16[2048,384]{1,0:T(8,128)(2,1)}, u32[]{:S(2)}, u32[]{:S(2)}) collective-permute-start(bf16[2048,384]{1,0:T(8,128)(2,1)S(1)} %constant_dynamic-update-slice_fusion.4.refs_4_.refs_5_), channel_id=1, source_target_pairs={{0,12},{4,0},{8,4},{12,8},{16,28},{20,16},{24,20},{28,24},{32,44},... | collective-permute-start | bytes 4718600 | tf_op jit(solution)/shard_map/ppermute | solution.py:324
  233.2 33.3 %collective-permute-start.33 = (bf16[2048,384]{1,0:T(8,128)(2,1)S(1)}, bf16[2048,384]{1,0:T(8,128)(2,1)}, u32[]{:S(2)}, u32[]{:S(2)}) collective-permute-start(bf16[2048,384]{1,0:T(8,128)(2,1)S(1)} %constant_dynamic-update-slice_fusion.4.refs_4_.refs_5_), channel_id=1, source_target_pairs={{0,4},{4,8},{8,12},{12,0},{16,20},{20,24},{24,28},{28,16},{32,36},... | collective-permute-start | bytes 4718600 | tf_op jit(solution)/shard_map/ppermute | solution.py:324
  239.0 1.9 copy-start.2
  267.8 10.4 %copy-start.3 = (f32[1024,1024]{1,0:T(8,128)S(1)}, f32[1024,1024]{1,0:T(8,128)}, u32[]{:S(2)}) copy-start(f32[1024,1024]{1,0:T(8,128)} %copy-done.2) | copy-start | bytes 12582916
  271.7 26.2 %collective-permute-start.36 = (bf16[1024,384]{1,0:T(8,128)(2,1)S(1)}, bf16[1024,384]{1,0:T(8,128)(2,1)S(1)}, u32[]{:S(2)}, u32[]{:S(2)}) collective-permute-start(bf16[1024,384]{1,0:T(8,128)(2,1)S(1)} %slice.71), channel_id=1, source_target_pairs={{0,16},{4,20},{8,24},{12,28},{16,32},{20,36},{24,40},{28,44},{32,4... | collective-permute-start | bytes 2359304 | tf_op jit(solution)/shard_map/ppermute | solution.py:324
  272.5 25.4 %collective-permute-start.38 = (bf16[1024,384]{1,0:T(8,128)(2,1)S(1)}, bf16[1024,384]{1,0:T(8,128)(2,1)S(1)}, u32[]{:S(2)}, u32[]{:S(2)}) collective-permute-start(bf16[1024,384]{1,0:T(8,128)(2,1)S(1)} %slice.73), channel_id=1, source_target_pairs={{0,4},{4,8},{8,12},{12,0},{16,20},{20,24},{24,28},{28,16},{32,36},... | collective-permute-start | bytes 2359304 | tf_op jit(solution)/shard_map/ppermute | solution.py:324
  272.5 25.4 %collective-permute-start.37 = (bf16[1024,384]{1,0:T(8,128)(2,1)S(1)}, bf16[1024,384]{1,0:T(8,128)(2,1)S(1)}, u32[]{:S(2)}, u32[]{:S(2)}) collective-permute-start(bf16[1024,384]{1,0:T(8,128)(2,1)S(1)} %slice.72), channel_id=1, source_target_pairs={{0,48},{4,52},{8,56},{12,60},{16,0},{20,4},{24,8},{28,12},{32,16},... | collective-permute-start | bytes 2359304 | tf_op jit(solution)/shard_map/ppermute | solution.py:324
  275.5 22.4 %collective-permute-start.39 = (bf16[1024,384]{1,0:T(8,128)(2,1)S(1)}, bf16[1024,384]{1,0:T(8,128)(2,1)S(1)}, u32[]{:S(2)}, u32[]{:S(2)}) collective-permute-start(bf16[1024,384]{1,0:T(8,128)(2,1)S(1)} %slice.74), channel_id=1, source_target_pairs={{0,12},{4,0},{8,4},{12,8},{16,28},{20,16},{24,20},{28,24},{32,44},... | collective-permute-start | bytes 2359304 | tf_op jit(solution)/shard_map/ppermute | solution.py:324
  291.5 17.2 %collective-permute-start.35 = (bf16[1,512,384]{2,1,0:T(8,128)(2,1)S(1)}, bf16[1,512,384]{2,1,0:T(8,128)(2,1)S(1)}, u32[]{:S(2)}, u32[]{:S(2)}) collective-permute-start(bf16[1,512,384]{2,1,0:T(8,128)(2,1)S(1)} %bitcast.61), channel_id=1, source_target_pairs={{0,64},{1,65},{2,66},{3,67},{64,0},{65,1},{66,2},{67,3},{4,68},{5,... | collective-permute-start | bytes 1179656 | tf_op jit(solution)/shard_map/ppermute | solution.py:382
  297.9 14.9 %copy-start.1 = (f32[1,16,128,128]{3,2,1,0:T(8,128)S(1)}, f32[1,16,128,128]{3,2,1,0:T(8,128)}, u32[]{:S(2)}) copy-start(f32[1,16,128,128]{3,2,1,0:T(8,128)} %param.13) | copy-start | bytes 3145732
  305.2 4.4 %collective-permute-start.41 = (bf16[16,256]{1,0:T(8,128)(2,1)S(1)}, bf16[16,256]{1,0:T(8,128)(2,1)S(1)}, u32[]{:S(2)}, u32[]{:S(2)}) collective-permute-start(bf16[16,256]{1,0:T(8,128)(2,1)S(1)} %get-tuple-element.62), channel_id=1, source_target_pairs={{1,66},{2,65},{3,64},{0,67},{65,2},{66,1},{67,0},{64,3},{5,70},{6,... | collective-permute-start | bytes 24584 | tf_op jit(solution)/shard_map/ppermute | solution.py:382
  308.2 3.2 %collective-permute-start.42 = (bf16[16,256]{1,0:T(8,128)(2,1)S(1)}, bf16[16,256]{1,0:T(8,128)(2,1)S(1)}, u32[]{:S(2)}, u32[]{:S(2)}) collective-permute-start(bf16[16,256]{1,0:T(8,128)(2,1)S(1)} %get-tuple-element.63), channel_id=1, source_target_pairs={{0,65},{1,64},{2,67},{3,66},{64,1},{65,0},{66,3},{67,2},{4,69},{5,... | collective-permute-start | bytes 24584 | tf_op jit(solution)/shard_map/ppermute | solution.py:382
  308.7 2.7 collective-permute-start.40

commit v10 on v8

--- a/solution.py
+++ b/solution.py
@@ -397,8 +397,8 @@
     bias = jnp.concatenate(
         [
             enc_bias,
+            lax.ppermute(second_bias, "head", paired(1)),
             lax.ppermute(first_bias, "head", paired(0)),
-            lax.ppermute(second_bias, "head", paired(1)),
         ],
         axis=1,
     )
@@ -406,10 +406,9 @@
 
     packed = lax.all_to_all(packed, "seq", 0, 0, tiled=True)
     first, second = halves(enc_weight[0])
-    packed, after, before, inverse, bias, first = lax.optimization_barrier(
-        (packed, after, before, inverse, bias, first)
-    )
-    first = lax.ppermute(first, "head", paired(0))
+    packed, after, before, inverse, bias = lax.optimization_barrier(
+        (packed, after, before, inverse, bias)
+    )
     prior = lax.dynamic_index_in_dim(prior_state[0], place, 0, False)
     gain = lax.dynamic_slice_in_dim(norm_gain, place * HD, HD, 1)
     attended = attend(packed, prior, gain, groups)
@@ -426,7 +425,7 @@
     across = [from_head(parts[0], 1), from_head(parts[1], -1)]
     rows = own.shape[0] // 2
     joined = [jnp.concatenate(line, axis=0) for line in lines([own[:rows], own[rows:]])]
-    _, second = lax.optimization_barrier((joined, second))
+    _, across, second = lax.optimization_barrier((joined, across, second))
     second = lax.all_to_all(
         jnp.broadcast_to(second[None], (2, *second.shape)),
         "head",
@@ -438,13 +437,14 @@
     second = lax.dynamic_index_in_dim(second, odd, 0, False)
     weights = [weight, after, *across, before]
     layer_out = project(source, inverse, weights, planes(joined, near(joined)), residual[0])
-    layer_out, first = lax.optimization_barrier((layer_out, first))
     opposite = from_head(layer_out, 2)
+    opposite, first = lax.optimization_barrier((opposite, first))
+    first = lax.ppermute(first, "head", paired(0))
     joined = [jnp.concatenate(line, axis=0) for line in lines([layer_out, opposite])]
     beside = near(joined)
-    acc = encode(source, [enc_weight[0], first], joined, 0)
-    beside, acc, second = lax.optimization_barrier((beside, acc, second))
-    encoders = [enc_weight[0], first, second]
+    acc = encode(source, [enc_weight[0], second], joined, 0)
+    beside, acc = lax.optimization_barrier((beside, acc))
+    encoders = [enc_weight[0], second, first]
     gathered = planes(joined, beside)
     acc = encode(source, encoders, listed(gathered, [0, 1, 2]), 0, late=2, acc=acc)
     acc, layer_out = lax.optimization_barrier((acc, layer_out))
@@ -452,8 +452,8 @@
     pooled = pooled.astype(jnp.bfloat16)
     pools = pooled.shape[0] // 2
     mine = from_section(pooled[:, : 2 * half])
-    first = from_section(pooled[:, 2 * half : 3 * half], paired(0))
-    second = from_section(pooled[:, 3 * half :], paired(1))
+    second = from_section(pooled[:, 2 * half : 3 * half], paired(1))
+    first = from_section(pooled[:, 3 * half :], paired(0))
     after, before = jnp.where(odd, second, first), jnp.where(odd, first, second)
     turned = [
         mine[:pools],

time: 268 us -> 241 us (0.90)
  waiting for transfers between devices: 105 us -> 74.9 us
    ppermute x28, waiting for transfers between devices: 62.8 us -> 29.5 us  [moved(): return lax.ppermute(x, 'seq', pairs)]
    ppermute x1, waiting for transfers between devices: 0.63 us -> 21.5 us  [local(): lax.ppermute(second_bias, 'head', paired(1))]
    ppermute x1, waiting for transfers between devices: 12.4 us -> 0.01 us  [local(): lax.ppermute(first_bias, 'head', paired(0))]
    ppermute x8, waiting for transfers between devices: 19.2 us -> 6.8 us  [from_head(): lax.ppermute(x, 'head', [((i + by) % groups, i) for i in range(groups)])]
    ppermute x4, starting transfers between devices: 6.35 us -> 13.3 us  [from_section(): return lax.ppermute(x, ('section', 'head'), both)]
    ppermute x1, waiting for transfers between devices: 0.01 us -> 3.55 us  [local(): first = lax.ppermute(first, 'head', paired(0))]
    ppermute x8, starting transfers between devices: 9.81 us -> 6.88 us  [from_head(): lax.ppermute(x, 'head', [((i + by) % groups, i) for i in range(groups)])]
  transfers between devices with their start and end apart: 46 -> 46, of which waited for: 18 -> 16; matrix products, arithmetic and copies ran while one was open for 11% -> 12% of each run, Pallas kernels for 16% -> 15%
where the time goes in v10:
time: 241 us; the launch traced here: 239 us
  starting transfers between devices  82.1 us (34%)
  waiting for transfers between devices  74.9 us (31%)
  Pallas kernels  47.5 us (20%)
  local copies, waits for them, and re-layouts  32.7 us (14%)
    ppermute x28, starting transfers between devices, moved(): return lax.ppermute(x, 'seq', pairs)  40.6 us
    ppermute x28, waiting for transfers between devices, moved(): return lax.ppermute(x, 'seq', pairs)  29.5 us
    pallas_call x3, Pallas kernels, encode(): pl.pallas_call(functools.partial(encode_kernel, len(encoders), len(arrays...  26.4 us
    ppermute x1, waiting for transfers between devices, local(): lax.ppermute(second_bias, 'head', paired(1))  21.5 us
    ppermute x4, starting transfers between devices, from_section(): return lax.ppermute(x, ('section', 'head'), both)  13.3 us
    slice x8, local copies, waits for them, and re-layouts, planes(): across = (moved(up[:middle], axis, 1), moved(down[middle:], axis, -1))  11.3 us
    pallas_call x1, Pallas kernels, project(): pl.pallas_call(functools.partial(project_kernel, len(arrays), 0, False),...  10.5 us
    all_to_all x1, waiting for transfers between devices, local(): lax.all_to_all(jnp.broadcast_to(second[None], (2, *second.shape)), 'head'...  8.34 us
  transfers between devices with their start and end apart: 46, of which 16 were waited for; matrix products, arithmetic and copies ran while one was open for 12% of the time, Pallas kernels for 15%

profile of v10, /device:TPU:1, one launch (start us, length us, event | category | flops | bytes accessed | tf_op | source)
XLA Modules:
  0.0 239.4 jit_solution(10492781364904411303)
XLA Ops:
  0.6 3.4 %collective-permute-start = (bf16[2048,384]{1,0:T(8,128)(2,1)}, bf16[2048,384]{1,0:T(8,128)(2,1)}, u32[]{:S(2)}, u32[]{:S(2)}) collective-permute-start(bf16[2048,384]{1,0:T(8,128)(2,1)} %bitcast.66), channel_id=1, source_target_pairs={{1,0},{2,1},{3,2},{0,3},{5,4},{6,5},{7,6},{4,7},{9,8},{10,9},{11,1... | collective-permute-start | bytes 4718600 | tf_op jit(solution)/shard_map/ppermute | solution.py:371
  4.7 2.7 %collective-permute-start.5 = (f32[1,256]{1,0:T(1,128)S(1)}, f32[1,256]{1,0:T(1,128)S(1)}, u32[]{:S(2)}, u32[]{:S(2)}) collective-permute-start(f32[1,256]{1,0:T(1,128)S(1)} %get-tuple-element.68), channel_id=1, source_target_pairs={{1,2},{2,1},{3,0},{0,3},{5,6},{6,5},{7,4},{4,7},{9,10},{10,9},{11,... | collective-permute-start | bytes 3080 | tf_op jit(solution)/shard_map/ppermute | solution.py:400
  8.1 1.6 shard_map.113
  9.7 1.2 copy-done.2
  10.9 7.9 %all-to-all-start = ((bf16[16,400,128]{2,1,0:T(8,128)(2,1)}), bf16[16,400,128]{2,1,0:T(8,128)(2,1)S(1)}, u32[]{:S(2)}, u32[]{:S(2)}) async-start(bf16[16,400,128]{2,1,0:T(8,128)(2,1)} %copy-done.2), calls=%async_computation | async-start | bytes 3276800 | tf_op jit(solution)/shard_map/all_to_all | solution.py:407
  19.0 21.5 %collective-permute-done.5 = f32[1,256]{1,0:T(1,128)S(1)} collective-permute-done((f32[1,256]{1,0:T(1,128)S(1)}, f32[1,256]{1,0:T(1,128)S(1)}, u32[]{:S(2)}, u32[]{:S(2)}) %collective-permute-start.5) | collective-permute-done | bytes 1056 | tf_op jit(solution)/shard_map/ppermute | solution.py:400
  40.5 0.9 collective-permute-start.4
  41.5 3.1 %collective-permute-done.3 = f32[1,2048]{1,0:T(1,128)S(1)} collective-permute-done((f32[1,2048]{1,0:T(1,128)S(1)}, f32[1,2048]{1,0:T(1,128)S(1)}, u32[]{:S(2)}, u32[]{:S(2)}) %collective-permute-start.3) | collective-permute-done | bytes 8224 | tf_op jit(solution)/shard_map/ppermute | solution.py:371
  44.6 4.1 %shard_map.114 = bf16[4,512,128]{2,1,0:T(8,128)(2,1)} custom-call(bf16[16,400,128]{2,1,0:T(8,128)(2,1)S(1)} %all-to-all-done.packed_ref, f32[128,128]{1,0:T(8,128)S(1)} %dynamic-slice_bitcast_fusion.7.prior_ref, f32[1,128]{1,0:T(1,128)S(1)} %constant_dynamic-slice_fusion.gain_ref), custom_call_target="tpu_custom_call" | custom-call | tf_op jit(solution)/shard_map/pallas_call | solution.py:89
  48.7 3.5 %all-to-all-start.1 = ((bf16[4,512,128]{2,1,0:T(8,128)(2,1)}), bf16[4,512,128]{2,1,0:T(8,128)(2,1)S(1)}, u32[]{:S(2)}, u32[]{:S(2)}) async-start(bf16[4,512,128]{2,1,0:T(8,128)(2,1)} %shard_map.114), calls=%async_computation.1 | async-start | bytes 1048576 | tf_op jit(solution)/shard_map/all_to_all | solution.py:416
  52.2 2.1 slice.63
  54.4 2.1 slice.64
  56.5 2.6 %all-to-all-done.1 = bf16[4,512,128]{2,1,0:T(8,128)(2,1)S(1)} async-done(((bf16[4,512,128]{2,1,0:T(8,128)(2,1)}), bf16[4,512,128]{2,1,0:T(8,128)(2,1)S(1)}, u32[]{:S(2)}, u32[]{:S(2)}) %all-to-all-start.1) | async-done | bytes 524320 | tf_op jit(solution)/shard_map/all_to_all | solution.py:416
  59.2 1.0 collective-permute-start.13
  60.3 1.7 collective-permute-start.10
  62.0 2.2 collective-permute-start.11
  64.2 1.2 collective-permute-start.12
  65.4 1.3 collective-permute-start.7
  66.7 1.2 collective-permute-done.10
  67.9 2.7 %collective-permute-start.8 = (bf16[256,512]{1,0:T(8,128)(2,1)S(1)}, bf16[256,512]{1,0:T(8,128)(2,1)S(1)}, u32[]{:S(2)}, u32[]{:S(2)}) collective-permute-start(bf16[256,512]{1,0:T(8,128)(2,1)S(1)} %get-tuple-element.49), channel_id=1, source_target_pairs={{0,12},{4,0},{8,4},{12,8},{16,28},{20,16},{24,20},{28,24},{32,44},... | collective-permute-start | bytes 786440 | tf_op jit(solution)/shard_map/ppermute | solution.py:324
  70.6 2.9 %collective-permute-start.9 = (bf16[256,512]{1,0:T(8,128)(2,1)S(1)}, bf16[256,512]{1,0:T(8,128)(2,1)S(1)}, u32[]{:S(2)}, u32[]{:S(2)}) collective-permute-start(bf16[256,512]{1,0:T(8,128)(2,1)S(1)} %get-tuple-element.49), channel_id=1, source_target_pairs={{0,8},{4,12},{8,0},{12,4},{16,24},{20,28},{24,16},{28,20},{32,40},... | collective-permute-start | bytes 786440 | tf_op jit(solution)/shard_map/ppermute | solution.py:324
  74.5 2.8 %collective-permute-start.21 = (bf16[1024,512]{1,0:T(8,128)(2,1)S(1)}, bf16[1024,512]{1,0:T(8,128)(2,1)}, u32[]{:S(2)}, u32[]{:S(2)}) collective-permute-start(bf16[1024,512]{1,0:T(8,128)(2,1)S(1)} %pad_maximum_fusion.2.refs_8_), channel_id=1, source_target_pairs={{0,12},{4,0},{8,4},{12,8},{16,28},{20,16},{24,20},{28,24},{32,44},... | collective-permute-start | bytes 3145736 | tf_op jit(solution)/shard_map/ppermute | solution.py:324
  77.3 1.3 collective-permute-done.9
  80.3 2.7 %collective-permute-start.17 = (bf16[1024,512]{1,0:T(8,128)(2,1)S(1)}, bf16[1024,512]{1,0:T(8,128)(2,1)}, u32[]{:S(2)}, u32[]{:S(2)}) collective-permute-start(bf16[1024,512]{1,0:T(8,128)(2,1)S(1)} %pad_maximum_fusion.1.refs_7_), channel_id=1, source_target_pairs={{0,48},{4,52},{8,56},{12,60},{16,0},{20,4},{24,8},{28,12},{32,16},... | collective-permute-start | bytes 3145736 | tf_op jit(solution)/shard_map/ppermute | solution.py:324
  83.1 4.9 %dynamic-slice_bitcast_fusion = (bf16[6144,256]{1,0:T(8,128)(2,1)}, bf16[6144,256]{1,0:T(8,128)(2,1)S(1)}) fusion(bf16[1,6144,512]{2,1,0:T(8,128)(2,1)} %param.18, s32[]{:T(128)S(6)} %select_n.260, s32[]{:T(128)S(6)} %select_n.259), kind=kLoop, calls=%fused_computation | loop fusion | bytes 12582920 | tf_op jit(solution)/shard_map/dynamic_slice | solution.py:394
  88.0 3.1 %broadcast_in_dim.12 = bf16[2,6144,256]{2,1,0:T(8,128)(2,1)} broadcast(bf16[6144,256]{1,0:T(8,128)(2,1)S(1)} %get-tuple-element.30), dimensions={1,2} | broadcast | bytes 9437184 | tf_op jit(solution)/shard_map/broadcast_in_dim | solution.py:430
  91.1 6.7 %all-to-all-start.2 = ((bf16[2,6144,256]{2,1,0:T(8,128)(2,1)}), bf16[2,6144,256]{2,1,0:T(8,128)(2,1)}, u32[]{:S(2)}, u32[]{:S(2)}) async-start(bf16[2,6144,256]{2,1,0:T(8,128)(2,1)} %broadcast_in_dim.12), calls=%async_computation.2 | async-start | bytes 12582912 | tf_op jit(solution)/shard_map/all_to_all | solution.py:429
  97.8 3.3 %collective-permute-done.19.refs_10_ = bf16[1024,512]{1,0:T(8,128)(2,1)S(1)} collective-permute-done((bf16[1024,512]{1,0:T(8,128)(2,1)S(1)}, bf16[1024,512]{1,0:T(8,128)(2,1)S(1)}, u32[]{:S(2)}, u32[]{:S(2)}) %collective-permute-start.19) | collective-permute-done | bytes 1048608 | tf_op jit(solution)/shard_map/ppermute | solution.py:324
  102.6 1.9 slice.87
  104.5 2.0 collective-permute-start.22
  106.5 1.9 slice.84
  108.3 1.0 collective-permute-start.16
  109.4 1.9 slice.85
  111.3 1.6 collective-permute-start.18
  113.0 10.5 %shard_map.115 = (f32[512,384]{1,0:T(8,128)S(1)}, f32[512,128]{1,0:T(8,128)S(1)}) custom-call(s32[32]{0:T(128)S(1)} %stack.98.refs_0_, f32[16,512]{1,0:T(8,128)S(1)} %pad_maximum_fusion.4.refs_1_, bf16[2048,384]{1,0:T(8,128)(2,1)} %bitcast.68, bf16[2048,384]{1,0:T(8,128)(2,1)} %collective-permute-done.refs_3_, bf16[1024,384]{1,0:T(8,128)(2,1)} %copy-done.7, ...), custom_call_target="tpu_custom_call" | custom-call | tf_op jit(solution)/shard_map/pallas_call | solution.py:229
  124.3 4.9 %shard_map.116 = bf16[512,384]{1,0:T(8,128)(2,1)S(1)} custom-call(s32[32]{0:T(128)S(1)} %stack.98.refs_0_, f32[16,512]{1,0:T(8,128)S(1)} %copy-done.5, bf16[2048,384]{1,0:T(8,128)(2,1)} %bitcast.69, bf16[2048,384]{1,0:T(8,128)(2,1)} %collective-permute-done.refs_3_, bf16[1024,384]{1,0:T(8,128)(2,1)} %copy-done.7, ...), custom_call_target="tpu_custom_call" | custom-call | tf_op jit(solution)/shard_map/pallas_call | solution.py:238
  129.3 1.0 collective-permute-start.23
  130.2 1.0 collective-permute-start.25
  131.2 1.7 collective-permute-start.26
  132.9 0.9 collective-permute-start.27
  133.8 3.7 %collective-permute-done.23 = bf16[512,384]{1,0:T(8,128)(2,1)S(1)} collective-permute-done((bf16[512,384]{1,0:T(8,128)(2,1)S(1)}, bf16[512,384]{1,0:T(8,128)(2,1)S(1)}, u32[]{:S(2)}, u32[]{:S(2)}) %collective-permute-start.23) | collective-permute-done | bytes 393248 | tf_op jit(solution)/shard_map/ppermute | solution.py:371
  138.0 4.6 %collective-permute-done.25 = bf16[512,384]{1,0:T(8,128)(2,1)S(1)} collective-permute-done((bf16[512,384]{1,0:T(8,128)(2,1)S(1)}, bf16[512,384]{1,0:T(8,128)(2,1)S(1)}, u32[]{:S(2)}, u32[]{:S(2)}) %collective-permute-start.25) | collective-permute-done | bytes 393248 | tf_op jit(solution)/shard_map/ppermute | solution.py:324
  142.7 1.5 collective-permute-start.29
  145.2 1.1 collective-permute-done.28
  146.3 1.3 collective-permute-start.32
  147.6 2.1 collective-permute-done.29
  149.8 2.8 %collective-permute-done.30 = bf16[512,384]{1,0:T(8,128)(2,1)S(1)} collective-permute-done((bf16[512,384]{1,0:T(8,128)(2,1)S(1)}, bf16[512,384]{1,0:T(8,128)(2,1)S(1)}, u32[]{:S(2)}, u32[]{:S(2)}) %collective-permute-start.30) | collective-permute-done | bytes 393248 | tf_op jit(solution)/shard_map/ppermute | solution.py:324
  152.8 2.7 %collective-permute-start.34 = (bf16[2048,384]{1,0:T(8,128)(2,1)S(1)}, bf16[2048,384]{1,0:T(8,128)(2,1)}, u32[]{:S(2)}, u32[]{:S(2)}) collective-permute-start(bf16[2048,384]{1,0:T(8,128)(2,1)S(1)} %constant_dynamic-update-slice_fusion.refs_4_.refs_5_), channel_id=1, source_target_pairs={{0,12},{4,0},{8,4},{12,8},{16,28},{20,16},{24,20},{28,24},{32,44},... | collective-permute-start | bytes 4718600 | tf_op jit(solution)/shard_map/ppermute | solution.py:324
  155.4 8.3 %all-to-all-done.2 = bf16[2,6144,256]{2,1,0:T(8,128)(2,1)} async-done(((bf16[2,6144,256]{2,1,0:T(8,128)(2,1)}), bf16[2,6144,256]{2,1,0:T(8,128)(2,1)}, u32[]{:S(2)}, u32[]{:S(2)}) %all-to-all-start.2) | async-done | bytes 6291488 | tf_op jit(solution)/shard_map/all_to_all | solution.py:429
  163.8 3.8 %dynamic-slice_bitcast_fusion.1.refs_2_ = bf16[6144,256]{1,0:T(8,128)(2,1)} fusion(bf16[2,6144,256]{2,1,0:T(8,128)(2,1)} %all-to-all-done.2, s32[]{:T(128)S(6)} %select_n.271), kind=kLoop, calls=%fused_computation.1 | loop fusion | bytes 6291460 | tf_op jit(solution)/shard_map/jit(dynamic_index_in_dim)/squeeze | solution.py:437
  167.6 5.7 %shard_map.117.refs_10_ = f32[1024,1024]{1,0:T(8,128)S(1)} custom-call(s32[32]{0:T(128)S(1)} %stack.98.refs_0_, bf16[6144,512]{1,0:T(8,128)(2,1)} %bitcast.63, bf16[6144,256]{1,0:T(8,128)(2,1)} %dynamic-slice_bitcast_fusion.1.refs_2_, bf16[2048,384]{1,0:T(8,128)(2,1)S(1)} %pad_maximum_fusion.refs_3_.refs_4_, ...), custom_call_target="tpu_custom_call" | custom-call | tf_op jit(solution)/shard_map/pallas_call | solution.py:303
  173.3 13.0 %collective-permute-done.31.refs_6_ = bf16[2048,384]{1,0:T(8,128)(2,1)} collective-permute-done((bf16[2048,384]{1,0:T(8,128)(2,1)S(1)}, bf16[2048,384]{1,0:T(8,128)(2,1)}, u32[]{:S(2)}, u32[]{:S(2)}) %collective-permute-start.31) | collective-permute-done | bytes 1572896 | tf_op jit(solution)/shard_map/ppermute | solution.py:324
  186.3 1.2 slice.71
  187.5 1.7 collective-permute-start.36
  189.2 1.2 slice.72
  190.4 2.1 collective-permute-start.37
  192.5 1.2 slice.73
  193.8 1.2 slice.74
  195.0 2.7 %collective-permute-start.39 = (bf16[1024,384]{1,0:T(8,128)(2,1)S(1)}, bf16[1024,384]{1,0:T(8,128)(2,1)S(1)}, u32[]{:S(2)}, u32[]{:S(2)}) collective-permute-start(bf16[1024,384]{1,0:T(8,128)(2,1)S(1)} %slice.74), channel_id=1, source_target_pairs={{0,12},{4,0},{8,4},{12,8},{16,28},{20,16},{24,20},{28,24},{32,44},... | collective-permute-start | bytes 2359304 | tf_op jit(solution)/shard_map/ppermute | solution.py:324
  197.7 3.6 %collective-permute-done.24.refs_3_ = bf16[6144,256]{1,0:T(8,128)(2,1)} collective-permute-done((bf16[6144,256]{1,0:T(8,128)(2,1)}, bf16[6144,256]{1,0:T(8,128)(2,1)}, u32[]{:S(2)}, u32[]{:S(2)}) %collective-permute-start.24) | collective-permute-done | bytes 3145760 | tf_op jit(solution)/shard_map/ppermute | solution.py:442
  201.3 13.4 %shard_map.118.refs_8_ = f32[1024,1024]{1,0:T(8,128)S(1)} custom-call(s32[32]{0:T(128)S(1)} %stack.98.refs_0_, bf16[6144,512]{1,0:T(8,128)(2,1)} %bitcast.64, bf16[6144,256]{1,0:T(8,128)(2,1)} %dynamic-slice_bitcast_fusion.1.refs_2_, bf16[6144,256]{1,0:T(8,128)(2,1)} %collective-permute-done.24.refs_3_, ...), custom_call_target="tpu_custom_call" | custom-call | tf_op jit(solution)/shard_map/pallas_call | solution.py:303
  214.8 7.3 %shard_map.119 = f32[16,1024]{1,0:T(8,128)S(1)} custom-call(s32[32]{0:T(128)S(1)} %stack.98.refs_0_, bf16[6144,512]{1,0:T(8,128)(2,1)} %bitcast.65, bf16[6144,256]{1,0:T(8,128)(2,1)} %dynamic-slice_bitcast_fusion.1.refs_2_, bf16[6144,256]{1,0:T(8,128)(2,1)} %collective-permute-done.24.refs_3_, bf16[1024,384]{1,0:T(8,128)(2,1)S(1)} %collective-permute-done.36.refs_4_, ...), custom_call_target="tpu_custom_call" | custom-call | tf_op jit(solution)/shard_map/pallas_call | solution.py:303
  222.1 12.8 %collective-permute-start.41 = (bf16[16,256]{1,0:T(8,128)(2,1)S(1)}, bf16[16,256]{1,0:T(8,128)(2,1)S(1)}, u32[]{:S(2)}, u32[]{:S(2)}) collective-permute-start(bf16[16,256]{1,0:T(8,128)(2,1)S(1)} %get-tuple-element.58), channel_id=1, source_target_pairs={{1,66},{2,65},{3,64},{0,67},{65,2},{66,1},{67,0},{64,3},{5,70},{6,... | collective-permute-start | bytes 24584 | tf_op jit(solution)/shard_map/ppermute | solution.py:382
  236.2 1.7 collective-permute-done.42
  (100 shorter events, 11.4 us)
Async XLA Ops:
  0.6 18.3 %copy-start = (f32[1,16,128,128]{3,2,1,0:T(8,128)S(1)}, f32[1,16,128,128]{3,2,1,0:T(8,128)}, u32[]{:S(2)}) copy-start(f32[1,16,128,128]{3,2,1,0:T(8,128)} %param.13) | copy-start | bytes 3145732
  0.6 44.0 %collective-permute-start = (bf16[2048,384]{1,0:T(8,128)(2,1)}, bf16[2048,384]{1,0:T(8,128)(2,1)}, u32[]{:S(2)}, u32[]{:S(2)}) collective-permute-start(bf16[2048,384]{1,0:T(8,128)(2,1)} %bitcast.66), channel_id=1, source_target_pairs={{1,0},{2,1},{3,2},{0,3},{5,4},{6,5},{7,6},{4,7},{9,8},{10,9},{11,1... | collective-permute-start | bytes 4718600 | tf_op jit(solution)/shard_map/ppermute | solution.py:371
  4.0 40.6 %collective-permute-start.1 = (bf16[2048,384]{1,0:T(8,128)(2,1)}, bf16[2048,384]{1,0:T(8,128)(2,1)}, u32[]{:S(2)}, u32[]{:S(2)}) collective-permute-start(bf16[2048,384]{1,0:T(8,128)(2,1)} %bitcast.67), channel_id=1, source_target_pairs={{3,0},{0,1},{1,2},{2,3},{7,4},{4,5},{5,6},{6,7},{11,8},{8,9},{9,10... | collective-permute-start | bytes 4718600 | tf_op jit(solution)/shard_map/ppermute | solution.py:371
  4.7 35.8 %collective-permute-start.5 = (f32[1,256]{1,0:T(1,128)S(1)}, f32[1,256]{1,0:T(1,128)S(1)}, u32[]{:S(2)}, u32[]{:S(2)}) collective-permute-start(f32[1,256]{1,0:T(1,128)S(1)} %get-tuple-element.68), channel_id=1, source_target_pairs={{1,2},{2,1},{3,0},{0,3},{5,6},{6,5},{7,4},{4,7},{9,10},{10,9},{11,... | collective-permute-start | bytes 3080 | tf_op jit(solution)/shard_map/ppermute | solution.py:400
  7.4 33.1 %collective-permute-start.6 = (f32[1,256]{1,0:T(1,128)S(1)}, f32[1,256]{1,0:T(1,128)S(1)}, u32[]{:S(2)}, u32[]{:S(2)}) collective-permute-start(f32[1,256]{1,0:T(1,128)S(1)} %get-tuple-element.69), channel_id=1, source_target_pairs={{0,1},{1,0},{2,3},{3,2},{4,5},{5,4},{6,7},{7,6},{8,9},{9,8},{10,11... | collective-permute-start | bytes 3080 | tf_op jit(solution)/shard_map/ppermute | solution.py:401
  7.4 0.7 copy-start.6
  9.7 1.2 copy-start.2
  10.9 7.9 %copy-start.8 = (f32[1,2048]{1,0:T(1,128)S(1)}, f32[1,2048]{1,0:T(1,128)}, u32[]{:S(2)}) copy-start(f32[1,2048]{1,0:T(1,128)} %param.15) | copy-start | bytes 24580
  10.9 30.5 %copy-start.9 = (f32[1,512]{1,0:T(1,128)S(1)}, f32[1,512]{1,0:T(1,128)}, u32[]{:S(2)}) copy-start(f32[1,512]{1,0:T(1,128)} %param.19) | copy-start | bytes 6148
  10.9 33.7 %all-to-all-start = ((bf16[16,400,128]{2,1,0:T(8,128)(2,1)}), bf16[16,400,128]{2,1,0:T(8,128)(2,1)S(1)}, u32[]{:S(2)}, u32[]{:S(2)}) async-start(bf16[16,400,128]{2,1,0:T(8,128)(2,1)} %copy-done.2), calls=%async_computation | async-start | bytes 3276800 | tf_op jit(solution)/shard_map/all_to_all | solution.py:407
  18.8 22.6 %collective-permute-start.2 = (f32[1,2048]{1,0:T(1,128)S(1)}, f32[1,2048]{1,0:T(1,128)S(1)}, u32[]{:S(2)}, u32[]{:S(2)}) collective-permute-start(f32[1,2048]{1,0:T(1,128)S(1)} %copy-done.8), channel_id=1, source_target_pairs={{1,0},{2,1},{3,2},{0,3},{5,4},{6,5},{7,6},{4,7},{9,8},{10,9},{11,1... | collective-permute-start | bytes 24584 | tf_op jit(solution)/shard_map/ppermute | solution.py:371
  40.5 4.0 %collective-permute-start.3 = (f32[1,2048]{1,0:T(1,128)S(1)}, f32[1,2048]{1,0:T(1,128)S(1)}, u32[]{:S(2)}, u32[]{:S(2)}) collective-permute-start(f32[1,2048]{1,0:T(1,128)S(1)} %copy-done.8), channel_id=1, source_target_pairs={{2,0},{3,1},{0,2},{1,3},{6,4},{7,5},{4,6},{5,7},{10,8},{11,9},{8,1... | collective-permute-start | bytes 24584 | tf_op jit(solution)/shard_map/ppermute | solution.py:371
  40.5 4.0 %collective-permute-start.4 = (f32[1,2048]{1,0:T(1,128)S(1)}, f32[1,2048]{1,0:T(1,128)S(1)}, u32[]{:S(2)}, u32[]{:S(2)}) collective-permute-start(f32[1,2048]{1,0:T(1,128)S(1)} %copy-done.8), channel_id=1, source_target_pairs={{3,0},{0,1},{1,2},{2,3},{7,4},{4,5},{5,6},{6,7},{11,8},{8,9},{9,10... | collective-permute-start | bytes 24584 | tf_op jit(solution)/shard_map/ppermute | solution.py:371
  44.6 68.4 %copy-start.4 = (f32[16,512]{1,0:T(8,128)}, f32[16,512]{1,0:T(8,128)S(1)}, u32[]{:S(2)}) copy-start(f32[16,512]{1,0:T(8,128)S(1)} %pad_maximum_fusion.4.refs_1_) | copy-start | bytes 98308
  48.7 10.4 %all-to-all-start.1 = ((bf16[4,512,128]{2,1,0:T(8,128)(2,1)}), bf16[4,512,128]{2,1,0:T(8,128)(2,1)S(1)}, u32[]{:S(2)}, u32[]{:S(2)}) async-start(bf16[4,512,128]{2,1,0:T(8,128)(2,1)} %shard_map.114), calls=%async_computation.1 | async-start | bytes 1048576 | tf_op jit(solution)/shard_map/all_to_all | solution.py:416
  59.2 20.3 %collective-permute-start.13 = (bf16[1024,384]{1,0:T(8,128)(2,1)}, bf16[1024,384]{1,0:T(8,128)(2,1)S(1)}, u32[]{:S(2)}, u32[]{:S(2)}) collective-permute-start(bf16[1024,384]{1,0:T(8,128)(2,1)} %slice.63), channel_id=1, source_target_pairs={{1,0},{2,1},{3,2},{0,3},{5,4},{6,5},{7,6},{4,7},{9,8},{10,9},{11,1... | collective-permute-start | bytes 2359304 | tf_op jit(solution)/shard_map/ppermute | solution.py:371
  60.3 7.6 %collective-permute-start.10 = (bf16[256,512]{1,0:T(8,128)(2,1)S(1)}, bf16[256,512]{1,0:T(8,128)(2,1)S(1)}, u32[]{:S(2)}, u32[]{:S(2)}) collective-permute-start(bf16[256,512]{1,0:T(8,128)(2,1)S(1)} %get-tuple-element.48), channel_id=1, source_target_pairs={{0,16},{4,20},{8,24},{12,28},{16,32},{20,36},{24,40},{28,44},{32,4... | collective-permute-start | bytes 786440 | tf_op jit(solution)/shard_map/ppermute | solution.py:324
  62.0 8.6 %collective-permute-start.11 = (bf16[256,512]{1,0:T(8,128)(2,1)S(1)}, bf16[256,512]{1,0:T(8,128)(2,1)S(1)}, u32[]{:S(2)}, u32[]{:S(2)}) collective-permute-start(bf16[256,512]{1,0:T(8,128)(2,1)S(1)} %get-tuple-element.48), channel_id=1, source_target_pairs={{0,48},{4,52},{8,56},{12,60},{16,0},{20,4},{24,8},{28,12},{32,16},... | collective-permute-start | bytes 786440 | tf_op jit(solution)/shard_map/ppermute | solution.py:324
  64.2 9.3 %collective-permute-start.12 = (bf16[256,512]{1,0:T(8,128)(2,1)S(1)}, bf16[256,512]{1,0:T(8,128)(2,1)S(1)}, u32[]{:S(2)}, u32[]{:S(2)}) collective-permute-start(bf16[256,512]{1,0:T(8,128)(2,1)S(1)} %get-tuple-element.48), channel_id=1, source_target_pairs={{0,32},{4,36},{8,40},{12,44},{16,48},{20,52},{24,56},{28,60},{32,0... | collective-permute-start | bytes 786440 | tf_op jit(solution)/shard_map/ppermute | solution.py:324
  65.4 8.6 %collective-permute-start.7 = (bf16[256,512]{1,0:T(8,128)(2,1)S(1)}, bf16[256,512]{1,0:T(8,128)(2,1)S(1)}, u32[]{:S(2)}, u32[]{:S(2)}) collective-permute-start(bf16[256,512]{1,0:T(8,128)(2,1)S(1)} %get-tuple-element.49), channel_id=1, source_target_pairs={{0,4},{4,8},{8,12},{12,0},{16,20},{20,24},{24,28},{28,16},{32,36},... | collective-permute-start | bytes 786440 | tf_op jit(solution)/shard_map/ppermute | solution.py:324
  67.9 6.7 %collective-permute-start.8 = (bf16[256,512]{1,0:T(8,128)(2,1)S(1)}, bf16[256,512]{1,0:T(8,128)(2,1)S(1)}, u32[]{:S(2)}, u32[]{:S(2)}) collective-permute-start(bf16[256,512]{1,0:T(8,128)(2,1)S(1)} %get-tuple-element.49), channel_id=1, source_target_pairs={{0,12},{4,0},{8,4},{12,8},{16,28},{20,16},{24,20},{28,24},{32,44},... | collective-permute-start | bytes 786440 | tf_op jit(solution)/shard_map/ppermute | solution.py:324
  70.6 8.1 %collective-permute-start.9 = (bf16[256,512]{1,0:T(8,128)(2,1)S(1)}, bf16[256,512]{1,0:T(8,128)(2,1)S(1)}, u32[]{:S(2)}, u32[]{:S(2)}) collective-permute-start(bf16[256,512]{1,0:T(8,128)(2,1)S(1)} %get-tuple-element.49), channel_id=1, source_target_pairs={{0,8},{4,12},{8,0},{12,4},{16,24},{20,28},{24,16},{28,20},{32,40},... | collective-permute-start | bytes 786440 | tf_op jit(solution)/shard_map/ppermute | solution.py:324
  73.5 14.5 %collective-permute-start.14 = (bf16[1024,384]{1,0:T(8,128)(2,1)}, bf16[1024,384]{1,0:T(8,128)(2,1)}, u32[]{:S(2)}, u32[]{:S(2)}) collective-permute-start(bf16[1024,384]{1,0:T(8,128)(2,1)} %slice.64), channel_id=1, source_target_pairs={{3,0},{0,1},{1,2},{2,3},{7,4},{4,5},{5,6},{6,7},{11,8},{8,9},{9,10... | collective-permute-start | bytes 2359304 | tf_op jit(solution)/shard_map/ppermute | solution.py:371
  74.1 27.0 %collective-permute-start.19 = (bf16[1024,512]{1,0:T(8,128)(2,1)S(1)}, bf16[1024,512]{1,0:T(8,128)(2,1)S(1)}, u32[]{:S(2)}, u32[]{:S(2)}) collective-permute-start(bf16[1024,512]{1,0:T(8,128)(2,1)S(1)} %pad_maximum_fusion.2.refs_8_), channel_id=1, source_target_pairs={{0,4},{4,8},{8,12},{12,0},{16,20},{20,24},{24,28},{28,16},{32,36},... | collective-permute-start | bytes 3145736 | tf_op jit(solution)/shard_map/ppermute | solution.py:324
  74.5 28.1 %collective-permute-start.21 = (bf16[1024,512]{1,0:T(8,128)(2,1)S(1)}, bf16[1024,512]{1,0:T(8,128)(2,1)}, u32[]{:S(2)}, u32[]{:S(2)}) collective-permute-start(bf16[1024,512]{1,0:T(8,128)(2,1)S(1)} %pad_maximum_fusion.2.refs_8_), channel_id=1, source_target_pairs={{0,12},{4,0},{8,4},{12,8},{16,28},{20,16},{24,20},{28,24},{32,44},... | collective-permute-start | bytes 3145736 | tf_op jit(solution)/shard_map/ppermute | solution.py:324
  78.7 27.7 %collective-permute-start.15 = (bf16[1024,512]{1,0:T(8,128)(2,1)S(1)}, bf16[1024,512]{1,0:T(8,128)(2,1)}, u32[]{:S(2)}, u32[]{:S(2)}) collective-permute-start(bf16[1024,512]{1,0:T(8,128)(2,1)S(1)} %pad_maximum_fusion.1.refs_7_), channel_id=1, source_target_pairs={{0,16},{4,20},{8,24},{12,28},{16,32},{20,36},{24,40},{28,44},{32,4... | collective-permute-start | bytes 3145736 | tf_op jit(solution)/shard_map/ppermute | solution.py:324
  79.5 0.9 copy-start.7
  80.3 29.0 %collective-permute-start.17 = (bf16[1024,512]{1,0:T(8,128)(2,1)S(1)}, bf16[1024,512]{1,0:T(8,128)(2,1)}, u32[]{:S(2)}, u32[]{:S(2)}) collective-permute-start(bf16[1024,512]{1,0:T(8,128)(2,1)S(1)} %pad_maximum_fusion.1.refs_7_), channel_id=1, source_target_pairs={{0,48},{4,52},{8,56},{12,60},{16,0},{20,4},{24,8},{28,12},{32,16},... | collective-permute-start | bytes 3145736 | tf_op jit(solution)/shard_map/ppermute | solution.py:324
  91.1 72.7 %all-to-all-start.2 = ((bf16[2,6144,256]{2,1,0:T(8,128)(2,1)}), bf16[2,6144,256]{2,1,0:T(8,128)(2,1)}, u32[]{:S(2)}, u32[]{:S(2)}) async-start(bf16[2,6144,256]{2,1,0:T(8,128)(2,1)} %broadcast_in_dim.12), calls=%async_computation.2 | async-start | bytes 12582912 | tf_op jit(solution)/shard_map/all_to_all | solution.py:429
  101.9 21.6 %collective-permute-start.20 = (bf16[512,512]{1,0:T(8,128)(2,1)}, bf16[512,512]{1,0:T(8,128)(2,1)}, u32[]{:S(2)}, u32[]{:S(2)}) collective-permute-start(bf16[512,512]{1,0:T(8,128)(2,1)} %slice.86), channel_id=1, source_target_pairs={{0,4},{4,8},{8,12},{12,0},{16,20},{20,24},{24,28},{28,16},{32,36},... | collective-permute-start | bytes 1572872 | tf_op jit(solution)/shard_map/ppermute | solution.py:324
  104.5 19.0 %collective-permute-start.22 = (bf16[512,512]{1,0:T(8,128)(2,1)}, bf16[512,512]{1,0:T(8,128)(2,1)}, u32[]{:S(2)}, u32[]{:S(2)}) collective-permute-start(bf16[512,512]{1,0:T(8,128)(2,1)} %slice.87), channel_id=1, source_target_pairs={{0,12},{4,0},{8,4},{12,8},{16,28},{20,16},{24,20},{28,24},{32,44},... | collective-permute-start | bytes 1572872 | tf_op jit(solution)/shard_map/ppermute | solution.py:324
  108.3 15.2 %collective-permute-start.16 = (bf16[512,512]{1,0:T(8,128)(2,1)}, bf16[512,512]{1,0:T(8,128)(2,1)}, u32[]{:S(2)}, u32[]{:S(2)}) collective-permute-start(bf16[512,512]{1,0:T(8,128)(2,1)} %slice.84), channel_id=1, source_target_pairs={{0,16},{4,20},{8,24},{12,28},{16,32},{20,36},{24,40},{28,44},{32,4... | collective-permute-start | bytes 1572872 | tf_op jit(solution)/shard_map/ppermute | solution.py:324
  111.3 12.3 %collective-permute-start.18 = (bf16[512,512]{1,0:T(8,128)(2,1)}, bf16[512,512]{1,0:T(8,128)(2,1)}, u32[]{:S(2)}, u32[]{:S(2)}) collective-permute-start(bf16[512,512]{1,0:T(8,128)(2,1)} %slice.85), channel_id=1, source_target_pairs={{0,48},{4,52},{8,56},{12,60},{16,0},{20,4},{24,8},{28,12},{32,16},... | collective-permute-start | bytes 1572872 | tf_op jit(solution)/shard_map/ppermute | solution.py:324
  113.0 10.5 %copy-start.3 = (bf16[1,512,384]{2,1,0:T(8,128)(2,1)S(1)}, bf16[1,512,384]{2,1,0:T(8,128)(2,1)}, u32[]{:S(2)}) copy-start(bf16[1,512,384]{2,1,0:T(8,128)(2,1)} %param.16) | copy-start | bytes 1179652
  123.5 0.8 copy-start.5
  129.3 8.3 %collective-permute-start.23 = (bf16[512,384]{1,0:T(8,128)(2,1)S(1)}, bf16[512,384]{1,0:T(8,128)(2,1)S(1)}, u32[]{:S(2)}, u32[]{:S(2)}) collective-permute-start(bf16[512,384]{1,0:T(8,128)(2,1)S(1)} %shard_map.116), channel_id=1, source_target_pairs={{2,0},{3,1},{0,2},{1,3},{6,4},{7,5},{4,6},{5,7},{10,8},{11,9},{8,1... | collective-permute-start | bytes 1179656 | tf_op jit(solution)/shard_map/ppermute | solution.py:371
  130.2 12.5 %collective-permute-start.25 = (bf16[512,384]{1,0:T(8,128)(2,1)S(1)}, bf16[512,384]{1,0:T(8,128)(2,1)S(1)}, u32[]{:S(2)}, u32[]{:S(2)}) collective-permute-start(bf16[512,384]{1,0:T(8,128)(2,1)S(1)} %shard_map.116), channel_id=1, source_target_pairs={{0,4},{4,8},{8,12},{12,0},{16,20},{20,24},{24,28},{28,16},{32,36},... | collective-permute-start | bytes 1179656 | tf_op jit(solution)/shard_map/ppermute | solution.py:324
  131.2 12.9 %collective-permute-start.26 = (bf16[512,384]{1,0:T(8,128)(2,1)S(1)}, bf16[512,384]{1,0:T(8,128)(2,1)S(1)}, u32[]{:S(2)}, u32[]{:S(2)}) collective-permute-start(bf16[512,384]{1,0:T(8,128)(2,1)S(1)} %shard_map.116), channel_id=1, source_target_pairs={{0,12},{4,0},{8,4},{12,8},{16,28},{20,16},{24,20},{28,24},{32,44},... | collective-permute-start | bytes 1179656 | tf_op jit(solution)/shard_map/ppermute | solution.py:324
  132.9 11.6 %collective-permute-start.27 = (bf16[512,384]{1,0:T(8,128)(2,1)S(1)}, bf16[512,384]{1,0:T(8,128)(2,1)S(1)}, u32[]{:S(2)}, u32[]{:S(2)}) collective-permute-start(bf16[512,384]{1,0:T(8,128)(2,1)S(1)} %shard_map.116), channel_id=1, source_target_pairs={{0,8},{4,12},{8,0},{12,4},{16,24},{20,28},{24,16},{28,20},{32,40},... | collective-permute-start | bytes 1179656 | tf_op jit(solution)/shard_map/ppermute | solution.py:324
  137.6 63.7 %collective-permute-start.24 = (bf16[6144,256]{1,0:T(8,128)(2,1)}, bf16[6144,256]{1,0:T(8,128)(2,1)}, u32[]{:S(2)}, u32[]{:S(2)}) collective-permute-start(bf16[6144,256]{1,0:T(8,128)(2,1)} %get-tuple-element.36), channel_id=1, source_target_pairs={{0,1},{1,0},{2,3},{3,2},{4,5},{5,4},{6,7},{7,6},{8,9},{9,8},{10,11... | collective-permute-start | bytes 9437192 | tf_op jit(solution)/shard_map/ppermute | solution.py:442
  138.0 8.2 %collective-permute-start.28 = (bf16[512,384]{1,0:T(8,128)(2,1)S(1)}, bf16[512,384]{1,0:T(8,128)(2,1)S(1)}, u32[]{:S(2)}, u32[]{:S(2)}) collective-permute-start(bf16[512,384]{1,0:T(8,128)(2,1)S(1)} %collective-permute-done.23), channel_id=1, source_target_pairs={{0,16},{4,20},{8,24},{12,28},{16,32},{20,36},{24,40},{28,44},{32,4... | collective-permute-start | bytes 1179656 | tf_op jit(solution)/shard_map/ppermute | solution.py:324
  142.7 7.0 %collective-permute-start.29 = (bf16[512,384]{1,0:T(8,128)(2,1)S(1)}, bf16[512,384]{1,0:T(8,128)(2,1)S(1)}, u32[]{:S(2)}, u32[]{:S(2)}) collective-permute-start(bf16[512,384]{1,0:T(8,128)(2,1)S(1)} %collective-permute-done.23), channel_id=1, source_target_pairs={{0,48},{4,52},{8,56},{12,60},{16,0},{20,4},{24,8},{28,12},{32,16},... | collective-permute-start | bytes 1179656 | tf_op jit(solution)/shard_map/ppermute | solution.py:324
  144.2 8.5 %collective-permute-start.30 = (bf16[512,384]{1,0:T(8,128)(2,1)S(1)}, bf16[512,384]{1,0:T(8,128)(2,1)S(1)}, u32[]{:S(2)}, u32[]{:S(2)}) collective-permute-start(bf16[512,384]{1,0:T(8,128)(2,1)S(1)} %collective-permute-done.23), channel_id=1, source_target_pairs={{0,32},{4,36},{8,40},{12,44},{16,48},{20,52},{24,56},{28,60},{32,0... | collective-permute-start | bytes 1179656 | tf_op jit(solution)/shard_map/ppermute | solution.py:324
  144.7 41.6 %collective-permute-start.31 = (bf16[2048,384]{1,0:T(8,128)(2,1)S(1)}, bf16[2048,384]{1,0:T(8,128)(2,1)}, u32[]{:S(2)}, u32[]{:S(2)}) collective-permute-start(bf16[2048,384]{1,0:T(8,128)(2,1)S(1)} %pad_maximum_fusion.refs_3_.refs_4_), channel_id=1, source_target_pairs={{0,16},{4,20},{8,24},{12,28},{16,32},{20,36},{24,40},{28,44},{32,4... | collective-permute-start | bytes 4718600 | tf_op jit(solution)/shard_map/ppermute | solution.py:324
  146.3 40.0 %collective-permute-start.32 = (bf16[2048,384]{1,0:T(8,128)(2,1)S(1)}, bf16[2048,384]{1,0:T(8,128)(2,1)}, u32[]{:S(2)}, u32[]{:S(2)}) collective-permute-start(bf16[2048,384]{1,0:T(8,128)(2,1)S(1)} %pad_maximum_fusion.refs_3_.refs_4_), channel_id=1, source_target_pairs={{0,48},{4,52},{8,56},{12,60},{16,0},{20,4},{24,8},{28,12},{32,16},... | collective-permute-start | bytes 4718600 | tf_op jit(solution)/shard_map/ppermute | solution.py:324
  152.7 33.6 %collective-permute-start.33 = (bf16[2048,384]{1,0:T(8,128)(2,1)S(1)}, bf16[2048,384]{1,0:T(8,128)(2,1)}, u32[]{:S(2)}, u32[]{:S(2)}) collective-permute-start(bf16[2048,384]{1,0:T(8,128)(2,1)S(1)} %constant_dynamic-update-slice_fusion.refs_4_.refs_5_), channel_id=1, source_target_pairs={{0,4},{4,8},{8,12},{12,0},{16,20},{20,24},{24,28},{28,16},{32,36},... | collective-permute-start | bytes 4718600 | tf_op jit(solution)/shard_map/ppermute | solution.py:324
  152.8 33.5 %collective-permute-start.34 = (bf16[2048,384]{1,0:T(8,128)(2,1)S(1)}, bf16[2048,384]{1,0:T(8,128)(2,1)}, u32[]{:S(2)}, u32[]{:S(2)}) collective-permute-start(bf16[2048,384]{1,0:T(8,128)(2,1)S(1)} %constant_dynamic-update-slice_fusion.refs_4_.refs_5_), channel_id=1, source_target_pairs={{0,12},{4,0},{8,4},{12,8},{16,28},{20,16},{24,20},{28,24},{32,44},... | collective-permute-start | bytes 4718600 | tf_op jit(solution)/shard_map/ppermute | solution.py:324
  187.5 27.2 %collective-permute-start.36 = (bf16[1024,384]{1,0:T(8,128)(2,1)S(1)}, bf16[1024,384]{1,0:T(8,128)(2,1)S(1)}, u32[]{:S(2)}, u32[]{:S(2)}) collective-permute-start(bf16[1024,384]{1,0:T(8,128)(2,1)S(1)} %slice.71), channel_id=1, source_target_pairs={{0,16},{4,20},{8,24},{12,28},{16,32},{20,36},{24,40},{28,44},{32,4... | collective-permute-start | bytes 2359304 | tf_op jit(solution)/shard_map/ppermute | solution.py:324
  190.4 24.4 %collective-permute-start.37 = (bf16[1024,384]{1,0:T(8,128)(2,1)S(1)}, bf16[1024,384]{1,0:T(8,128)(2,1)S(1)}, u32[]{:S(2)}, u32[]{:S(2)}) collective-permute-start(bf16[1024,384]{1,0:T(8,128)(2,1)S(1)} %slice.72), channel_id=1, source_target_pairs={{0,48},{4,52},{8,56},{12,60},{16,0},{20,4},{24,8},{28,12},{32,16},... | collective-permute-start | bytes 2359304 | tf_op jit(solution)/shard_map/ppermute | solution.py:324
  193.7 21.0 %collective-permute-start.38 = (bf16[1024,384]{1,0:T(8,128)(2,1)S(1)}, bf16[1024,384]{1,0:T(8,128)(2,1)S(1)}, u32[]{:S(2)}, u32[]{:S(2)}) collective-permute-start(bf16[1024,384]{1,0:T(8,128)(2,1)S(1)} %slice.73), channel_id=1, source_target_pairs={{0,4},{4,8},{8,12},{12,0},{16,20},{20,24},{24,28},{28,16},{32,36},... | collective-permute-start | bytes 2359304 | tf_op jit(solution)/shard_map/ppermute | solution.py:324
  195.0 19.7 %collective-permute-start.39 = (bf16[1024,384]{1,0:T(8,128)(2,1)S(1)}, bf16[1024,384]{1,0:T(8,128)(2,1)S(1)}, u32[]{:S(2)}, u32[]{:S(2)}) collective-permute-start(bf16[1024,384]{1,0:T(8,128)(2,1)S(1)} %slice.74), channel_id=1, source_target_pairs={{0,12},{4,0},{8,4},{12,8},{16,28},{20,16},{24,20},{28,24},{32,44},... | collective-permute-start | bytes 2359304 | tf_op jit(solution)/shard_map/ppermute | solution.py:324
  214.8 24.7 %copy-start.1 = (f32[1,16,128,128]{3,2,1,0:T(8,128)S(1)}, f32[1,16,128,128]{3,2,1,0:T(8,128)}, u32[]{:S(2)}) copy-start(f32[1,16,128,128]{3,2,1,0:T(8,128)} %param.13) | copy-start | bytes 3145732
  222.1 14.1 %collective-permute-start.41 = (bf16[16,256]{1,0:T(8,128)(2,1)S(1)}, bf16[16,256]{1,0:T(8,128)(2,1)S(1)}, u32[]{:S(2)}, u32[]{:S(2)}) collective-permute-start(bf16[16,256]{1,0:T(8,128)(2,1)S(1)} %get-tuple-element.58), channel_id=1, source_target_pairs={{1,66},{2,65},{3,64},{0,67},{65,2},{66,1},{67,0},{64,3},{5,70},{6,... | collective-permute-start | bytes 24584 | tf_op jit(solution)/shard_map/ppermute | solution.py:382
  234.9 3.1 %collective-permute-start.42 = (bf16[16,256]{1,0:T(8,128)(2,1)S(1)}, bf16[16,256]{1,0:T(8,128)(2,1)S(1)}, u32[]{:S(2)}, u32[]{:S(2)}) collective-permute-start(bf16[16,256]{1,0:T(8,128)(2,1)S(1)} %get-tuple-element.59), channel_id=1, source_target_pairs={{0,65},{1,64},{2,67},{3,66},{64,1},{65,0},{66,3},{67,2},{4,69},{5,... | collective-permute-start | bytes 24584 | tf_op jit(solution)/shard_map/ppermute | solution.py:382
  234.9 3.1 %collective-permute-start.40 = (bf16[16,512]{1,0:T(8,128)(2,1)S(1)}, bf16[16,512]{1,0:T(8,128)(2,1)S(1)}, u32[]{:S(2)}, u32[]{:S(2)}) collective-permute-start(bf16[16,512]{1,0:T(8,128)(2,1)S(1)} %slice.88), channel_id=1, source_target_pairs={{0,64},{1,65},{2,66},{3,67},{64,0},{65,1},{66,2},{67,3},{4,68},{5,... | collective-permute-start | bytes 49160 | tf_op jit(solution)/shard_map/ppermute | solution.py:382
  234.9 3.8 %collective-permute-start.35 = (bf16[1,512,384]{2,1,0:T(8,128)(2,1)S(1)}, bf16[1,512,384]{2,1,0:T(8,128)(2,1)S(1)}, u32[]{:S(2)}, u32[]{:S(2)}) collective-permute-start(bf16[1,512,384]{2,1,0:T(8,128)(2,1)S(1)} %bitcast.61), channel_id=1, source_target_pairs={{0,64},{1,65},{2,66},{3,67},{64,0},{65,1},{66,2},{67,3},{4,68},{5,... | collective-permute-start | bytes 1179656 | tf_op jit(solution)/shard_map/ppermute | solution.py:382

commit v11 on v10

--- a/solution.py
+++ b/solution.py
@@ -394,6 +394,7 @@
         return [lax.dynamic_slice_in_dim(x, n * half, half, 1) for n in (odd, 1 - odd)]
 
     first_bias, second_bias = halves(enc_bias)
+    packed, first_bias, second_bias = lax.optimization_barrier((packed, first_bias, second_bias))
     bias = jnp.concatenate(
         [
             enc_bias,

time: 241 us -> 240 us (level)
  no operation moved by 1% of the time
where the time goes in v11:
time: 240 us; the launch traced here: 239 us
  starting transfers between devices  83.1 us (35%)
  waiting for transfers between devices  75 us (31%)
  Pallas kernels  47.5 us (20%)
  local copies, waits for them, and re-layouts  31.5 us (13%)
    ppermute x28, starting transfers between devices, moved(): return lax.ppermute(x, 'seq', pairs)  40.6 us
    ppermute x28, waiting for transfers between devices, moved(): return lax.ppermute(x, 'seq', pairs)  29.5 us
    pallas_call x3, Pallas kernels, encode(): pl.pallas_call(functools.partial(encode_kernel, len(encoders), len(arrays...  26.4 us
    ppermute x1, waiting for transfers between devices, local(): lax.ppermute(second_bias, 'head', paired(1))  21.7 us
    ppermute x4, starting transfers between devices, from_section(): return lax.ppermute(x, ('section', 'head'), both)  13.3 us
    slice x8, local copies, waits for them, and re-layouts, planes(): across = (moved(up[:middle], axis, 1), moved(down[middle:], axis, -1))  11.3 us
    pallas_call x1, Pallas kernels, project(): pl.pallas_call(functools.partial(project_kernel, len(arrays), 0, False),...  10.5 us
    all_to_all x1, waiting for transfers between devices, local(): lax.all_to_all(jnp.broadcast_to(second[None], (2, *second.shape)), 'head'...  8.34 us
  transfers between devices with their start and end apart: 46, of which 16 were waited for; matrix products, arithmetic and copies ran while one was open for 12% of the time, Pallas kernels for 15%

profile of v11, /device:TPU:1, one launch (start us, length us, event | category | flops | bytes accessed | tf_op | source)
XLA Modules:
  0.0 239.4 jit_solution(12053892535688172672)
XLA Ops:
  0.6 3.4 %collective-permute-start = (bf16[2048,384]{1,0:T(8,128)(2,1)}, bf16[2048,384]{1,0:T(8,128)(2,1)}, u32[]{:S(2)}, u32[]{:S(2)}) collective-permute-start(bf16[2048,384]{1,0:T(8,128)(2,1)} %bitcast.66), channel_id=1, source_target_pairs={{1,0},{2,1},{3,2},{0,3},{5,4},{6,5},{7,6},{4,7},{9,8},{10,9},{11,1... | collective-permute-start | bytes 4718600 | tf_op jit(solution)/shard_map/ppermute | solution.py:371
  5.4 1.6 shard_map.113
  7.1 2.8 %collective-permute-start.5 = (f32[1,256]{1,0:T(1,128)S(1)}, f32[1,256]{1,0:T(1,128)S(1)}, u32[]{:S(2)}, u32[]{:S(2)}) collective-permute-start(f32[1,256]{1,0:T(1,128)S(1)} %get-tuple-element.28), channel_id=1, source_target_pairs={{1,2},{2,1},{3,0},{0,3},{5,6},{6,5},{7,4},{4,7},{9,10},{10,9},{11,... | collective-permute-start | bytes 3080 | tf_op jit(solution)/shard_map/ppermute | solution.py:401
  9.8 7.8 %all-to-all-start = ((bf16[16,400,128]{2,1,0:T(8,128)(2,1)}), bf16[16,400,128]{2,1,0:T(8,128)(2,1)S(1)}, u32[]{:S(2)}, u32[]{:S(2)}) async-start(bf16[16,400,128]{2,1,0:T(8,128)(2,1)} %copy-done.2), calls=%async_computation | async-start | bytes 3276800 | tf_op jit(solution)/shard_map/all_to_all | solution.py:408
  17.6 1.2 collective-permute-start.2
  18.8 21.7 %collective-permute-done.5 = f32[1,256]{1,0:T(1,128)S(1)} collective-permute-done((f32[1,256]{1,0:T(1,128)S(1)}, f32[1,256]{1,0:T(1,128)S(1)}, u32[]{:S(2)}, u32[]{:S(2)}) %collective-permute-start.5) | collective-permute-done | bytes 1056 | tf_op jit(solution)/shard_map/ppermute | solution.py:401
  40.5 0.9 collective-permute-start.4
  41.5 3.1 %collective-permute-done.3 = f32[1,2048]{1,0:T(1,128)S(1)} collective-permute-done((f32[1,2048]{1,0:T(1,128)S(1)}, f32[1,2048]{1,0:T(1,128)S(1)}, u32[]{:S(2)}, u32[]{:S(2)}) %collective-permute-start.3) | collective-permute-done | bytes 8224 | tf_op jit(solution)/shard_map/ppermute | solution.py:371
  44.6 4.1 %shard_map.114 = bf16[4,512,128]{2,1,0:T(8,128)(2,1)} custom-call(bf16[16,400,128]{2,1,0:T(8,128)(2,1)S(1)} %all-to-all-done.packed_ref, f32[128,128]{1,0:T(8,128)S(1)} %dynamic-slice_bitcast_fusion.7.prior_ref, f32[1,128]{1,0:T(1,128)S(1)} %constant_dynamic-slice_fusion.gain_ref), custom_call_target="tpu_custom_call" | custom-call | tf_op jit(solution)/shard_map/pallas_call | solution.py:89
  48.7 3.5 %all-to-all-start.1 = ((bf16[4,512,128]{2,1,0:T(8,128)(2,1)}), bf16[4,512,128]{2,1,0:T(8,128)(2,1)S(1)}, u32[]{:S(2)}, u32[]{:S(2)}) async-start(bf16[4,512,128]{2,1,0:T(8,128)(2,1)} %shard_map.114), calls=%async_computation.1 | async-start | bytes 1048576 | tf_op jit(solution)/shard_map/all_to_all | solution.py:417
  52.2 2.1 slice.63
  54.4 2.1 slice.64
  56.5 2.6 %all-to-all-done.1 = bf16[4,512,128]{2,1,0:T(8,128)(2,1)S(1)} async-done(((bf16[4,512,128]{2,1,0:T(8,128)(2,1)}), bf16[4,512,128]{2,1,0:T(8,128)(2,1)S(1)}, u32[]{:S(2)}, u32[]{:S(2)}) %all-to-all-start.1) | async-done | bytes 524320 | tf_op jit(solution)/shard_map/all_to_all | solution.py:417
  59.2 1.0 collective-permute-start.13
  60.3 1.7 collective-permute-start.10
  62.0 2.2 collective-permute-start.11
  64.2 1.2 collective-permute-start.12
  65.4 1.3 collective-permute-start.7
  66.7 1.2 collective-permute-done.10
  67.9 2.7 %collective-permute-start.8 = (bf16[256,512]{1,0:T(8,128)(2,1)S(1)}, bf16[256,512]{1,0:T(8,128)(2,1)S(1)}, u32[]{:S(2)}, u32[]{:S(2)}) collective-permute-start(bf16[256,512]{1,0:T(8,128)(2,1)S(1)} %get-tuple-element.55), channel_id=1, source_target_pairs={{0,12},{4,0},{8,4},{12,8},{16,28},{20,16},{24,20},{28,24},{32,44},... | collective-permute-start | bytes 786440 | tf_op jit(solution)/shard_map/ppermute | solution.py:324
  70.6 2.9 %collective-permute-start.9 = (bf16[256,512]{1,0:T(8,128)(2,1)S(1)}, bf16[256,512]{1,0:T(8,128)(2,1)S(1)}, u32[]{:S(2)}, u32[]{:S(2)}) collective-permute-start(bf16[256,512]{1,0:T(8,128)(2,1)S(1)} %get-tuple-element.55), channel_id=1, source_target_pairs={{0,8},{4,12},{8,0},{12,4},{16,24},{20,28},{24,16},{28,20},{32,40},... | collective-permute-start | bytes 786440 | tf_op jit(solution)/shard_map/ppermute | solution.py:324
  74.5 2.8 %collective-permute-start.21 = (bf16[1024,512]{1,0:T(8,128)(2,1)S(1)}, bf16[1024,512]{1,0:T(8,128)(2,1)}, u32[]{:S(2)}, u32[]{:S(2)}) collective-permute-start(bf16[1024,512]{1,0:T(8,128)(2,1)S(1)} %pad_maximum_fusion.2.refs_8_), channel_id=1, source_target_pairs={{0,12},{4,0},{8,4},{12,8},{16,28},{20,16},{24,20},{28,24},{32,44},... | collective-permute-start | bytes 3145736 | tf_op jit(solution)/shard_map/ppermute | solution.py:324
  77.3 1.3 collective-permute-done.9
  80.3 2.7 %collective-permute-start.17 = (bf16[1024,512]{1,0:T(8,128)(2,1)S(1)}, bf16[1024,512]{1,0:T(8,128)(2,1)}, u32[]{:S(2)}, u32[]{:S(2)}) collective-permute-start(bf16[1024,512]{1,0:T(8,128)(2,1)S(1)} %pad_maximum_fusion.1.refs_7_), channel_id=1, source_target_pairs={{0,48},{4,52},{8,56},{12,60},{16,0},{20,4},{24,8},{28,12},{32,16},... | collective-permute-start | bytes 3145736 | tf_op jit(solution)/shard_map/ppermute | solution.py:324
  83.1 4.9 %dynamic-slice_bitcast_fusion = (bf16[6144,256]{1,0:T(8,128)(2,1)}, bf16[6144,256]{1,0:T(8,128)(2,1)S(1)}) fusion(bf16[1,6144,512]{2,1,0:T(8,128)(2,1)} %param.18, s32[]{:T(128)S(6)} %select_n.259, s32[]{:T(128)S(6)} %select_n.260), kind=kLoop, calls=%fused_computation | loop fusion | bytes 12582920 | tf_op jit(solution)/shard_map/dynamic_slice | solution.py:394
  88.0 3.1 %broadcast_in_dim.12 = bf16[2,6144,256]{2,1,0:T(8,128)(2,1)} broadcast(bf16[6144,256]{1,0:T(8,128)(2,1)S(1)} %get-tuple-element.36), dimensions={1,2} | broadcast | bytes 9437184 | tf_op jit(solution)/shard_map/broadcast_in_dim | solution.py:431
  91.1 6.7 %all-to-all-start.2 = ((bf16[2,6144,256]{2,1,0:T(8,128)(2,1)}), bf16[2,6144,256]{2,1,0:T(8,128)(2,1)}, u32[]{:S(2)}, u32[]{:S(2)}) async-start(bf16[2,6144,256]{2,1,0:T(8,128)(2,1)} %broadcast_in_dim.12), calls=%async_computation.2 | async-start | bytes 12582912 | tf_op jit(solution)/shard_map/all_to_all | solution.py:430
  97.8 3.3 %collective-permute-done.19.refs_10_ = bf16[1024,512]{1,0:T(8,128)(2,1)S(1)} collective-permute-done((bf16[1024,512]{1,0:T(8,128)(2,1)S(1)}, bf16[1024,512]{1,0:T(8,128)(2,1)S(1)}, u32[]{:S(2)}, u32[]{:S(2)}) %collective-permute-start.19) | collective-permute-done | bytes 1048608 | tf_op jit(solution)/shard_map/ppermute | solution.py:324
  102.6 1.9 slice.87
  104.5 2.0 collective-permute-start.22
  106.5 1.9 slice.84
  108.3 1.0 collective-permute-start.16
  109.4 1.9 slice.85
  111.3 1.6 collective-permute-start.18
  113.0 10.5 %shard_map.115 = (f32[512,384]{1,0:T(8,128)S(1)}, f32[512,128]{1,0:T(8,128)S(1)}) custom-call(s32[32]{0:T(128)S(1)} %stack.98.refs_0_, f32[16,512]{1,0:T(8,128)S(1)} %pad_maximum_fusion.4.refs_1_, bf16[2048,384]{1,0:T(8,128)(2,1)} %bitcast.68, bf16[2048,384]{1,0:T(8,128)(2,1)} %collective-permute-done.refs_3_, bf16[1024,384]{1,0:T(8,128)(2,1)} %copy-done.7, ...), custom_call_target="tpu_custom_call" | custom-call | tf_op jit(solution)/shard_map/pallas_call | solution.py:229
  124.3 4.9 %shard_map.116 = bf16[512,384]{1,0:T(8,128)(2,1)S(1)} custom-call(s32[32]{0:T(128)S(1)} %stack.98.refs_0_, f32[16,512]{1,0:T(8,128)S(1)} %copy-done.5, bf16[2048,384]{1,0:T(8,128)(2,1)} %bitcast.69, bf16[2048,384]{1,0:T(8,128)(2,1)} %collective-permute-done.refs_3_, bf16[1024,384]{1,0:T(8,128)(2,1)} %copy-done.7, ...), custom_call_target="tpu_custom_call" | custom-call | tf_op jit(solution)/shard_map/pallas_call | solution.py:238
  129.3 1.0 collective-permute-start.23
  130.2 1.0 collective-permute-start.25
  131.2 1.7 collective-permute-start.26
  132.9 0.9 collective-permute-start.27
  133.8 3.7 %collective-permute-done.23 = bf16[512,384]{1,0:T(8,128)(2,1)S(1)} collective-permute-done((bf16[512,384]{1,0:T(8,128)(2,1)S(1)}, bf16[512,384]{1,0:T(8,128)(2,1)S(1)}, u32[]{:S(2)}, u32[]{:S(2)}) %collective-permute-start.23) | collective-permute-done | bytes 393248 | tf_op jit(solution)/shard_map/ppermute | solution.py:371
  138.0 4.6 %collective-permute-done.25 = bf16[512,384]{1,0:T(8,128)(2,1)S(1)} collective-permute-done((bf16[512,384]{1,0:T(8,128)(2,1)S(1)}, bf16[512,384]{1,0:T(8,128)(2,1)S(1)}, u32[]{:S(2)}, u32[]{:S(2)}) %collective-permute-start.25) | collective-permute-done | bytes 393248 | tf_op jit(solution)/shard_map/ppermute | solution.py:324
  142.7 1.5 collective-permute-start.29
  145.2 1.1 collective-permute-done.28
  146.3 1.3 collective-permute-start.32
  147.6 2.1 collective-permute-done.29
  149.8 2.8 %collective-permute-done.30 = bf16[512,384]{1,0:T(8,128)(2,1)S(1)} collective-permute-done((bf16[512,384]{1,0:T(8,128)(2,1)S(1)}, bf16[512,384]{1,0:T(8,128)(2,1)S(1)}, u32[]{:S(2)}, u32[]{:S(2)}) %collective-permute-start.30) | collective-permute-done | bytes 393248 | tf_op jit(solution)/shard_map/ppermute | solution.py:324
  152.8 2.7 %collective-permute-start.34 = (bf16[2048,384]{1,0:T(8,128)(2,1)S(1)}, bf16[2048,384]{1,0:T(8,128)(2,1)}, u32[]{:S(2)}, u32[]{:S(2)}) collective-permute-start(bf16[2048,384]{1,0:T(8,128)(2,1)S(1)} %constant_dynamic-update-slice_fusion.refs_4_.refs_5_), channel_id=1, source_target_pairs={{0,12},{4,0},{8,4},{12,8},{16,28},{20,16},{24,20},{28,24},{32,44},... | collective-permute-start | bytes 4718600 | tf_op jit(solution)/shard_map/ppermute | solution.py:324
  155.4 8.3 %all-to-all-done.2 = bf16[2,6144,256]{2,1,0:T(8,128)(2,1)} async-done(((bf16[2,6144,256]{2,1,0:T(8,128)(2,1)}), bf16[2,6144,256]{2,1,0:T(8,128)(2,1)}, u32[]{:S(2)}, u32[]{:S(2)}) %all-to-all-start.2) | async-done | bytes 6291488 | tf_op jit(solution)/shard_map/all_to_all | solution.py:430
  163.8 3.8 %dynamic-slice_bitcast_fusion.1.refs_2_ = bf16[6144,256]{1,0:T(8,128)(2,1)} fusion(bf16[2,6144,256]{2,1,0:T(8,128)(2,1)} %all-to-all-done.2, s32[]{:T(128)S(6)} %select_n.271), kind=kLoop, calls=%fused_computation.1 | loop fusion | bytes 6291460 | tf_op jit(solution)/shard_map/jit(dynamic_index_in_dim)/squeeze | solution.py:438
  167.6 5.7 %shard_map.117.refs_10_ = f32[1024,1024]{1,0:T(8,128)S(1)} custom-call(s32[32]{0:T(128)S(1)} %stack.98.refs_0_, bf16[6144,512]{1,0:T(8,128)(2,1)} %bitcast.63, bf16[6144,256]{1,0:T(8,128)(2,1)} %dynamic-slice_bitcast_fusion.1.refs_2_, bf16[2048,384]{1,0:T(8,128)(2,1)S(1)} %pad_maximum_fusion.refs_3_.refs_4_, ...), custom_call_target="tpu_custom_call" | custom-call | tf_op jit(solution)/shard_map/pallas_call | solution.py:303
  173.3 13.0 %collective-permute-done.31.refs_6_ = bf16[2048,384]{1,0:T(8,128)(2,1)} collective-permute-done((bf16[2048,384]{1,0:T(8,128)(2,1)S(1)}, bf16[2048,384]{1,0:T(8,128)(2,1)}, u32[]{:S(2)}, u32[]{:S(2)}) %collective-permute-start.31) | collective-permute-done | bytes 1572896 | tf_op jit(solution)/shard_map/ppermute | solution.py:324
  186.3 1.2 slice.71
  187.5 1.7 collective-permute-start.36
  189.2 1.2 slice.72
  190.4 2.1 collective-permute-start.37
  192.5 1.2 slice.73
  193.8 1.2 slice.74
  195.0 2.7 %collective-permute-start.39 = (bf16[1024,384]{1,0:T(8,128)(2,1)S(1)}, bf16[1024,384]{1,0:T(8,128)(2,1)S(1)}, u32[]{:S(2)}, u32[]{:S(2)}) collective-permute-start(bf16[1024,384]{1,0:T(8,128)(2,1)S(1)} %slice.74), channel_id=1, source_target_pairs={{0,12},{4,0},{8,4},{12,8},{16,28},{20,16},{24,20},{28,24},{32,44},... | collective-permute-start | bytes 2359304 | tf_op jit(solution)/shard_map/ppermute | solution.py:324
  197.7 3.6 %collective-permute-done.24.refs_3_ = bf16[6144,256]{1,0:T(8,128)(2,1)} collective-permute-done((bf16[6144,256]{1,0:T(8,128)(2,1)}, bf16[6144,256]{1,0:T(8,128)(2,1)}, u32[]{:S(2)}, u32[]{:S(2)}) %collective-permute-start.24) | collective-permute-done | bytes 3145760 | tf_op jit(solution)/shard_map/ppermute | solution.py:443
  201.3 13.4 %shard_map.118.refs_8_ = f32[1024,1024]{1,0:T(8,128)S(1)} custom-call(s32[32]{0:T(128)S(1)} %stack.98.refs_0_, bf16[6144,512]{1,0:T(8,128)(2,1)} %bitcast.64, bf16[6144,256]{1,0:T(8,128)(2,1)} %dynamic-slice_bitcast_fusion.1.refs_2_, bf16[6144,256]{1,0:T(8,128)(2,1)} %collective-permute-done.24.refs_3_, ...), custom_call_target="tpu_custom_call" | custom-call | tf_op jit(solution)/shard_map/pallas_call | solution.py:303
  214.8 7.3 %shard_map.119 = f32[16,1024]{1,0:T(8,128)S(1)} custom-call(s32[32]{0:T(128)S(1)} %stack.98.refs_0_, bf16[6144,512]{1,0:T(8,128)(2,1)} %bitcast.65, bf16[6144,256]{1,0:T(8,128)(2,1)} %dynamic-slice_bitcast_fusion.1.refs_2_, bf16[6144,256]{1,0:T(8,128)(2,1)} %collective-permute-done.24.refs_3_, bf16[1024,384]{1,0:T(8,128)(2,1)S(1)} %collective-permute-done.36.refs_4_, ...), custom_call_target="tpu_custom_call" | custom-call | tf_op jit(solution)/shard_map/pallas_call | solution.py:303
  222.1 12.8 %collective-permute-start.41 = (bf16[16,256]{1,0:T(8,128)(2,1)S(1)}, bf16[16,256]{1,0:T(8,128)(2,1)S(1)}, u32[]{:S(2)}, u32[]{:S(2)}) collective-permute-start(bf16[16,256]{1,0:T(8,128)(2,1)S(1)} %get-tuple-element.64), channel_id=1, source_target_pairs={{1,66},{2,65},{3,64},{0,67},{65,2},{66,1},{67,0},{64,3},{5,70},{6,... | collective-permute-start | bytes 24584 | tf_op jit(solution)/shard_map/ppermute | solution.py:382
  236.2 1.7 collective-permute-done.42
  (100 shorter events, 11.4 us)
Async XLA Ops:
  0.6 18.2 %copy-start = (f32[1,16,128,128]{3,2,1,0:T(8,128)S(1)}, f32[1,16,128,128]{3,2,1,0:T(8,128)}, u32[]{:S(2)}) copy-start(f32[1,16,128,128]{3,2,1,0:T(8,128)} %param.13) | copy-start | bytes 3145732
  0.6 44.0 %collective-permute-start = (bf16[2048,384]{1,0:T(8,128)(2,1)}, bf16[2048,384]{1,0:T(8,128)(2,1)}, u32[]{:S(2)}, u32[]{:S(2)}) collective-permute-start(bf16[2048,384]{1,0:T(8,128)(2,1)} %bitcast.66), channel_id=1, source_target_pairs={{1,0},{2,1},{3,2},{0,3},{5,4},{6,5},{7,6},{4,7},{9,8},{10,9},{11,1... | collective-permute-start | bytes 4718600 | tf_op jit(solution)/shard_map/ppermute | solution.py:371
  4.0 40.6 %collective-permute-start.1 = (bf16[2048,384]{1,0:T(8,128)(2,1)}, bf16[2048,384]{1,0:T(8,128)(2,1)}, u32[]{:S(2)}, u32[]{:S(2)}) collective-permute-start(bf16[2048,384]{1,0:T(8,128)(2,1)} %bitcast.67), channel_id=1, source_target_pairs={{3,0},{0,1},{1,2},{2,3},{7,4},{4,5},{5,6},{6,7},{11,8},{8,9},{9,10... | collective-permute-start | bytes 4718600 | tf_op jit(solution)/shard_map/ppermute | solution.py:371
  4.7 0.7 copy-start.6
  7.0 2.8 %copy-start.2 = (bf16[16,400,128]{2,1,0:T(8,128)(2,1)}, bf16[16,400,128]{2,1,0:T(8,128)(2,1)S(1)}, u32[]{:S(2)}) copy-start(bf16[16,400,128]{2,1,0:T(8,128)(2,1)S(1)} %shard_map.113) | copy-start | bytes 4915204
  7.0 10.6 %copy-start.8 = (f32[1,2048]{1,0:T(1,128)S(1)}, f32[1,2048]{1,0:T(1,128)}, u32[]{:S(2)}) copy-start(f32[1,2048]{1,0:T(1,128)} %param.15) | copy-start | bytes 24580
  7.0 34.4 %copy-start.9 = (f32[1,512]{1,0:T(1,128)S(1)}, f32[1,512]{1,0:T(1,128)}, u32[]{:S(2)}) copy-start(f32[1,512]{1,0:T(1,128)} %param.19) | copy-start | bytes 6148
  7.1 33.5 %collective-permute-start.5 = (f32[1,256]{1,0:T(1,128)S(1)}, f32[1,256]{1,0:T(1,128)S(1)}, u32[]{:S(2)}, u32[]{:S(2)}) collective-permute-start(f32[1,256]{1,0:T(1,128)S(1)} %get-tuple-element.28), channel_id=1, source_target_pairs={{1,2},{2,1},{3,0},{0,3},{5,6},{6,5},{7,4},{4,7},{9,10},{10,9},{11,... | collective-permute-start | bytes 3080 | tf_op jit(solution)/shard_map/ppermute | solution.py:401
  9.8 30.7 %collective-permute-start.6 = (f32[1,256]{1,0:T(1,128)S(1)}, f32[1,256]{1,0:T(1,128)S(1)}, u32[]{:S(2)}, u32[]{:S(2)}) collective-permute-start(f32[1,256]{1,0:T(1,128)S(1)} %get-tuple-element.29), channel_id=1, source_target_pairs={{0,1},{1,0},{2,3},{3,2},{4,5},{5,4},{6,7},{7,6},{8,9},{9,8},{10,11... | collective-permute-start | bytes 3080 | tf_op jit(solution)/shard_map/ppermute | solution.py:402
  9.8 34.8 %all-to-all-start = ((bf16[16,400,128]{2,1,0:T(8,128)(2,1)}), bf16[16,400,128]{2,1,0:T(8,128)(2,1)S(1)}, u32[]{:S(2)}, u32[]{:S(2)}) async-start(bf16[16,400,128]{2,1,0:T(8,128)(2,1)} %copy-done.2), calls=%async_computation | async-start | bytes 3276800 | tf_op jit(solution)/shard_map/all_to_all | solution.py:408
  17.6 23.8 %collective-permute-start.2 = (f32[1,2048]{1,0:T(1,128)S(1)}, f32[1,2048]{1,0:T(1,128)S(1)}, u32[]{:S(2)}, u32[]{:S(2)}) collective-permute-start(f32[1,2048]{1,0:T(1,128)S(1)} %copy-done.8), channel_id=1, source_target_pairs={{1,0},{2,1},{3,2},{0,3},{5,4},{6,5},{7,6},{4,7},{9,8},{10,9},{11,1... | collective-permute-start | bytes 24584 | tf_op jit(solution)/shard_map/ppermute | solution.py:371
  40.5 4.0 %collective-permute-start.3 = (f32[1,2048]{1,0:T(1,128)S(1)}, f32[1,2048]{1,0:T(1,128)S(1)}, u32[]{:S(2)}, u32[]{:S(2)}) collective-permute-start(f32[1,2048]{1,0:T(1,128)S(1)} %copy-done.8), channel_id=1, source_target_pairs={{2,0},{3,1},{0,2},{1,3},{6,4},{7,5},{4,6},{5,7},{10,8},{11,9},{8,1... | collective-permute-start | bytes 24584 | tf_op jit(solution)/shard_map/ppermute | solution.py:371
  40.5 4.0 %collective-permute-start.4 = (f32[1,2048]{1,0:T(1,128)S(1)}, f32[1,2048]{1,0:T(1,128)S(1)}, u32[]{:S(2)}, u32[]{:S(2)}) collective-permute-start(f32[1,2048]{1,0:T(1,128)S(1)} %copy-done.8), channel_id=1, source_target_pairs={{3,0},{0,1},{1,2},{2,3},{7,4},{4,5},{5,6},{6,7},{11,8},{8,9},{9,10... | collective-permute-start | bytes 24584 | tf_op jit(solution)/shard_map/ppermute | solution.py:371
  44.6 68.4 %copy-start.4 = (f32[16,512]{1,0:T(8,128)}, f32[16,512]{1,0:T(8,128)S(1)}, u32[]{:S(2)}) copy-start(f32[16,512]{1,0:T(8,128)S(1)} %pad_maximum_fusion.4.refs_1_) | copy-start | bytes 98308
  48.7 10.4 %all-to-all-start.1 = ((bf16[4,512,128]{2,1,0:T(8,128)(2,1)}), bf16[4,512,128]{2,1,0:T(8,128)(2,1)S(1)}, u32[]{:S(2)}, u32[]{:S(2)}) async-start(bf16[4,512,128]{2,1,0:T(8,128)(2,1)} %shard_map.114), calls=%async_computation.1 | async-start | bytes 1048576 | tf_op jit(solution)/shard_map/all_to_all | solution.py:417
  59.2 20.3 %collective-permute-start.13 = (bf16[1024,384]{1,0:T(8,128)(2,1)}, bf16[1024,384]{1,0:T(8,128)(2,1)S(1)}, u32[]{:S(2)}, u32[]{:S(2)}) collective-permute-start(bf16[1024,384]{1,0:T(8,128)(2,1)} %slice.63), channel_id=1, source_target_pairs={{1,0},{2,1},{3,2},{0,3},{5,4},{6,5},{7,6},{4,7},{9,8},{10,9},{11,1... | collective-permute-start | bytes 2359304 | tf_op jit(solution)/shard_map/ppermute | solution.py:371
  60.3 7.6 %collective-permute-start.10 = (bf16[256,512]{1,0:T(8,128)(2,1)S(1)}, bf16[256,512]{1,0:T(8,128)(2,1)S(1)}, u32[]{:S(2)}, u32[]{:S(2)}) collective-permute-start(bf16[256,512]{1,0:T(8,128)(2,1)S(1)} %get-tuple-element.54), channel_id=1, source_target_pairs={{0,16},{4,20},{8,24},{12,28},{16,32},{20,36},{24,40},{28,44},{32,4... | collective-permute-start | bytes 786440 | tf_op jit(solution)/shard_map/ppermute | solution.py:324
  62.0 8.6 %collective-permute-start.11 = (bf16[256,512]{1,0:T(8,128)(2,1)S(1)}, bf16[256,512]{1,0:T(8,128)(2,1)S(1)}, u32[]{:S(2)}, u32[]{:S(2)}) collective-permute-start(bf16[256,512]{1,0:T(8,128)(2,1)S(1)} %get-tuple-element.54), channel_id=1, source_target_pairs={{0,48},{4,52},{8,56},{12,60},{16,0},{20,4},{24,8},{28,12},{32,16},... | collective-permute-start | bytes 786440 | tf_op jit(solution)/shard_map/ppermute | solution.py:324
  64.2 9.3 %collective-permute-start.12 = (bf16[256,512]{1,0:T(8,128)(2,1)S(1)}, bf16[256,512]{1,0:T(8,128)(2,1)S(1)}, u32[]{:S(2)}, u32[]{:S(2)}) collective-permute-start(bf16[256,512]{1,0:T(8,128)(2,1)S(1)} %get-tuple-element.54), channel_id=1, source_target_pairs={{0,32},{4,36},{8,40},{12,44},{16,48},{20,52},{24,56},{28,60},{32,0... | collective-permute-start | bytes 786440 | tf_op jit(solution)/shard_map/ppermute | solution.py:324
  65.4 8.6 %collective-permute-start.7 = (bf16[256,512]{1,0:T(8,128)(2,1)S(1)}, bf16[256,512]{1,0:T(8,128)(2,1)S(1)}, u32[]{:S(2)}, u32[]{:S(2)}) collective-permute-start(bf16[256,512]{1,0:T(8,128)(2,1)S(1)} %get-tuple-element.55), channel_id=1, source_target_pairs={{0,4},{4,8},{8,12},{12,0},{16,20},{20,24},{24,28},{28,16},{32,36},... | collective-permute-start | bytes 786440 | tf_op jit(solution)/shard_map/ppermute | solution.py:324
  67.9 6.7 %collective-permute-start.8 = (bf16[256,512]{1,0:T(8,128)(2,1)S(1)}, bf16[256,512]{1,0:T(8,128)(2,1)S(1)}, u32[]{:S(2)}, u32[]{:S(2)}) collective-permute-start(bf16[256,512]{1,0:T(8,128)(2,1)S(1)} %get-tuple-element.55), channel_id=1, source_target_pairs={{0,12},{4,0},{8,4},{12,8},{16,28},{20,16},{24,20},{28,24},{32,44},... | collective-permute-start | bytes 786440 | tf_op jit(solution)/shard_map/ppermute | solution.py:324
  70.6 8.1 %collective-permute-start.9 = (bf16[256,512]{1,0:T(8,128)(2,1)S(1)}, bf16[256,512]{1,0:T(8,128)(2,1)S(1)}, u32[]{:S(2)}, u32[]{:S(2)}) collective-permute-start(bf16[256,512]{1,0:T(8,128)(2,1)S(1)} %get-tuple-element.55), channel_id=1, source_target_pairs={{0,8},{4,12},{8,0},{12,4},{16,24},{20,28},{24,16},{28,20},{32,40},... | collective-permute-start | bytes 786440 | tf_op jit(solution)/shard_map/ppermute | solution.py:324
  73.5 14.5 %collective-permute-start.14 = (bf16[1024,384]{1,0:T(8,128)(2,1)}, bf16[1024,384]{1,0:T(8,128)(2,1)}, u32[]{:S(2)}, u32[]{:S(2)}) collective-permute-start(bf16[1024,384]{1,0:T(8,128)(2,1)} %slice.64), channel_id=1, source_target_pairs={{3,0},{0,1},{1,2},{2,3},{7,4},{4,5},{5,6},{6,7},{11,8},{8,9},{9,10... | collective-permute-start | bytes 2359304 | tf_op jit(solution)/shard_map/ppermute | solution.py:371
  74.1 27.0 %collective-permute-start.19 = (bf16[1024,512]{1,0:T(8,128)(2,1)S(1)}, bf16[1024,512]{1,0:T(8,128)(2,1)S(1)}, u32[]{:S(2)}, u32[]{:S(2)}) collective-permute-start(bf16[1024,512]{1,0:T(8,128)(2,1)S(1)} %pad_maximum_fusion.2.refs_8_), channel_id=1, source_target_pairs={{0,4},{4,8},{8,12},{12,0},{16,20},{20,24},{24,28},{28,16},{32,36},... | collective-permute-start | bytes 3145736 | tf_op jit(solution)/shard_map/ppermute | solution.py:324
  74.5 28.1 %collective-permute-start.21 = (bf16[1024,512]{1,0:T(8,128)(2,1)S(1)}, bf16[1024,512]{1,0:T(8,128)(2,1)}, u32[]{:S(2)}, u32[]{:S(2)}) collective-permute-start(bf16[1024,512]{1,0:T(8,128)(2,1)S(1)} %pad_maximum_fusion.2.refs_8_), channel_id=1, source_target_pairs={{0,12},{4,0},{8,4},{12,8},{16,28},{20,16},{24,20},{28,24},{32,44},... | collective-permute-start | bytes 3145736 | tf_op jit(solution)/shard_map/ppermute | solution.py:324
  78.7 27.7 %collective-permute-start.15 = (bf16[1024,512]{1,0:T(8,128)(2,1)S(1)}, bf16[1024,512]{1,0:T(8,128)(2,1)}, u32[]{:S(2)}, u32[]{:S(2)}) collective-permute-start(bf16[1024,512]{1,0:T(8,128)(2,1)S(1)} %pad_maximum_fusion.1.refs_7_), channel_id=1, source_target_pairs={{0,16},{4,20},{8,24},{12,28},{16,32},{20,36},{24,40},{28,44},{32,4... | collective-permute-start | bytes 3145736 | tf_op jit(solution)/shard_map/ppermute | solution.py:324
  79.5 0.9 copy-start.7
  80.3 29.0 %collective-permute-start.17 = (bf16[1024,512]{1,0:T(8,128)(2,1)S(1)}, bf16[1024,512]{1,0:T(8,128)(2,1)}, u32[]{:S(2)}, u32[]{:S(2)}) collective-permute-start(bf16[1024,512]{1,0:T(8,128)(2,1)S(1)} %pad_maximum_fusion.1.refs_7_), channel_id=1, source_target_pairs={{0,48},{4,52},{8,56},{12,60},{16,0},{20,4},{24,8},{28,12},{32,16},... | collective-permute-start | bytes 3145736 | tf_op jit(solution)/shard_map/ppermute | solution.py:324
  91.1 72.7 %all-to-all-start.2 = ((bf16[2,6144,256]{2,1,0:T(8,128)(2,1)}), bf16[2,6144,256]{2,1,0:T(8,128)(2,1)}, u32[]{:S(2)}, u32[]{:S(2)}) async-start(bf16[2,6144,256]{2,1,0:T(8,128)(2,1)} %broadcast_in_dim.12), calls=%async_computation.2 | async-start | bytes 12582912 | tf_op jit(solution)/shard_map/all_to_all | solution.py:430
  101.9 21.6 %collective-permute-start.20 = (bf16[512,512]{1,0:T(8,128)(2,1)}, bf16[512,512]{1,0:T(8,128)(2,1)}, u32[]{:S(2)}, u32[]{:S(2)}) collective-permute-start(bf16[512,512]{1,0:T(8,128)(2,1)} %slice.86), channel_id=1, source_target_pairs={{0,4},{4,8},{8,12},{12,0},{16,20},{20,24},{24,28},{28,16},{32,36},... | collective-permute-start | bytes 1572872 | tf_op jit(solution)/shard_map/ppermute | solution.py:324
  104.5 19.0 %collective-permute-start.22 = (bf16[512,512]{1,0:T(8,128)(2,1)}, bf16[512,512]{1,0:T(8,128)(2,1)}, u32[]{:S(2)}, u32[]{:S(2)}) collective-permute-start(bf16[512,512]{1,0:T(8,128)(2,1)} %slice.87), channel_id=1, source_target_pairs={{0,12},{4,0},{8,4},{12,8},{16,28},{20,16},{24,20},{28,24},{32,44},... | collective-permute-start | bytes 1572872 | tf_op jit(solution)/shard_map/ppermute | solution.py:324
  108.3 15.2 %collective-permute-start.16 = (bf16[512,512]{1,0:T(8,128)(2,1)}, bf16[512,512]{1,0:T(8,128)(2,1)}, u32[]{:S(2)}, u32[]{:S(2)}) collective-permute-start(bf16[512,512]{1,0:T(8,128)(2,1)} %slice.84), channel_id=1, source_target_pairs={{0,16},{4,20},{8,24},{12,28},{16,32},{20,36},{24,40},{28,44},{32,4... | collective-permute-start | bytes 1572872 | tf_op jit(solution)/shard_map/ppermute | solution.py:324
  111.3 12.3 %collective-permute-start.18 = (bf16[512,512]{1,0:T(8,128)(2,1)}, bf16[512,512]{1,0:T(8,128)(2,1)}, u32[]{:S(2)}, u32[]{:S(2)}) collective-permute-start(bf16[512,512]{1,0:T(8,128)(2,1)} %slice.85), channel_id=1, source_target_pairs={{0,48},{4,52},{8,56},{12,60},{16,0},{20,4},{24,8},{28,12},{32,16},... | collective-permute-start | bytes 1572872 | tf_op jit(solution)/shard_map/ppermute | solution.py:324
  113.0 10.5 %copy-start.3 = (bf16[1,512,384]{2,1,0:T(8,128)(2,1)S(1)}, bf16[1,512,384]{2,1,0:T(8,128)(2,1)}, u32[]{:S(2)}) copy-start(bf16[1,512,384]{2,1,0:T(8,128)(2,1)} %param.16) | copy-start | bytes 1179652
  123.5 0.8 copy-start.5
  129.3 8.3 %collective-permute-start.23 = (bf16[512,384]{1,0:T(8,128)(2,1)S(1)}, bf16[512,384]{1,0:T(8,128)(2,1)S(1)}, u32[]{:S(2)}, u32[]{:S(2)}) collective-permute-start(bf16[512,384]{1,0:T(8,128)(2,1)S(1)} %shard_map.116), channel_id=1, source_target_pairs={{2,0},{3,1},{0,2},{1,3},{6,4},{7,5},{4,6},{5,7},{10,8},{11,9},{8,1... | collective-permute-start | bytes 1179656 | tf_op jit(solution)/shard_map/ppermute | solution.py:371
  130.2 12.5 %collective-permute-start.25 = (bf16[512,384]{1,0:T(8,128)(2,1)S(1)}, bf16[512,384]{1,0:T(8,128)(2,1)S(1)}, u32[]{:S(2)}, u32[]{:S(2)}) collective-permute-start(bf16[512,384]{1,0:T(8,128)(2,1)S(1)} %shard_map.116), channel_id=1, source_target_pairs={{0,4},{4,8},{8,12},{12,0},{16,20},{20,24},{24,28},{28,16},{32,36},... | collective-permute-start | bytes 1179656 | tf_op jit(solution)/shard_map/ppermute | solution.py:324
  131.2 12.9 %collective-permute-start.26 = (bf16[512,384]{1,0:T(8,128)(2,1)S(1)}, bf16[512,384]{1,0:T(8,128)(2,1)S(1)}, u32[]{:S(2)}, u32[]{:S(2)}) collective-permute-start(bf16[512,384]{1,0:T(8,128)(2,1)S(1)} %shard_map.116), channel_id=1, source_target_pairs={{0,12},{4,0},{8,4},{12,8},{16,28},{20,16},{24,20},{28,24},{32,44},... | collective-permute-start | bytes 1179656 | tf_op jit(solution)/shard_map/ppermute | solution.py:324
  132.9 11.6 %collective-permute-start.27 = (bf16[512,384]{1,0:T(8,128)(2,1)S(1)}, bf16[512,384]{1,0:T(8,128)(2,1)S(1)}, u32[]{:S(2)}, u32[]{:S(2)}) collective-permute-start(bf16[512,384]{1,0:T(8,128)(2,1)S(1)} %shard_map.116), channel_id=1, source_target_pairs={{0,8},{4,12},{8,0},{12,4},{16,24},{20,28},{24,16},{28,20},{32,40},... | collective-permute-start | bytes 1179656 | tf_op jit(solution)/shard_map/ppermute | solution.py:324
  137.6 63.7 %collective-permute-start.24 = (bf16[6144,256]{1,0:T(8,128)(2,1)}, bf16[6144,256]{1,0:T(8,128)(2,1)}, u32[]{:S(2)}, u32[]{:S(2)}) collective-permute-start(bf16[6144,256]{1,0:T(8,128)(2,1)} %get-tuple-element.42), channel_id=1, source_target_pairs={{0,1},{1,0},{2,3},{3,2},{4,5},{5,4},{6,7},{7,6},{8,9},{9,8},{10,11... | collective-permute-start | bytes 9437192 | tf_op jit(solution)/shard_map/ppermute | solution.py:443
  138.0 8.2 %collective-permute-start.28 = (bf16[512,384]{1,0:T(8,128)(2,1)S(1)}, bf16[512,384]{1,0:T(8,128)(2,1)S(1)}, u32[]{:S(2)}, u32[]{:S(2)}) collective-permute-start(bf16[512,384]{1,0:T(8,128)(2,1)S(1)} %collective-permute-done.23), channel_id=1, source_target_pairs={{0,16},{4,20},{8,24},{12,28},{16,32},{20,36},{24,40},{28,44},{32,4... | collective-permute-start | bytes 1179656 | tf_op jit(solution)/shard_map/ppermute | solution.py:324
  142.7 7.0 %collective-permute-start.29 = (bf16[512,384]{1,0:T(8,128)(2,1)S(1)}, bf16[512,384]{1,0:T(8,128)(2,1)S(1)}, u32[]{:S(2)}, u32[]{:S(2)}) collective-permute-start(bf16[512,384]{1,0:T(8,128)(2,1)S(1)} %collective-permute-done.23), channel_id=1, source_target_pairs={{0,48},{4,52},{8,56},{12,60},{16,0},{20,4},{24,8},{28,12},{32,16},... | collective-permute-start | bytes 1179656 | tf_op jit(solution)/shard_map/ppermute | solution.py:324
  144.2 8.5 %collective-permute-start.30 = (bf16[512,384]{1,0:T(8,128)(2,1)S(1)}, bf16[512,384]{1,0:T(8,128)(2,1)S(1)}, u32[]{:S(2)}, u32[]{:S(2)}) collective-permute-start(bf16[512,384]{1,0:T(8,128)(2,1)S(1)} %collective-permute-done.23), channel_id=1, source_target_pairs={{0,32},{4,36},{8,40},{12,44},{16,48},{20,52},{24,56},{28,60},{32,0... | collective-permute-start | bytes 1179656 | tf_op jit(solution)/shard_map/ppermute | solution.py:324
  144.7 41.6 %collective-permute-start.31 = (bf16[2048,384]{1,0:T(8,128)(2,1)S(1)}, bf16[2048,384]{1,0:T(8,128)(2,1)}, u32[]{:S(2)}, u32[]{:S(2)}) collective-permute-start(bf16[2048,384]{1,0:T(8,128)(2,1)S(1)} %pad_maximum_fusion.refs_3_.refs_4_), channel_id=1, source_target_pairs={{0,16},{4,20},{8,24},{12,28},{16,32},{20,36},{24,40},{28,44},{32,4... | collective-permute-start | bytes 4718600 | tf_op jit(solution)/shard_map/ppermute | solution.py:324
  146.3 40.0 %collective-permute-start.32 = (bf16[2048,384]{1,0:T(8,128)(2,1)S(1)}, bf16[2048,384]{1,0:T(8,128)(2,1)}, u32[]{:S(2)}, u32[]{:S(2)}) collective-permute-start(bf16[2048,384]{1,0:T(8,128)(2,1)S(1)} %pad_maximum_fusion.refs_3_.refs_4_), channel_id=1, source_target_pairs={{0,48},{4,52},{8,56},{12,60},{16,0},{20,4},{24,8},{28,12},{32,16},... | collective-permute-start | bytes 4718600 | tf_op jit(solution)/shard_map/ppermute | solution.py:324
  152.7 33.6 %collective-permute-start.33 = (bf16[2048,384]{1,0:T(8,128)(2,1)S(1)}, bf16[2048,384]{1,0:T(8,128)(2,1)}, u32[]{:S(2)}, u32[]{:S(2)}) collective-permute-start(bf16[2048,384]{1,0:T(8,128)(2,1)S(1)} %constant_dynamic-update-slice_fusion.refs_4_.refs_5_), channel_id=1, source_target_pairs={{0,4},{4,8},{8,12},{12,0},{16,20},{20,24},{24,28},{28,16},{32,36},... | collective-permute-start | bytes 4718600 | tf_op jit(solution)/shard_map/ppermute | solution.py:324
  152.8 33.5 %collective-permute-start.34 = (bf16[2048,384]{1,0:T(8,128)(2,1)S(1)}, bf16[2048,384]{1,0:T(8,128)(2,1)}, u32[]{:S(2)}, u32[]{:S(2)}) collective-permute-start(bf16[2048,384]{1,0:T(8,128)(2,1)S(1)} %constant_dynamic-update-slice_fusion.refs_4_.refs_5_), channel_id=1, source_target_pairs={{0,12},{4,0},{8,4},{12,8},{16,28},{20,16},{24,20},{28,24},{32,44},... | collective-permute-start | bytes 4718600 | tf_op jit(solution)/shard_map/ppermute | solution.py:324
  187.5 27.2 %collective-permute-start.36 = (bf16[1024,384]{1,0:T(8,128)(2,1)S(1)}, bf16[1024,384]{1,0:T(8,128)(2,1)S(1)}, u32[]{:S(2)}, u32[]{:S(2)}) collective-permute-start(bf16[1024,384]{1,0:T(8,128)(2,1)S(1)} %slice.71), channel_id=1, source_target_pairs={{0,16},{4,20},{8,24},{12,28},{16,32},{20,36},{24,40},{28,44},{32,4... | collective-permute-start | bytes 2359304 | tf_op jit(solution)/shard_map/ppermute | solution.py:324
  190.4 24.4 %collective-permute-start.37 = (bf16[1024,384]{1,0:T(8,128)(2,1)S(1)}, bf16[1024,384]{1,0:T(8,128)(2,1)S(1)}, u32[]{:S(2)}, u32[]{:S(2)}) collective-permute-start(bf16[1024,384]{1,0:T(8,128)(2,1)S(1)} %slice.72), channel_id=1, source_target_pairs={{0,48},{4,52},{8,56},{12,60},{16,0},{20,4},{24,8},{28,12},{32,16},... | collective-permute-start | bytes 2359304 | tf_op jit(solution)/shard_map/ppermute | solution.py:324
  193.7 21.0 %collective-permute-start.38 = (bf16[1024,384]{1,0:T(8,128)(2,1)S(1)}, bf16[1024,384]{1,0:T(8,128)(2,1)S(1)}, u32[]{:S(2)}, u32[]{:S(2)}) collective-permute-start(bf16[1024,384]{1,0:T(8,128)(2,1)S(1)} %slice.73), channel_id=1, source_target_pairs={{0,4},{4,8},{8,12},{12,0},{16,20},{20,24},{24,28},{28,16},{32,36},... | collective-permute-start | bytes 2359304 | tf_op jit(solution)/shard_map/ppermute | solution.py:324
  195.0 19.7 %collective-permute-start.39 = (bf16[1024,384]{1,0:T(8,128)(2,1)S(1)}, bf16[1024,384]{1,0:T(8,128)(2,1)S(1)}, u32[]{:S(2)}, u32[]{:S(2)}) collective-permute-start(bf16[1024,384]{1,0:T(8,128)(2,1)S(1)} %slice.74), channel_id=1, source_target_pairs={{0,12},{4,0},{8,4},{12,8},{16,28},{20,16},{24,20},{28,24},{32,44},... | collective-permute-start | bytes 2359304 | tf_op jit(solution)/shard_map/ppermute | solution.py:324
  214.8 24.7 %copy-start.1 = (f32[1,16,128,128]{3,2,1,0:T(8,128)S(1)}, f32[1,16,128,128]{3,2,1,0:T(8,128)}, u32[]{:S(2)}) copy-start(f32[1,16,128,128]{3,2,1,0:T(8,128)} %param.13) | copy-start | bytes 3145732
  222.1 14.1 %collective-permute-start.41 = (bf16[16,256]{1,0:T(8,128)(2,1)S(1)}, bf16[16,256]{1,0:T(8,128)(2,1)S(1)}, u32[]{:S(2)}, u32[]{:S(2)}) collective-permute-start(bf16[16,256]{1,0:T(8,128)(2,1)S(1)} %get-tuple-element.64), channel_id=1, source_target_pairs={{1,66},{2,65},{3,64},{0,67},{65,2},{66,1},{67,0},{64,3},{5,70},{6,... | collective-permute-start | bytes 24584 | tf_op jit(solution)/shard_map/ppermute | solution.py:382
  234.9 3.1 %collective-permute-start.42 = (bf16[16,256]{1,0:T(8,128)(2,1)S(1)}, bf16[16,256]{1,0:T(8,128)(2,1)S(1)}, u32[]{:S(2)}, u32[]{:S(2)}) collective-permute-start(bf16[16,256]{1,0:T(8,128)(2,1)S(1)} %get-tuple-element.65), channel_id=1, source_target_pairs={{0,65},{1,64},{2,67},{3,66},{64,1},{65,0},{66,3},{67,2},{4,69},{5,... | collective-permute-start | bytes 24584 | tf_op jit(solution)/shard_map/ppermute | solution.py:382
  234.9 3.1 %collective-permute-start.40 = (bf16[16,512]{1,0:T(8,128)(2,1)S(1)}, bf16[16,512]{1,0:T(8,128)(2,1)S(1)}, u32[]{:S(2)}, u32[]{:S(2)}) collective-permute-start(bf16[16,512]{1,0:T(8,128)(2,1)S(1)} %slice.88), channel_id=1, source_target_pairs={{0,64},{1,65},{2,66},{3,67},{64,0},{65,1},{66,2},{67,3},{4,68},{5,... | collective-permute-start | bytes 49160 | tf_op jit(solution)/shard_map/ppermute | solution.py:382
  234.9 3.8 %collective-permute-start.35 = (bf16[1,512,384]{2,1,0:T(8,128)(2,1)S(1)}, bf16[1,512,384]{2,1,0:T(8,128)(2,1)S(1)}, u32[]{:S(2)}, u32[]{:S(2)}) collective-permute-start(bf16[1,512,384]{2,1,0:T(8,128)(2,1)S(1)} %bitcast.61), channel_id=1, source_target_pairs={{0,64},{1,65},{2,66},{3,67},{64,0},{65,1},{66,2},{67,3},{4,68},{5,... | collective-permute-start | bytes 1179656 | tf_op jit(solution)/shard_map/ppermute | solution.py:382
